TPU v7x, 32 devices: a whole 2x2x4 slice. The times are simulated.
32 devices in a mesh: batch: 16 (over z, x, core), seq: 2 (over y).
Axes of the slice: x: 2, y: 2, z: 4, core: 2. Of those that a mesh axis runs over, the one named last changes fastest.
Arguments:
- hidden: bfloat16 [16, 448, 768], P('batch', 'seq'), may hold values from -6 to 6
- encoder: bfloat16 [16, 1536, 768], P(None, ('batch', 'seq')), may hold values from -6 to 6
- cotangent: bfloat16 [16, 448, 768], P('batch', 'seq'), may hold values from -6 to 6
- token_offsets: int32 [16], P('batch'), may hold values from 0 to 336, as said below
- token_lengths: int32 [16], P('batch'), may hold values from 112 to 448, as said below
- frame_counts: int32 [16], P('batch'), may hold values from 375 to 1500, as said below
- corpus_ids: int32 [16], P('batch'), may hold values from 0 to 8
- corpus_weights: float32 [9], replicated, may hold values from 0.25 to 4
- norm_gains: bfloat16 [768, 4], P('batch'), may hold values from 0.5 to 1.5
- norm_shifts: bfloat16 [768, 4], P('batch'), may hold values from -1 to 1
- self_in: bfloat16 [768, 2304], P('batch'), may hold values from -0.21875 to 0.21875
- self_out: bfloat16 [768, 768], P('batch'), may hold values from -0.875 to 0.875
- cross_query: bfloat16 [768, 768], P('batch'), may hold values from -0.21875 to 0.21875
- cross_kv: bfloat16 [768, 1536], P('batch'), may hold values from -0.21875 to 0.21875
- cross_out: bfloat16 [768, 768], P('batch'), may hold values from -1.25 to 1.25
- proj_bias: bfloat16 [768, 7], P('batch'), may hold values from -1 to 1
- up_weight: bfloat16 [768, 3072], P('batch'), may hold values from -0.21875 to 0.21875
- up_bias: bfloat16 [3072], P('batch'), may hold values from -1 to 1
- down_weight: bfloat16 [3072, 768], P('batch'), may hold values from -0.109375 to 0.109375
Outputs:
- layer_out: bfloat16 [16, 448, 768], P('batch', 'seq')
- grad_hidden: float32 [16, 448, 768], P('batch', 'seq')
- grad_encoder: float32 [16, 1536, 768], P(None, ('batch', 'seq'))
- grad_norm_gains: float32 [768, 4], P('batch')
- grad_norm_shifts: float32 [768, 4], P('batch')
- grad_self_in: float32 [768, 2304], P('batch')
- grad_self_out: float32 [768, 768], P('batch')
- grad_cross_query: float32 [768, 768], P('batch')
- grad_cross_kv: float32 [768, 1536], P('batch')
- grad_cross_out: float32 [768, 768], P('batch')
- grad_proj_bias: float32 [768, 7], P('batch')
- grad_up_weight: float32 [768, 3072], P('batch')
- grad_up_bias: float32 [3072], P('batch')
- grad_down_weight: float32 [3072, 768], P('batch')
Inputs may be any that keep to these rules, and one draw needn't show every extreme that they name: `token_lengths`: some sequence has exactly 448 live tokens and some exactly 112. token_offsets + token_lengths <= 448 for every sequence. The valid frames of a sequence are its first frame_counts slots; some sequence has exactly 1500.
All inputs are finite; a program needn't handle non-finite values.
Results may differ from a plain program's by a relative error of at most 0.023.
Values may be sent and summed in bfloat16 or wider, within the bound.
No kernel may reach another device: no remote copies, remote signals or barrier semaphores. Data moves between devices by JAX's collectives and lax.ppermute only.
A program may use at most 192 MiB of HBM per device.

v0:
```python
from functools import partial
import math

import jax
import jax.numpy as jnp
from jax import lax
from jax.sharding import PartitionSpec as P

HEADS = 12
HEAD_DIM = 64


EPS = 1e-05


def from_behind(block, axis, distance):
    devices = range(lax.axis_size(axis))
    route = [(i - distance, i) for i in devices if i - distance in devices]
    return lax.ppermute(block, axis, route)


def layer_parts(values):
    center = values - jnp.mean(values, axis=-1, keepdims=True)
    inv_std = lax.rsqrt(jnp.mean(center * center, axis=-1, keepdims=True) + EPS)
    return (center * inv_std, inv_std)


def layer_back(grad_side, normed, inv_std, gain):
    scaled = grad_side * gain
    mean_one = jnp.mean(scaled, axis=-1, keepdims=True)
    mean_two = jnp.mean(scaled * normed, axis=-1, keepdims=True)
    grad_in = inv_std * (scaled - mean_one - normed * mean_two)
    return (grad_in, jnp.sum(grad_side * normed, axis=(0, 1)), jnp.sum(grad_side, axis=(0, 1)))


def dot_right(left_side, weight):
    return jnp.dot(left_side, weight, preferred_element_type=jnp.float32)


def dot_left(grad_side, weight):
    return jnp.einsum("bcj,ij->bci", grad_side, weight, preferred_element_type=jnp.float32)


def weight_term(left_side, grad_side):
    return jnp.einsum("bci,bcj->ij", left_side, grad_side, preferred_element_type=jnp.float32)


def col_sum(grad_side):
    return jnp.sum(grad_side, axis=(0, 1), dtype=jnp.float32)


def head_step():
    return math.gcd(HEADS, 4)


def attend(queries, key_value, key_mask):
    seq_count, row_count, feat_width = queries.shape
    key_count = key_value.shape[1]
    heads_step = head_step()
    span_width = heads_step * HEAD_DIM
    score_scale = HEAD_DIM ** (-0.5)

    def head_block(group_index, state_pair):
        result, log_total = state_pair
        col_start = group_index * span_width
        query_heads = lax.dynamic_slice_in_dim(queries, col_start, span_width, 2).reshape(
            seq_count, row_count, heads_step, HEAD_DIM
        )
        key_heads = lax.dynamic_slice_in_dim(key_value, col_start, span_width, 2).reshape(
            seq_count, key_count, heads_step, HEAD_DIM
        )
        value_heads = lax.dynamic_slice_in_dim(
            key_value, feat_width + col_start, span_width, 2
        ).reshape(seq_count, key_count, heads_step, HEAD_DIM)
        scores = (
            jnp.einsum(
                "bqhd,bkhd->bhqk", query_heads, key_heads, preferred_element_type=jnp.float32
            )
            * score_scale
        )
        scores = jnp.where(key_mask[:, None], scores, -jnp.inf)
        row_top = jnp.max(scores, axis=-1, keepdims=True)
        exp_terms = jnp.exp(scores - row_top)
        row_total = jnp.sum(exp_terms, axis=-1, keepdims=True)
        probability = (exp_terms / row_total).astype(jnp.bfloat16)
        mixed_heads = jnp.einsum(
            "bhqk,bkhd->bqhd", probability, value_heads, preferred_element_type=jnp.float32
        )
        result = lax.dynamic_update_slice_in_dim(
            result,
            mixed_heads.reshape(seq_count, row_count, span_width).astype(jnp.bfloat16),
            col_start,
            2,
        )
        log_total = lax.dynamic_update_slice_in_dim(
            log_total, (row_top + jnp.log(row_total))[..., 0], group_index * heads_step, 1
        )
        return (result, log_total)

    start_state = (
        jnp.zeros((seq_count, row_count, feat_width), jnp.bfloat16),
        jnp.zeros((seq_count, HEADS, row_count), jnp.float32),
    )
    return lax.fori_loop(0, feat_width // span_width, head_block, start_state)


def attend_back(queries, key_value, key_mask, log_total, grad_mixed):
    seq_count, row_count, feat_width = queries.shape
    key_count = key_value.shape[1]
    heads_step = head_step()
    span_width = heads_step * HEAD_DIM
    score_scale = HEAD_DIM ** (-0.5)

    def head_block(group_index, state_pair):
        grad_queries, grad_pairs = state_pair
        col_start = group_index * span_width
        query_heads = lax.dynamic_slice_in_dim(queries, col_start, span_width, 2).reshape(
            seq_count, row_count, heads_step, HEAD_DIM
        )
        key_heads = lax.dynamic_slice_in_dim(key_value, col_start, span_width, 2).reshape(
            seq_count, key_count, heads_step, HEAD_DIM
        )
        value_heads = lax.dynamic_slice_in_dim(
            key_value, feat_width + col_start, span_width, 2
        ).reshape(seq_count, key_count, heads_step, HEAD_DIM)
        grad_heads = lax.dynamic_slice_in_dim(grad_mixed, col_start, span_width, 2).reshape(
            seq_count, row_count, heads_step, HEAD_DIM
        )
        block_total = lax.dynamic_slice_in_dim(log_total, group_index * heads_step, heads_step, 1)
        scores = (
            jnp.einsum(
                "bqhd,bkhd->bhqk", query_heads, key_heads, preferred_element_type=jnp.float32
            )
            * score_scale
        )
        probability = jnp.where(key_mask[:, None], jnp.exp(scores - block_total[..., None]), 0.0)
        grad_prob = jnp.einsum(
            "bqhd,bkhd->bhqk", grad_heads, value_heads, preferred_element_type=jnp.float32
        )
        grad_value = jnp.einsum(
            "bhqk,bqhd->bkhd",
            probability.astype(jnp.bfloat16),
            grad_heads,
            preferred_element_type=jnp.float32,
        )
        row_dot = jnp.sum(probability * grad_prob, axis=-1, keepdims=True)
        grad_scores = (probability * (grad_prob - row_dot)).astype(jnp.bfloat16)
        grad_query = (
            jnp.einsum(
                "bhqk,bkhd->bqhd", grad_scores, key_heads, preferred_element_type=jnp.float32
            )
            * score_scale
        )
        grad_key = (
            jnp.einsum(
                "bhqk,bqhd->bkhd", grad_scores, query_heads, preferred_element_type=jnp.float32
            )
            * score_scale
        )
        grad_queries = lax.dynamic_update_slice_in_dim(
            grad_queries, grad_query.reshape(seq_count, row_count, span_width), col_start, 2
        )
        grad_pairs = lax.dynamic_update_slice_in_dim(
            grad_pairs, grad_key.reshape(seq_count, key_count, span_width), col_start, 2
        )
        grad_pairs = lax.dynamic_update_slice_in_dim(
            grad_pairs,
            grad_value.reshape(seq_count, key_count, span_width),
            feat_width + col_start,
            2,
        )
        return (grad_queries, grad_pairs)

    start_state = (
        jnp.zeros((seq_count, row_count, feat_width), jnp.float32),
        jnp.zeros((seq_count, key_count, 2 * feat_width), jnp.float32),
    )
    return lax.fori_loop(0, feat_width // span_width, head_block, start_state)


def body(
    hidden,
    encoder,
    cotangent,
    token_offsets,
    token_lengths,
    frame_counts,
    corpus_ids,
    corpus_weights,
    norm_gains,
    norm_shifts,
    self_in,
    self_out,
    cross_query,
    cross_kv,
    cross_out,
    proj_bias,
    up_weight,
    up_bias,
    down_weight,
):
    (
        gains_all,
        shifts_all,
        self_in_all,
        self_out_all,
        query_all,
        kv_all,
        cross_out_all,
        bias_all,
        up_all,
        up_bias_all,
        down_all,
    ) = (
        lax.all_gather(norm_gains, "batch", axis=0, tiled=True),
        lax.all_gather(norm_shifts, "batch", axis=0, tiled=True),
        lax.all_gather(self_in, "batch", axis=0, tiled=True),
        lax.all_gather(self_out, "batch", axis=0, tiled=True),
        lax.all_gather(cross_query, "batch", axis=0, tiled=True),
        lax.all_gather(cross_kv, "batch", axis=0, tiled=True),
        lax.all_gather(cross_out, "batch", axis=0, tiled=True),
        lax.all_gather(proj_bias, "batch", axis=0, tiled=True),
        lax.all_gather(up_weight, "batch", axis=0, tiled=True),
        lax.all_gather(up_bias, "batch", axis=0, tiled=True),
        lax.all_gather(down_weight, "batch", axis=0, tiled=True),
    )
    gains = gains_all.astype(jnp.float32)
    shifts = shifts_all.astype(jnp.float32)
    biases = bias_all.astype(jnp.float32)
    seq_count, row_count, model_width = hidden.shape
    seq_index = lax.axis_index("seq")
    positions = seq_index * row_count + jnp.arange(row_count, dtype=jnp.int32)
    offsets = token_offsets[:, None]
    zero_row = jnp.zeros((model_width,), jnp.float32)
    inputs = hidden.astype(jnp.float32)
    normed_one, scale_one = layer_parts(inputs)
    act_one = (normed_one * gains[:, 0] + shifts[:, 0]).astype(jnp.bfloat16)
    qkv_bias = jnp.concatenate([biases[:, 0], zero_row, biases[:, 1]])
    qkv_local = (dot_right(act_one, self_in_all) + qkv_bias).astype(jnp.bfloat16)
    self_query = qkv_local[..., :model_width]
    pair_local = qkv_local[..., model_width:]
    pair_past = from_behind(pair_local, "seq", 1)
    self_pairs = jnp.concatenate([pair_past, pair_local], axis=1)
    key_pos = jnp.concatenate([positions - row_count, positions])[None, None, :]
    query_pos = positions[None, :, None]
    self_mask = (key_pos <= query_pos) & ((key_pos >= offsets[:, :, None]) | (key_pos == query_pos))
    self_mixed, self_total = attend(self_query, self_pairs, self_mask)
    after_self = inputs + dot_right(self_mixed, self_out_all) + biases[:, 2]
    normed_two, scale_two = layer_parts(after_self)
    act_two = (normed_two * gains[:, 1] + shifts[:, 1]).astype(jnp.bfloat16)
    cross_queries = (dot_right(act_two, query_all) + biases[:, 3]).astype(jnp.bfloat16)
    frame_half = lax.all_to_all(encoder, "batch", split_axis=0, concat_axis=1, tiled=True)
    kv_bias = jnp.concatenate([zero_row, biases[:, 4]])
    half_pairs = (dot_right(frame_half, kv_all) + kv_bias).astype(jnp.bfloat16)
    cross_pairs = lax.all_gather(half_pairs, "seq", axis=1, tiled=True)
    half_slots = frame_half.shape[1]
    owner_frames = encoder.shape[1]
    gathered = jnp.arange(lax.axis_size("seq") * half_slots, dtype=jnp.int32)
    half_index = gathered // half_slots
    within = gathered % half_slots
    frame_ids = (
        within // owner_frames * lax.axis_size("seq") + half_index
    ) * owner_frames + within % owner_frames
    frame_mask = frame_ids[None, None, :] < frame_counts[:, None, None]
    cross_mixed, cross_total = attend(cross_queries, cross_pairs, frame_mask)
    after_cross = after_self + dot_right(cross_mixed, cross_out_all) + biases[:, 5]
    normed_three, scale_three = layer_parts(after_cross)
    act_three = (normed_three * gains[:, 2] + shifts[:, 2]).astype(jnp.bfloat16)
    up_value = dot_right(act_three, up_all) + up_bias_all.astype(jnp.float32)
    gelu_value, gelu_pull = jax.vjp(partial(jax.nn.gelu, approximate=False), up_value)
    hidden_act = gelu_value.astype(jnp.bfloat16)
    after_mlp = after_cross + dot_right(hidden_act, down_all) + biases[:, 6]
    normed_last, scale_last = layer_parts(after_mlp)
    result = (normed_last * gains[:, 3] + shifts[:, 3]).astype(jnp.bfloat16)
    corpus_match = (
        corpus_ids[:, None] == jnp.arange(corpus_weights.shape[0], dtype=jnp.int32)[None, :]
    )
    seq_weight = jnp.sum(jnp.where(corpus_match, corpus_weights[None, :], 0.0), axis=1)
    live_rows = (positions[None, :] >= offsets) & (
        positions[None, :] < offsets + token_lengths[:, None]
    )
    grad_out = (
        cotangent.astype(jnp.float32) * jnp.where(live_rows, seq_weight[:, None], 0.0)[..., None]
    )
    grad_mlp, gain_last, shift_last = layer_back(grad_out, normed_last, scale_last, gains[:, 3])
    grad_down = grad_mlp.astype(jnp.bfloat16)
    down_term = weight_term(hidden_act, grad_down)
    down_bias = col_sum(grad_down)
    grad_act = dot_left(grad_down, down_all)
    grad_up = gelu_pull(grad_act)[0].astype(jnp.bfloat16)
    up_term = weight_term(act_three, grad_up)
    up_bias_term = col_sum(grad_up)
    back_three, gain_three, shift_three = layer_back(
        dot_left(grad_up, up_all), normed_three, scale_three, gains[:, 2]
    )
    grad_cross = grad_mlp + back_three
    grad_cross_in = grad_cross.astype(jnp.bfloat16)
    cross_out_term = weight_term(cross_mixed, grad_cross_in)
    cross_out_bias = col_sum(grad_cross_in)
    grad_cross_mixed = dot_left(grad_cross_in, cross_out_all).astype(jnp.bfloat16)
    grad_cross_query, grad_cross_pairs = attend_back(
        cross_queries, cross_pairs, frame_mask, cross_total, grad_cross_mixed
    )
    half_grads = lax.psum_scatter(
        grad_cross_pairs.astype(jnp.bfloat16), "seq", scatter_dimension=1, tiled=True
    )
    kv_term = weight_term(frame_half, half_grads)
    kv_bias_term = col_sum(half_grads[..., model_width:])
    owner_grads = dot_left(half_grads, kv_all)
    grad_encoder = lax.all_to_all(
        owner_grads.astype(jnp.bfloat16), "batch", split_axis=1, concat_axis=0, tiled=True
    ).astype(owner_grads.dtype)
    grad_cq = grad_cross_query.astype(jnp.bfloat16)
    query_term = weight_term(act_two, grad_cq)
    query_bias = col_sum(grad_cq)
    back_two, gain_two, shift_two = layer_back(
        dot_left(grad_cq, query_all), normed_two, scale_two, gains[:, 1]
    )
    grad_self = grad_cross + back_two
    grad_self_in = grad_self.astype(jnp.bfloat16)
    self_out_term = weight_term(self_mixed, grad_self_in)
    self_out_bias = col_sum(grad_self_in)
    grad_self_mixed = dot_left(grad_self_in, self_out_all).astype(jnp.bfloat16)
    grad_self_query, grad_self_pairs = attend_back(
        self_query, self_pairs, self_mask, self_total, grad_self_mixed
    )
    returned = from_behind(grad_self_pairs[:, :row_count].astype(jnp.bfloat16), "seq", -1).astype(
        jnp.float32
    )
    grad_pair_local = grad_self_pairs[:, row_count:] + returned
    grad_qkv = jnp.concatenate([grad_self_query, grad_pair_local], axis=-1).astype(jnp.bfloat16)
    qkv_term = weight_term(act_one, grad_qkv)
    qkv_sums = col_sum(grad_qkv)
    back_one, gain_one, shift_one = layer_back(
        dot_left(grad_qkv, self_in_all), normed_one, scale_one, gains[:, 0]
    )
    grad_hidden = grad_self + back_one
    gain_term = jnp.stack([gain_one, gain_two, gain_three, gain_last], axis=1)
    shift_term = jnp.stack([shift_one, shift_two, shift_three, shift_last], axis=1)
    bias_term = jnp.stack(
        [
            qkv_sums[:model_width],
            qkv_sums[2 * model_width :],
            self_out_bias,
            query_bias,
            kv_bias_term,
            cross_out_bias,
            down_bias,
        ],
        axis=1,
    )
    summed = (
        lax.psum_scatter(gain_term, "batch", scatter_dimension=0, tiled=True),
        lax.psum_scatter(shift_term, "batch", scatter_dimension=0, tiled=True),
        lax.psum_scatter(qkv_term, "batch", scatter_dimension=0, tiled=True),
        lax.psum_scatter(self_out_term, "batch", scatter_dimension=0, tiled=True),
        lax.psum_scatter(query_term, "batch", scatter_dimension=0, tiled=True),
        lax.psum_scatter(kv_term, "batch", scatter_dimension=0, tiled=True),
        lax.psum_scatter(cross_out_term, "batch", scatter_dimension=0, tiled=True),
        lax.psum_scatter(bias_term, "batch", scatter_dimension=0, tiled=True),
        lax.psum_scatter(up_term, "batch", scatter_dimension=0, tiled=True),
        lax.psum_scatter(up_bias_term, "batch", scatter_dimension=0, tiled=True),
        lax.psum_scatter(down_term, "batch", scatter_dimension=0, tiled=True),
    )
    summed = (
        lax.psum(summed[0].astype(jnp.bfloat16), "seq").astype(jnp.float32),
        lax.psum(summed[1].astype(jnp.bfloat16), "seq").astype(jnp.float32),
        lax.psum(summed[2].astype(jnp.bfloat16), "seq").astype(jnp.float32),
        lax.psum(summed[3].astype(jnp.bfloat16), "seq").astype(jnp.float32),
        lax.psum(summed[4].astype(jnp.bfloat16), "seq").astype(jnp.float32),
        lax.psum(summed[5].astype(jnp.bfloat16), "seq").astype(jnp.float32),
        lax.psum(summed[6].astype(jnp.bfloat16), "seq").astype(jnp.float32),
        lax.psum(summed[7].astype(jnp.bfloat16), "seq").astype(jnp.float32),
        lax.psum(summed[8].astype(jnp.bfloat16), "seq").astype(jnp.float32),
        lax.psum(summed[9].astype(jnp.bfloat16), "seq").astype(jnp.float32),
        lax.psum(summed[10].astype(jnp.bfloat16), "seq").astype(jnp.float32),
    )
    return (
        result,
        grad_hidden,
        grad_encoder,
        summed[0],
        summed[1],
        summed[2],
        summed[3],
        summed[4],
        summed[5],
        summed[6],
        summed[7],
        summed[8],
        summed[9],
        summed[10],
    )


def solution(mesh):
    in_specs = (
        P("batch", "seq", None),
        P(None, ("batch", "seq"), None),
        P("batch", "seq", None),
        P("batch"),
        P("batch"),
        P("batch"),
        P("batch"),
        P(),
        P("batch", None),
        P("batch", None),
        P("batch", None),
        P("batch", None),
        P("batch", None),
        P("batch", None),
        P("batch", None),
        P("batch", None),
        P("batch", None),
        P("batch"),
        P("batch", None),
    )
    out_specs = (
        P("batch", "seq", None),
        P("batch", "seq", None),
        P(None, ("batch", "seq"), None),
        P("batch", None),
        P("batch", None),
        P("batch", None),
        P("batch", None),
        P("batch", None),
        P("batch", None),
        P("batch", None),
        P("batch", None),
        P("batch", None),
        P("batch"),
        P("batch", None),
    )
    return jax.shard_map(body, mesh=mesh, in_specs=in_specs, out_specs=out_specs, check_vma=False)
```

profile of v0, /device:TPU:0, one launch (start us, length us, event | category | flops | bytes accessed | tf_op | source)
XLA Modules:
  0.0 1395.9 jit_solution(15837638674551797385)
XLA Ops:
  9.4 7.4 all-to-all-start
  17.4 40.0 %all-gather.3 = bf16[16,48,7]{1,2,0:T(8,128)(2,1)S(1)} all-gather(bf16[1,48,7]{1,2,0:T(8,128)(2,1)S(1)} %bitcast.414), channel_id=1, replica_groups=mesh['batch'=16,'seq'=2] {'batch'}, dimensions={0}, use_global_device_ids=true | all-gather | bytes 11424 | tf_op jit(solution)/shard_map/all_gather | solution.py:222
  58.2 8.3 all-gather.17.cloned.1.call-done
  72.9 19.2 %all-gather.1 = bf16[16,48,4]{1,2,0:T(4,128)(2,1)S(1)} all-gather(bf16[1,48,4]{1,2,0:T(4,128)(2,1)S(1)} %bitcast.415), channel_id=1, replica_groups=mesh['batch'=16,'seq'=2] {'batch'}, dimensions={0}, use_global_device_ids=true | all-gather | bytes 6528 | tf_op jit(solution)/shard_map/all_gather | solution.py:215
  92.2 17.5 %all-gather.2 = bf16[16,48,4]{1,2,0:T(4,128)(2,1)S(1)} all-gather(bf16[1,48,4]{1,2,0:T(4,128)(2,1)S(1)} %bitcast.416), channel_id=1, replica_groups=mesh['batch'=16,'seq'=2] {'batch'}, dimensions={0}, use_global_device_ids=true | all-gather | bytes 6528 | tf_op jit(solution)/shard_map/all_gather | solution.py:216
  124.5 32.1 %all-reduce.1 = bf16[3072]{0:T(1024)(128)(2,1)S(1)} all-reduce(bf16[3072]{0:T(1024)(128)(2,1)S(1)} %dynamic-update-slice), channel_id=1, replica_groups=mesh['batch'=16,'seq'=2] {'batch'}, use_global_device_ids=true, to_apply=%add.1 | all-reduce | flops 3072 | bytes 12288
  165.2 21.0 %while.72 = (s32[]{:T(128)}, bf16[1,224,768]{1,2,0:T(8,128)(2,1)}, f32[1,12,224]{2,1,0:T(8,128)}, bf16[1,448,1536]{1,2,0:T(8,128)(2,1)S(1)}, bf16[1,224,768]{1,2...) while((s32[]{:T(128)}, bf16[1,224,768]{1,2,0:T(8,128)(2,1)}, ...), condition=%wide.region_5.6_spmd.clone, body=%wide.region_2.5_spmd.clone.sunk | while | flops 108035208 | bytes 7331712 | solution.py:104
  196.1 61.6 %all-gather.27.cloned.1.call-done = bf16[1536,1536]{1,0:T(8,128)(2,1)} async-done(((bf16[768,1536]{1,0:T(8,128)(2,1)}), bf16[1536,1536]{1,0:T(8,128)(2,1)}) %all-gather.27.cloned.1.call-update) | async-done | bytes 4718608 | tf_op jit(solution)/shard_map/all_gather | solution.py:255
  257.8 6.6 copy.81
  264.4 32.9 %while.73 = (s32[]{:T(128)}, bf16[1,224,768]{1,2,0:T(8,128)(2,1)S(1)}, f32[1,12,224]{2,1,0:T(8,128)S(1)}, bf16[1,1536,1536]{1,2,0:T(8,128)(2,1)}, bf16[1,224,768...) while((s32[]{:T(128)}, ...), condition=%wide.region_11.12_spmd.clone, body=%wide.region_8.11_spmd.clone.sunk | while | flops 368937600 | bytes 44011340 | solution.py:104
  300.3 52.4 %all-gather.23.cloned.1.call-done = bf16[768,3072]{1,0:T(8,128)(2,1)} async-done(((bf16[48,3072]{1,0:T(8,128)(2,1)}), bf16[768,3072]{1,0:T(8,128)(2,1)}) %all-gather.23.cloned.1.call-update) | async-done | bytes 4718608 | tf_op jit(solution)/shard_map/all_gather | solution.py:223
  352.8 10.5 multiply_convert_fusion.2
  363.3 43.5 %all-gather.25.cloned.1.call-done = bf16[3072,768]{1,0:T(8,128)(2,1)} async-done(((bf16[192,768]{1,0:T(8,128)(2,1)}), bf16[3072,768]{1,0:T(8,128)(2,1)}) %all-gather.25.cloned.1.call-update) | async-done | bytes 4718608 | tf_op jit(solution)/shard_map/all_gather | solution.py:225
  424.9 48.8 %while.74 = (s32[]{:T(128)}, bf16[1,224,768]{1,2,0:T(8,128)(2,1)S(1)}, bf16[1,1536,1536]{1,2,0:T(8,128)(2,1)}, bf16[1,1536,1536]{1,2,0:T(8,128)(2,1)}, bf16[1,22...) while((s32[]{:T(128)}, ...), condition=%wide.region_23.24_spmd.clone, body=%wide.region_21.23_spmd.clone.sunk | while | flops 894134912 | bytes 69571448 | solution.py:178
  488.6 23.2 %while.75 = (s32[]{:T(128)}, bf16[1,224,768]{2,1,0:T(8,128)(2,1)S(1)}, f32[1,448,1536]{1,2,0:T(8,128)}, bf16[1,448,1536]{1,2,0:T(8,128)(2,1)}, bf16[1,224,768]{1...) while((s32[]{:T(128)}, ...), condition=%wide.region_28.29_spmd.clone, body=%wide.region_26.28_spmd.clone.sunk | while | flops 261143680 | bytes 21226452 | solution.py:178
  518.9 26.9 %collective-permute-done.1 = bf16[1,224,1536]{2,1,0:T(8,128)(2,1)S(1)} collective-permute-done((bf16[1,224,1536]{2,1,0:T(8,128)(2,1)S(1)}, bf16[1,224,1536]{2,1,0:T(8,128)(2,1)S(1)}, u32[]{:S(2)}, u32[]{:S(2)}) %collective-permute-start.1) | collective-permute-done | bytes 688160 | tf_op jit(solution)/shard_map/ppermute | solution.py:19
  553.9 5.2 fusion.120
  560.7 5.1 fusion.100
  567.1 5.8 convolution_bitcast_fusion
  572.9 6.6 copy.98
  587.6 8.9 reduce.102
  600.5 5.7 all-to-all-start.1
  616.3 65.4 %reduce-scatter.24.cloned.1.call-done = f32[48,768]{1,0:T(8,128)} async-done(((f32[768,768]{1,0:T(8,128)}), f32[48,768]{1,0:T(8,128)}) %reduce-scatter.24.cloned.1.call-update) | async-done | bytes 147472 | tf_op jit(solution)/shard_map/reduce_scatter | solution.py:356
  683.2 64.6 %reduce-scatter.28.cloned.1.call-done = f32[48,768]{1,0:T(8,128)} async-done(((f32[768,768]{1,0:T(8,128)}), f32[48,768]{1,0:T(8,128)}) %reduce-scatter.28.cloned.1.call-update) | async-done | bytes 147472 | tf_op jit(solution)/shard_map/reduce_scatter | solution.py:359
  749.3 91.6 %reduce-scatter.22.cloned.1.call-done = f32[48,2304]{1,0:T(8,128)} async-done(((f32[768,2304]{1,0:T(8,128)}), f32[48,2304]{1,0:T(8,128)}) %reduce-scatter.22.cloned.1.call-update) | async-done | bytes 442384 | tf_op jit(solution)/shard_map/reduce_scatter | solution.py:355
  842.7 113.7 %reduce-scatter.30.cloned.1.call-done = f32[48,3072]{1,0:T(8,128)} async-done(((f32[768,3072]{1,0:T(8,128)}), f32[48,3072]{1,0:T(8,128)}) %reduce-scatter.30.cloned.1.call-update) | async-done | bytes 589840 | tf_op jit(solution)/shard_map/reduce_scatter | solution.py:361
  958.1 113.2 %reduce-scatter.32.cloned.1.call-done = f32[192,768]{1,0:T(8,128)} async-done(((f32[3072,768]{1,0:T(8,128)}), f32[192,768]{1,0:T(8,128)}) %reduce-scatter.32.cloned.1.call-update) | async-done | bytes 589840 | tf_op jit(solution)/shard_map/reduce_scatter | solution.py:363
  1073.2 77.8 %reduce-scatter.38.cloned.1.call-done = f32[48,1536]{1,0:T(8,128)} async-done(((f32[768,1536]{1,0:T(8,128)}), f32[48,1536]{1,0:T(8,128)}) %reduce-scatter.38.cloned.1.call-update) | async-done | bytes 294928
  1153.4 58.2 %all-reduce.2 = bf16[3072]{0:T(1024)(128)(2,1)S(1)} all-reduce(f32[3072]{0:T(1024)S(1)} %copy-done.66), channel_id=13, replica_groups=mesh['batch'=16,'seq'=2] {'batch'}, use_global_device_ids=true, to_apply=%region_65.66.clone | all-reduce | flops 3072 | bytes 18432
  1213.6 54.9 %reduce-scatter.34.cloned.1.call-done = f32[48,4]{1,0:T(8,128)} async-done(((f32[768,4]{1,0:T(8,128)}), f32[48,4]{1,0:T(8,128)}) %reduce-scatter.34.cloned.1.call-update) | async-done | bytes 784
  1269.4 57.9 %reduce-scatter.40.cloned.1.call-done = f32[48,7]{1,0:T(8,128)} async-done(((f32[768,7]{1,0:T(8,128)}), f32[48,7]{1,0:T(8,128)}) %reduce-scatter.40.cloned.1.call-update) | async-done | bytes 1360
  1341.5 38.1 %all-reduce.7.cloned.1.call-done = (bf16[48,1536]{0,1:T(8,128)(2,1)}, bf16[48,2304]{1,0:T(8,128)(2,1)}, bf16[48,768]{1,0:T(8,128)(2,1)}, bf16[48,768]{1,0:T(8,12...) async-done(((bf16[48,1536]{0,1:T(8,128)(2,1)}, bf16[48,2304]{1,0:T(8,128)(2,1)}, bf16[48,768]{1,0:T(8,128)(2,1)}, ...) | async-done | bytes 1179664 | tf_op jit(solution)/shard_map/psum | solution.py:371
  (527 shorter events, 277.3 us)
Async XLA Ops:
  7.2 59.2 %all-gather.17.cloned.1.call-start = ((), (), s32[]{:S(2)}) async-start(), calls=%async_computation.15 | async-start | bytes 2506752 | tf_op jit(solution)/shard_map/all_gather | solution.py:220
  7.9 106.9 %all-gather.13.cloned.1.call-start = ((), (), s32[]{:S(2)}) async-start(), calls=%async_computation.13 | async-start | bytes 3760128 | tf_op jit(solution)/shard_map/all_gather | solution.py:217
  8.7 177.6 %all-gather.15.cloned.1.call-start = ((), (), s32[]{:S(2)}) async-start(), calls=%async_computation.14 | async-start | bytes 1253376 | tf_op jit(solution)/shard_map/all_gather | solution.py:218
  9.4 48.8 %all-to-all-start = ((bf16[16,48,768]{2,1,0:T(8,128)(2,1)}), bf16[16,48,768]{2,1,0:T(8,128)(2,1)S(1)}, u32[]{:S(2)}, u32[]{:S(2)}) async-start(bf16[16,48,768]{2,1,0:T(8,128)(2,1)} %param.28), calls=%async_computation | async-start | bytes 2359296 | tf_op jit(solution)/shard_map/all_to_all | solution.py:252
  16.8 177.4 %all-gather.19.cloned.1.call-start = ((), (), s32[]{:S(2)}) async-start(), calls=%async_computation.16 | async-start | bytes 1253376 | tf_op jit(solution)/shard_map/all_gather | solution.py:219
  17.4 240.4 %all-gather.27.cloned.1.call-start = ((), (), s32[]{:S(2)}) async-start(), calls=%async_computation.27 | async-start | bytes 7077888 | tf_op jit(solution)/shard_map/all_gather | solution.py:255
  71.5 226.7 %all-gather.21.cloned.1.call-start = ((), (), s32[]{:S(2)}) async-start(), calls=%async_computation.17 | async-start | bytes 1253376 | tf_op jit(solution)/shard_map/all_gather | solution.py:221
  72.1 280.6 %all-gather.23.cloned.1.call-start = ((), (), s32[]{:S(2)}) async-start(), calls=%async_computation.18 | async-start | bytes 5013504 | tf_op jit(solution)/shard_map/all_gather | solution.py:223
  72.9 334.0 %all-gather.25.cloned.1.call-start = ((), (), s32[]{:S(2)}) async-start(), calls=%async_computation.19 | async-start | bytes 5013504 | tf_op jit(solution)/shard_map/all_gather | solution.py:225
  110.5 83.6 %copy-start.37 = (f32[768]{0:T(1024)}, f32[768]{0:T(1024)S(1)}, u32[]{:S(2)}) copy-start(f32[768]{0:T(1024)S(1)} %get-tuple-element.1142) | copy-start | bytes 9220
  118.0 43.5 %collective-permute-start = (bf16[1,224,1536]{2,1,0:T(8,128)(2,1)S(1)}, bf16[1,224,1536]{2,1,0:T(8,128)(2,1)}, u32[]{:S(2)}, u32[]{:S(2)}) collective-permute-start(bf16[1,224,1536]{2,1,0:T(8,128)(2,1)S(1)} %slice.97), channel_id=1, source_target_pairs={{0,1},{2,3},{4,5},{6,7},{8,9},{10,11},{12,13},{14,15},{16,17},{18,... | collective-permute-start | bytes 2064392 | tf_op jit(solution)/shard_map/ppermute | solution.py:19
  122.3 443.7 %reduce-scatter.20.cloned.1.call-start = ((), (), s32[]{:S(2)}) async-start(), calls=%async_computation.20 | async-start | bytes 7077888 | tf_op jit(solution)/shard_map/reduce_scatter | solution.py:304
  188.8 75.5 %copy-start.45 = (f32[224]{0:T(256)}, f32[224]{0:T(256)S(1)}, u32[]{:S(2)}) copy-start(f32[224]{0:T(256)S(1)} %broadcast_multiply_fusion.10) | copy-start | bytes 2692
  189.1 75.3 %copy-start.49 = (f32[224]{0:T(256)}, f32[224]{0:T(256)S(1)}, u32[]{:S(2)}) copy-start(f32[224]{0:T(256)S(1)} %add_rsqrt_fusion.2) | copy-start | bytes 2692
  297.4 66.0 %copy-start.16 = (bf16[1,224,768]{1,2,0:T(8,128)(2,1)}, bf16[1,224,768]{1,2,0:T(8,128)(2,1)S(1)}, u32[]{:S(2)}) copy-start(bf16[1,224,768]{1,2,0:T(8,128)(2,1)S(1)} %get-tuple-element.723) | copy-start | bytes 1032196
  297.4 55.4 %copy-start.67 = (f32[3072]{0:T(1024)S(1)}, f32[3072]{0:T(1024)}, u32[]{:S(2)}) copy-start(f32[3072]{0:T(1024)} %convert_element_type.340) | copy-start | bytes 36868
  300.1 119.2 %copy-start.4 = (f32[1,224,768]{2,1,0:T(8,128)}, f32[1,224,768]{2,1,0:T(8,128)S(1)}, u32[]{:S(2)}) copy-start(f32[1,224,768]{2,1,0:T(8,128)S(1)} %get-tuple-element.1132) | copy-start | bytes 2064388
  300.3 119.0 %copy-start.64 = (f32[224]{0:T(256)}, f32[224]{0:T(256)S(1)}, u32[]{:S(2)}) copy-start(f32[224]{0:T(256)S(1)} %add_rsqrt_fusion.1) | copy-start | bytes 2692
  473.8 140.9 %reduce-scatter.26.cloned.1.call-start = ((), (), s32[]{:S(2)}) async-start(), calls=%async_computation.23 | async-start | bytes 2506752 | tf_op jit(solution)/shard_map/reduce_scatter | solution.py:357
  476.6 205.1 %reduce-scatter.24.cloned.1.call-start = ((), (), s32[]{:S(2)}) async-start(), calls=%async_computation.22 | async-start | bytes 2506752 | tf_op jit(solution)/shard_map/reduce_scatter | solution.py:356
  483.9 263.9 %reduce-scatter.28.cloned.1.call-start = ((), (), s32[]{:S(2)}) async-start(), calls=%async_computation.24 | async-start | bytes 2506752 | tf_op jit(solution)/shard_map/reduce_scatter | solution.py:359
  485.9 355.0 %reduce-scatter.22.cloned.1.call-start = ((), (), s32[]{:S(2)}) async-start(), calls=%async_computation.21 | async-start | bytes 7520256 | tf_op jit(solution)/shard_map/reduce_scatter | solution.py:355
  517.6 28.2 %collective-permute-start.1 = (bf16[1,224,1536]{2,1,0:T(8,128)(2,1)S(1)}, bf16[1,224,1536]{2,1,0:T(8,128)(2,1)S(1)}, u32[]{:S(2)}, u32[]{:S(2)}) collective-permute-start(bf16[1,224,1536]{2,1,0:T(8,128)(2,1)S(1)} %slice.135), channel_id=1, source_target_pairs={{1,0},{3,2},{5,4},{7,6},{9,8},{11,10},{13,12},{15,14},{17,16},{19,... | collective-permute-start | bytes 2064392 | tf_op jit(solution)/shard_map/ppermute | solution.py:19
  552.4 404.0 %reduce-scatter.30.cloned.1.call-start = ((), (), s32[]{:S(2)}) async-start(), calls=%async_computation.25 | async-start | bytes 10027008 | tf_op jit(solution)/shard_map/reduce_scatter | solution.py:361
  559.1 512.2 %reduce-scatter.32.cloned.1.call-start = ((), (), s32[]{:S(2)}) async-start(), calls=%async_computation.26 | async-start | bytes 10027008 | tf_op jit(solution)/shard_map/reduce_scatter | solution.py:363
  565.9 585.1 %reduce-scatter.38.cloned.1.call-start = ((), (), s32[]{:S(2)}) async-start(), calls=%async_computation.30 | async-start | bytes 5013504
  600.5 734.9 %all-to-all-start.1 = ((bf16[16,2,18432]{2,1,0:T(2,128)(2,1)}), bf16[16,2,18432]{2,1,0:T(2,128)(2,1)}, u32[]{:S(2)}, u32[]{:S(2)}) async-start(bf16[16,2,18432]{2,1,0:T(2,128)(2,1)} %reshape.1345), calls=%async_computation.2 | async-start | bytes 2359296 | tf_op jit(solution)/shard_map/all_to_all | solution.py:310
  606.3 606.5 %reduce-scatter.36.cloned.1.call-start = ((), (), s32[]{:S(2)}) async-start(), calls=%async_computation.29 | async-start | bytes 417792
  610.8 657.7 %reduce-scatter.34.cloned.1.call-start = ((), (), s32[]{:S(2)}) async-start(), calls=%async_computation.28 | async-start | bytes 417792
  612.1 715.2 %reduce-scatter.40.cloned.1.call-start = ((), (), s32[]{:S(2)}) async-start(), calls=%async_computation.31 | async-start | bytes 417792
  614.6 538.8 %copy-start.66 = (f32[3072]{0:T(1024)S(1)}, f32[3072]{0:T(1024)}, u32[]{:S(2)}) copy-start(f32[3072]{0:T(1024)} %get-tuple-element.1139) | copy-start | bytes 36868
  614.7 764.9 %all-reduce.7.cloned.1.call-start = ((), (), s32[]{:S(2)}) async-start(), calls=%async_computation.32 | async-start | bytes 2850816 | tf_op jit(solution)/shard_map/psum | solution.py:371
  (88 other events, 695.8 us)
Sparse Core Ops, SparseCore 0:
  10.3 56.0 all-gather.16
  68.7 46.0 all-gather.12
  117.1 37.5 all-gather.14
  156.8 37.2 all-gather.18
  196.1 61.6 all-gather.26
  259.9 38.3 all-gather.20
  300.5 52.1 all-gather.22
  355.0 51.7 all-gather.24
  473.9 67.2 reduce-scatter.19
  545.3 65.3 reduce-scatter.25
  615.0 66.6 reduce-scatter.23
  685.8 61.9 reduce-scatter.27
  751.8 89.0 reduce-scatter.21
  845.4 110.8 reduce-scatter.29
  960.3 111.0 reduce-scatter.31
  1075.6 75.3 reduce-scatter.37
  1154.9 54.6 reduce-scatter.35
  1213.9 54.6 reduce-scatter.33
  1272.6 54.6 reduce-scatter.39
  1331.3 48.2 all-reduce.6
where the time goes:
time: 1400 us
  waiting for transfers between devices  884 us (63%)
  blocking collectives  172 us (12%)
  matrix products  136 us (10%)
  local copies, waits for them, and re-layouts  106 us (8%)
  other arithmetic  59.3 us (4%)
  starting transfers between devices  19.7 us (1%)
  between operations  18.9 us (1%)
    unnamed x24, waiting for transfers between devices  195 us
    reduce_scatter x1, waiting for transfers between devices, body(): lax.psum_scatter(up_term, 'batch', scatter_dimension=0, tiled=True)  114 us
    reduce_scatter x1, waiting for transfers between devices, body(): lax.psum_scatter(down_term, 'batch', scatter_dimension=0, tiled=True)  113 us
    reduce_scatter x1, waiting for transfers between devices, body(): lax.psum_scatter(qkv_term, 'batch', scatter_dimension=0, tiled=True)  91.6 us
    unnamed x2, blocking collectives  90.3 us
    reduce_scatter x1, waiting for transfers between devices, body(): lax.psum_scatter(self_out_term, 'batch', scatter_dimension=0, tiled=True)  65.4 us
    reduce_scatter x1, waiting for transfers between devices, body(): lax.psum_scatter(cross_out_term, 'batch', scatter_dimension=0, tiled=True)  64.6 us
    all_gather x1, waiting for transfers between devices, body(): cross_pairs = lax.all_gather(half_pairs, 'seq', axis=1, tiled=True)  61.6 us
  transfers between devices with their start and end apart: 24, of which 17 were waited for; matrix products, arithmetic and copies ran while one was open for 15% of the time, Pallas kernels for 0%

commit v1 on v0

--- a/solution.py
+++ b/solution.py
@@ -4,6 +4,8 @@
 import jax
 import jax.numpy as jnp
 from jax import lax
+from jax.experimental import pallas as pl
+from jax.experimental.pallas import tpu as pltpu
 from jax.sharding import PartitionSpec as P
 
 HEADS = 12
@@ -11,12 +13,6 @@
 
 
 EPS = 1e-05
-
-
-def from_behind(block, axis, distance):
-    devices = range(lax.axis_size(axis))
-    route = [(i - distance, i) for i in devices if i - distance in devices]
-    return lax.ppermute(block, axis, route)
 
 
 def layer_parts(values):
@@ -176,6 +172,137 @@
         jnp.zeros((seq_count, key_count, 2 * feat_width), jnp.float32),
     )
     return lax.fori_loop(0, feat_width // span_width, head_block, start_state)
+
+
+CORES = 2
+PAIR = 2
+FLIP = [(0, 1), (1, 0)]
+
+
+def partners(stride, radix, step):
+    pairs = []
+    for i in range(lax.axis_size("batch")):
+        digit = i // stride % radix
+        pairs.append((i, i + ((digit ^ step) - digit) * stride))
+    return pairs
+
+
+def swap(block, stride, radix=2, step=1):
+    return lax.ppermute(block, "batch", partners(stride, radix, step))
+
+
+def swap_seq(block):
+    return lax.ppermute(block, "seq", FLIP)
+
+
+def place_of():
+    batch = lax.axis_index("batch")
+    return (
+        batch // (CORES * PAIR),
+        batch // CORES % PAIR,
+        batch % CORES,
+        lax.axis_index("seq"),
+    )
+
+
+def splits(rows):
+    depth = lax.axis_size("batch") // (CORES * PAIR)
+    return rows % 48 == 0 and depth == 4 and lax.axis_size("seq") == 2
+
+
+def place_kernel(where_ref, *refs, depth, rows):
+    pieces, out_ref, sem = refs[:8], refs[8], refs[9]
+    third = rows // 3
+    deep, wide, core, seq = where_ref[0], where_ref[1], where_ref[2], where_ref[3]
+    started = []
+    for c in range(2):
+        column, across, side, side_across = pieces[4 * c : 4 * c + 4]
+        for w, (body, edge) in enumerate(((column, side), (across, side_across))):
+            for k in range(depth):
+                base = (((deep ^ k) * PAIR + (wide ^ w)) * CORES + (core ^ c)) * rows
+                for source, start, count in (
+                    (body, base + seq * third, 2 * third),
+                    (edge, base + (1 - seq) * 2 * third, third),
+                ):
+                    copy = pltpu.make_async_copy(
+                        source.at[k], out_ref.at[pl.ds(pl.multiple_of(start, 16), count)], sem
+                    )
+                    copy.start()
+                    started.append(copy)
+    for copy in started:
+        copy.wait()
+
+
+def gather_rows(shard):
+    rows, cols = shard.shape
+    if not splits(rows):
+        return lax.all_gather(shard, "batch", axis=0, tiled=True)
+    third = rows // 3
+    size = lax.axis_size("batch")
+    depth = size // (CORES * PAIR)
+    deep, wide, core, seq = place_of()
+    part = lax.dynamic_slice_in_dim(shard, seq * third, 2 * third, 0)
+    column = jnp.stack(
+        [part] + [swap(part, CORES * PAIR, depth, k) for k in range(1, depth)]
+    )
+    across = swap(column, CORES)
+    side = swap_seq(lax.dynamic_slice_in_dim(column, seq * third, third, 1))
+    side_across = swap_seq(lax.dynamic_slice_in_dim(across, seq * third, third, 1))
+    mine = (column, across, side, side_across)
+    other = tuple(swap(piece, 1) for piece in mine)
+    total = size * rows
+    return pl.pallas_call(
+        partial(place_kernel, depth=depth, rows=rows),
+        out_shape=jax.ShapeDtypeStruct((total, cols), shard.dtype),
+        in_specs=[pl.BlockSpec(memory_space=pltpu.SMEM)]
+        + [pl.BlockSpec(memory_space=pl.ANY)] * 8,
+        out_specs=pl.BlockSpec(memory_space=pltpu.VMEM),
+        scratch_shapes=[pltpu.SemaphoreType.DMA],
+        cost_estimate=pl.CostEstimate(
+            flops=0, transcendentals=0, bytes_accessed=4 * total * cols
+        ),
+        name="place_rows",
+    )(jnp.stack([deep, wide, core, seq]).astype(jnp.int32), *mine, *other)
+
+
+def narrow(values):
+    return lax.reduce_precision(values, 8, 7).astype(jnp.bfloat16)
+
+
+def reduce_rows(grads):
+    size = lax.axis_size("batch")
+    rows, cols = grads.shape[0] // size, grads.shape[1]
+    grads = grads.astype(jnp.bfloat16)
+    if not splits(rows):
+        mine = lax.psum_scatter(grads, "batch", scatter_dimension=0, tiled=True)
+        return lax.psum(mine, "seq").astype(jnp.float32)
+    third = rows // 3
+    depth = size // (CORES * PAIR)
+    deep, wide, core, seq = place_of()
+    grid = grads.reshape(depth, PAIR, CORES, rows, cols)
+    pick = lax.dynamic_index_in_dim
+    came = swap(pick(grid, 1 - core, 2, keepdims=False), 1)
+    chip = pick(grid, core, 2, keepdims=False).astype(jnp.float32) + came.astype(jnp.float32)
+    edge = lax.dynamic_slice_in_dim(chip, (1 - seq) * 2 * third, third, 2)
+    came = swap_seq(edge.astype(jnp.bfloat16)).astype(jnp.float32)
+    kept = lax.dynamic_slice_in_dim(chip, seq * third, 2 * third, 2)
+    blank = jnp.zeros_like(came)
+    kept = kept + jnp.where(
+        seq == 0, jnp.concatenate([came, blank], axis=2), jnp.concatenate([blank, came], axis=2)
+    )
+    came = swap(pick(kept, 1 - wide, 1, keepdims=False).astype(jnp.bfloat16), CORES)
+    pair = pick(kept, wide, 1, keepdims=False) + came.astype(jnp.float32)
+    total = pick(pair, deep, 0, keepdims=False)
+    for k in range(1, depth):
+        came = swap(
+            pick(pair, deep ^ k, 0, keepdims=False).astype(jnp.bfloat16), CORES * PAIR, depth, k
+        )
+        total = total + came.astype(jnp.float32)
+    mine = narrow(total)
+    came = swap_seq(mine)
+    low = jnp.where(seq == 0, mine, came).astype(jnp.float32)
+    high = jnp.where(seq == 0, came, mine).astype(jnp.float32)
+    return jnp.concatenate([low[:third], low[third:] + high[:third], high[third:]], axis=0)
 
 
 def body(
@@ -199,49 +326,71 @@
     up_bias,
     down_weight,
 ):
-    (
-        gains_all,
-        shifts_all,
-        self_in_all,
-        self_out_all,
-        query_all,
-        kv_all,
-        cross_out_all,
-        bias_all,
-        up_all,
-        up_bias_all,
-        down_all,
-    ) = (
-        lax.all_gather(norm_gains, "batch", axis=0, tiled=True),
-        lax.all_gather(norm_shifts, "batch", axis=0, tiled=True),
-        lax.all_gather(self_in, "batch", axis=0, tiled=True),
-        lax.all_gather(self_out, "batch", axis=0, tiled=True),
-        lax.all_gather(cross_query, "batch", axis=0, tiled=True),
-        lax.all_gather(cross_kv, "batch", axis=0, tiled=True),
-        lax.all_gather(cross_out, "batch", axis=0, tiled=True),
-        lax.all_gather(proj_bias, "batch", axis=0, tiled=True),
-        lax.all_gather(up_weight, "batch", axis=0, tiled=True),
-        lax.all_gather(up_bias, "batch", axis=0, tiled=True),
-        lax.all_gather(down_weight, "batch", axis=0, tiled=True),
-    )
-    gains = gains_all.astype(jnp.float32)
-    shifts = shifts_all.astype(jnp.float32)
-    biases = bias_all.astype(jnp.float32)
-    seq_count, row_count, model_width = hidden.shape
+    model_width = hidden.shape[2]
+    shard_rows = norm_gains.shape[0]
+    wide_cols = up_weight.shape[1]
+    blocks = wide_cols // model_width
+    size = lax.axis_size("batch")
+
+    tail_width = 128
+    small = jnp.concatenate(
+        [norm_gains, norm_shifts, proj_bias, up_bias.reshape(shard_rows, blocks)], axis=1
+    )
+    small_cols = small.shape[1]
+    small = jnp.pad(small, ((0, 0), (0, tail_width - small_cols)))
+    first_all = gather_rows(jnp.concatenate([self_in, small], axis=1))
+    second_all = gather_rows(
+        jnp.concatenate([self_out, cross_query, cross_kv, cross_out], axis=1)
+    )
+    up_blocks = up_weight.reshape(shard_rows, blocks, model_width).transpose(1, 0, 2)
+    third_all = lax.all_gather(
+        jnp.concatenate([up_blocks.reshape(-1, model_width), down_weight], axis=1),
+        "batch",
+        axis=0,
+        tiled=True,
+    )
+    frame_mine = lax.all_to_all(encoder, "batch", split_axis=0, concat_axis=1, tiled=True)
+    frame_other = swap_seq(frame_mine)
+    hidden_other = swap_seq(hidden)
+
+    self_in_all = first_all[:, : 3 * model_width]
+    small_all = first_all[:, 3 * model_width : 3 * model_width + small_cols]
+    self_out_all = second_all[:, :model_width]
+    query_all = second_all[:, model_width : 2 * model_width]
+    kv_all = second_all[:, 2 * model_width : 4 * model_width]
+    cross_out_all = second_all[:, 4 * model_width :]
+    down_all = third_all[:, model_width:]
+    up_all = (
+        third_all[:, :model_width]
+        .reshape(size, blocks, shard_rows, model_width)
+        .transpose(0, 2, 1, 3)
+        .reshape(model_width, wide_cols)
+    )
+    gains = small_all[:, :4].astype(jnp.float32)
+    shifts = small_all[:, 4:8].astype(jnp.float32)
+    biases = small_all[:, 8:15].astype(jnp.float32)
+    up_bias_all = small_all[:, 15:].reshape(-1).astype(jnp.float32)
+
+    seq_count, row_count, _ = hidden.shape
     seq_index = lax.axis_index("seq")
-    positions = seq_index * row_count + jnp.arange(row_count, dtype=jnp.int32)
+    slots = jnp.arange(row_count, dtype=jnp.int32)
+    positions = seq_index * row_count + slots
+    positions_other = (1 - seq_index) * row_count + slots
     offsets = token_offsets[:, None]
     zero_row = jnp.zeros((model_width,), jnp.float32)
     inputs = hidden.astype(jnp.float32)
     normed_one, scale_one = layer_parts(inputs)
     act_one = (normed_one * gains[:, 0] + shifts[:, 0]).astype(jnp.bfloat16)
+    normed_far, _ = layer_parts(hidden_other.astype(jnp.float32))
+    act_far = (normed_far * gains[:, 0] + shifts[:, 0]).astype(jnp.bfloat16)
     qkv_bias = jnp.concatenate([biases[:, 0], zero_row, biases[:, 1]])
     qkv_local = (dot_right(act_one, self_in_all) + qkv_bias).astype(jnp.bfloat16)
     self_query = qkv_local[..., :model_width]
-    pair_local = qkv_local[..., model_width:]
-    pair_past = from_behind(pair_local, "seq", 1)
-    self_pairs = jnp.concatenate([pair_past, pair_local], axis=1)
-    key_pos = jnp.concatenate([positions - row_count, positions])[None, None, :]
+    pair_far = (
+        dot_right(act_far, self_in_all[:, model_width:]) + qkv_bias[model_width:]
+    ).astype(jnp.bfloat16)
+    self_pairs = jnp.concatenate([pair_far, qkv_local[..., model_width:]], axis=1)
+    key_pos = jnp.concatenate([positions_other, positions])[None, None, :]
     query_pos = positions[None, :, None]
     self_mask = (key_pos <= query_pos) & ((key_pos >= offsets[:, :, None]) | (key_pos == query_pos))
     self_mixed, self_total = attend(self_query, self_pairs, self_mask)
@@ -249,24 +398,21 @@
     normed_two, scale_two = layer_parts(after_self)
     act_two = (normed_two * gains[:, 1] + shifts[:, 1]).astype(jnp.bfloat16)
     cross_queries = (dot_right(act_two, query_all) + biases[:, 3]).astype(jnp.bfloat16)
-    frame_half = lax.all_to_all(encoder, "batch", split_axis=0, concat_axis=1, tiled=True)
+    frames = jnp.concatenate([frame_mine, frame_other], axis=1)
     kv_bias = jnp.concatenate([zero_row, biases[:, 4]])
-    half_pairs = (dot_right(frame_half, kv_all) + kv_bias).astype(jnp.bfloat16)
-    cross_pairs = lax.all_gather(half_pairs, "seq", axis=1, tiled=True)
-    half_slots = frame_half.shape[1]
+    cross_pairs = (dot_right(frames, kv_all) + kv_bias).astype(jnp.bfloat16)
+    half_slots = frame_mine.shape[1]
     owner_frames = encoder.shape[1]
-    gathered = jnp.arange(lax.axis_size("seq") * half_slots, dtype=jnp.int32)
-    half_index = gathered // half_slots
+    gathered = jnp.arange(2 * half_slots, dtype=jnp.int32)
+    half_index = (gathered // half_slots) ^ seq_index
     within = gathered % half_slots
-    frame_ids = (
-        within // owner_frames * lax.axis_size("seq") + half_index
-    ) * owner_frames + within % owner_frames
+    frame_ids = (within // owner_frames * 2 + half_index) * owner_frames + within % owner_frames
     frame_mask = frame_ids[None, None, :] < frame_counts[:, None, None]
     cross_mixed, cross_total = attend(cross_queries, cross_pairs, frame_mask)
     after_cross = after_self + dot_right(cross_mixed, cross_out_all) + biases[:, 5]
     normed_three, scale_three = layer_parts(after_cross)
     act_three = (normed_three * gains[:, 2] + shifts[:, 2]).astype(jnp.bfloat16)
-    up_value = dot_right(act_three, up_all) + up_bias_all.astype(jnp.float32)
+    up_value = dot_right(act_three, up_all) + up_bias_all
     gelu_value, gelu_pull = jax.vjp(partial(jax.nn.gelu, approximate=False), up_value)
     hidden_act = gelu_value.astype(jnp.bfloat16)
     after_mlp = after_cross + dot_right(hidden_act, down_all) + biases[:, 6]
@@ -284,11 +430,11 @@
     )
     grad_mlp, gain_last, shift_last = layer_back(grad_out, normed_last, scale_last, gains[:, 3])
     grad_down = grad_mlp.astype(jnp.bfloat16)
-    down_term = weight_term(hidden_act, grad_down)
+    down_sum = reduce_rows(weight_term(hidden_act, grad_down))
     down_bias = col_sum(grad_down)
     grad_act = dot_left(grad_down, down_all)
     grad_up = gelu_pull(grad_act)[0].astype(jnp.bfloat16)
-    up_term = weight_term(act_three, grad_up)
+    up_sum = reduce_rows(weight_term(act_three, grad_up))
     up_bias_term = col_sum(grad_up)
     back_three, gain_three, shift_three = layer_back(
         dot_left(grad_up, up_all), normed_three, scale_three, gains[:, 2]
@@ -301,18 +447,19 @@
     grad_cross_query, grad_cross_pairs = attend_back(
         cross_queries, cross_pairs, frame_mask, cross_total, grad_cross_mixed
     )
-    half_grads = lax.psum_scatter(
-        grad_cross_pairs.astype(jnp.bfloat16), "seq", scatter_dimension=1, tiled=True
-    )
-    kv_term = weight_term(frame_half, half_grads)
-    kv_bias_term = col_sum(half_grads[..., model_width:])
-    owner_grads = dot_left(half_grads, kv_all)
+    grad_frames_in = grad_cross_pairs.astype(jnp.bfloat16)
+    kv_term = weight_term(frames, grad_frames_in)
+    kv_bias_term = col_sum(grad_frames_in[..., model_width:])
+    frame_grads = dot_left(grad_frames_in, kv_all)
+    frame_came = swap_seq(frame_grads[:, half_slots:].astype(jnp.bfloat16))
+    owner_grads = frame_grads[:, :half_slots] + frame_came.astype(jnp.float32)
     grad_encoder = lax.all_to_all(
         owner_grads.astype(jnp.bfloat16), "batch", split_axis=1, concat_axis=0, tiled=True
-    ).astype(owner_grads.dtype)
+    ).astype(jnp.float32)
     grad_cq = grad_cross_query.astype(jnp.bfloat16)
     query_term = weight_term(act_two, grad_cq)
     query_bias = col_sum(grad_cq)
+    cross_sum = reduce_rows(jnp.concatenate([cross_out_term, kv_term, query_term], axis=1))
     back_two, gain_two, shift_two = layer_back(
         dot_left(grad_cq, query_all), normed_two, scale_two, gains[:, 1]
     )
@@ -324,23 +471,37 @@
     grad_self_query, grad_self_pairs = attend_back(
         self_query, self_pairs, self_mask, self_total, grad_self_mixed
     )
-    returned = from_behind(grad_self_pairs[:, :row_count].astype(jnp.bfloat16), "seq", -1).astype(
-        jnp.float32
-    )
-    grad_pair_local = grad_self_pairs[:, row_count:] + returned
-    grad_qkv = jnp.concatenate([grad_self_query, grad_pair_local], axis=-1).astype(jnp.bfloat16)
+    grad_pairs_in = grad_self_pairs.astype(jnp.bfloat16)
+    grad_qkv = jnp.concatenate(
+        [grad_self_query.astype(jnp.bfloat16), grad_pairs_in[:, row_count:]], axis=-1
+    )
+    grad_far = grad_pairs_in[:, :row_count]
+    far_term = weight_term(act_far, grad_far)
     qkv_term = weight_term(act_one, grad_qkv)
+    qkv_term = jnp.concatenate(
+        [qkv_term[:, :model_width], qkv_term[:, model_width:] + far_term], axis=1
+    )
     qkv_sums = col_sum(grad_qkv)
+    value_sums = qkv_sums[2 * model_width :] + col_sum(grad_far[..., model_width:])
+    norm_far = swap_seq(
+        dot_left(grad_far, self_in_all[:, model_width:]).astype(jnp.bfloat16)
+    ).astype(jnp.float32)
     back_one, gain_one, shift_one = layer_back(
-        dot_left(grad_qkv, self_in_all), normed_one, scale_one, gains[:, 0]
+        dot_left(grad_qkv, self_in_all) + norm_far, normed_one, scale_one, gains[:, 0]
     )
     grad_hidden = grad_self + back_one
-    gain_term = jnp.stack([gain_one, gain_two, gain_three, gain_last], axis=1)
-    shift_term = jnp.stack([shift_one, shift_two, shift_three, shift_last], axis=1)
-    bias_term = jnp.stack(
+    small_term = jnp.stack(
         [
+            gain_one,
+            gain_two,
+            gain_three,
+            gain_last,
+            shift_one,
+            shift_two,
+            shift_three,
+            shift_last,
             qkv_sums[:model_width],
-            qkv_sums[2 * model_width :],
+            value_sums,
             self_out_bias,
             query_bias,
             kv_bias_term,
@@ -349,47 +510,25 @@
         ],
         axis=1,
     )
-    summed = (
-        lax.psum_scatter(gain_term, "batch", scatter_dimension=0, tiled=True),
-        lax.psum_scatter(shift_term, "batch", scatter_dimension=0, tiled=True),
-        lax.psum_scatter(qkv_term, "batch", scatter_dimension=0, tiled=True),
-        lax.psum_scatter(self_out_term, "batch", scatter_dimension=0, tiled=True),
-        lax.psum_scatter(query_term, "batch", scatter_dimension=0, tiled=True),
-        lax.psum_scatter(kv_term, "batch", scatter_dimension=0, tiled=True),
-        lax.psum_scatter(cross_out_term, "batch", scatter_dimension=0, tiled=True),
-        lax.psum_scatter(bias_term, "batch", scatter_dimension=0, tiled=True),
-        lax.psum_scatter(up_term, "batch", scatter_dimension=0, tiled=True),
-        lax.psum_scatter(up_bias_term, "batch", scatter_dimension=0, tiled=True),
-        lax.psum_scatter(down_term, "batch", scatter_dimension=0, tiled=True),
-    )
-    summed = (
-        lax.psum(summed[0].astype(jnp.bfloat16), "seq").astype(jnp.float32),
-        lax.psum(summed[1].astype(jnp.bfloat16), "seq").astype(jnp.float32),
-        lax.psum(summed[2].astype(jnp.bfloat16), "seq").astype(jnp.float32),
-        lax.psum(summed[3].astype(jnp.bfloat16), "seq").astype(jnp.float32),
-        lax.psum(summed[4].astype(jnp.bfloat16), "seq").astype(jnp.float32),
-        lax.psum(summed[5].astype(jnp.bfloat16), "seq").astype(jnp.float32),
-        lax.psum(summed[6].astype(jnp.bfloat16), "seq").astype(jnp.float32),
-        lax.psum(summed[7].astype(jnp.bfloat16), "seq").astype(jnp.float32),
-        lax.psum(summed[8].astype(jnp.bfloat16), "seq").astype(jnp.float32),
-        lax.psum(summed[9].astype(jnp.bfloat16), "seq").astype(jnp.float32),
-        lax.psum(summed[10].astype(jnp.bfloat16), "seq").astype(jnp.float32),
-    )
+    small_term = jnp.concatenate([small_term, up_bias_term.reshape(model_width, blocks)], axis=1)
+    small_term = jnp.pad(small_term, ((0, 0), (0, tail_width - small_cols)))
+    self_sum = reduce_rows(jnp.concatenate([self_out_term, qkv_term, small_term], axis=1))
+    small_sum = self_sum[:, 4 * model_width :]
     return (
         result,
         grad_hidden,
         grad_encoder,
-        summed[0],
-        summed[1],
-        summed[2],
-        summed[3],
-        summed[4],
-        summed[5],
-        summed[6],
-        summed[7],
-        summed[8],
-        summed[9],
-        summed[10],
+        small_sum[:, :4],
+        small_sum[:, 4:8],
+        self_sum[:, model_width : 4 * model_width],
+        self_sum[:, :model_width],
+        cross_sum[:, 3 * model_width :],
+        cross_sum[:, model_width : 3 * model_width],
+        cross_sum[:, :model_width],
+        small_sum[:, 8:15],
+        up_sum,
+        small_sum[:, 15:small_cols].reshape(-1),
+        down_sum,
     )
 
 

time: 1400 us -> 628 us (0.45)
  waiting for transfers between devices: 884 us -> 162 us
  blocking collectives: 172 us -> 0 us
  starting transfers between devices: 19.7 us -> 94.3 us
  local copies, waits for them, and re-layouts: 106 us -> 130 us
  other arithmetic: 59.3 us -> 80.1 us
  matrix products: 136 us -> 122 us
    reduce_scatter x7 -> x0, waiting for transfers between devices: 449 us -> none  [the longest x1 114 us: body(): lax.psum_scatter(up_term, 'batch', scatter_dimension=0, tiled=True)]
    unnamed x24 -> x1, waiting for transfers between devices: 195 us -> 0.02 us
    all_gather x8 -> x1, waiting for transfers between devices: 176 us -> 0.01 us  [body(): lax.all_gather(jnp.concatenate([up_blocks.reshape(-1, model_width), down_...]
    ppermute x2 -> x52, waiting for transfers between devices: 26.9 us -> 162 us  [the longest x36 94.5 us: swap(): return lax.ppermute(block, 'batch', partners(stride, radix, step))]
    unnamed x2 -> x0, blocking collectives: 90.3 us -> none
    ppermute x2 -> x52, starting transfers between devices: 5.55 us -> 83.1 us  [the longest x36 65.8 us: swap(): return lax.ppermute(block, 'batch', partners(stride, radix, step))]
    all_gather x3 -> x0, blocking collectives: 76.7 us -> none  [the longest x1 40 us: body(): lax.all_gather(proj_bias, 'batch', axis=0, tiled=True)]
    psum x1 -> x0, waiting for transfers between devices: 38.1 us -> none  [body(): lax.psum(summed[5].astype(jnp.bfloat16), 'seq').astype(jnp.float32)]
  transfers between devices with their start and end apart: 24 -> 55, of which waited for: 17 -> 17; matrix products, arithmetic and copies ran while one was open for 15% -> 30% of each run, Pallas kernels for 0% -> 2%
where the time goes in v1:
time: 628 us; the launch traced here: 620 us
  waiting for transfers between devices  162 us (26%)
  local copies, waits for them, and re-layouts  130 us (21%)
  matrix products  122 us (19%)
  starting transfers between devices  94.3 us (15%)
  other arithmetic  80.1 us (13%)
  between operations  18.6 us (3%)
  Pallas kernels  11.1 us (2%)
    ppermute x36, waiting for transfers between devices, swap(): return lax.ppermute(block, 'batch', partners(stride, radix, step))  94.5 us
    ppermute x16, waiting for transfers between devices, swap_seq(): return lax.ppermute(block, 'seq', FLIP)  67.6 us
    ppermute x36, starting transfers between devices, swap(): return lax.ppermute(block, 'batch', partners(stride, radix, step))  65.8 us
    unnamed x249, local copies, waits for them, and re-layouts  34.5 us
    dot_general x8, matrix products, dot_left(): jnp.einsum('bcj,ij->bci', grad_side, weight, preferred_element_type=jnp.f...  26.8 us
    dot_general x8, matrix products, dot_right(): return jnp.dot(left_side, weight, preferred_element_type=jnp.float32)  24.4 us
    dot_general x12, matrix products, head_block(): jnp.einsum('bqhd,bkhd->bhqk', query_heads, key_heads, preferred_element_t...  21.6 us
    dot_general x8, matrix products, weight_term(): jnp.einsum('bci,bcj->ij', left_side, grad_side, preferred_element_type=jn...  21.3 us
  transfers between devices with their start and end apart: 55, of which 17 were waited for; matrix products, arithmetic and copies ran while one was open for 30% of the time, Pallas kernels for 2%

profile of v1, /device:TPU:0, one launch (start us, length us, event | category | flops | bytes accessed | tf_op | source)
XLA Modules:
  0.0 619.9 jit_solution(11886099784761122672)
XLA Ops:
  11.4 5.1 collective-permute-start.3
  22.0 5.3 all-to-all-start
  35.1 22.3 %collective-permute-done.2 = bf16[32,2432]{1,0:T(8,128)(2,1)S(1)} collective-permute-done((bf16[32,2432]{1,0:T(8,128)(2,1)S(1)}, bf16[32,2432]{1,0:T(8,128)(2,1)S(1)}, u32[]{:S(2)}, u32[]{:S(2)}) %collective-permute-start.2) | collective-permute-done | bytes 155680 | tf_op jit(solution)/shard_map/ppermute | solution.py:191
  59.1 24.4 %collective-permute-done.12 = bf16[32,3840]{1,0:T(8,128)(2,1)} collective-permute-done((bf16[32,3840]{1,0:T(8,128)(2,1)S(1)}, bf16[32,3840]{1,0:T(8,128)(2,1)}, u32[]{:S(2)}, u32[]{:S(2)}) %collective-permute-start.12) | collective-permute-done | bytes 245792 | tf_op jit(solution)/shard_map/ppermute | solution.py:191
  92.5 15.7 %collective-permute-done.6.refs_3_ = bf16[4,16,2432]{2,1,0:T(8,128)(2,1)S(1)} collective-permute-done((bf16[4,16,2432]{2,1,0:T(8,128)(2,1)S(1)}, bf16[4,16,2432]{2,1,0:T(8,128)(2,1)S(1)}, u32[]{:S(2)}, u32[]{:S(2)}) %collective-permute-start.6) | collective-permute-done | bytes 311328 | tf_op jit(solution)/shard_map/ppermute | solution.py:195
  108.2 23.5 %collective-permute-done.14.refs_1_ = bf16[4,32,3840]{2,1,0:T(8,128)(2,1)} collective-permute-done((bf16[4,32,3840]{2,1,0:T(8,128)(2,1)}, bf16[4,32,3840]{2,1,0:T(8,128)(2,1)}, u32[]{:S(2)}, u32[]{:S(2)}) %collective-permute-start.14) | collective-permute-done | bytes 983072 | tf_op jit(solution)/shard_map/ppermute | solution.py:191
  135.3 5.0 place_rows.2
  156.1 8.5 %while.72 = (s32[]{:T(128)}, bf16[1,224,768]{1,2,0:T(8,128)(2,1)}, f32[1,12,224]{2,1,0:T(8,128)S(1)}, bf16[1,448,1536]{1,2,0:T(8,128)(2,1)S(1)}, bf16[1,224,768]...) while((s32[]{:T(128)}, bf16[1,224,768]{1,2,0:T(8,128)(2,1)}, ...), condition=%wide.region_7.8_spmd.clone, body=%wide.region_4.7_spmd.clone.sunk | while | flops 108035208 | bytes 7332744 | solution.py:100
  165.0 6.1 place_rows.3
  175.6 6.9 %collective-permute-done.21 = bf16[1,768,768]{1,2,0:T(8,128)(2,1)} collective-permute-done((bf16[1,768,768]{1,2,0:T(8,128)(2,1)}, bf16[1,768,768]{1,2,0:T(8,128)(2,1)}, u32[]{:S(2)}, u32[]{:S(2)}) %collective-permute-start.21) | collective-permute-done | bytes 1179680 | tf_op jit(solution)/shard_map/ppermute | solution.py:195
  182.5 8.0 %fusion.28 = bf16[1,1536,1536]{2,1,0:T(8,128)(2,1)} fusion(f32[1536]{0:T(1024)S(1)} %concatenate.109, bf16[768,3840]{1,0:T(8,128)(2,1)} %place_rows.3, bf16[1,768,768]{1,2,0:T(8,128)(2,1)} %collective-permute-done.21, bf16[1,768,768]{1,2,0:T(8,128)(2,1)S(1)} %copy-done.27), kind=kOutput, calls=%fused_computation.84 | convolution fusion | flops 3633315840 | bytes 9443328 | tf_op jit(solution)/shard_map/dot_general | solution.py:33
  190.6 6.7 %copy.146 = bf16[1,1536,1536]{1,2,0:T(8,128)(2,1)} copy(bf16[1,1536,1536]{2,1,0:T(8,128)(2,1)} %fusion.28) | data formatting | bytes 9437184
  197.3 18.8 %while.73 = (s32[]{:T(128)}, bf16[1,224,768]{1,2,0:T(8,128)(2,1)S(1)}, f32[1,12,224]{2,1,0:T(8,128)S(1)}, bf16[1,1536,1536]{1,2,0:T(8,128)(2,1)}, bf16[1,224,768...) while((s32[]{:T(128)}, ...), condition=%wide.region_13.14_spmd.clone, body=%wide.region_10.13_spmd.clone.sunk | while | flops 368939136 | bytes 21991236 | solution.py:100
  227.9 7.1 %multiply_convert_fusion.2 = (bf16[224,3072]{1,0:T(8,128)(2,1)S(1)}, f32[224,3072]{1,0:T(8,128)S(1)}, f32[224,3072]{1,0:T(8,128)S(1)}) fusion(f32[3072]{0:T(1024)S(1)} %reshape.1392, bf16[768,3072]{1,0:T(8,128)(2,1)S(1)} %bitcast.572, f32[1,224,768]{2,1,0:T(8,128)S(1)} %get-tuple-element.1180, f32[768]{0:T(1024)S(1)} %get-tuple-element.1027, ...), kind=kOutput, calls=%fused_computation.118 | convolution fusion | flops 1103241216 | bytes 12308224 | tf_op jit(solution)/shard_map/dot_general | solution.py:33
  251.5 48.9 %while.74 = (s32[]{:T(128)}, bf16[1,224,768]{1,2,0:T(8,128)(2,1)S(1)}, bf16[1,1536,1536]{1,2,0:T(8,128)(2,1)}, bf16[1,1536,1536]{1,2,0:T(8,128)(2,1)}, bf16[1,22...) while((s32[]{:T(128)}, ...), condition=%wide.region_25.26_spmd.clone, body=%wide.region_23.25_spmd.clone.sunk | while | flops 894136448 | bytes 69571472 | solution.py:174
  258.3 4.7 multiply_reduce_fusion.12
  274.6 4.7 multiply_reduce_fusion.12
  290.9 4.7 multiply_reduce_fusion.12
  310.3 23.9 %while.75 = (s32[]{:T(128)}, bf16[1,224,768]{1,2,0:T(8,128)(2,1)}, bf16[1,448,1536]{1,2,0:T(8,128)(2,1)}, bf16[1,448,1536]{1,2,0:T(8,128)(2,1)}, bf16[1,224,768]...) while((s32[]{:T(128)}, bf16[1,224,768]{1,2,0:T(8,128)(2,1)}, ...), condition=%wide.region_30.31_spmd.clone, body=%wide.region_28.30_spmd.clone.sunk | while | flops 261258368 | bytes 16819108 | solution.py:174
  338.9 6.9 %fusion.39 = f32[1,1536,768]{2,1,0:T(8,128)S(1)} fusion(bf16[1,1536,1536]{1,2,0:T(8,128)(2,1)} %get-tuple-element.729, bf16[768,3840]{1,0:T(8,128)(2,1)} %place_rows.3), kind=kOutput, calls=%fused_computation.106 | convolution fusion | flops 3623878656 | bytes 11796480 | tf_op jit(solution)/shard_map/bcj,ij->bci/dot_general | solution.py:37
  362.5 6.7 %fusion.43 = bf16[4,2,2,48,1536]{4,3,2,1,0:T(8,128)(2,1)S(1)} fusion(bf16[4,2,2,48,1536]{4,3,2,1,0:T(8,128)(2,1)S(1)} %bitcast.579, bf16[1,1536,1536]{1,2,0:T(8,128)(2,1)} %get-tuple-element.729), kind=kOutput, calls=%fused_computation.108 | convolution fusion | flops 3625058304 | bytes 9437184 | tf_op jit(solution)/shard_map/bci,bcj->ij/dot_general | solution.py:41
  422.5 9.9 %reduce.114 = bf16[768,768]{1,0:T(8,128)(2,1)} reduce(bf16[768,1,768]{2,1,0:T(2,128)(2,1)} %bitcast.567, bf16[]{:T(256)} %broadcast.879), dimensions={1}, to_apply=%bitcast.416.reduce_sub_computation | reduce | bytes 2359298
  436.2 5.9 all-to-all-start.1
  458.3 7.7 %collective-permute-done.32 = bf16[4,2,16,3072]{3,2,1,0:T(8,128)(2,1)S(1)} collective-permute-done((bf16[4,2,16,3072]{3,2,1,0:T(8,128)(2,1)S(1)}, bf16[4,2,16,3072]{3,2,1,0:T(8,128)(2,1)S(1)}, u32[]{:S(2)}, u32[]{:S(2)}) %collective-permute-start.32) | collective-permute-done | bytes 786464 | tf_op jit(solution)/shard_map/ppermute | solution.py:195
  469.7 13.2 %collective-permute-done.39 = bf16[4,2,16,3072]{3,2,0,1:T(8,128)(2,1)S(1)} collective-permute-done((bf16[4,2,16,3072]{3,2,0,1:T(8,128)(2,1)S(1)}, bf16[4,2,16,3072]{3,2,0,1:T(8,128)(2,1)S(1)}, u32[]{:S(2)}, u32[]{:S(2)}) %collective-permute-start.39) | collective-permute-done | bytes 786464 | tf_op jit(solution)/shard_map/ppermute | solution.py:195
  486.5 13.1 %collective-permute-done.46 = bf16[4,2,64,768]{3,2,0,1:T(8,128)(2,1)S(1)} collective-permute-done((bf16[4,2,64,768]{3,2,0,1:T(8,128)(2,1)S(1)}, bf16[4,2,64,768]{3,2,0,1:T(8,128)(2,1)S(1)}, u32[]{:S(2)}, u32[]{:S(2)}) %collective-permute-start.46) | collective-permute-done | bytes 786464 | tf_op jit(solution)/shard_map/ppermute | solution.py:195
  503.2 5.9 reshape.1440
  534.5 14.4 %collective-permute-start.42 = (bf16[32,3072]{1,0:T(8,128)(2,1)S(1)}, bf16[32,3072]{1,0:T(8,128)(2,1)S(1)}, u32[]{:S(2)}, u32[]{:S(2)}) collective-permute-start(bf16[32,3072]{1,0:T(8,128)(2,1)S(1)} %get-tuple-element.1146), channel_id=1, source_target_pairs={{0,16},{2,18},{4,20},{6,22},{8,24},{10,26},{12,28},{14,30},{16,0},... | collective-permute-start | bytes 589832 | tf_op jit(solution)/shard_map/ppermute | solution.py:191
  554.2 11.6 %collective-permute-start.49 = (bf16[128,768]{1,0:T(8,128)(2,1)S(1)}, bf16[128,768]{1,0:T(8,128)(2,1)S(1)}, u32[]{:S(2)}, u32[]{:S(2)}) collective-permute-start(bf16[128,768]{1,0:T(8,128)(2,1)S(1)} %get-tuple-element.1143), channel_id=1, source_target_pairs={{0,16},{2,18},{4,20},{6,22},{8,24},{10,26},{12,28},{14,30},{16,0},... | collective-permute-start | bytes 589832 | tf_op jit(solution)/shard_map/ppermute | solution.py:191
  570.3 6.9 %collective-permute-done.49 = bf16[128,768]{1,0:T(8,128)(2,1)S(1)} collective-permute-done((bf16[128,768]{1,0:T(8,128)(2,1)S(1)}, bf16[128,768]{1,0:T(8,128)(2,1)S(1)}, u32[]{:S(2)}, u32[]{:S(2)}) %collective-permute-start.49) | collective-permute-done | bytes 196640 | tf_op jit(solution)/shard_map/ppermute | solution.py:191
  589.0 5.4 collective-permute-done.29
  594.4 7.9 %collective-permute-done.28 = bf16[32,3200]{1,0:T(8,128)(2,1)S(1)} collective-permute-done((bf16[32,3200]{1,0:T(8,128)(2,1)S(1)}, bf16[32,3200]{1,0:T(8,128)(2,1)S(1)}, u32[]{:S(2)}, u32[]{:S(2)}) %collective-permute-start.28) | collective-permute-done | bytes 204832 | tf_op jit(solution)/shard_map/ppermute | solution.py:191
  (685 shorter events, 334.2 us)
Async XLA Ops:
  16.5 40.9 %collective-permute-start.2 = (bf16[32,2432]{1,0:T(8,128)(2,1)S(1)}, bf16[32,2432]{1,0:T(8,128)(2,1)S(1)}, u32[]{:S(2)}, u32[]{:S(2)}) collective-permute-start(bf16[32,2432]{1,0:T(8,128)(2,1)S(1)} %fusion.185), channel_id=1, source_target_pairs={{0,16},{2,18},{4,20},{6,22},{8,24},{10,26},{12,28},{14,30},{16,0},... | collective-permute-start | bytes 466952 | tf_op jit(solution)/shard_map/ppermute | solution.py:191
  16.5 42.2 %collective-permute-start.1 = (bf16[32,2432]{1,0:T(8,128)(2,1)S(1)}, bf16[32,2432]{1,0:T(8,128)(2,1)S(1)}, u32[]{:S(2)}, u32[]{:S(2)}) collective-permute-start(bf16[32,2432]{1,0:T(8,128)(2,1)S(1)} %fusion.185), channel_id=1, source_target_pairs={{0,8},{2,10},{4,12},{6,14},{8,0},{10,2},{12,4},{14,6},{16,24},{18,... | collective-permute-start | bytes 466952 | tf_op jit(solution)/shard_map/ppermute | solution.py:191
  18.2 40.8 %collective-permute-start.13 = (bf16[32,3840]{1,0:T(8,128)(2,1)S(1)}, bf16[32,3840]{1,0:T(8,128)(2,1)}, u32[]{:S(2)}, u32[]{:S(2)}) collective-permute-start(bf16[32,3840]{1,0:T(8,128)(2,1)S(1)} %fusion.172), channel_id=1, source_target_pairs={{0,24},{2,26},{4,28},{6,30},{8,16},{10,18},{12,20},{14,22},{16,8},... | collective-permute-start | bytes 737288 | tf_op jit(solution)/shard_map/ppermute | solution.py:191
  22.0 61.5 %collective-permute-start.12 = (bf16[32,3840]{1,0:T(8,128)(2,1)S(1)}, bf16[32,3840]{1,0:T(8,128)(2,1)}, u32[]{:S(2)}, u32[]{:S(2)}) collective-permute-start(bf16[32,3840]{1,0:T(8,128)(2,1)S(1)} %fusion.172), channel_id=1, source_target_pairs={{0,16},{2,18},{4,20},{6,22},{8,24},{10,26},{12,28},{14,30},{16,0},... | collective-permute-start | bytes 737288 | tf_op jit(solution)/shard_map/ppermute | solution.py:191
  22.0 129.7 %all-to-all-start = ((bf16[16,48,768]{2,1,0:T(8,128)(2,1)}), bf16[16,48,768]{2,1,0:T(8,128)(2,1)}, u32[]{:S(2)}, u32[]{:S(2)}) async-start(bf16[16,48,768]{2,1,0:T(8,128)(2,1)} %param.28), calls=%async_computation | async-start | bytes 2359296 | tf_op jit(solution)/shard_map/all_to_all | solution.py:352
  27.3 194.8 %all-gather.2.cloned.1.call-start = ((), (), s32[]{:S(2)}) async-start(), calls=%async_computation.2 | async-start | bytes 10027008 | tf_op jit(solution)/shard_map/all_gather | solution.py:346
  33.2 51.8 %collective-permute-start.11 = (bf16[32,3840]{1,0:T(8,128)(2,1)S(1)}, bf16[32,3840]{1,0:T(8,128)(2,1)S(1)}, u32[]{:S(2)}, u32[]{:S(2)}) collective-permute-start(bf16[32,3840]{1,0:T(8,128)(2,1)S(1)} %fusion.172), channel_id=1, source_target_pairs={{0,8},{2,10},{4,12},{6,14},{8,0},{10,2},{12,4},{14,6},{16,24},{18,... | collective-permute-start | bytes 737288 | tf_op jit(solution)/shard_map/ppermute | solution.py:191
  57.4 32.3 %collective-permute-start = (bf16[1,224,768]{2,1,0:T(8,128)(2,1)S(1)}, bf16[1,224,768]{2,1,0:T(8,128)(2,1)S(1)}, u32[]{:S(2)}, u32[]{:S(2)}) collective-permute-start(bf16[1,224,768]{2,1,0:T(8,128)(2,1)S(1)} %copy-done.19), channel_id=1, source_target_pairs={{0,1},{1,0},{2,3},{3,2},{4,5},{5,4},{6,7},{7,6},{8,9},{9,8},{10,11... | collective-permute-start | bytes 1032200 | tf_op jit(solution)/shard_map/ppermute | solution.py:195
  58.9 31.6 %collective-permute-start.4 = (bf16[4,32,2432]{2,1,0:T(8,128)(2,1)S(1)}, bf16[4,32,2432]{2,1,0:T(8,128)(2,1)S(1)}, u32[]{:S(2)}, u32[]{:S(2)}) collective-permute-start(bf16[4,32,2432]{2,1,0:T(8,128)(2,1)S(1)} %pad_maximum_fusion.6.refs_0_), channel_id=1, source_target_pairs={{0,4},{2,6},{4,0},{6,2},{8,12},{10,14},{12,8},{14,10},{16,20},{18,... | collective-permute-start | bytes 1867784 | tf_op jit(solution)/shard_map/ppermute | solution.py:191
  59.0 75.0 %collective-permute-start.7 = (bf16[4,32,2432]{2,1,0:T(8,128)(2,1)S(1)}, bf16[4,32,2432]{2,1,0:T(8,128)(2,1)S(1)}, u32[]{:S(2)}, u32[]{:S(2)}) collective-permute-start(bf16[4,32,2432]{2,1,0:T(8,128)(2,1)S(1)} %pad_maximum_fusion.6.refs_0_), channel_id=1, source_target_pairs={{0,2},{2,0},{4,6},{6,4},{8,10},{10,8},{12,14},{14,12},{16,18},{18,... | collective-permute-start | bytes 1867784 | tf_op jit(solution)/shard_map/ppermute | solution.py:191
  87.1 44.5 %collective-permute-start.14 = (bf16[4,32,3840]{2,1,0:T(8,128)(2,1)}, bf16[4,32,3840]{2,1,0:T(8,128)(2,1)}, u32[]{:S(2)}, u32[]{:S(2)}) collective-permute-start(bf16[4,32,3840]{2,1,0:T(8,128)(2,1)} %pad_maximum_fusion.5.refs_0_), channel_id=1, source_target_pairs={{0,4},{2,6},{4,0},{6,2},{8,12},{10,14},{12,8},{14,10},{16,20},{18,... | collective-permute-start | bytes 2949128 | tf_op jit(solution)/shard_map/ppermute | solution.py:191
  89.7 43.8 %collective-permute-start.15 = (bf16[4,16,3840]{2,1,0:T(8,128)(2,1)S(1)}, bf16[4,16,3840]{2,1,0:T(8,128)(2,1)}, u32[]{:S(2)}, u32[]{:S(2)}) collective-permute-start(bf16[4,16,3840]{2,1,0:T(8,128)(2,1)S(1)} %constant_dynamic-slice_fusion.19), channel_id=1, source_target_pairs={{0,1},{1,0},{2,3},{3,2},{4,5},{5,4},{6,7},{7,6},{8,9},{9,8},{10,11... | collective-permute-start | bytes 1474568 | tf_op jit(solution)/shard_map/ppermute | solution.py:195
  92.4 41.9 %collective-permute-start.8 = (bf16[4,32,2432]{2,1,0:T(8,128)(2,1)S(1)}, bf16[4,32,2432]{2,1,0:T(8,128)(2,1)S(1)}, u32[]{:S(2)}, u32[]{:S(2)}) collective-permute-start(bf16[4,32,2432]{2,1,0:T(8,128)(2,1)S(1)} %collective-permute-done.4.refs_1_), channel_id=1, source_target_pairs={{0,2},{2,0},{4,6},{6,4},{8,10},{10,8},{12,14},{14,12},{16,18},{18,... | collective-permute-start | bytes 1867784 | tf_op jit(solution)/shard_map/ppermute | solution.py:191
  133.5 31.4 %collective-permute-start.17 = (bf16[4,32,3840]{2,1,0:T(8,128)(2,1)}, bf16[4,32,3840]{2,1,0:T(8,128)(2,1)}, u32[]{:S(2)}, u32[]{:S(2)}) collective-permute-start(bf16[4,32,3840]{2,1,0:T(8,128)(2,1)} %pad_maximum_fusion.5.refs_0_), channel_id=1, source_target_pairs={{0,2},{2,0},{4,6},{6,4},{8,10},{10,8},{12,14},{14,12},{16,18},{18,... | collective-permute-start | bytes 2949128 | tf_op jit(solution)/shard_map/ppermute | solution.py:191
  134.0 30.9 %collective-permute-start.19 = (bf16[4,16,3840]{2,1,0:T(8,128)(2,1)}, bf16[4,16,3840]{2,1,0:T(8,128)(2,1)}, u32[]{:S(2)}, u32[]{:S(2)}) collective-permute-start(bf16[4,16,3840]{2,1,0:T(8,128)(2,1)} %collective-permute-done.15.refs_2_), channel_id=1, source_target_pairs={{0,2},{2,0},{4,6},{6,4},{8,10},{10,8},{12,14},{14,12},{16,18},{18,... | collective-permute-start | bytes 1474568 | tf_op jit(solution)/shard_map/ppermute | solution.py:191
  134.3 30.7 %collective-permute-start.18 = (bf16[4,32,3840]{2,1,0:T(8,128)(2,1)}, bf16[4,32,3840]{2,1,0:T(8,128)(2,1)}, u32[]{:S(2)}, u32[]{:S(2)}) collective-permute-start(bf16[4,32,3840]{2,1,0:T(8,128)(2,1)} %collective-permute-done.14.refs_1_), channel_id=1, source_target_pairs={{0,2},{2,0},{4,6},{6,4},{8,10},{10,8},{12,14},{14,12},{16,18},{18,... | collective-permute-start | bytes 2949128 | tf_op jit(solution)/shard_map/ppermute | solution.py:191
  154.1 28.4 %collective-permute-start.21 = (bf16[1,768,768]{1,2,0:T(8,128)(2,1)}, bf16[1,768,768]{1,2,0:T(8,128)(2,1)}, u32[]{:S(2)}, u32[]{:S(2)}) collective-permute-start(bf16[1,768,768]{1,2,0:T(8,128)(2,1)} %copy.145), channel_id=1, source_target_pairs={{0,1},{1,0},{2,3},{3,2},{4,5},{5,4},{6,7},{7,6},{8,9},{9,8},{10,11... | collective-permute-start | bytes 3538952 | tf_op jit(solution)/shard_map/ppermute | solution.py:195
  356.4 41.9 %collective-permute-start.22 = (bf16[1,224,768]{2,1,0:T(8,128)(2,1)}, bf16[1,224,768]{2,1,0:T(8,128)(2,1)}, u32[]{:S(2)}, u32[]{:S(2)}) collective-permute-start(bf16[1,224,768]{2,1,0:T(8,128)(2,1)} %fusion.89), channel_id=1, source_target_pairs={{0,1},{1,0},{2,3},{3,2},{4,5},{5,4},{6,7},{7,6},{8,9},{9,8},{10,11... | collective-permute-start | bytes 1032200 | tf_op jit(solution)/shard_map/ppermute | solution.py:195
  358.9 58.2 %collective-permute-start.23 = (bf16[1,768,768]{2,1,0:T(8,128)(2,1)}, bf16[1,768,768]{2,1,0:T(8,128)(2,1)}, u32[]{:S(2)}, u32[]{:S(2)}) collective-permute-start(bf16[1,768,768]{2,1,0:T(8,128)(2,1)} %slice.426), channel_id=1, source_target_pairs={{0,1},{1,0},{2,3},{3,2},{4,5},{5,4},{6,7},{7,6},{8,9},{9,8},{10,11... | collective-permute-start | bytes 3538952 | tf_op jit(solution)/shard_map/ppermute | solution.py:195
  373.2 68.9 %collective-permute-start.31 = (bf16[4,2,48,3072]{3,2,1,0:T(8,128)(2,1)}, bf16[4,2,48,3072]{3,2,1,0:T(8,128)(2,1)}, u32[]{:S(2)}, u32[]{:S(2)}) collective-permute-start(bf16[4,2,48,3072]{3,2,1,0:T(8,128)(2,1)} %dynamic-slice_bitcast_fusion.3), channel_id=1, source_target_pairs={{0,2},{2,0},{4,6},{6,4},{8,10},{10,8},{12,14},{14,12},{16,18},{18,... | collective-permute-start | bytes 7077896 | tf_op jit(solution)/shard_map/ppermute | solution.py:191
  376.5 70.3 %collective-permute-start.38 = (bf16[4,2,48,3072]{3,2,0,1:T(8,128)(2,1)}, bf16[4,2,48,3072]{3,2,0,1:T(8,128)(2,1)}, u32[]{:S(2)}, u32[]{:S(2)}) collective-permute-start(bf16[4,2,48,3072]{3,2,0,1:T(8,128)(2,1)} %bitcast.414), channel_id=1, source_target_pairs={{0,2},{2,0},{4,6},{6,4},{8,10},{10,8},{12,14},{14,12},{16,18},{18,... | collective-permute-start | bytes 7077896 | tf_op jit(solution)/shard_map/ppermute | solution.py:191
  379.1 71.3 %collective-permute-start.45 = (bf16[4,2,192,768]{3,2,0,1:T(8,128)(2,1)}, bf16[4,2,192,768]{3,2,0,1:T(8,128)(2,1)}, u32[]{:S(2)}, u32[]{:S(2)}) collective-permute-start(bf16[4,2,192,768]{3,2,0,1:T(8,128)(2,1)} %bitcast.413), channel_id=1, source_target_pairs={{0,2},{2,0},{4,6},{6,4},{8,10},{10,8},{12,14},{14,12},{16,18},{18,... | collective-permute-start | bytes 7077896 | tf_op jit(solution)/shard_map/ppermute | solution.py:191
  415.5 38.5 %collective-permute-start.24 = (bf16[4,2,48,3200]{3,2,1,0:T(8,128)(2,1)}, bf16[4,2,48,3200]{3,2,1,0:T(8,128)(2,1)}, u32[]{:S(2)}, u32[]{:S(2)}) collective-permute-start(bf16[4,2,48,3200]{3,2,1,0:T(8,128)(2,1)} %dynamic-slice_bitcast_fusion.2), channel_id=1, source_target_pairs={{0,2},{2,0},{4,6},{6,4},{8,10},{10,8},{12,14},{14,12},{16,18},{18,... | collective-permute-start | bytes 7372808 | tf_op jit(solution)/shard_map/ppermute | solution.py:191
  436.2 67.1 %all-to-all-start.1 = ((bf16[16,2,18432]{2,1,0:T(2,128)(2,1)}), bf16[16,2,18432]{2,1,0:T(2,128)(2,1)}, u32[]{:S(2)}, u32[]{:S(2)}) async-start(bf16[16,2,18432]{2,1,0:T(2,128)(2,1)} %reshape.1439), calls=%async_computation.1 | async-start | bytes 2359296 | tf_op jit(solution)/shard_map/all_to_all | solution.py:456
  449.4 33.4 %collective-permute-start.39 = (bf16[4,2,16,3072]{3,2,0,1:T(8,128)(2,1)S(1)}, bf16[4,2,16,3072]{3,2,0,1:T(8,128)(2,1)S(1)}, u32[]{:S(2)}, u32[]{:S(2)}) collective-permute-start(bf16[4,2,16,3072]{3,2,0,1:T(8,128)(2,1)S(1)} %dynamic-slice_convert_fusion.5), channel_id=1, source_target_pairs={{0,1},{1,0},{2,3},{3,2},{4,5},{5,4},{6,7},{7,6},{8,9},{9,8},{10,11... | collective-permute-start | bytes 2359304 | tf_op jit(solution)/shard_map/ppermute | solution.py:195
  452.8 46.8 %collective-permute-start.46 = (bf16[4,2,64,768]{3,2,0,1:T(8,128)(2,1)S(1)}, bf16[4,2,64,768]{3,2,0,1:T(8,128)(2,1)S(1)}, u32[]{:S(2)}, u32[]{:S(2)}) collective-permute-start(bf16[4,2,64,768]{3,2,0,1:T(8,128)(2,1)S(1)} %dynamic-slice_convert_fusion.3), channel_id=1, source_target_pairs={{0,1},{1,0},{2,3},{3,2},{4,5},{5,4},{6,7},{7,6},{8,9},{9,8},{10,11... | collective-permute-start | bytes 2359304 | tf_op jit(solution)/shard_map/ppermute | solution.py:195
  457.3 59.7 %collective-permute-start.25 = (bf16[4,2,16,3200]{3,2,1,0:T(8,128)(2,1)}, bf16[4,2,16,3200]{3,2,1,0:T(8,128)(2,1)}, u32[]{:S(2)}, u32[]{:S(2)}) collective-permute-start(bf16[4,2,16,3200]{3,2,1,0:T(8,128)(2,1)} %dynamic-slice_convert_fusion.1), channel_id=1, source_target_pairs={{0,1},{1,0},{2,3},{3,2},{4,5},{5,4},{6,7},{7,6},{8,9},{9,8},{10,11... | collective-permute-start | bytes 2457608 | tf_op jit(solution)/shard_map/ppermute | solution.py:195
  467.6 54.9 %collective-permute-start.33 = (bf16[4,32,3072]{2,1,0:T(8,128)(2,1)}, bf16[4,32,3072]{2,1,0:T(8,128)(2,1)}, u32[]{:S(2)}, u32[]{:S(2)}) collective-permute-start(bf16[4,32,3072]{2,1,0:T(8,128)(2,1)} %fusion.114), channel_id=1, source_target_pairs={{0,4},{2,6},{4,0},{6,2},{8,12},{10,14},{12,8},{14,10},{16,20},{18,... | collective-permute-start | bytes 2359304 | tf_op jit(solution)/shard_map/ppermute | solution.py:191
  484.5 42.8 %collective-permute-start.40 = (bf16[4,32,3072]{2,1,0:T(8,128)(2,1)}, bf16[4,32,3072]{2,1,0:T(8,128)(2,1)}, u32[]{:S(2)}, u32[]{:S(2)}) collective-permute-start(bf16[4,32,3072]{2,1,0:T(8,128)(2,1)} %fusion.115), channel_id=1, source_target_pairs={{0,4},{2,6},{4,0},{6,2},{8,12},{10,14},{12,8},{14,10},{16,20},{18,... | collective-permute-start | bytes 2359304 | tf_op jit(solution)/shard_map/ppermute | solution.py:191
  501.2 28.6 %collective-permute-start.47 = (bf16[4,128,768]{2,1,0:T(8,128)(2,1)}, bf16[4,128,768]{2,1,0:T(8,128)(2,1)}, u32[]{:S(2)}, u32[]{:S(2)}) collective-permute-start(bf16[4,128,768]{2,1,0:T(8,128)(2,1)} %fusion.116), channel_id=1, source_target_pairs={{0,4},{2,6},{4,0},{6,2},{8,12},{10,14},{12,8},{14,10},{16,20},{18,... | collective-permute-start | bytes 2359304 | tf_op jit(solution)/shard_map/ppermute | solution.py:191
  520.8 63.5 %collective-permute-start.26 = (bf16[4,32,3200]{2,1,0:T(8,128)(2,1)S(1)}, bf16[4,32,3200]{2,1,0:T(8,128)(2,1)S(1)}, u32[]{:S(2)}, u32[]{:S(2)}) collective-permute-start(bf16[4,32,3200]{2,1,0:T(8,128)(2,1)S(1)} %fusion.113), channel_id=1, source_target_pairs={{0,4},{2,6},{4,0},{6,2},{8,12},{10,14},{12,8},{14,10},{16,20},{18,... | collective-permute-start | bytes 2457608 | tf_op jit(solution)/shard_map/ppermute | solution.py:191
  534.5 33.1 %collective-permute-start.42 = (bf16[32,3072]{1,0:T(8,128)(2,1)S(1)}, bf16[32,3072]{1,0:T(8,128)(2,1)S(1)}, u32[]{:S(2)}, u32[]{:S(2)}) collective-permute-start(bf16[32,3072]{1,0:T(8,128)(2,1)S(1)} %get-tuple-element.1146), channel_id=1, source_target_pairs={{0,16},{2,18},{4,20},{6,22},{8,24},{10,26},{12,28},{14,30},{16,0},... | collective-permute-start | bytes 589832 | tf_op jit(solution)/shard_map/ppermute | solution.py:191
  (148 other events, 1914.1 us)
Sparse Core Ops, SparseCore 0:
  30.9 121.9 all-gather.1

commit v2 on v1

v2 whole, which is shorter than its diff:
```python
from functools import partial

import jax
import jax.numpy as jnp
from jax import lax
from jax.experimental import pallas as pl
from jax.experimental.pallas import tpu as pltpu
from jax.sharding import PartitionSpec as P

HEAD_DIM = 64
LANES = 128


EPS = 1e-05

def layer_parts(values):
    center = values - jnp.mean(values, axis=-1, keepdims=True)
    inv_std = lax.rsqrt(jnp.mean(center * center, axis=-1, keepdims=True) + EPS)
    return (center * inv_std, inv_std)


def layer_back(grad_side, normed, inv_std, gain):
    scaled = grad_side * gain
    mean_one = jnp.mean(scaled, axis=-1, keepdims=True)
    mean_two = jnp.mean(scaled * normed, axis=-1, keepdims=True)
    grad_in = inv_std * (scaled - mean_one - normed * mean_two)
    return (grad_in, jnp.sum(grad_side * normed, axis=0), jnp.sum(grad_side, axis=0))


def dot_right(left_side, weight):
    return jnp.dot(left_side, weight, preferred_element_type=jnp.float32)


def dot_left(grad_side, weight):
    return jnp.einsum("cj,ij->ci", grad_side, weight, preferred_element_type=jnp.float32)


def weight_term(left_side, grad_side):
    return jnp.einsum(
        "ci,cj->ij", left_side, grad_side, preferred_element_type=jnp.float32
    ).astype(jnp.bfloat16)


def col_sum(grad_side):
    return jnp.sum(grad_side, axis=0, dtype=jnp.float32)


def hold(steps, values):
    return lax.optimization_barrier((steps, values))

ROWS_BY_LANES = (((1,), (1,)), ((), ()))
DOWN_BOTH = (((0,), (0,)), ((), ()))


def head_parts(block):
    lane = lax.broadcasted_iota(jnp.int32, block.shape, 1)
    zero = jnp.zeros_like(block)
    return (
        jnp.where(lane < HEAD_DIM, block, zero),
        jnp.where(lane < HEAD_DIM, zero, block),
    )


def dot_of(left, right, dims):
    return lax.dot_general(left, right, dims, preferred_element_type=jnp.float32)


def attend_kernel(query_ref, key_ref, value_ref, bias_ref, mixed_ref, total_ref):
    score_scale = HEAD_DIM ** (-0.5)
    key, value = key_ref[...], value_ref[...]
    queries = head_parts(query_ref[...] * jnp.bfloat16(score_scale))
    scores = [dot_of(key, query, ROWS_BY_LANES) + bias_ref[...] for query in queries]
    tops = [jnp.max(item, axis=0, keepdims=True) for item in scores]
    terms = [jnp.exp(item - top) for item, top in zip(scores, tops)]
    totals = [jnp.sum(item, axis=0, keepdims=True) for item in terms]
    sides = [dot_of(value, item.astype(jnp.bfloat16), DOWN_BOTH) for item in terms]
    for head in range(2):
        total_ref[0, head : head + 1, :] = tops[head] + jnp.log(totals[head])
    mixed = [
        sides[head][head * HEAD_DIM : (head + 1) * HEAD_DIM] / totals[head] for head in range(2)
    ]
    mixed_ref[...] = jnp.concatenate(mixed, axis=0).T.astype(jnp.bfloat16)


def attend_back_kernel(
    query_ref, key_ref, value_ref, bias_ref, total_ref, grad_ref, gq_ref, gk_ref, gv_ref
):
    score_scale = HEAD_DIM ** (-0.5)
    key, value = key_ref[...], value_ref[...]
    queries = head_parts(query_ref[...] * jnp.bfloat16(score_scale))
    grads = head_parts(grad_ref[...])
    scores = [dot_of(key, query, ROWS_BY_LANES) + bias_ref[...] for query in queries]
    terms = [
        jnp.exp(item - total_ref[0, head : head + 1, :]) for head, item in enumerate(scores)
    ]
    grad_terms = [
        item * dot_of(value, grad, ROWS_BY_LANES) for item, grad in zip(terms, grads)
    ]
    row_dots = [jnp.sum(item, axis=0, keepdims=True) for item in grad_terms]
    grad_scores = [
        (grad_term - term * row_dot).astype(jnp.bfloat16)
        for grad_term, term, row_dot in zip(grad_terms, terms, row_dots)
    ]
    values = [
        jnp.dot(item.astype(jnp.bfloat16), grad, preferred_element_type=jnp.float32)
        for item, grad in zip(terms, grads)
    ]
    keys = [
        jnp.dot(item, query, preferred_element_type=jnp.float32)
        for item, query in zip(grad_scores, queries)
    ]
    sides = [dot_of(key, item, DOWN_BOTH) for item in grad_scores]
    gk_ref[...] = (keys[0] + keys[1]).astype(jnp.bfloat16)
    gv_ref[...] = (values[0] + values[1]).astype(jnp.bfloat16)
    picked = [
        sides[head][head * HEAD_DIM : (head + 1) * HEAD_DIM] * score_scale for head in range(2)
    ]
    gq_ref[...] = jnp.concatenate(picked, axis=0).T.astype(jnp.bfloat16)


def head_specs(rows, keys, blocks):
    return [
        pl.BlockSpec((rows, LANES), lambda i: (0, i)),
        pl.BlockSpec((keys, LANES), lambda i: (0, i)),
        pl.BlockSpec((keys, LANES), lambda i: (0, i + blocks)),
        pl.BlockSpec((keys, rows), lambda i: (0, 0)),
    ]


def attend(queries, pairs, bias):
    rows, width = queries.shape
    keys = pairs.shape[0]
    blocks = width // LANES
    work = 4 * rows * keys * width
    return pl.pallas_call(
        attend_kernel,
        grid=(blocks,),
        out_shape=(
            jax.ShapeDtypeStruct((rows, width), jnp.bfloat16),
            jax.ShapeDtypeStruct((blocks, 2, rows), jnp.float32),
        ),
        in_specs=head_specs(rows, keys, blocks),
        out_specs=(
            pl.BlockSpec((rows, LANES), lambda i: (0, i)),
            pl.BlockSpec((1, 2, rows), lambda i: (i, 0, 0)),
        ),
        cost_estimate=pl.CostEstimate(
            flops=4 * work, transcendentals=0, bytes_accessed=4 * keys * width
        ),
        name="attend",
    )(queries, pairs, pairs, bias)


def attend_back(queries, pairs, bias, totals, grads):
    rows, width = queries.shape
    keys = pairs.shape[0]
    blocks = width // LANES
    work = 10 * rows * keys * width
    return pl.pallas_call(
        attend_back_kernel,
        grid=(blocks,),
        out_shape=(
            jax.ShapeDtypeStruct((rows, width), jnp.bfloat16),
            jax.ShapeDtypeStruct((keys, width), jnp.bfloat16),
            jax.ShapeDtypeStruct((keys, width), jnp.bfloat16),
        ),
        in_specs=head_specs(rows, keys, blocks)
        + [
            pl.BlockSpec((1, 2, rows), lambda i: (i, 0, 0)),
            pl.BlockSpec((rows, LANES), lambda i: (0, i)),
        ],
        out_specs=(
            pl.BlockSpec((rows, LANES), lambda i: (0, i)),
            pl.BlockSpec((keys, LANES), lambda i: (0, i)),
            pl.BlockSpec((keys, LANES), lambda i: (0, i)),
        ),
        cost_estimate=pl.CostEstimate(
            flops=4 * work, transcendentals=0, bytes_accessed=8 * keys * width
        ),
        name="attend_back",
    )(queries, pairs, pairs, bias, totals, grads)


CORES = 2
PAIR = 2
FLIP = [(0, 1), (1, 0)]


def partners(stride, radix, step):
    pairs = []
    for i in range(lax.axis_size("batch")):
        digit = i // stride % radix
        pairs.append((i, i + ((digit ^ step) - digit) * stride))
    return pairs


def swap(block, stride, radix=2, step=1):
    return lax.ppermute(block, "batch", partners(stride, radix, step))


def swap_seq(block):
    return lax.ppermute(block, "seq", FLIP)


def place_of():
    batch = lax.axis_index("batch")
    return (
        batch // (CORES * PAIR),
        batch // CORES % PAIR,
        batch % CORES,
        lax.axis_index("seq"),
    )


def splits(rows):
    depth = lax.axis_size("batch") // (CORES * PAIR)
    return rows % 48 == 0 and depth == 4 and lax.axis_size("seq") == 2


def place_kernel(where_ref, *refs, depth, rows, half):
    pieces, out_ref, sem = refs[:8], refs[8], refs[9]
    deep, wide, core, seq = where_ref[0], where_ref[1], where_ref[2], where_ref[3]
    started = []
    for c in range(2):
        column, across, side, side_across = pieces[4 * c : 4 * c + 4]
        for w, (near, far) in enumerate(((column, side), (across, side_across))):
            for k in range(depth):
                base = (((deep ^ k) * PAIR + (wide ^ w)) * CORES + (core ^ c)) * rows
                row_span = pl.ds(pl.multiple_of(base, 16), rows)
                for source, part in ((near, seq), (far, 1 - seq)):
                    col_span = pl.ds(pl.multiple_of(part * half, LANES), half)
                    copy = pltpu.make_async_copy(
                        source.at[k], out_ref.at[row_span, col_span], sem
                    )
                    copy.start()
                    started.append(copy)
    for copy in started:
        copy.wait()


class Gather:
    def __init__(self, shard, last):
        self.rows, self.cols = shard.shape
        self.half = self.cols // 2
        self.last = last
        self.depth = lax.axis_size("batch") // (CORES * PAIR)
        self.state = (shard,)
        self.todo = (
            [self.by_depth, self.by_both, self.by_last, self.place]
            if splits(self.rows)
            else [self.plain]
        )

    def step(self):
        if self.todo:
            self.state = self.todo.pop(0)(*self.state)
        return self

    def result(self):
        while self.todo:
            self.step()
        return self.state[0]

    def plain(self, shard):
        return (lax.all_gather(shard, "batch", axis=0, tiled=True),)

    def by_depth(self, shard):
        part = lax.dynamic_slice_in_dim(shard, lax.axis_index("seq") * self.half, self.half, 1)
        came = [swap(part, CORES * PAIR, self.depth, k) for k in range(1, self.depth)]
        return (jnp.stack([part] + came),)

    def by_both(self, column):
        return column, swap(column, CORES), swap_seq(column)

    def by_last(self, column, across, side):
        far = swap_seq(across) if self.last == "seq" else swap(side, CORES)
        return column, across, side, far

    def place(self, *mine):
        other = tuple(swap(piece, 1) for piece in mine)
        total = lax.axis_size("batch") * self.rows
        call = pl.pallas_call(
            partial(place_kernel, depth=self.depth, rows=self.rows, half=self.half),
            out_shape=jax.ShapeDtypeStruct((total, self.cols), mine[0].dtype),
            in_specs=[pl.BlockSpec(memory_space=pltpu.SMEM)]
            + [pl.BlockSpec(memory_space=pl.ANY)] * 8,
            out_specs=pl.BlockSpec(memory_space=pltpu.VMEM),
            scratch_shapes=[pltpu.SemaphoreType.DMA],
            cost_estimate=pl.CostEstimate(
                flops=0, transcendentals=0, bytes_accessed=4 * total * self.cols
            ),
            name="place_rows",
        )
        return (call(jnp.stack(place_of()).astype(jnp.int32), *mine, *other),)


def narrow(values):
    return lax.reduce_precision(values, 8, 7).astype(jnp.bfloat16)


class Reduction:
    def __init__(self, *terms):
        self.size = lax.axis_size("batch")
        self.rows = terms[0].shape[0] // self.size
        self.state = terms
        self.fast = splits(self.rows)
        self.todo = (
            [self.by_core, self.by_seq, self.by_pair, self.by_depth, self.finish, self.join]
            if self.fast
            else [self.plain]
        )

    def step(self):
        if self.todo:
            self.state = self.todo.pop(0)(*self.state)
        return self

    def result(self):
        while self.todo:
            self.step()
        return self.state[0]

    def plain(self, *terms):
        terms = jnp.concatenate(terms, axis=1)
        mine = lax.psum_scatter(terms, "batch", scatter_dimension=0, tiled=True)
        return (lax.psum(mine, "seq").astype(jnp.float32),)

    def by_core(self, *terms):
        _, _, core, _ = place_of()
        grids = [term.reshape(-1, PAIR, CORES, self.rows, term.shape[1]) for term in terms]
        return tuple(
            jnp.concatenate(
                [lax.dynamic_index_in_dim(grid, which, 2, keepdims=False) for grid in grids], axis=-1
            )
            for which in (core, 1 - core)
        )

    def by_seq(self, kept, sent):
        seq, third = lax.axis_index("seq"), self.rows // 3
        chip = kept.astype(jnp.float32) + swap(sent, 1).astype(jnp.float32)
        edge = lax.dynamic_slice_in_dim(chip, (1 - seq) * 2 * third, third, 2)
        kept = lax.dynamic_slice_in_dim(chip, seq * third, 2 * third, 2)
        return kept.astype(jnp.bfloat16), edge.astype(jnp.bfloat16)

    def by_pair(self, kept, sent):
        _, wide, _, seq = place_of()
        came = swap_seq(sent)
        blank = jnp.zeros_like(came)
        came = jnp.where(
            seq == 0,
            jnp.concatenate([came, blank], axis=2),
            jnp.concatenate([blank, came], axis=2),
        )
        kept = kept.astype(jnp.float32) + came.astype(jnp.float32)
        mine = lax.dynamic_index_in_dim(kept, wide, 1, keepdims=False)
        sent = lax.dynamic_index_in_dim(kept, 1 - wide, 1, keepdims=False)
        return mine.astype(jnp.bfloat16), sent.astype(jnp.bfloat16)

    def by_depth(self, kept, sent):
        deep, _, _, _ = place_of()
        kept = kept.astype(jnp.float32) + swap(sent, CORES).astype(jnp.float32)
        return tuple(
            lax.dynamic_index_in_dim(kept, deep ^ k, 0, keepdims=False).astype(jnp.bfloat16)
            for k in range(self.size // (CORES * PAIR))
        )

    def finish(self, kept, *sent):
        depth = self.size // (CORES * PAIR)
        total = kept.astype(jnp.float32)
        for k, block in enumerate(sent, 1):
            total = total + swap(block, CORES * PAIR, depth, k).astype(jnp.float32)
        return (narrow(total),)

    def join(self, mine):
        seq, third = lax.axis_index("seq"), self.rows // 3
        came = swap_seq(mine)
        low = jnp.where(seq == 0, mine, came).astype(jnp.float32)
        high = jnp.where(seq == 0, came, mine).astype(jnp.float32)
        return (
            jnp.concatenate([low[:third], low[third:] + high[:third], high[third:]], axis=0),
        )


def advance(works, values):
    for work in works:
        work.step()
    states, values = lax.optimization_barrier(([work.state for work in works], values))
    for work, state in zip(works, states):
        work.state = state
    return values


def body(
    hidden,
    encoder,
    cotangent,
    token_offsets,
    token_lengths,
    frame_counts,
    corpus_ids,
    corpus_weights,
    norm_gains,
    norm_shifts,
    self_in,
    self_out,
    cross_query,
    cross_kv,
    cross_out,
    proj_bias,
    up_weight,
    up_bias,
    down_weight,
):
    hidden, cotangent = hidden[0], cotangent[0]
    row_count, model_width = hidden.shape
    shard_rows = norm_gains.shape[0]
    wide_cols = up_weight.shape[1]
    blocks = wide_cols // model_width
    size = lax.axis_size("batch")

    tail_width = 2 * LANES
    small = jnp.concatenate(
        [norm_gains, norm_shifts, proj_bias, up_bias.reshape(shard_rows, blocks)], axis=1
    )
    small_cols = small.shape[1]
    small = jnp.pad(small, ((0, 0), (0, tail_width - small_cols)))
    first = Gather(jnp.concatenate([self_in, small], axis=1), "seq")
    second = Gather(jnp.concatenate([self_out, cross_query, cross_kv, cross_out], axis=1), "pair")
    up_blocks = up_weight.reshape(shard_rows, blocks, model_width).transpose(1, 0, 2)
    third = jnp.concatenate([up_blocks.reshape(-1, model_width), down_weight], axis=1)
    hidden_other = swap_seq(hidden)
    first.step()
    second.state, encoder, first.state = lax.optimization_barrier(
        (second.state, encoder, first.state)
    )
    second.step()
    first.step()
    frame_mine = lax.all_to_all(encoder, "batch", split_axis=0, concat_axis=0, tiled=True)
    frame_mine = frame_mine.reshape(-1, model_width)
    third, second.state = lax.optimization_barrier((third, second.state))
    third_all = lax.all_gather(third, "batch", axis=0, tiled=True)
    first.step()
    second.step()
    frame_other = swap_seq(frame_mine)
    first_all, second_all = first.result(), second.result()

    self_in_all = first_all[:, : 3 * model_width]
    small_all = first_all[:, 3 * model_width : 3 * model_width + small_cols]
    self_out_all = second_all[:, :model_width]
    query_all = second_all[:, model_width : 2 * model_width]
    kv_all = second_all[:, 2 * model_width : 4 * model_width]
    cross_out_all = second_all[:, 4 * model_width :]
    down_all = third_all[:, model_width:]
    up_all = (
        third_all[:, :model_width]
        .reshape(size, blocks, shard_rows, model_width)
        .transpose(0, 2, 1, 3)
        .reshape(model_width, wide_cols)
    )
    gains = small_all[:, :4].astype(jnp.float32)
    shifts = small_all[:, 4:8].astype(jnp.float32)
    biases = small_all[:, 8:15].astype(jnp.float32)
    up_bias_all = small_all[:, 15:].reshape(-1).astype(jnp.float32)

    offset, length, frame_count = token_offsets[0], token_lengths[0], frame_counts[0]
    seq_index = lax.axis_index("seq")
    slots = jnp.arange(row_count, dtype=jnp.int32)
    positions = seq_index * row_count + slots
    positions_other = (1 - seq_index) * row_count + slots
    zero_row = jnp.zeros((model_width,), jnp.float32)
    inputs = hidden.astype(jnp.float32)
    normed_one, scale_one = layer_parts(inputs)
    act_one = (normed_one * gains[:, 0] + shifts[:, 0]).astype(jnp.bfloat16)
    normed_far, _ = layer_parts(hidden_other.astype(jnp.float32))
    act_far = (normed_far * gains[:, 0] + shifts[:, 0]).astype(jnp.bfloat16)
    qkv_bias = jnp.concatenate([biases[:, 0], zero_row, biases[:, 1]])
    qkv_local = (dot_right(act_one, self_in_all) + qkv_bias).astype(jnp.bfloat16)
    self_query = qkv_local[:, :model_width]
    pair_far = (
        dot_right(act_far, self_in_all[:, model_width:]) + qkv_bias[model_width:]
    ).astype(jnp.bfloat16)
    self_pairs = jnp.concatenate([pair_far, qkv_local[:, model_width:]], axis=0)
    key_pos = jnp.concatenate([positions_other, positions])[:, None]
    query_pos = positions[None, :]
    self_mask = (key_pos <= query_pos) & ((key_pos >= offset) | (key_pos == query_pos))
    self_bias = jnp.where(self_mask, 0.0, -jnp.inf)
    self_mixed, self_total = attend(self_query, self_pairs, self_bias)
    after_self = inputs + dot_right(self_mixed, self_out_all) + biases[:, 2]
    normed_two, scale_two = layer_parts(after_self)
    act_two = (normed_two * gains[:, 1] + shifts[:, 1]).astype(jnp.bfloat16)
    cross_queries = (dot_right(act_two, query_all) + biases[:, 3]).astype(jnp.bfloat16)
    frames = jnp.concatenate([frame_mine, frame_other], axis=0)
    kv_bias = jnp.concatenate([zero_row, biases[:, 4]])
    cross_pairs = (dot_right(frames, kv_all) + kv_bias).astype(jnp.bfloat16)
    half_slots = frame_mine.shape[0]
    owner_frames = encoder.shape[1]
    gathered = jnp.arange(2 * half_slots, dtype=jnp.int32)
    half_index = (gathered // half_slots) ^ seq_index
    within = gathered % half_slots
    frame_ids = (within // owner_frames * 2 + half_index) * owner_frames + within % owner_frames
    frame_bias = jnp.broadcast_to(
        jnp.where(frame_ids < frame_count, 0.0, -jnp.inf)[:, None], (2 * half_slots, row_count)
    )
    cross_mixed, cross_total = attend(cross_queries, cross_pairs, frame_bias)
    after_cross = after_self + dot_right(cross_mixed, cross_out_all) + biases[:, 5]
    normed_three, scale_three = layer_parts(after_cross)
    act_three = (normed_three * gains[:, 2] + shifts[:, 2]).astype(jnp.bfloat16)
    up_value = dot_right(act_three, up_all) + up_bias_all
    gelu_value, gelu_pull = jax.vjp(partial(jax.nn.gelu, approximate=False), up_value)
    hidden_act = gelu_value.astype(jnp.bfloat16)
    after_mlp = after_cross + dot_right(hidden_act, down_all) + biases[:, 6]
    normed_last, scale_last = layer_parts(after_mlp)
    result = (normed_last * gains[:, 3] + shifts[:, 3]).astype(jnp.bfloat16)
    corpus_match = corpus_ids[0] == jnp.arange(corpus_weights.shape[0], dtype=jnp.int32)
    seq_weight = jnp.sum(jnp.where(corpus_match, corpus_weights, 0.0))
    live_rows = (positions >= offset) & (positions < offset + length)
    grad_out = cotangent.astype(jnp.float32) * jnp.where(live_rows, seq_weight, 0.0)[:, None]
    grad_mlp, gain_last, shift_last = layer_back(grad_out, normed_last, scale_last, gains[:, 3])
    grad_down = grad_mlp.astype(jnp.bfloat16)
    down_bias = col_sum(grad_down)
    grad_act = dot_left(grad_down, down_all)
    grad_up = gelu_pull(grad_act)[0].astype(jnp.bfloat16)
    up_bias_term = col_sum(grad_up)
    wide_term = jnp.concatenate(
        [weight_term(hidden_act, grad_down).reshape(size, -1, model_width)]
        + [
            weight_term(act_three, part).reshape(size, shard_rows, model_width)
            for part in jnp.split(grad_up, blocks, axis=1)
        ],
        axis=1,
    )
    wide_term, grad_up = lax.optimization_barrier((wide_term, grad_up))
    wide_sum = lax.psum_scatter(wide_term, "batch", scatter_dimension=0, tiled=True)[0]
    back_three, gain_three, shift_three = layer_back(
        dot_left(grad_up, up_all), normed_three, scale_three, gains[:, 2]
    )
    grad_cross = grad_mlp + back_three
    grad_cross_in = grad_cross.astype(jnp.bfloat16)
    cross_out_term = weight_term(cross_mixed, grad_cross_in)
    cross_out_bias = col_sum(grad_cross_in)
    grad_cross_mixed = dot_left(grad_cross_in, cross_out_all).astype(jnp.bfloat16)
    grad_cq, grad_frame_key, grad_frame_value = attend_back(
        cross_queries, cross_pairs, frame_bias, cross_total, grad_cross_mixed
    )
    kv_bias_term = col_sum(grad_cross_mixed)
    frame_grads = dot_left(grad_frame_key, kv_all[:, :model_width]) + dot_left(
        grad_frame_value, kv_all[:, model_width:]
    )
    frame_mine_grads = frame_grads[:half_slots]
    frame_sent = frame_grads[half_slots:].astype(jnp.bfloat16)
    grad_cq, (frame_sent, frame_mine_grads) = hold(grad_cq, (frame_sent, frame_mine_grads))
    query_term = weight_term(act_two, grad_cq)
    query_bias = col_sum(grad_cq)
    back_two, gain_two, shift_two = layer_back(
        dot_left(grad_cq, query_all), normed_two, scale_two, gains[:, 1]
    )
    grad_self = grad_cross + back_two
    grad_self_in = grad_self.astype(jnp.bfloat16)
    self_out_term = weight_term(self_mixed, grad_self_in)
    self_out_bias = col_sum(grad_self_in)
    grad_self_mixed = dot_left(grad_self_in, self_out_all).astype(jnp.bfloat16)
    cross_sum = Reduction(
        cross_out_term,
        weight_term(frames, grad_frame_key),
        weight_term(frames, grad_frame_value),
        query_term,
    )
    grad_self_mixed = advance([cross_sum], grad_self_mixed)
    grad_self_query, grad_self_key, grad_self_value = attend_back(
        self_query, self_pairs, self_bias, self_total, grad_self_mixed
    )
    owner_grads = (frame_mine_grads + swap_seq(frame_sent).astype(jnp.float32)).astype(
        jnp.bfloat16
    )
    grad_self_query, grad_self_key, grad_self_value, owner_grads = advance(
        [cross_sum],
        (grad_self_query, grad_self_key, grad_self_value, owner_grads),
    )
    grad_encoder = lax.all_to_all(
        owner_grads.reshape(size, owner_frames, model_width),
        "batch",
        split_axis=0,
        concat_axis=0,
        tiled=True,
    ).astype(jnp.float32)
    grad_pairs = jnp.concatenate([grad_self_key, grad_self_value], axis=1)
    grad_qkv = jnp.concatenate([grad_self_query, grad_pairs[row_count:]], axis=1)
    grad_far = grad_pairs[:row_count]
    both_acts = jnp.concatenate([act_far, act_one], axis=0)
    small_now = [
        weight_term(act_one, grad_self_query),
        weight_term(both_acts, grad_self_key),
        weight_term(both_acts, grad_self_value),
    ]
    query_sums = col_sum(grad_self_query)
    value_sums = col_sum(grad_self_mixed)
    norm_far = dot_left(grad_far, self_in_all[:, model_width:]).astype(jnp.bfloat16)
    back_side = dot_left(grad_qkv, self_in_all) + swap_seq(norm_far).astype(jnp.float32)
    back_one, gain_one, shift_one = layer_back(back_side, normed_one, scale_one, gains[:, 0])
    grad_hidden = grad_self + back_one
    small_term = jnp.stack(
        [
            gain_one,
            gain_two,
            gain_three,
            gain_last,
            shift_one,
            shift_two,
            shift_three,
            shift_last,
            query_sums,
            value_sums,
            self_out_bias,
            query_bias,
            kv_bias_term,
            cross_out_bias,
            down_bias,
        ],
        axis=1,
    )
    small_term = jnp.concatenate([small_term, up_bias_term.reshape(model_width, blocks)], axis=1)
    small_term = jnp.pad(small_term, ((0, 0), (0, tail_width - small_cols))).astype(jnp.bfloat16)
    self_sum = Reduction(self_out_term, *small_now, small_term)
    wide_sum = wide_sum.astype(jnp.float32) + swap_seq(wide_sum).astype(jnp.float32)
    inner_rows = down_weight.shape[0]
    up_sum = (
        wide_sum[inner_rows:]
        .reshape(blocks, shard_rows, model_width)
        .transpose(1, 0, 2)
        .reshape(shard_rows, wide_cols)
    )
    cross_sum, self_sum = cross_sum.result(), self_sum.result()
    small_sum = self_sum[:, 4 * model_width :]
    return (
        result[None],
        grad_hidden[None],
        grad_encoder,
        small_sum[:, :4],
        small_sum[:, 4:8],
        self_sum[:, model_width : 4 * model_width],
        self_sum[:, :model_width],
        cross_sum[:, 3 * model_width :],
        cross_sum[:, model_width : 3 * model_width],
        cross_sum[:, :model_width],
        small_sum[:, 8:15],
        up_sum,
        small_sum[:, 15:small_cols].reshape(-1),
        wide_sum[:inner_rows],
    )


def solution(mesh):
    in_specs = (
        P("batch", "seq", None),
        P(None, ("batch", "seq"), None),
        P("batch", "seq", None),
        P("batch"),
        P("batch"),
        P("batch"),
        P("batch"),
        P(),
        P("batch", None),
        P("batch", None),
        P("batch", None),
        P("batch", None),
        P("batch", None),
        P("batch", None),
        P("batch", None),
        P("batch", None),
        P("batch", None),
        P("batch"),
        P("batch", None),
    )
    out_specs = (
        P("batch", "seq", None),
        P("batch", "seq", None),
        P(None, ("batch", "seq"), None),
        P("batch", None),
        P("batch", None),
        P("batch", None),
        P("batch", None),
        P("batch", None),
        P("batch", None),
        P("batch", None),
        P("batch", None),
        P("batch", None),
        P("batch"),
        P("batch", None),
    )
    return jax.shard_map(body, mesh=mesh, in_specs=in_specs, out_specs=out_specs, check_vma=False)
```

time: 628 us -> 493 us (0.79)
  local copies, waits for them, and re-layouts: 130 us -> 61.8 us
  matrix products: 122 us -> 69.1 us
  Pallas kernels: 11.1 us -> 57.1 us
  other arithmetic: 80.1 us -> 39.1 us
  starting transfers between devices: 94.3 us -> 75.5 us
    dot_general x58 -> x22, matrix products: 97.8 us -> 43.4 us  [the longest x9 27.3 us: dot_left(): jnp.einsum('cj,ij->ci', grad_side, weight, preferred_element_type=jnp.flo...]
    pallas_call x2 -> x6, Pallas kernels: 11.1 us -> 57.1 us  [the longest x2 26.4 us: attend_back(): pl.pallas_call(attend_back_kernel, grid=(blocks,), out_shape=(jax.ShapeDt...]
    ppermute x36 -> x27, waiting for transfers between devices: 94.5 us -> 122 us  [swap(): return lax.ppermute(block, 'batch', partners(stride, radix, step))]
    ppermute x16 -> x12, waiting for transfers between devices: 67.6 us -> 41.2 us  [swap_seq(): return lax.ppermute(block, 'seq', FLIP)]
    ppermute x36 -> x27, starting transfers between devices: 65.8 us -> 39.7 us  [swap(): return lax.ppermute(block, 'batch', partners(stride, radix, step))]
    dynamic_slice x44 -> x13, local copies, waits for them, and re-layouts: 26.6 us -> 0.69 us  [the longest x12 0.66 us: by_core(): lax.dynamic_index_in_dim(grid, which, 2, keepdims=False)]
    unnamed x249 -> x96, local copies, waits for them, and re-layouts: 34.5 us -> 19.5 us
    dynamic_update_slice x24 -> x0, local copies, waits for them, and re-layouts: 14.1 us -> none  [the longest x6 5.02 us: head_block(): lax.dynamic_update_slice_in_dim(grad_pairs, grad_key.reshape(seq_count, k...]
  transfers between devices with their start and end apart: 55 -> 43, of which waited for: 17 -> 18; matrix products, arithmetic and copies ran while one was open for 30% -> 20% of each run, Pallas kernels for 2% -> 8%
where the time goes in v2:
time: 493 us; the launch traced here: 484 us
  waiting for transfers between devices  164 us (33%)
  starting transfers between devices  75.5 us (15%)
  matrix products  69.1 us (14%)
  local copies, waits for them, and re-layouts  61.8 us (13%)
  Pallas kernels  57.1 us (12%)
  other arithmetic  39.1 us (8%)
  between operations  18.1 us (4%)
    ppermute x27, waiting for transfers between devices, swap(): return lax.ppermute(block, 'batch', partners(stride, radix, step))  122 us
    ppermute x12, waiting for transfers between devices, swap_seq(): return lax.ppermute(block, 'seq', FLIP)  41.2 us
    ppermute x27, starting transfers between devices, swap(): return lax.ppermute(block, 'batch', partners(stride, radix, step))  39.7 us
    dot_general x9, matrix products, dot_left(): jnp.einsum('cj,ij->ci', grad_side, weight, preferred_element_type=jnp.flo...  27.3 us
    pallas_call x2, Pallas kernels, attend_back(): pl.pallas_call(attend_back_kernel, grid=(blocks,), out_shape=(jax.ShapeDt...  26.4 us
    dot_general x8, matrix products, dot_right(): return jnp.dot(left_side, weight, preferred_element_type=jnp.float32)  25.7 us
    pallas_call x2, Pallas kernels, attend(): pl.pallas_call(attend_kernel, grid=(blocks,), out_shape=(jax.ShapeDtypeSt...  19.7 us
    unnamed x96, local copies, waits for them, and re-layouts  19.5 us
  transfers between devices with their start and end apart: 43, of which 18 were waited for; matrix products, arithmetic and copies ran while one was open for 20% of the time, Pallas kernels for 8%

profile of v2, /device:TPU:0, one launch (start us, length us, event | category | flops | bytes accessed | tf_op | source)
XLA Modules:
  0.0 484.4 jit_solution(5515711889702060123)
XLA Ops:
  21.0 5.8 %collective-permute-done.1 = bf16[48,1280]{1,0:T(8,128)(2,1)S(1)} collective-permute-done((bf16[48,1280]{1,0:T(8,128)(2,1)S(1)}, bf16[48,1280]{1,0:T(8,128)(2,1)S(1)}, u32[]{:S(2)}, u32[]{:S(2)}) %collective-permute-start.1) | collective-permute-done | bytes 122912 | tf_op jit(solution)/shard_map/ppermute | solution.py:198
  31.4 3.4 collective-permute-done.11
  34.8 9.6 %collective-permute-done.12 = bf16[48,1920]{1,0:T(8,128)(2,1)S(1)} collective-permute-done((bf16[48,1920]{1,0:T(8,128)(2,1)S(1)}, bf16[48,1920]{1,0:T(8,128)(2,1)S(1)}, u32[]{:S(2)}, u32[]{:S(2)}) %collective-permute-start.12) | collective-permute-done | bytes 184352 | tf_op jit(solution)/shard_map/ppermute | solution.py:198
  52.6 9.1 %collective-permute-done.3.refs_1_ = bf16[4,48,1280]{2,1,0:T(8,128)(2,1)} collective-permute-done((bf16[4,48,1280]{2,1,0:T(8,128)(2,1)S(1)}, bf16[4,48,1280]{2,1,0:T(8,128)(2,1)}, u32[]{:S(2)}, u32[]{:S(2)}) %collective-permute-start.3) | collective-permute-done | bytes 491552 | tf_op jit(solution)/shard_map/ppermute | solution.py:198
  68.0 9.8 %all-to-all-start = ((bf16[16,48,768]{2,1,0:T(8,128)(2,1)}), bf16[16,48,768]{2,1,0:T(8,128)(2,1)S(1)}, u32[]{:S(2)}, u32[]{:S(2)}) async-start(bf16[16,48,768]{2,1,0:T(8,128)(2,1)} %param.20), calls=%async_computation | async-start | bytes 2359296 | tf_op jit(solution)/shard_map/all_to_all | solution.py:438
  79.2 9.6 %collective-permute-done.15.refs_2_ = bf16[4,48,1920]{2,1,0:T(8,128)(2,1)} collective-permute-done((bf16[4,48,1920]{2,1,0:T(8,128)(2,1)S(1)}, bf16[4,48,1920]{2,1,0:T(8,128)(2,1)}, u32[]{:S(2)}, u32[]{:S(2)}) %collective-permute-start.15) | collective-permute-done | bytes 737312 | tf_op jit(solution)/shard_map/ppermute | solution.py:202
  91.4 4.8 place_rows.2
  102.0 27.7 %collective-permute-done.16.refs_3_ = bf16[4,48,1920]{2,1,0:T(8,128)(2,1)} collective-permute-done((bf16[4,48,1920]{2,1,0:T(8,128)(2,1)}, bf16[4,48,1920]{2,1,0:T(8,128)(2,1)}, u32[]{:S(2)}, u32[]{:S(2)}) %collective-permute-start.16) | collective-permute-done | bytes 737312 | tf_op jit(solution)/shard_map/ppermute | solution.py:198
  134.3 7.6 %attend.2 = (bf16[224,768]{1,0:T(8,128)(2,1)}, f32[6,2,224]{2,1,0:T(2,128)}) custom-call(bf16[224,768]{1,0:T(8,128)(2,1)} %slice.247.query_ref, bf16[448,1536]{1,0:T(8,128)(2,1)} %pad_maximum_fusion.3.key_ref.value_ref, bf16[448,1536]{1,0:T(8,128)(2,1)} %pad_maximum_fusion.3.key_ref.value_ref, f32[448,224]{1,0:T(8,128)} %and_select_fusion.bias_ref), custom_call_target="tpu_custom_call" | custom-call | flops 1233125376 | bytes 1376256 | tf_op jit(solution)/shard_map/attend/pallas_call | solution.py:135
  142.2 6.2 %place_rows.3 = bf16[768,3840]{1,0:T(8,128)(2,1)} custom-call(s32[4]{0:T(128)} %pad_add_fusion.1.where_ref, bf16[4,48,1920]{2,1,0:T(8,128)(2,1)} %copy-done.4, bf16[4,48,1920]{2,1,0:T(8,128)(2,1)} %collective-permute-done.14.refs_1_, bf16[4,48,1920]{2,1,0:T(8,128)(2,1)} %collective-permute-done.15.refs_2_, ...), custom_call_target="tpu_custom_call" | custom-call | bytes 11796480 | tf_op jit(solution)/shard_map/place_rows/pallas_call | solution.py:294
  152.9 9.0 %collective-permute-done.21 = bf16[768,768]{1,0:T(8,128)(2,1)} collective-permute-done((bf16[768,768]{1,0:T(8,128)(2,1)S(1)}, bf16[768,768]{1,0:T(8,128)(2,1)}, u32[]{:S(2)}, u32[]{:S(2)}) %collective-permute-start.21) | collective-permute-done | bytes 1179680 | tf_op jit(solution)/shard_map/ppermute | solution.py:202
  161.9 8.0 %add_convert_fusion.key_ref.value_ref = bf16[1536,1536]{1,0:T(8,128)(2,1)} fusion(f32[1536]{0:T(1024)S(1)} %concatenate.89, bf16[768,3840]{1,0:T(8,128)(2,1)} %place_rows.3, bf16[768,768]{1,0:T(8,128)(2,1)} %collective-permute-done.21, bf16[768,768]{1,0:T(8,128)(2,1)S(1)} %bitcast.212), kind=kOutput, calls=%fused_computation | convolution fusion | flops 3633315840 | bytes 9443328 | tf_op jit(solution)/shard_map/dot_general | solution.py:31
  171.4 12.1 %attend.3 = (bf16[224,768]{1,0:T(8,128)(2,1)}, f32[6,2,224]{2,1,0:T(2,128)}) custom-call(bf16[224,768]{1,0:T(8,128)(2,1)} %fusion.32.query_ref, bf16[1536,1536]{1,0:T(8,128)(2,1)} %add_convert_fusion.key_ref.value_ref, bf16[1536,1536]{1,0:T(8,128)(2,1)} %add_convert_fusion.key_ref.value_ref, f32[1536,224]{1,0:T(8,128)} %broadcast_in_dim.41.bias_ref), custom_call_target="tpu_custom_call" | custom-call | flops 4227858432 | bytes 4718592 | tf_op jit(solution)/shard_map/attend/pallas_call | solution.py:135
  191.7 8.5 %multiply_convert_fusion = (bf16[224,3072]{1,0:T(8,128)(2,1)S(1)}, f32[224,3072]{1,0:T(8,128)S(1)}, f32[224,3072]{1,0:T(8,128)S(1)}) fusion(f32[3072]{0:T(1024)S(1)} %reshape.329, bf16[224,768]{1,0:T(8,128)(2,1)S(1)} %add_convert_fusion.4, bf16[768,3072]{1,0:T(8,128)(2,1)S(1)} %bitcast.196), kind=kOutput, calls=%fused_computation.21 | convolution fusion | flops 1102381056 | bytes 11956224 | tf_op jit(solution)/shard_map/dot_general | solution.py:31
  216.7 4.5 multiply_reduce_fusion
  224.1 18.1 %attend_back.2 = (bf16[224,768]{1,0:T(8,128)(2,1)}, bf16[1536,768]{1,0:T(8,128)(2,1)}, bf16[1536,768]{1,0:T(8,128)(2,1)}) custom-call(bf16[224,768]{1,0:T(8,128)(2,1)} %fusion.32.query_ref, bf16[1536,1536]{1,0:T(8,128)(2,1)} %add_convert_fusion.key_ref.value_ref, bf16[1536,1536]{1,0:T(8,128)(2,1)} %add_convert_fusion.key_ref.value_ref, ...), custom_call_target="tpu_custom_call" | custom-call | flops 10569646080 | bytes 9437184 | tf_op jit(solution)/shard_map/attend_back/pallas_call | solution.py:159
  242.2 4.2 fusion.36
  246.4 3.3 convolution_add_fusion.1
  260.6 3.4 convolution_convert_fusion.11
  264.1 3.3 convolution_convert_fusion.12
  287.4 8.3 %attend_back.3 = (bf16[224,768]{1,0:T(8,128)(2,1)}, bf16[448,768]{1,0:T(8,128)(2,1)}, bf16[448,768]{1,0:T(8,128)(2,1)}) custom-call(bf16[224,768]{1,0:T(8,128)(2,1)} %slice.247.query_ref, bf16[448,1536]{1,0:T(8,128)(2,1)} %pad_maximum_fusion.3.key_ref.value_ref, bf16[448,1536]{1,0:T(8,128)(2,1)} %pad_maximum_fusion.3.key_ref.value_ref, ...), custom_call_target="tpu_custom_call" | custom-call | flops 3082813440 | bytes 2752512 | tf_op jit(solution)/shard_map/attend_back/pallas_call | solution.py:159
  298.5 3.7 add_convert_fusion.2
  323.6 4.1 fusion.68
  328.2 3.6 concatenate.96
  333.6 5.5 %collective-permute-done.32 = bf16[4,2,16,3072]{3,2,0,1:T(8,128)(2,1)} collective-permute-done((bf16[4,2,16,3072]{3,2,0,1:T(8,128)(2,1)}, bf16[4,2,16,3072]{3,2,0,1:T(8,128)(2,1)}, u32[]{:S(2)}, u32[]{:S(2)}) %collective-permute-start.32) | collective-permute-done | bytes 786464 | tf_op jit(solution)/shard_map/ppermute | solution.py:202
  343.7 12.3 %all-to-all-start.1 = ((bf16[16,48,768]{2,1,0:T(8,128)(2,1)}), bf16[16,48,768]{2,1,0:T(8,128)(2,1)}, u32[]{:S(2)}, u32[]{:S(2)}) async-start(bf16[16,48,768]{2,1,0:T(8,128)(2,1)} %bitcast.200), calls=%async_computation.1 | async-start | bytes 2359296 | tf_op jit(solution)/shard_map/all_to_all | solution.py:579
  356.0 28.0 %collective-permute-done.33 = bf16[4,32,3072]{2,1,0:T(8,128)(2,1)} collective-permute-done((bf16[4,32,3072]{2,1,0:T(8,128)(2,1)S(1)}, bf16[4,32,3072]{2,1,0:T(8,128)(2,1)}, u32[]{:S(2)}, u32[]{:S(2)}) %collective-permute-start.33) | collective-permute-done | bytes 786464 | tf_op jit(solution)/shard_map/ppermute | solution.py:198
  396.1 16.9 %collective-permute-done.35 = bf16[32,3072]{1,0:T(8,128)(2,1)S(1)} collective-permute-done((bf16[32,3072]{1,0:T(8,128)(2,1)S(1)}, bf16[32,3072]{1,0:T(8,128)(2,1)S(1)}, u32[]{:S(2)}, u32[]{:S(2)}) %collective-permute-start.35) | collective-permute-done | bytes 196640 | tf_op jit(solution)/shard_map/ppermute | solution.py:198
  419.6 12.5 %collective-permute-done.27 = bf16[4,32,3328]{2,1,0:T(8,128)(2,1)S(1)} collective-permute-done((bf16[4,32,3328]{2,1,0:T(8,128)(2,1)S(1)}, bf16[4,32,3328]{2,1,0:T(8,128)(2,1)S(1)}, u32[]{:S(2)}, u32[]{:S(2)}) %collective-permute-start.27) | collective-permute-done | bytes 852000 | tf_op jit(solution)/shard_map/ppermute | solution.py:198
  432.3 10.1 %collective-permute-start.28 = (bf16[32,3328]{1,0:T(8,128)(2,1)S(1)}, bf16[32,3328]{1,0:T(8,128)(2,1)S(1)}, u32[]{:S(2)}, u32[]{:S(2)}) collective-permute-start(bf16[32,3328]{1,0:T(8,128)(2,1)S(1)} %get-tuple-element.202), channel_id=1, source_target_pairs={{0,8},{2,10},{4,12},{6,14},{8,0},{10,2},{12,4},{14,6},{16,24},{18,... | collective-permute-start | bytes 638984 | tf_op jit(solution)/shard_map/ppermute | solution.py:198
  448.9 7.2 %collective-permute-done.29 = bf16[32,3328]{1,0:T(8,128)(2,1)S(1)} collective-permute-done((bf16[32,3328]{1,0:T(8,128)(2,1)S(1)}, bf16[32,3328]{1,0:T(8,128)(2,1)S(1)}, u32[]{:S(2)}, u32[]{:S(2)}) %collective-permute-start.29) | collective-permute-done | bytes 213024 | tf_op jit(solution)/shard_map/ppermute | solution.py:198
  469.5 6.0 %collective-permute-done.38 = bf16[384,768]{1,0:T(8,128)(2,1)S(1)} collective-permute-done((bf16[384,768]{1,0:T(8,128)(2,1)}, bf16[384,768]{1,0:T(8,128)(2,1)S(1)}, u32[]{:S(2)}, u32[]{:S(2)}) %collective-permute-start.38) | collective-permute-done | bytes 589856 | tf_op jit(solution)/shard_map/ppermute | solution.py:202
  (330 shorter events, 180.3 us)
Async XLA Ops:
  7.2 178.7 %all-gather.2.cloned.1.call-start = ((), (), s32[]{:S(2)}) async-start(), calls=%async_computation.3 | async-start | bytes 10027008 | tf_op jit(solution)/shard_map/all_gather | solution.py:441
  14.5 12.3 %collective-permute-start.1 = (bf16[48,1280]{1,0:T(8,128)(2,1)S(1)}, bf16[48,1280]{1,0:T(8,128)(2,1)S(1)}, u32[]{:S(2)}, u32[]{:S(2)}) collective-permute-start(bf16[48,1280]{1,0:T(8,128)(2,1)S(1)} %fusion.106), channel_id=1, source_target_pairs={{0,16},{2,18},{4,20},{6,22},{8,24},{10,26},{12,28},{14,30},{16,0},... | collective-permute-start | bytes 368648 | tf_op jit(solution)/shard_map/ppermute | solution.py:198
  28.9 15.5 %collective-permute-start.12 = (bf16[48,1920]{1,0:T(8,128)(2,1)S(1)}, bf16[48,1920]{1,0:T(8,128)(2,1)S(1)}, u32[]{:S(2)}, u32[]{:S(2)}) collective-permute-start(bf16[48,1920]{1,0:T(8,128)(2,1)S(1)} %constant_dynamic-slice_fusion.8), channel_id=1, source_target_pairs={{0,16},{2,18},{4,20},{6,22},{8,24},{10,26},{12,28},{14,30},{16,0},... | collective-permute-start | bytes 552968 | tf_op jit(solution)/shard_map/ppermute | solution.py:198
  30.0 14.4 %collective-permute-start.13 = (bf16[48,1920]{1,0:T(8,128)(2,1)S(1)}, bf16[48,1920]{1,0:T(8,128)(2,1)S(1)}, u32[]{:S(2)}, u32[]{:S(2)}) collective-permute-start(bf16[48,1920]{1,0:T(8,128)(2,1)S(1)} %constant_dynamic-slice_fusion.8), channel_id=1, source_target_pairs={{0,24},{2,26},{4,28},{6,30},{8,16},{10,18},{12,20},{14,22},{16,8},... | collective-permute-start | bytes 552968 | tf_op jit(solution)/shard_map/ppermute | solution.py:198
  44.6 20.3 %collective-permute-start.10 = (bf16[224,768]{1,0:T(8,128)(2,1)S(1)}, bf16[224,768]{1,0:T(8,128)(2,1)S(1)}, u32[]{:S(2)}, u32[]{:S(2)}) collective-permute-start(bf16[224,768]{1,0:T(8,128)(2,1)S(1)} %bitcast.189), channel_id=1, source_target_pairs={{0,1},{1,0},{2,3},{3,2},{4,5},{5,4},{6,7},{7,6},{8,9},{9,8},{10,11... | collective-permute-start | bytes 1032200 | tf_op jit(solution)/shard_map/ppermute | solution.py:202
  48.9 12.8 %collective-permute-start.3 = (bf16[4,48,1280]{2,1,0:T(8,128)(2,1)S(1)}, bf16[4,48,1280]{2,1,0:T(8,128)(2,1)}, u32[]{:S(2)}, u32[]{:S(2)}) collective-permute-start(bf16[4,48,1280]{2,1,0:T(8,128)(2,1)S(1)} %pad_maximum_fusion.12.refs_0_), channel_id=1, source_target_pairs={{0,4},{2,6},{4,0},{6,2},{8,12},{10,14},{12,8},{14,10},{16,20},{18,... | collective-permute-start | bytes 1474568 | tf_op jit(solution)/shard_map/ppermute | solution.py:198
  52.1 25.9 %collective-permute-start.4 = (bf16[4,48,1280]{2,1,0:T(8,128)(2,1)S(1)}, bf16[4,48,1280]{2,1,0:T(8,128)(2,1)}, u32[]{:S(2)}, u32[]{:S(2)}) collective-permute-start(bf16[4,48,1280]{2,1,0:T(8,128)(2,1)S(1)} %pad_maximum_fusion.12.refs_0_), channel_id=1, source_target_pairs={{0,1},{1,0},{2,3},{3,2},{4,5},{5,4},{6,7},{7,6},{8,9},{9,8},{10,11... | collective-permute-start | bytes 1474568 | tf_op jit(solution)/shard_map/ppermute | solution.py:202
  52.6 25.8 %collective-permute-start.6 = (bf16[4,48,1280]{2,1,0:T(8,128)(2,1)S(1)}, bf16[4,48,1280]{2,1,0:T(8,128)(2,1)}, u32[]{:S(2)}, u32[]{:S(2)}) collective-permute-start(bf16[4,48,1280]{2,1,0:T(8,128)(2,1)S(1)} %pad_maximum_fusion.12.refs_0_), channel_id=1, source_target_pairs={{0,2},{2,0},{4,6},{6,4},{8,10},{10,8},{12,14},{14,12},{16,18},{18,... | collective-permute-start | bytes 1474568 | tf_op jit(solution)/shard_map/ppermute | solution.py:198
  61.8 16.8 %collective-permute-start.5 = (bf16[4,48,1280]{2,1,0:T(8,128)(2,1)}, bf16[4,48,1280]{2,1,0:T(8,128)(2,1)}, u32[]{:S(2)}, u32[]{:S(2)}) collective-permute-start(bf16[4,48,1280]{2,1,0:T(8,128)(2,1)} %collective-permute-done.3.refs_1_), channel_id=1, source_target_pairs={{0,1},{1,0},{2,3},{3,2},{4,5},{5,4},{6,7},{7,6},{8,9},{9,8},{10,11... | collective-permute-start | bytes 1474568 | tf_op jit(solution)/shard_map/ppermute | solution.py:202
  62.8 26.0 %collective-permute-start.15 = (bf16[4,48,1920]{2,1,0:T(8,128)(2,1)S(1)}, bf16[4,48,1920]{2,1,0:T(8,128)(2,1)}, u32[]{:S(2)}, u32[]{:S(2)}) collective-permute-start(bf16[4,48,1920]{2,1,0:T(8,128)(2,1)S(1)} %pad_maximum_fusion.4.refs_0_), channel_id=1, source_target_pairs={{0,1},{1,0},{2,3},{3,2},{4,5},{5,4},{6,7},{7,6},{8,9},{9,8},{10,11... | collective-permute-start | bytes 2211848 | tf_op jit(solution)/shard_map/ppermute | solution.py:202
  64.8 24.0 %collective-permute-start.14 = (bf16[4,48,1920]{2,1,0:T(8,128)(2,1)S(1)}, bf16[4,48,1920]{2,1,0:T(8,128)(2,1)}, u32[]{:S(2)}, u32[]{:S(2)}) collective-permute-start(bf16[4,48,1920]{2,1,0:T(8,128)(2,1)S(1)} %pad_maximum_fusion.4.refs_0_), channel_id=1, source_target_pairs={{0,4},{2,6},{4,0},{6,2},{8,12},{10,14},{12,8},{14,10},{16,20},{18,... | collective-permute-start | bytes 2211848 | tf_op jit(solution)/shard_map/ppermute | solution.py:198
  68.0 65.4 %all-to-all-start = ((bf16[16,48,768]{2,1,0:T(8,128)(2,1)}), bf16[16,48,768]{2,1,0:T(8,128)(2,1)S(1)}, u32[]{:S(2)}, u32[]{:S(2)}) async-start(bf16[16,48,768]{2,1,0:T(8,128)(2,1)} %param.20), calls=%async_computation | async-start | bytes 2359296 | tf_op jit(solution)/shard_map/all_to_all | solution.py:438
  77.8 387.6 %reduce-scatter.2.cloned.1.call-start = ((), (), s32[]{:S(2)}) async-start(), calls=%async_computation.4 | async-start | bytes 10027008 | tf_op jit(solution)/shard_map/reduce_scatter | solution.py:533
  78.0 12.4 %collective-permute-start.7 = (bf16[4,48,1280]{2,1,0:T(8,128)(2,1)}, bf16[4,48,1280]{2,1,0:T(8,128)(2,1)}, u32[]{:S(2)}, u32[]{:S(2)}) collective-permute-start(bf16[4,48,1280]{2,1,0:T(8,128)(2,1)} %collective-permute-done.3.refs_1_), channel_id=1, source_target_pairs={{0,2},{2,0},{4,6},{6,4},{8,10},{10,8},{12,14},{14,12},{16,18},{18,... | collective-permute-start | bytes 1474568 | tf_op jit(solution)/shard_map/ppermute | solution.py:198
  88.8 53.3 %collective-permute-start.17 = (bf16[4,48,1920]{2,1,0:T(8,128)(2,1)S(1)}, bf16[4,48,1920]{2,1,0:T(8,128)(2,1)}, u32[]{:S(2)}, u32[]{:S(2)}) collective-permute-start(bf16[4,48,1920]{2,1,0:T(8,128)(2,1)S(1)} %pad_maximum_fusion.4.refs_0_), channel_id=1, source_target_pairs={{0,2},{2,0},{4,6},{6,4},{8,10},{10,8},{12,14},{14,12},{16,18},{18,... | collective-permute-start | bytes 2211848 | tf_op jit(solution)/shard_map/ppermute | solution.py:198
  88.8 40.8 %collective-permute-start.16 = (bf16[4,48,1920]{2,1,0:T(8,128)(2,1)}, bf16[4,48,1920]{2,1,0:T(8,128)(2,1)}, u32[]{:S(2)}, u32[]{:S(2)}) collective-permute-start(bf16[4,48,1920]{2,1,0:T(8,128)(2,1)} %collective-permute-done.15.refs_2_), channel_id=1, source_target_pairs={{0,4},{2,6},{4,0},{6,2},{8,12},{10,14},{12,8},{14,10},{16,20},{18,... | collective-permute-start | bytes 2211848 | tf_op jit(solution)/shard_map/ppermute | solution.py:198
  90.3 51.8 %collective-permute-start.19 = (bf16[4,48,1920]{2,1,0:T(8,128)(2,1)}, bf16[4,48,1920]{2,1,0:T(8,128)(2,1)}, u32[]{:S(2)}, u32[]{:S(2)}) collective-permute-start(bf16[4,48,1920]{2,1,0:T(8,128)(2,1)} %collective-permute-done.15.refs_2_), channel_id=1, source_target_pairs={{0,2},{2,0},{4,6},{6,4},{8,10},{10,8},{12,14},{14,12},{16,18},{18,... | collective-permute-start | bytes 2211848 | tf_op jit(solution)/shard_map/ppermute | solution.py:198
  90.6 51.6 %collective-permute-start.18 = (bf16[4,48,1920]{2,1,0:T(8,128)(2,1)}, bf16[4,48,1920]{2,1,0:T(8,128)(2,1)}, u32[]{:S(2)}, u32[]{:S(2)}) collective-permute-start(bf16[4,48,1920]{2,1,0:T(8,128)(2,1)} %collective-permute-done.14.refs_1_), channel_id=1, source_target_pairs={{0,2},{2,0},{4,6},{6,4},{8,10},{10,8},{12,14},{14,12},{16,18},{18,... | collective-permute-start | bytes 2211848 | tf_op jit(solution)/shard_map/ppermute | solution.py:198
  129.7 12.5 %collective-permute-start.20 = (bf16[4,48,1920]{2,1,0:T(8,128)(2,1)}, bf16[4,48,1920]{2,1,0:T(8,128)(2,1)}, u32[]{:S(2)}, u32[]{:S(2)}) collective-permute-start(bf16[4,48,1920]{2,1,0:T(8,128)(2,1)} %collective-permute-done.16.refs_3_), channel_id=1, source_target_pairs={{0,2},{2,0},{4,6},{6,4},{8,10},{10,8},{12,14},{14,12},{16,18},{18,... | collective-permute-start | bytes 2211848 | tf_op jit(solution)/shard_map/ppermute | solution.py:198
  133.4 28.5 %collective-permute-start.21 = (bf16[768,768]{1,0:T(8,128)(2,1)S(1)}, bf16[768,768]{1,0:T(8,128)(2,1)}, u32[]{:S(2)}, u32[]{:S(2)}) collective-permute-start(bf16[768,768]{1,0:T(8,128)(2,1)S(1)} %bitcast.211), channel_id=1, source_target_pairs={{0,1},{1,0},{2,3},{3,2},{4,5},{5,4},{6,7},{7,6},{8,9},{9,8},{10,11... | collective-permute-start | bytes 3538952 | tf_op jit(solution)/shard_map/ppermute | solution.py:202
  269.7 32.5 %collective-permute-start.22 = (bf16[4,2,48,3072]{3,2,0,1:T(8,128)(2,1)}, bf16[4,2,48,3072]{3,2,0,1:T(8,128)(2,1)}, u32[]{:S(2)}, u32[]{:S(2)}) collective-permute-start(bf16[4,2,48,3072]{3,2,0,1:T(8,128)(2,1)} %pad_maximum_fusion.2), channel_id=1, source_target_pairs={{0,2},{2,0},{4,6},{6,4},{8,10},{10,8},{12,14},{14,12},{16,18},{18,... | collective-permute-start | bytes 7077896 | tf_op jit(solution)/shard_map/ppermute | solution.py:198
  269.8 28.7 %collective-permute-start.23 = (bf16[768,768]{1,0:T(8,128)(2,1)}, bf16[768,768]{1,0:T(8,128)(2,1)}, u32[]{:S(2)}, u32[]{:S(2)}) collective-permute-start(bf16[768,768]{1,0:T(8,128)(2,1)} %slice.352), channel_id=1, source_target_pairs={{0,1},{1,0},{2,3},{3,2},{4,5},{5,4},{6,7},{7,6},{8,9},{9,8},{10,11... | collective-permute-start | bytes 3538952 | tf_op jit(solution)/shard_map/ppermute | solution.py:202
  313.3 25.8 %collective-permute-start.32 = (bf16[4,2,16,3072]{3,2,0,1:T(8,128)(2,1)}, bf16[4,2,16,3072]{3,2,0,1:T(8,128)(2,1)}, u32[]{:S(2)}, u32[]{:S(2)}) collective-permute-start(bf16[4,2,16,3072]{3,2,0,1:T(8,128)(2,1)} %dynamic-slice_convert_fusion.7), channel_id=1, source_target_pairs={{0,1},{1,0},{2,3},{3,2},{4,5},{5,4},{6,7},{7,6},{8,9},{9,8},{10,11... | collective-permute-start | bytes 2359304 | tf_op jit(solution)/shard_map/ppermute | solution.py:202
  333.6 57.7 %collective-permute-start.25 = (bf16[4,2,48,3328]{3,2,1,0:T(8,128)(2,1)}, bf16[4,2,48,3328]{3,2,1,0:T(8,128)(2,1)}, u32[]{:S(2)}, u32[]{:S(2)}) collective-permute-start(bf16[4,2,48,3328]{3,2,1,0:T(8,128)(2,1)} %get-tuple-element.225), channel_id=1, source_target_pairs={{0,2},{2,0},{4,6},{6,4},{8,10},{10,8},{12,14},{14,12},{16,18},{18,... | collective-permute-start | bytes 7667720 | tf_op jit(solution)/shard_map/ppermute | solution.py:198
  341.7 42.3 %collective-permute-start.33 = (bf16[4,32,3072]{2,1,0:T(8,128)(2,1)S(1)}, bf16[4,32,3072]{2,1,0:T(8,128)(2,1)}, u32[]{:S(2)}, u32[]{:S(2)}) collective-permute-start(bf16[4,32,3072]{2,1,0:T(8,128)(2,1)S(1)} %fusion.60), channel_id=1, source_target_pairs={{0,4},{2,6},{4,0},{6,2},{8,12},{10,14},{12,8},{14,10},{16,20},{18,... | collective-permute-start | bytes 2359304 | tf_op jit(solution)/shard_map/ppermute | solution.py:198
  343.7 114.7 %all-to-all-start.1 = ((bf16[16,48,768]{2,1,0:T(8,128)(2,1)}), bf16[16,48,768]{2,1,0:T(8,128)(2,1)}, u32[]{:S(2)}, u32[]{:S(2)}) async-start(bf16[16,48,768]{2,1,0:T(8,128)(2,1)} %bitcast.200), calls=%async_computation.1 | async-start | bytes 2359296 | tf_op jit(solution)/shard_map/all_to_all | solution.py:579
  388.0 25.0 %collective-permute-start.35 = (bf16[32,3072]{1,0:T(8,128)(2,1)S(1)}, bf16[32,3072]{1,0:T(8,128)(2,1)S(1)}, u32[]{:S(2)}, u32[]{:S(2)}) collective-permute-start(bf16[32,3072]{1,0:T(8,128)(2,1)S(1)} %get-tuple-element.207), channel_id=1, source_target_pairs={{0,16},{2,18},{4,20},{6,22},{8,24},{10,26},{12,28},{14,30},{16,0},... | collective-permute-start | bytes 589832 | tf_op jit(solution)/shard_map/ppermute | solution.py:198
  389.9 23.1 %collective-permute-start.36 = (bf16[32,3072]{1,0:T(8,128)(2,1)S(1)}, bf16[32,3072]{1,0:T(8,128)(2,1)S(1)}, u32[]{:S(2)}, u32[]{:S(2)}) collective-permute-start(bf16[32,3072]{1,0:T(8,128)(2,1)S(1)} %get-tuple-element.206), channel_id=1, source_target_pairs={{0,24},{2,26},{4,28},{6,30},{8,16},{10,18},{12,20},{14,22},{16,8},... | collective-permute-start | bytes 589832 | tf_op jit(solution)/shard_map/ppermute | solution.py:198
  394.5 21.4 %collective-permute-start.26 = (bf16[4,2,16,3328]{3,2,1,0:T(8,128)(2,1)S(1)}, bf16[4,2,16,3328]{3,2,1,0:T(8,128)(2,1)S(1)}, u32[]{:S(2)}, u32[]{:S(2)}) collective-permute-start(bf16[4,2,16,3328]{3,2,1,0:T(8,128)(2,1)S(1)} %dynamic-slice_convert_fusion.4), channel_id=1, source_target_pairs={{0,1},{1,0},{2,3},{3,2},{4,5},{5,4},{6,7},{7,6},{8,9},{9,8},{10,11... | collective-permute-start | bytes 2555912 | tf_op jit(solution)/shard_map/ppermute | solution.py:202
  416.4 15.6 %collective-permute-start.27 = (bf16[4,32,3328]{2,1,0:T(8,128)(2,1)S(1)}, bf16[4,32,3328]{2,1,0:T(8,128)(2,1)S(1)}, u32[]{:S(2)}, u32[]{:S(2)}) collective-permute-start(bf16[4,32,3328]{2,1,0:T(8,128)(2,1)S(1)} %fusion.50), channel_id=1, source_target_pairs={{0,4},{2,6},{4,0},{6,2},{8,12},{10,14},{12,8},{14,10},{16,20},{18,... | collective-permute-start | bytes 2555912 | tf_op jit(solution)/shard_map/ppermute | solution.py:198
  432.3 16.6 %collective-permute-start.28 = (bf16[32,3328]{1,0:T(8,128)(2,1)S(1)}, bf16[32,3328]{1,0:T(8,128)(2,1)S(1)}, u32[]{:S(2)}, u32[]{:S(2)}) collective-permute-start(bf16[32,3328]{1,0:T(8,128)(2,1)S(1)} %get-tuple-element.202), channel_id=1, source_target_pairs={{0,8},{2,10},{4,12},{6,14},{8,0},{10,2},{12,4},{14,6},{16,24},{18,... | collective-permute-start | bytes 638984 | tf_op jit(solution)/shard_map/ppermute | solution.py:198
  442.4 13.8 %collective-permute-start.29 = (bf16[32,3328]{1,0:T(8,128)(2,1)S(1)}, bf16[32,3328]{1,0:T(8,128)(2,1)S(1)}, u32[]{:S(2)}, u32[]{:S(2)}) collective-permute-start(bf16[32,3328]{1,0:T(8,128)(2,1)S(1)} %get-tuple-element.204), channel_id=1, source_target_pairs={{0,16},{2,18},{4,20},{6,22},{8,24},{10,26},{12,28},{14,30},{16,0},... | collective-permute-start | bytes 638984 | tf_op jit(solution)/shard_map/ppermute | solution.py:198
  (52 other events, 539.1 us)
Sparse Core Ops, SparseCore 0:
  44.7 110.5 all-gather.1
  271.0 153.9 reduce-scatter.1

commit v3 on v2

--- a/solution.py
+++ b/solution.py
@@ -83,7 +83,7 @@
 
 
 def attend_back_kernel(
-    query_ref, key_ref, value_ref, bias_ref, total_ref, grad_ref, gq_ref, gk_ref, gv_ref
+    query_ref, key_ref, value_ref, bias_ref, total_ref, grad_ref, gq_ref, pair_ref
 ):
     score_scale = HEAD_DIM ** (-0.5)
     key, value = key_ref[...], value_ref[...]
@@ -110,8 +110,8 @@
         for item, query in zip(grad_scores, queries)
     ]
     sides = [dot_of(key, item, DOWN_BOTH) for item in grad_scores]
-    gk_ref[...] = (keys[0] + keys[1]).astype(jnp.bfloat16)
-    gv_ref[...] = (values[0] + values[1]).astype(jnp.bfloat16)
+    pair_ref[0] = (keys[0] + keys[1]).astype(jnp.bfloat16)
+    pair_ref[1] = (values[0] + values[1]).astype(jnp.bfloat16)
     picked = [
         sides[head][head * HEAD_DIM : (head + 1) * HEAD_DIM] * score_scale for head in range(2)
     ]
@@ -131,7 +131,6 @@
     rows, width = queries.shape
     keys = pairs.shape[0]
     blocks = width // LANES
-    work = 4 * rows * keys * width
     return pl.pallas_call(
         attend_kernel,
         grid=(blocks,),
@@ -144,9 +143,7 @@
             pl.BlockSpec((rows, LANES), lambda i: (0, i)),
             pl.BlockSpec((1, 2, rows), lambda i: (i, 0, 0)),
         ),
-        cost_estimate=pl.CostEstimate(
-            flops=4 * work, transcendentals=0, bytes_accessed=4 * keys * width
-        ),
+        cost_estimate=pl.CostEstimate(flops=0, transcendentals=0, bytes_accessed=0),
         name="attend",
     )(queries, pairs, pairs, bias)
 
@@ -155,14 +152,12 @@
     rows, width = queries.shape
     keys = pairs.shape[0]
     blocks = width // LANES
-    work = 10 * rows * keys * width
     return pl.pallas_call(
         attend_back_kernel,
         grid=(blocks,),
         out_shape=(
             jax.ShapeDtypeStruct((rows, width), jnp.bfloat16),
-            jax.ShapeDtypeStruct((keys, width), jnp.bfloat16),
-            jax.ShapeDtypeStruct((keys, width), jnp.bfloat16),
+            jax.ShapeDtypeStruct((2, keys, width), jnp.bfloat16),
         ),
         in_specs=head_specs(rows, keys, blocks)
         + [
@@ -171,12 +166,9 @@
         ],
         out_specs=(
             pl.BlockSpec((rows, LANES), lambda i: (0, i)),
-            pl.BlockSpec((keys, LANES), lambda i: (0, i)),
-            pl.BlockSpec((keys, LANES), lambda i: (0, i)),
+            pl.BlockSpec((2, keys, LANES), lambda i: (0, 0, i)),
         ),
-        cost_estimate=pl.CostEstimate(
-            flops=4 * work, transcendentals=0, bytes_accessed=8 * keys * width
-        ),
+        cost_estimate=pl.CostEstimate(flops=0, transcendentals=0, bytes_accessed=0),
         name="attend_back",
     )(queries, pairs, pairs, bias, totals, grads)
 
@@ -286,9 +278,7 @@
             + [pl.BlockSpec(memory_space=pl.ANY)] * 8,
             out_specs=pl.BlockSpec(memory_space=pltpu.VMEM),
             scratch_shapes=[pltpu.SemaphoreType.DMA],
-            cost_estimate=pl.CostEstimate(
-                flops=0, transcendentals=0, bytes_accessed=4 * total * self.cols
-            ),
+            cost_estimate=pl.CostEstimate(flops=0, transcendentals=0, bytes_accessed=0),
             name="place_rows",
         )
         return (call(jnp.stack(place_of()).astype(jnp.int32), *mine, *other),)
@@ -298,14 +288,128 @@
     return lax.reduce_precision(values, 8, 7).astype(jnp.bfloat16)
 
 
+def grad_kernel(where_ref, *refs, count, first, rows, blend):
+    terms, refs = [refs[4 * i : 4 * i + 4] for i in range(count)], refs[4 * count :]
+    extras, (kept_ref, sent_ref, total_ref) = refs[:blend], refs[blend:]
+    wide, core, seq = where_ref[1], where_ref[2], where_ref[3]
+    height = total_ref.shape[0]
+    groups = CORES * kept_ref.shape[0] * rows // height
+
+    def group_step(group, carry):
+        start = 0
+        for left_ref, far_left_ref, right_ref, far_right_ref in terms:
+            width = far_right_ref.shape[1]
+            span = pl.ds(pl.multiple_of(group * height, LANES), height)
+            if len(right_ref.shape) == 3:
+                right = right_ref[core]
+            else:
+                right = right_ref[:, pl.ds(pl.multiple_of(core * width, LANES), width)]
+            total_ref[:, :width] = dot_of(left_ref[:, span], right, DOWN_BOTH) + dot_of(
+                far_left_ref[:, span], far_right_ref[...], DOWN_BOTH
+            )
+            cols = slice(start, start + width)
+            for place, near, far in routes(group, height, first, rows, wide, seq):
+                for out_ref, base in ((kept_ref, near), (sent_ref, far)):
+                    picked = total_ref[pl.ds(pl.multiple_of(base, 16), rows), :width]
+                    out_ref[place, :, cols] = picked.astype(jnp.bfloat16)
+            start += width
+        if blend:
+            cols = slice(start, start + LANES)
+            for place, near, far in routes(group, height, first, rows, wide, seq):
+                for out_ref, base in ((kept_ref, near), (sent_ref, far)):
+                    picked = pl.ds(pl.multiple_of(group * height + base, 16), rows)
+                    out_ref[place, :, cols] = (
+                        extras[0][picked, :].astype(jnp.float32)
+                        + extras[1][picked, :].astype(jnp.float32)
+                    ).astype(jnp.bfloat16)
+        return carry
+
+    lax.fori_loop(0, groups, group_step, 0)
+
+
+def routes(group, height, first, rows, wide, seq):
+    if first == "seq":
+        pairs = height // (2 * rows)
+        return [
+            (group * pairs + i, (2 * i + seq) * rows, (2 * i + 1 - seq) * rows)
+            for i in range(pairs)
+        ]
+    quads = height // (4 * rows)
+    return [
+        (
+            (group * quads + i) * 2 + j,
+            (4 * i + 2 * wide + j) * rows,
+            (4 * i + 2 * (1 - wide) + j) * rows,
+        )
+        for i in range(quads)
+        for j in range(2)
+    ]
+
+
+def self_tail_kernel(query_ref, pair_ref, weight_ref, near_ref, far_ref, *refs):
+    vectors, base_ref, (side_ref, sent_ref, column_ref) = refs[:-4], refs[-4], refs[-3:]
+    rows, width = query_ref.shape
+    both = dot_of(pair_ref[0], weight_ref[:, width : 2 * width], ROWS_BY_LANES) + dot_of(
+        pair_ref[1], weight_ref[:, 2 * width : 3 * width], ROWS_BY_LANES
+    )
+    far = both[:rows]
+    side = both[rows:] + dot_of(query_ref[...], weight_ref[:, :width], ROWS_BY_LANES)
+    side_ref[...] = side
+    sent_ref[...] = far.astype(jnp.bfloat16)
+    sums = [
+        jnp.sum(side * near_ref[...] + far * far_ref[...], axis=0, keepdims=True),
+        jnp.sum(side + far, axis=0, keepdims=True),
+        jnp.sum(query_ref[...].astype(jnp.float32), axis=0, keepdims=True),
+    ]
+    count = len(sums) + len(vectors)
+    lane = lax.broadcasted_iota(jnp.int32, (LANES, LANES), 1)
+    blank = jnp.zeros((LANES - count, LANES), jnp.float32)
+    for i in range(width // LANES):
+        here = slice(i * LANES, (i + 1) * LANES)
+        block = jnp.concatenate(
+            [item[:, here] for item in sums] + [row[i : i + 1, :] for row in vectors] + [blank],
+            axis=0,
+        )
+        column_ref[here, :] = jnp.where(
+            lane < count, block.T, base_ref[here, :].astype(jnp.float32)
+        ).astype(jnp.bfloat16)
+
+
+def self_tail(query, pairs, weight, near, far, vectors, base):
+    rows, width = query.shape
+    return pl.pallas_call(
+        self_tail_kernel,
+        out_shape=(
+            jax.ShapeDtypeStruct((rows, width), jnp.float32),
+            jax.ShapeDtypeStruct((rows, width), jnp.bfloat16),
+            jax.ShapeDtypeStruct(base.shape, jnp.bfloat16),
+        ),
+        cost_estimate=pl.CostEstimate(flops=0, transcendentals=0, bytes_accessed=0),
+        name="self_tail",
+    )(query, pairs, weight, near, far, *[vector.reshape(-1, LANES) for vector in vectors], base)
+
+
+def half_of(right, which):
+    if right.ndim == 3:
+        return lax.dynamic_index_in_dim(right, which, 0, keepdims=False)
+    width = right.shape[1] // CORES
+    return lax.dynamic_slice_in_dim(right, which * width, width, 1)
+
+
 class Reduction:
-    def __init__(self, *terms):
+    def __init__(self, terms, first, extra=None):
         self.size = lax.axis_size("batch")
-        self.rows = terms[0].shape[0] // self.size
-        self.state = terms
+        self.depth = self.size // (CORES * PAIR)
+        self.rows = terms[0][0].shape[1] // self.size
+        self.first = first
+        self.terms, self.extra = terms, extra
         self.fast = splits(self.rows)
+        self.widths = [
+            right.shape[2] if right.ndim == 3 else right.shape[1] // CORES for _, _, right in terms
+        ]
+        self.state = ()
         self.todo = (
-            [self.by_core, self.by_seq, self.by_pair, self.by_depth, self.finish, self.join]
+            [self.begin, self.by_first, self.by_second, self.by_depth, self.by_seq, self.finish]
             if self.fast
             else [self.plain]
         )
@@ -318,75 +422,132 @@
     def result(self):
         while self.todo:
             self.step()
-        return self.state[0]
-
-    def plain(self, *terms):
-        terms = jnp.concatenate(terms, axis=1)
-        mine = lax.psum_scatter(terms, "batch", scatter_dimension=0, tiled=True)
-        return (lax.psum(mine, "seq").astype(jnp.float32),)
-
-    def by_core(self, *terms):
-        _, _, core, _ = place_of()
-        grids = [term.reshape(-1, PAIR, CORES, self.rows, term.shape[1]) for term in terms]
+            self.state = self.launch(*self.state)
+        return self.state
+
+    def plain(self):
+        whole = [
+            weight_term(left, jnp.concatenate(list(right), axis=1) if right.ndim == 3 else right)
+            for left, _, right in self.terms
+        ] + ([] if self.extra is None else [self.extra])
+        mine = lax.psum_scatter(
+            jnp.concatenate(whole, axis=1), "batch", scatter_dimension=0, tiled=True
+        )
+        mine = lax.psum(mine, "seq").astype(jnp.float32)
+        ends = [0]
+        for item in whole:
+            ends.append(ends[-1] + item.shape[1])
+        return tuple(mine[:, i:j] for i, j in zip(ends, ends[1:]))
+
+    def begin(self):
+        self.sender = self.along_seq if self.first == "seq" else self.along_pair
+        where = jnp.stack(place_of()).astype(jnp.int32)
+        operands = [where]
+        for left, far_left, right in self.terms:
+            operands += [left, far_left, right, swap(half_of(right, 1 - where[2]), 1)]
+        if self.extra is not None:
+            operands += [self.extra, swap(self.extra, 1)]
+        blend = 0 if self.extra is None else 2
+        total = sum(self.widths) + (LANES if blend else 0)
+        shape = jax.ShapeDtypeStruct((self.depth * PAIR, self.rows, total), jnp.bfloat16)
+        height = 3 * LANES
         return tuple(
-            jnp.concatenate(
-                [lax.dynamic_index_in_dim(grid, which, 2, keepdims=False) for grid in grids], axis=-1
-            )
-            for which in (core, 1 - core)
-        )
-
-    def by_seq(self, kept, sent):
-        seq, third = lax.axis_index("seq"), self.rows // 3
-        chip = kept.astype(jnp.float32) + swap(sent, 1).astype(jnp.float32)
-        edge = lax.dynamic_slice_in_dim(chip, (1 - seq) * 2 * third, third, 2)
-        kept = lax.dynamic_slice_in_dim(chip, seq * third, 2 * third, 2)
-        return kept.astype(jnp.bfloat16), edge.astype(jnp.bfloat16)
-
-    def by_pair(self, kept, sent):
+            pl.pallas_call(
+                partial(
+                    grad_kernel,
+                    count=len(self.terms),
+                    first=self.first,
+                    rows=self.rows,
+                    blend=blend,
+                ),
+                out_shape=(shape, shape),
+                in_specs=[pl.BlockSpec(memory_space=pltpu.SMEM)]
+                + [pl.BlockSpec(memory_space=pltpu.VMEM)] * (len(operands) - 1),
+                out_specs=(pl.BlockSpec(memory_space=pltpu.VMEM),) * 2,
+                scratch_shapes=[pltpu.VMEM((height, max(self.widths)), jnp.float32)],
+                cost_estimate=pl.CostEstimate(flops=0, transcendentals=0, bytes_accessed=0),
+                name="grad_blocks",
+            )(*operands)
+        )
+
+    def launch(self, kept, *sent):
+        if not self.fast:
+            return (kept, *sent)
+        return (kept, *self.sender(*sent))
+
+    def along_seq(self, block):
+        return (swap_seq(block),)
+
+    def along_pair(self, block):
+        return (swap(block, CORES),)
+
+    def along_depth(self, *blocks):
+        return tuple(
+            swap(block, CORES * PAIR, self.depth, k) for k, block in enumerate(blocks, 1)
+        )
+
+    def along_core(self, block):
+        return (swap(block, 1),)
+
+    def by_first(self, kept, came):
         _, wide, _, seq = place_of()
-        came = swap_seq(sent)
-        blank = jnp.zeros_like(came)
-        came = jnp.where(
-            seq == 0,
-            jnp.concatenate([came, blank], axis=2),
-            jnp.concatenate([blank, came], axis=2),
-        )
+        self.sender = self.along_pair if self.first == "seq" else self.along_seq
         kept = kept.astype(jnp.float32) + came.astype(jnp.float32)
-        mine = lax.dynamic_index_in_dim(kept, wide, 1, keepdims=False)
-        sent = lax.dynamic_index_in_dim(kept, 1 - wide, 1, keepdims=False)
-        return mine.astype(jnp.bfloat16), sent.astype(jnp.bfloat16)
-
-    def by_depth(self, kept, sent):
+        kept = kept.reshape(self.depth, 2, self.rows, -1)
+        which = wide if self.first == "seq" else seq
+        return tuple(
+            lax.dynamic_index_in_dim(kept, i, 1, keepdims=False).astype(jnp.bfloat16)
+            for i in (which, 1 - which)
+        )
+
+    def by_second(self, kept, came):
         deep, _, _, _ = place_of()
-        kept = kept.astype(jnp.float32) + swap(sent, CORES).astype(jnp.float32)
+        self.sender = self.along_depth
+        kept = kept.astype(jnp.float32) + came.astype(jnp.float32)
         return tuple(
             lax.dynamic_index_in_dim(kept, deep ^ k, 0, keepdims=False).astype(jnp.bfloat16)
-            for k in range(self.size // (CORES * PAIR))
-        )
-
-    def finish(self, kept, *sent):
-        depth = self.size // (CORES * PAIR)
+            for k in range(self.depth)
+        )
+
+    def by_depth(self, kept, *came):
         total = kept.astype(jnp.float32)
-        for k, block in enumerate(sent, 1):
-            total = total + swap(block, CORES * PAIR, depth, k).astype(jnp.float32)
-        return (narrow(total),)
-
-    def join(self, mine):
-        seq, third = lax.axis_index("seq"), self.rows // 3
-        came = swap_seq(mine)
-        low = jnp.where(seq == 0, mine, came).astype(jnp.float32)
-        high = jnp.where(seq == 0, came, mine).astype(jnp.float32)
-        return (
-            jnp.concatenate([low[:third], low[third:] + high[:third], high[third:]], axis=0),
-        )
-
-
-def advance(works, values):
+        for block in came:
+            total = total + block.astype(jnp.float32)
+        self.sender = self.along_seq
+        total = narrow(total)
+        return total, total
+
+    def by_seq(self, mine, came):
+        _, _, core, seq = place_of()
+        same = seq == core
+        self.sender = self.along_core
+        return jnp.where(same, mine, came), jnp.where(same, came, mine)
+
+    def finish(self, mine, came):
+        _, _, core, _ = place_of()
+        self.fast = False
+        low = jnp.where(core == 0, mine, came).astype(jnp.float32)
+        high = jnp.where(core == 0, came, mine).astype(jnp.float32)
+        results, start = [], 0
+        for width in self.widths:
+            cols = slice(start, start + width)
+            results.append(jnp.concatenate([low[:, cols], high[:, cols]], axis=1))
+            start += width
+        if self.extra is not None:
+            results.append(mine[:, start:].astype(jnp.float32))
+        return tuple(results)
+
+
+def advance(works, values=(), after=()):
     for work in works:
         work.step()
-    states, values = lax.optimization_barrier(([work.state for work in works], values))
+    states = [work.state for work in works]
+    heads = [work.state[0] for work in after]
+    states, heads, values = lax.optimization_barrier((states, heads, values))
     for work, state in zip(works, states):
-        work.state = state
+        work.state = work.launch(*state)
+    for work, head in zip(after, heads):
+        work.state = (head, *work.state[1:])
     return values
 
 
@@ -419,6 +580,7 @@
     size = lax.axis_size("batch")
 
     tail_width = 2 * LANES
+    far = lambda block: swap(block, 1)
     small = jnp.concatenate(
         [norm_gains, norm_shifts, proj_bias, up_bias.reshape(shard_rows, blocks)], axis=1
     )
@@ -430,33 +592,24 @@
     third = jnp.concatenate([up_blocks.reshape(-1, model_width), down_weight], axis=1)
     hidden_other = swap_seq(hidden)
     first.step()
-    second.state, encoder, first.state = lax.optimization_barrier(
-        (second.state, encoder, first.state)
-    )
+    second.state, encoder, first.state, hidden_other = lax.optimization_barrier(
+        (second.state, encoder, first.state, hidden_other)
+    )
+    first.step()
     second.step()
+    first.state, second.state, third, encoder = lax.optimization_barrier(
+        (first.state, second.state, third, encoder)
+    )
     first.step()
+    second.step()
     frame_mine = lax.all_to_all(encoder, "batch", split_axis=0, concat_axis=0, tiled=True)
     frame_mine = frame_mine.reshape(-1, model_width)
-    third, second.state = lax.optimization_barrier((third, second.state))
     third_all = lax.all_gather(third, "batch", axis=0, tiled=True)
-    first.step()
-    second.step()
     frame_other = swap_seq(frame_mine)
-    first_all, second_all = first.result(), second.result()
+    first_all = first.result()
 
     self_in_all = first_all[:, : 3 * model_width]
     small_all = first_all[:, 3 * model_width : 3 * model_width + small_cols]
-    self_out_all = second_all[:, :model_width]
-    query_all = second_all[:, model_width : 2 * model_width]
-    kv_all = second_all[:, 2 * model_width : 4 * model_width]
-    cross_out_all = second_all[:, 4 * model_width :]
-    down_all = third_all[:, model_width:]
-    up_all = (
-        third_all[:, :model_width]
-        .reshape(size, blocks, shard_rows, model_width)
-        .transpose(0, 2, 1, 3)
-        .reshape(model_width, wide_cols)
-    )
     gains = small_all[:, :4].astype(jnp.float32)
     shifts = small_all[:, 4:8].astype(jnp.float32)
     biases = small_all[:, 8:15].astype(jnp.float32)
@@ -484,7 +637,24 @@
     query_pos = positions[None, :]
     self_mask = (key_pos <= query_pos) & ((key_pos >= offset) | (key_pos == query_pos))
     self_bias = jnp.where(self_mask, 0.0, -jnp.inf)
+    self_query, self_pairs, second.state = lax.optimization_barrier(
+        (self_query, self_pairs, second.state)
+    )
+    second.step()
     self_mixed, self_total = attend(self_query, self_pairs, self_bias)
+    self_mixed, second.state = lax.optimization_barrier((self_mixed, second.state))
+    second_all = second.result()
+    self_out_all = second_all[:, :model_width]
+    query_all = second_all[:, model_width : 2 * model_width]
+    kv_all = second_all[:, 2 * model_width : 4 * model_width]
+    cross_out_all = second_all[:, 4 * model_width :]
+    down_all = third_all[:, model_width:]
+    up_all = (
+        third_all[:, :model_width]
+        .reshape(size, blocks, shard_rows, model_width)
+        .transpose(0, 2, 1, 3)
+        .reshape(model_width, wide_cols)
+    )
     after_self = inputs + dot_right(self_mixed, self_out_all) + biases[:, 2]
     normed_two, scale_two = layer_parts(after_self)
     act_two = (normed_two * gains[:, 1] + shifts[:, 1]).astype(jnp.bfloat16)
@@ -520,7 +690,10 @@
     down_bias = col_sum(grad_down)
     grad_act = dot_left(grad_down, down_all)
     grad_up = gelu_pull(grad_act)[0].astype(jnp.bfloat16)
-    up_bias_term = col_sum(grad_up)
+    up_bias_columns = jnp.pad(
+        col_sum(grad_up).astype(jnp.bfloat16).reshape(model_width, blocks),
+        ((0, 0), (small_cols - blocks, LANES - small_cols)),
+    )
     wide_term = jnp.concatenate(
         [weight_term(hidden_act, grad_down).reshape(size, -1, model_width)]
         + [
@@ -536,114 +709,115 @@
     )
     grad_cross = grad_mlp + back_three
     grad_cross_in = grad_cross.astype(jnp.bfloat16)
-    cross_out_term = weight_term(cross_mixed, grad_cross_in)
     cross_out_bias = col_sum(grad_cross_in)
     grad_cross_mixed = dot_left(grad_cross_in, cross_out_all).astype(jnp.bfloat16)
-    grad_cq, grad_frame_key, grad_frame_value = attend_back(
+    grad_cq, grad_frame_pairs = attend_back(
         cross_queries, cross_pairs, frame_bias, cross_total, grad_cross_mixed
     )
+    frame_grads = dot_left(grad_frame_pairs[0], kv_all[:, :model_width]) + dot_left(
+        grad_frame_pairs[1], kv_all[:, model_width:]
+    )
+    frame_grads = frame_grads.astype(jnp.bfloat16)
+    grad_cq, frame_kept, frame_sent = lax.optimization_barrier(
+        (grad_cq, frame_grads[:half_slots], frame_grads[half_slots:])
+    )
+    frame_came = swap_seq(frame_sent)
     kv_bias_term = col_sum(grad_cross_mixed)
-    frame_grads = dot_left(grad_frame_key, kv_all[:, :model_width]) + dot_left(
-        grad_frame_value, kv_all[:, model_width:]
-    )
-    frame_mine_grads = frame_grads[:half_slots]
-    frame_sent = frame_grads[half_slots:].astype(jnp.bfloat16)
-    grad_cq, (frame_sent, frame_mine_grads) = hold(grad_cq, (frame_sent, frame_mine_grads))
-    query_term = weight_term(act_two, grad_cq)
     query_bias = col_sum(grad_cq)
     back_two, gain_two, shift_two = layer_back(
         dot_left(grad_cq, query_all), normed_two, scale_two, gains[:, 1]
     )
     grad_self = grad_cross + back_two
     grad_self_in = grad_self.astype(jnp.bfloat16)
-    self_out_term = weight_term(self_mixed, grad_self_in)
     self_out_bias = col_sum(grad_self_in)
     grad_self_mixed = dot_left(grad_self_in, self_out_all).astype(jnp.bfloat16)
     cross_sum = Reduction(
-        cross_out_term,
-        weight_term(frames, grad_frame_key),
-        weight_term(frames, grad_frame_value),
-        query_term,
+        [
+            (frames, far(frames), grad_frame_pairs),
+            (cross_mixed, far(cross_mixed), grad_cross_in),
+            (act_two, far(act_two), grad_cq),
+            (self_mixed, far(self_mixed), grad_self_in),
+        ],
+        "seq",
     )
     grad_self_mixed = advance([cross_sum], grad_self_mixed)
-    grad_self_query, grad_self_key, grad_self_value = attend_back(
+    grad_self_query, grad_self_pairs = attend_back(
         self_query, self_pairs, self_bias, self_total, grad_self_mixed
     )
-    owner_grads = (frame_mine_grads + swap_seq(frame_sent).astype(jnp.float32)).astype(
-        jnp.bfloat16
-    )
-    grad_self_query, grad_self_key, grad_self_value, owner_grads = advance(
-        [cross_sum],
-        (grad_self_query, grad_self_key, grad_self_value, owner_grads),
-    )
+    both_acts = jnp.concatenate([act_far, act_one], axis=0)
+    self_pair_sum = Reduction([(both_acts, far(both_acts), grad_self_pairs)], "pair")
+    grad_self_query, grad_self_pairs = advance(
+        [self_pair_sum], (grad_self_query, grad_self_pairs)
+    )
+    value_sums = col_sum(grad_self_mixed)
+    norm_side, norm_far, small_term = self_tail(
+        grad_self_query,
+        grad_self_pairs,
+        first_all,
+        normed_one,
+        normed_far,
+        [
+            value_sums,
+            self_out_bias,
+            query_bias,
+            kv_bias_term,
+            cross_out_bias,
+            down_bias,
+            gain_two,
+            gain_three,
+            gain_last,
+            shift_two,
+            shift_three,
+            shift_last,
+        ],
+        up_bias_columns,
+    )
+    self_sum = Reduction([(act_one, far(act_one), grad_self_query)], "seq", small_term)
+    owner_grads = frame_kept.astype(jnp.float32) + frame_came.astype(jnp.float32)
+    norm_far, owner_grads = advance([self_sum], (norm_far, owner_grads.astype(jnp.bfloat16)))
+    norm_came = swap_seq(norm_far)
     grad_encoder = lax.all_to_all(
         owner_grads.reshape(size, owner_frames, model_width),
         "batch",
         split_axis=0,
         concat_axis=0,
         tiled=True,
-    ).astype(jnp.float32)
-    grad_pairs = jnp.concatenate([grad_self_key, grad_self_value], axis=1)
-    grad_qkv = jnp.concatenate([grad_self_query, grad_pairs[row_count:]], axis=1)
-    grad_far = grad_pairs[:row_count]
-    both_acts = jnp.concatenate([act_far, act_one], axis=0)
-    small_now = [
-        weight_term(act_one, grad_self_query),
-        weight_term(both_acts, grad_self_key),
-        weight_term(both_acts, grad_self_value),
-    ]
-    query_sums = col_sum(grad_self_query)
-    value_sums = col_sum(grad_self_mixed)
-    norm_far = dot_left(grad_far, self_in_all[:, model_width:]).astype(jnp.bfloat16)
-    back_side = dot_left(grad_qkv, self_in_all) + swap_seq(norm_far).astype(jnp.float32)
-    back_one, gain_one, shift_one = layer_back(back_side, normed_one, scale_one, gains[:, 0])
+    )
+    advance([cross_sum, self_pair_sum], after=[self_sum])
+    norm_came = advance([self_sum], norm_came, after=[cross_sum, self_pair_sum])
+    advance([cross_sum, self_pair_sum], after=[self_sum])
+    grad_encoder, wide_sum = advance(
+        [self_sum], (grad_encoder, wide_sum), after=[cross_sum, self_pair_sum]
+    )
+    grad_encoder = grad_encoder.astype(jnp.float32)
+    back_one, _, _ = layer_back(
+        norm_side + norm_came.astype(jnp.float32), normed_one, scale_one, gains[:, 0]
+    )
     grad_hidden = grad_self + back_one
-    small_term = jnp.stack(
-        [
-            gain_one,
-            gain_two,
-            gain_three,
-            gain_last,
-            shift_one,
-            shift_two,
-            shift_three,
-            shift_last,
-            query_sums,
-            value_sums,
-            self_out_bias,
-            query_bias,
-            kv_bias_term,
-            cross_out_bias,
-            down_bias,
-        ],
-        axis=1,
-    )
-    small_term = jnp.concatenate([small_term, up_bias_term.reshape(model_width, blocks)], axis=1)
-    small_term = jnp.pad(small_term, ((0, 0), (0, tail_width - small_cols))).astype(jnp.bfloat16)
-    self_sum = Reduction(self_out_term, *small_now, small_term)
     wide_sum = wide_sum.astype(jnp.float32) + swap_seq(wide_sum).astype(jnp.float32)
     inner_rows = down_weight.shape[0]
-    up_sum = (
+    grad_up_weight = (
         wide_sum[inner_rows:]
         .reshape(blocks, shard_rows, model_width)
         .transpose(1, 0, 2)
         .reshape(shard_rows, wide_cols)
     )
-    cross_sum, self_sum = cross_sum.result(), self_sum.result()
-    small_sum = self_sum[:, 4 * model_width :]
+    grad_cross_kv, grad_cross_out, grad_cross_query, grad_self_out = cross_sum.result()
+    grad_self_keys = self_pair_sum.result()[0]
+    grad_self_queries, small_sum = self_sum.result()
     return (
         result[None],
         grad_hidden[None],
         grad_encoder,
-        small_sum[:, :4],
-        small_sum[:, 4:8],
-        self_sum[:, model_width : 4 * model_width],
-        self_sum[:, :model_width],
-        cross_sum[:, 3 * model_width :],
-        cross_sum[:, model_width : 3 * model_width],
-        cross_sum[:, :model_width],
-        small_sum[:, 8:15],
-        up_sum,
+        jnp.concatenate([small_sum[:, :1], small_sum[:, 9:12]], axis=1),
+        jnp.concatenate([small_sum[:, 1:2], small_sum[:, 12:15]], axis=1),
+        jnp.concatenate([grad_self_queries, grad_self_keys], axis=1),
+        grad_self_out,
+        grad_cross_query,
+        grad_cross_kv,
+        grad_cross_out,
+        small_sum[:, 2:9],
+        grad_up_weight,
         small_sum[:, 15:small_cols].reshape(-1),
         wide_sum[:inner_rows],
     )

time: 493 us -> 426 us (0.86)
  waiting for transfers between devices: 164 us -> 103 us
  Pallas kernels: 57.1 us -> 83.7 us
  matrix products: 69.1 us -> 48.9 us
  local copies, waits for them, and re-layouts: 61.8 us -> 46 us
  other arithmetic: 39.1 us -> 46.9 us
    ppermute x27 -> x45, waiting for transfers between devices: 122 us -> 64.9 us  [swap(): return lax.ppermute(block, 'batch', partners(stride, radix, step))]
    pallas_call x0 -> x4, Pallas kernels: none -> 26.8 us  [the longest x3 21.1 us: begin(): pl.pallas_call(partial(grad_kernel, count=len(self.terms), first=self.fir...]
    dot_general x13 -> x5, matrix products: 16.1 us -> 3.58 us  [weight_term(): jnp.einsum('ci,cj->ij', left_side, grad_side, preferred_element_type=jnp....]
    another operation x15 -> x0, local copies, waits for them, and re-layouts: 11.8 us -> none  [body(): jnp.stack([gain_one, gain_two, gain_three, gain_last, shift_one, shift_tw...]
    dot_general x9 -> x7, matrix products: 27.3 us -> 19.4 us  [dot_left(): jnp.einsum('cj,ij->ci', grad_side, weight, preferred_element_type=jnp.flo...]
    all_to_all x1, starting transfers between devices: 12.3 us -> 5.28 us  [body(): lax.all_to_all(owner_grads.reshape(size, owner_frames, model_width), 'bat...]
    concatenate x4 -> x9, other arithmetic: 2.08 us -> 8.78 us  [the longest x1 3.18 us: body(): frames = jnp.concatenate([frame_mine, frame_other], axis=0)]
    ppermute x12 -> x14, waiting for transfers between devices: 41.2 us -> 37.7 us  [swap_seq(): return lax.ppermute(block, 'seq', FLIP)]
  transfers between devices with their start and end apart: 43 -> 63, of which waited for: 18 -> 20; matrix products, arithmetic and copies ran while one was open for 20% -> 24% of each run, Pallas kernels for 8% -> 20%
where the time goes in v3:
time: 426 us; the launch traced here: 419 us
  waiting for transfers between devices  103 us (24%)
  Pallas kernels  83.7 us (20%)
  starting transfers between devices  72.3 us (17%)
  matrix products  48.9 us (11%)
  other arithmetic  46.9 us (11%)
  local copies, waits for them, and re-layouts  46 us (11%)
  between operations  18.2 us (4%)
    ppermute x45, waiting for transfers between devices, swap(): return lax.ppermute(block, 'batch', partners(stride, radix, step))  64.9 us
    ppermute x45, starting transfers between devices, swap(): return lax.ppermute(block, 'batch', partners(stride, radix, step))  42.7 us
    ppermute x14, waiting for transfers between devices, swap_seq(): return lax.ppermute(block, 'seq', FLIP)  37.7 us
    pallas_call x2, Pallas kernels, attend_back(): pl.pallas_call(attend_back_kernel, grid=(blocks,), out_shape=(jax.ShapeDt...  26.4 us
    dot_general x8, matrix products, dot_right(): return jnp.dot(left_side, weight, preferred_element_type=jnp.float32)  25.9 us
    pallas_call x3, Pallas kernels, begin(): pl.pallas_call(partial(grad_kernel, count=len(self.terms), first=self.fir...  21.1 us
    pallas_call x2, Pallas kernels, attend(): pl.pallas_call(attend_kernel, grid=(blocks,), out_shape=(jax.ShapeDtypeSt...  19.6 us
    dot_general x7, matrix products, dot_left(): jnp.einsum('cj,ij->ci', grad_side, weight, preferred_element_type=jnp.flo...  19.4 us
  transfers between devices with their start and end apart: 63, of which 20 were waited for; matrix products, arithmetic and copies ran while one was open for 24% of the time, Pallas kernels for 20%

profile of v3, /device:TPU:0, one launch (start us, length us, event | category | flops | bytes accessed | tf_op | source)
XLA Modules:
  0.0 418.8 jit_solution(12197349518352955977)
XLA Ops:
  11.4 3.1 collective-permute-start
  22.7 4.1 collective-permute-done.1
  37.3 9.7 %collective-permute-done.7 = bf16[48,1920]{1,0:T(8,128)(2,1)S(1)} collective-permute-done((bf16[48,1920]{1,0:T(8,128)(2,1)S(1)}, bf16[48,1920]{1,0:T(8,128)(2,1)S(1)}, u32[]{:S(2)}, u32[]{:S(2)}) %collective-permute-start.7) | collective-permute-done | bytes 184352 | tf_op jit(solution)/shard_map/ppermute | solution.py:190
  49.6 6.9 %collective-permute-done.9.refs_3_ = bf16[4,48,1280]{2,1,0:T(8,128)(2,1)} collective-permute-done((bf16[4,48,1280]{2,1,0:T(8,128)(2,1)}, bf16[4,48,1280]{2,1,0:T(8,128)(2,1)}, u32[]{:S(2)}, u32[]{:S(2)}) %collective-permute-start.9) | collective-permute-done | bytes 491552 | tf_op jit(solution)/shard_map/ppermute | solution.py:194
  57.4 9.4 %all-to-all-start = ((bf16[16,48,768]{2,1,0:T(8,128)(2,1)}), bf16[16,48,768]{2,1,0:T(8,128)(2,1)S(1)}, u32[]{:S(2)}, u32[]{:S(2)}) async-start(bf16[16,48,768]{2,1,0:T(8,128)(2,1)} %param.20), calls=%async_computation | async-start | bytes 2359296 | tf_op jit(solution)/shard_map/all_to_all | solution.py:605
  67.5 4.9 %place_rows.2.weight_ref = bf16[768,2560]{1,0:T(8,128)(2,1)} custom-call(s32[4]{0:T(128)} %pad_add_fusion.1.where_ref, bf16[4,48,1280]{2,1,0:T(8,128)(2,1)} %copy-done.18, bf16[4,48,1280]{2,1,0:T(8,128)(2,1)} %collective-permute-done.4.refs_1_, bf16[4,48,1280]{2,1,0:T(8,128)(2,1)} %collective-permute-done.5.refs_2_, ...), custom_call_target="tpu_custom_call" | custom-call | tf_op jit(solution)/shard_map/place_rows/pallas_call | solution.py:284
  89.3 7.5 %attend.2 = (bf16[224,768]{1,0:T(8,128)(2,1)}, f32[6,2,224]{2,1,0:T(2,128)}) custom-call(bf16[224,768]{1,0:T(8,128)(2,1)} %slice.242.query_ref, bf16[448,1536]{1,0:T(8,128)(2,1)} %pad_maximum_fusion.1.key_ref.value_ref, bf16[448,1536]{1,0:T(8,128)(2,1)} %pad_maximum_fusion.1.key_ref.value_ref, f32[448,224]{1,0:T(8,128)} %and_select_fusion.bias_ref), custom_call_target="tpu_custom_call" | custom-call | tf_op jit(solution)/shard_map/attend/pallas_call | solution.py:134
  96.8 20.6 %collective-permute-done.16.refs_3_ = bf16[4,48,1920]{2,1,0:T(8,128)(2,1)} collective-permute-done((bf16[4,48,1920]{2,1,0:T(8,128)(2,1)}, bf16[4,48,1920]{2,1,0:T(8,128)(2,1)}, u32[]{:S(2)}, u32[]{:S(2)}) %collective-permute-start.16) | collective-permute-done | bytes 737312 | tf_op jit(solution)/shard_map/ppermute | solution.py:190
  123.2 6.0 %place_rows.3 = bf16[768,3840]{1,0:T(8,128)(2,1)} custom-call(s32[4]{0:T(128)} %pad_add_fusion.1.where_ref, bf16[4,48,1920]{2,1,0:T(8,128)(2,1)} %copy-done.7, bf16[4,48,1920]{2,1,0:T(8,128)(2,1)} %collective-permute-done.14.refs_1_, bf16[4,48,1920]{2,1,0:T(8,128)(2,1)} %collective-permute-done.15.refs_2_, ...), custom_call_target="tpu_custom_call" | custom-call | tf_op jit(solution)/shard_map/place_rows/pallas_call | solution.py:284
  134.8 15.1 %collective-permute-done.21 = bf16[768,768]{1,0:T(8,128)(2,1)} collective-permute-done((bf16[768,768]{1,0:T(8,128)(2,1)S(1)}, bf16[768,768]{1,0:T(8,128)(2,1)}, u32[]{:S(2)}, u32[]{:S(2)}) %collective-permute-start.21) | collective-permute-done | bytes 1179680 | tf_op jit(solution)/shard_map/ppermute | solution.py:194
  149.9 8.0 %add_convert_fusion.key_ref.value_ref = bf16[1536,1536]{1,0:T(8,128)(2,1)} fusion(f32[1536]{0:T(1024)S(1)} %concatenate.73, bf16[768,3840]{1,0:T(8,128)(2,1)} %place_rows.3, bf16[768,768]{1,0:T(8,128)(2,1)} %collective-permute-done.21, bf16[768,768]{1,0:T(8,128)(2,1)S(1)} %bitcast.184), kind=kOutput, calls=%fused_computation | convolution fusion | flops 3633315840 | bytes 9443328 | tf_op jit(solution)/shard_map/dot_general | solution.py:31
  159.3 12.1 %attend.3 = (bf16[224,768]{1,0:T(8,128)(2,1)}, f32[6,2,224]{2,1,0:T(2,128)}) custom-call(bf16[224,768]{1,0:T(8,128)(2,1)} %fusion.30.query_ref, bf16[1536,1536]{1,0:T(8,128)(2,1)} %add_convert_fusion.key_ref.value_ref, bf16[1536,1536]{1,0:T(8,128)(2,1)} %add_convert_fusion.key_ref.value_ref, f32[1536,224]{1,0:T(8,128)} %broadcast_in_dim.41.bias_ref), custom_call_target="tpu_custom_call" | custom-call | tf_op jit(solution)/shard_map/attend/pallas_call | solution.py:134
  179.7 8.5 %multiply_convert_fusion = (bf16[224,3072]{1,0:T(8,128)(2,1)S(1)}, f32[224,3072]{1,0:T(8,128)S(1)}, f32[224,3072]{1,0:T(8,128)S(1)}) fusion(f32[3072]{0:T(1024)S(1)} %reshape.350, bf16[224,768]{1,0:T(8,128)(2,1)S(1)} %add_convert_fusion.5, bf16[768,3072]{1,0:T(8,128)(2,1)S(1)} %bitcast.181), kind=kOutput, calls=%fused_computation.14 | convolution fusion | flops 1102381056 | bytes 11956224 | tf_op jit(solution)/shard_map/dot_general | solution.py:31
  208.2 3.2 pad_maximum_fusion.refs_0_
  211.9 5.1 %multiply_reduce_fusion.1 = (f32[768]{0:T(1024)}, f32[224]{0:T(256)S(1)}, f32[224]{0:T(256)S(1)}, f32[768]{0:T(1024)}, f32[224,768]{1,0:T(8,128)S(1)}) fusion(f32[224,768]{1,0:T(8,128)S(1)} %get-tuple-element.264, f32[224]{0:T(256)S(1)} %add_rsqrt_fusion.1, f32[224]{0:T(256)S(1)} %broadcast_multiply_fusion.9, f32[768]{0:T(1024)S(1)} %get-tuple-element.276, ...), kind=kOutput, calls=%fused_computation.99 | convolution fusion | flops 1058510848 | bytes 7483904 | tf_op jit(solution)/shard_map/cj,ij->ci/dot_general | solution.py:35
  219.5 3.2 convert_reduce_fusion.4
  222.8 18.3 %attend_back.2 = (bf16[224,768]{1,0:T(8,128)(2,1)}, bf16[2,1536,768]{2,1,0:T(8,128)(2,1)}) custom-call(bf16[224,768]{1,0:T(8,128)(2,1)} %fusion.30.query_ref, bf16[1536,1536]{1,0:T(8,128)(2,1)} %add_convert_fusion.key_ref.value_ref, bf16[1536,1536]{1,0:T(8,128)(2,1)} %add_convert_fusion.key_ref.value_ref, f32[1536,224]{1,0:T(8,128)} %broadcast_in_dim.41.bias_ref, ...), custom_call_target="tpu_custom_call" | custom-call | tf_op jit(solution)/shard_map/attend_back/pallas_call | solution.py:155
  245.0 4.1 fusion.17
  259.7 13.0 %grad_blocks.3 = (bf16[8,48,1920]{2,1,0:T(8,128)(2,1)}, bf16[8,48,1920]{2,1,0:T(8,128)(2,1)}) custom-call(s32[4]{0:T(128)} %pad_add_fusion.1.where_ref, bf16[1536,768]{1,0:T(8,128)(2,1)} %pad_maximum_fusion.refs_0_, bf16[1536,768]{1,0:T(8,128)(2,1)} %collective-permute-done.23.refs_1_, bf16[2,1536,768]{2,1,0:T(8,128)(2,1)} %get-tuple-element.119.refs_2_, ...), custom_call_target="tpu_custom_call" | custom-call | tf_op jit(solution)/shard_map/grad_blocks/pallas_call | solution.py:455
  272.7 8.0 %attend_back.3 = (bf16[224,768]{1,0:T(8,128)(2,1)}, bf16[2,448,768]{2,1,0:T(8,128)(2,1)}) custom-call(bf16[224,768]{1,0:T(8,128)(2,1)} %slice.242.query_ref, bf16[448,1536]{1,0:T(8,128)(2,1)} %pad_maximum_fusion.1.key_ref.value_ref, bf16[448,1536]{1,0:T(8,128)(2,1)} %pad_maximum_fusion.1.key_ref.value_ref, f32[448,224]{1,0:T(8,128)} %and_select_fusion.bias_ref, ...), custom_call_target="tpu_custom_call" | custom-call | tf_op jit(solution)/shard_map/attend_back/pallas_call | solution.py:155
  285.3 5.0 %grad_blocks.4 = (bf16[8,48,768]{2,1,0:T(8,128)(2,1)}, bf16[8,48,768]{2,1,0:T(8,128)(2,1)}) custom-call(s32[4]{0:T(128)} %pad_add_fusion.1.where_ref, bf16[448,768]{1,0:T(8,128)(2,1)} %pad_maximum_fusion.3.refs_0_, bf16[448,768]{1,0:T(8,128)(2,1)} %collective-permute-done.22.refs_1_, bf16[2,448,768]{2,1,0:T(8,128)(2,1)} %get-tuple-element.130.refs_2_.pair_ref, ...), custom_call_target="tpu_custom_call" | custom-call | tf_op jit(solution)/shard_map/grad_blocks/pallas_call | solution.py:455
  294.7 5.7 %self_tail.1 = (f32[224,768]{1,0:T(8,128)}, bf16[224,768]{1,0:T(8,128)(2,1)}, bf16[768,128]{1,0:T(8,128)(2,1)}) custom-call(bf16[224,768]{1,0:T(8,128)(2,1)} %get-tuple-element.129.query_ref.refs_2_, bf16[2,448,768]{2,1,0:T(8,128)(2,1)} %get-tuple-element.130.refs_2_.pair_ref, bf16[768,2560]{1,0:T(8,128)(2,1)} %place_rows.2.weight_ref, ...), custom_call_target="tpu_custom_call" | custom-call | tf_op jit(solution)/shard_map/self_tail/pallas_call | solution.py:380
  304.8 3.2 grad_blocks.5
  309.9 5.3 %all-to-all-start.1 = ((bf16[16,48,768]{2,1,0:T(8,128)(2,1)}), bf16[16,48,768]{2,1,0:T(8,128)(2,1)S(1)}, u32[]{:S(2)}, u32[]{:S(2)}) async-start(bf16[16,48,768]{2,1,0:T(8,128)(2,1)} %bitcast.67), calls=%async_computation.1 | async-start | bytes 2359296 | tf_op jit(solution)/shard_map/all_to_all | solution.py:779
  320.9 5.7 %collective-permute-done.38 = bf16[8,48,512]{2,1,0:T(8,128)(2,1)} collective-permute-done((bf16[8,48,512]{2,1,0:T(8,128)(2,1)}, bf16[8,48,512]{2,1,0:T(8,128)(2,1)}, u32[]{:S(2)}, u32[]{:S(2)}) %collective-permute-start.38) | collective-permute-done | bytes 393248 | tf_op jit(solution)/shard_map/ppermute | solution.py:194
  344.2 13.4 %collective-permute-done.40 = bf16[4,48,1920]{2,1,0:T(8,128)(2,1)S(1)} collective-permute-done((bf16[4,48,1920]{2,1,0:T(8,128)(2,1)}, bf16[4,48,1920]{2,1,0:T(8,128)(2,1)S(1)}, u32[]{:S(2)}, u32[]{:S(2)}) %collective-permute-start.40) | collective-permute-done | bytes 737312 | tf_op jit(solution)/shard_map/ppermute | solution.py:190
  357.9 3.3 collective-permute-start.53
  364.6 3.1 collective-permute-done.42
  367.8 4.2 %collective-permute-start.49 = (bf16[48,768]{1,0:T(8,128)(2,1)}, bf16[48,768]{1,0:T(8,128)(2,1)}, u32[]{:S(2)}, u32[]{:S(2)}) collective-permute-start(bf16[48,768]{1,0:T(8,128)(2,1)} %get-tuple-element.167), channel_id=1, source_target_pairs={{0,16},{2,18},{4,20},{6,22},{8,24},{10,26},{12,28},{14,30},{16,0},... | collective-permute-start | bytes 221192 | tf_op jit(solution)/shard_map/ppermute | solution.py:190
  375.3 4.1 collective-permute-done.54
  381.6 3.6 collective-permute-start.43
  391.1 5.3 %collective-permute-done.44 = bf16[48,512]{0,1:T(8,128)(2,1)S(1)} collective-permute-done((bf16[48,512]{0,1:T(8,128)(2,1)S(1)}, bf16[48,512]{0,1:T(8,128)(2,1)S(1)}, u32[]{:S(2)}, u32[]{:S(2)}) %collective-permute-start.44) | collective-permute-done | bytes 49184 | tf_op jit(solution)/shard_map/ppermute | solution.py:190
  (348 shorter events, 168.0 us)
Async XLA Ops:
  7.2 166.7 %all-gather.2.cloned.1.call-start = ((), (), s32[]{:S(2)}) async-start(), calls=%async_computation.3 | async-start | bytes 10027008 | tf_op jit(solution)/shard_map/all_gather | solution.py:607
  26.9 20.2 %collective-permute-start.4 = (bf16[4,48,1280]{2,1,0:T(8,128)(2,1)S(1)}, bf16[4,48,1280]{2,1,0:T(8,128)(2,1)}, u32[]{:S(2)}, u32[]{:S(2)}) collective-permute-start(bf16[4,48,1280]{2,1,0:T(8,128)(2,1)S(1)} %pad_maximum_fusion.5.refs_0_), channel_id=1, source_target_pairs={{0,4},{2,6},{4,0},{6,2},{8,12},{10,14},{12,8},{14,10},{16,20},{18,... | collective-permute-start | bytes 1474568 | tf_op jit(solution)/shard_map/ppermute | solution.py:190
  28.5 18.7 %collective-permute-start.5 = (bf16[4,48,1280]{2,1,0:T(8,128)(2,1)S(1)}, bf16[4,48,1280]{2,1,0:T(8,128)(2,1)}, u32[]{:S(2)}, u32[]{:S(2)}) collective-permute-start(bf16[4,48,1280]{2,1,0:T(8,128)(2,1)S(1)} %pad_maximum_fusion.5.refs_0_), channel_id=1, source_target_pairs={{0,1},{1,0},{2,3},{3,2},{4,5},{5,4},{6,7},{7,6},{8,9},{9,8},{10,11... | collective-permute-start | bytes 1474568 | tf_op jit(solution)/shard_map/ppermute | solution.py:194
  49.0 18.5 %collective-permute-start.11 = (bf16[4,48,1280]{2,1,0:T(8,128)(2,1)}, bf16[4,48,1280]{2,1,0:T(8,128)(2,1)}, u32[]{:S(2)}, u32[]{:S(2)}) collective-permute-start(bf16[4,48,1280]{2,1,0:T(8,128)(2,1)} %collective-permute-done.4.refs_1_), channel_id=1, source_target_pairs={{0,2},{2,0},{4,6},{6,4},{8,10},{10,8},{12,14},{14,12},{16,18},{18,... | collective-permute-start | bytes 1474568 | tf_op jit(solution)/shard_map/ppermute | solution.py:190
  49.1 17.8 %collective-permute-start.10 = (bf16[4,48,1280]{2,1,0:T(8,128)(2,1)S(1)}, bf16[4,48,1280]{2,1,0:T(8,128)(2,1)}, u32[]{:S(2)}, u32[]{:S(2)}) collective-permute-start(bf16[4,48,1280]{2,1,0:T(8,128)(2,1)S(1)} %pad_maximum_fusion.5.refs_0_), channel_id=1, source_target_pairs={{0,2},{2,0},{4,6},{6,4},{8,10},{10,8},{12,14},{14,12},{16,18},{18,... | collective-permute-start | bytes 1474568 | tf_op jit(solution)/shard_map/ppermute | solution.py:190
  49.6 17.9 %collective-permute-start.12 = (bf16[4,48,1280]{2,1,0:T(8,128)(2,1)}, bf16[4,48,1280]{2,1,0:T(8,128)(2,1)}, u32[]{:S(2)}, u32[]{:S(2)}) collective-permute-start(bf16[4,48,1280]{2,1,0:T(8,128)(2,1)} %collective-permute-done.5.refs_2_), channel_id=1, source_target_pairs={{0,2},{2,0},{4,6},{6,4},{8,10},{10,8},{12,14},{14,12},{16,18},{18,... | collective-permute-start | bytes 1474568 | tf_op jit(solution)/shard_map/ppermute | solution.py:190
  56.8 27.2 %collective-permute-start.14 = (bf16[4,48,1920]{2,1,0:T(8,128)(2,1)S(1)}, bf16[4,48,1920]{2,1,0:T(8,128)(2,1)}, u32[]{:S(2)}, u32[]{:S(2)}) collective-permute-start(bf16[4,48,1920]{2,1,0:T(8,128)(2,1)S(1)} %pad_maximum_fusion.2.refs_0_), channel_id=1, source_target_pairs={{0,4},{2,6},{4,0},{6,2},{8,12},{10,14},{12,8},{14,10},{16,20},{18,... | collective-permute-start | bytes 2211848 | tf_op jit(solution)/shard_map/ppermute | solution.py:190
  57.4 64.4 %all-to-all-start = ((bf16[16,48,768]{2,1,0:T(8,128)(2,1)}), bf16[16,48,768]{2,1,0:T(8,128)(2,1)S(1)}, u32[]{:S(2)}, u32[]{:S(2)}) async-start(bf16[16,48,768]{2,1,0:T(8,128)(2,1)} %param.20), calls=%async_computation | async-start | bytes 2359296 | tf_op jit(solution)/shard_map/all_to_all | solution.py:605
  66.8 306.0 %reduce-scatter.2.cloned.1.call-start = ((), (), s32[]{:S(2)}) async-start(), calls=%async_computation.4 | async-start | bytes 10027008 | tf_op jit(solution)/shard_map/reduce_scatter | solution.py:706
  66.9 19.0 %collective-permute-start.15 = (bf16[4,48,1920]{2,1,0:T(8,128)(2,1)S(1)}, bf16[4,48,1920]{2,1,0:T(8,128)(2,1)}, u32[]{:S(2)}, u32[]{:S(2)}) collective-permute-start(bf16[4,48,1920]{2,1,0:T(8,128)(2,1)S(1)} %pad_maximum_fusion.2.refs_0_), channel_id=1, source_target_pairs={{0,1},{1,0},{2,3},{3,2},{4,5},{5,4},{6,7},{7,6},{8,9},{9,8},{10,11... | collective-permute-start | bytes 2211848 | tf_op jit(solution)/shard_map/ppermute | solution.py:194
  85.9 31.5 %collective-permute-start.16 = (bf16[4,48,1920]{2,1,0:T(8,128)(2,1)}, bf16[4,48,1920]{2,1,0:T(8,128)(2,1)}, u32[]{:S(2)}, u32[]{:S(2)}) collective-permute-start(bf16[4,48,1920]{2,1,0:T(8,128)(2,1)} %collective-permute-done.15.refs_2_), channel_id=1, source_target_pairs={{0,4},{2,6},{4,0},{6,2},{8,12},{10,14},{12,8},{14,10},{16,20},{18,... | collective-permute-start | bytes 2211848 | tf_op jit(solution)/shard_map/ppermute | solution.py:190
  121.9 28.0 %collective-permute-start.21 = (bf16[768,768]{1,0:T(8,128)(2,1)S(1)}, bf16[768,768]{1,0:T(8,128)(2,1)}, u32[]{:S(2)}, u32[]{:S(2)}) collective-permute-start(bf16[768,768]{1,0:T(8,128)(2,1)S(1)} %bitcast.183), channel_id=1, source_target_pairs={{0,1},{1,0},{2,3},{3,2},{4,5},{5,4},{6,7},{7,6},{8,9},{9,8},{10,11... | collective-permute-start | bytes 3538952 | tf_op jit(solution)/shard_map/ppermute | solution.py:194
  207.7 47.8 %collective-permute-start.29 = (bf16[224,768]{1,0:T(8,128)(2,1)}, bf16[224,768]{1,0:T(8,128)(2,1)}, u32[]{:S(2)}, u32[]{:S(2)}) collective-permute-start(bf16[224,768]{1,0:T(8,128)(2,1)} %get-tuple-element.108.refs_12_), channel_id=1, source_target_pairs={{0,2},{2,0},{4,6},{6,4},{8,10},{10,8},{12,14},{14,12},{16,18},{18,... | collective-permute-start | bytes 1032200 | tf_op jit(solution)/shard_map/ppermute | solution.py:190
  207.7 47.9 %collective-permute-start.27 = (bf16[224,768]{1,0:T(8,128)(2,1)}, bf16[224,768]{1,0:T(8,128)(2,1)}, u32[]{:S(2)}, u32[]{:S(2)}) collective-permute-start(bf16[224,768]{1,0:T(8,128)(2,1)} %add_convert_fusion.6.refs_8_), channel_id=1, source_target_pairs={{0,2},{2,0},{4,6},{6,4},{8,10},{10,8},{12,14},{14,12},{16,18},{18,... | collective-permute-start | bytes 1032200 | tf_op jit(solution)/shard_map/ppermute | solution.py:190
  208.2 47.8 %collective-permute-start.25 = (bf16[224,768]{1,0:T(8,128)(2,1)}, bf16[224,768]{1,0:T(8,128)(2,1)}, u32[]{:S(2)}, u32[]{:S(2)}) collective-permute-start(bf16[224,768]{1,0:T(8,128)(2,1)} %get-tuple-element.114.refs_4_), channel_id=1, source_target_pairs={{0,2},{2,0},{4,6},{6,4},{8,10},{10,8},{12,14},{14,12},{16,18},{18,... | collective-permute-start | bytes 1032200 | tf_op jit(solution)/shard_map/ppermute | solution.py:190
  211.4 46.0 %collective-permute-start.23 = (bf16[1536,768]{1,0:T(8,128)(2,1)}, bf16[1536,768]{1,0:T(8,128)(2,1)}, u32[]{:S(2)}, u32[]{:S(2)}) collective-permute-start(bf16[1536,768]{1,0:T(8,128)(2,1)} %pad_maximum_fusion.refs_0_), channel_id=1, source_target_pairs={{0,2},{2,0},{4,6},{6,4},{8,10},{10,8},{12,14},{14,12},{16,18},{18,... | collective-permute-start | bytes 7077896 | tf_op jit(solution)/shard_map/ppermute | solution.py:190
  257.4 26.6 %collective-permute-start.22 = (bf16[448,768]{1,0:T(8,128)(2,1)S(1)}, bf16[448,768]{1,0:T(8,128)(2,1)}, u32[]{:S(2)}, u32[]{:S(2)}) collective-permute-start(bf16[448,768]{1,0:T(8,128)(2,1)S(1)} %copy-done.9), channel_id=1, source_target_pairs={{0,2},{2,0},{4,6},{6,4},{8,10},{10,8},{12,14},{14,12},{16,18},{18,... | collective-permute-start | bytes 2064392 | tf_op jit(solution)/shard_map/ppermute | solution.py:190
  257.8 42.5 %collective-permute-start.37 = (bf16[768,768]{1,0:T(8,128)(2,1)}, bf16[768,768]{1,0:T(8,128)(2,1)}, u32[]{:S(2)}, u32[]{:S(2)}) collective-permute-start(bf16[768,768]{1,0:T(8,128)(2,1)} %get-tuple-element.141), channel_id=1, source_target_pairs={{0,1},{1,0},{2,3},{3,2},{4,5},{5,4},{6,7},{7,6},{8,9},{9,8},{10,11... | collective-permute-start | bytes 3538952 | tf_op jit(solution)/shard_map/ppermute | solution.py:194
  282.8 35.4 %collective-permute-start.32 = (bf16[8,48,1920]{2,1,0:T(8,128)(2,1)}, bf16[8,48,1920]{2,1,0:T(8,128)(2,1)}, u32[]{:S(2)}, u32[]{:S(2)}) collective-permute-start(bf16[8,48,1920]{2,1,0:T(8,128)(2,1)} %get-tuple-element.133), channel_id=1, source_target_pairs={{0,1},{1,0},{2,3},{3,2},{4,5},{5,4},{6,7},{7,6},{8,9},{9,8},{10,11... | collective-permute-start | bytes 4423688 | tf_op jit(solution)/shard_map/ppermute | solution.py:194
  283.8 19.6 %collective-permute-start.34 = (bf16[224,768]{1,0:T(8,128)(2,1)S(1)}, bf16[224,768]{1,0:T(8,128)(2,1)}, u32[]{:S(2)}, u32[]{:S(2)}) collective-permute-start(bf16[224,768]{1,0:T(8,128)(2,1)S(1)} %copy-done.6), channel_id=1, source_target_pairs={{0,2},{2,0},{4,6},{6,4},{8,10},{10,8},{12,14},{14,12},{16,18},{18,... | collective-permute-start | bytes 1032200 | tf_op jit(solution)/shard_map/ppermute | solution.py:190
  290.3 25.0 %collective-permute-start.33 = (bf16[8,48,768]{2,1,0:T(8,128)(2,1)}, bf16[8,48,768]{2,1,0:T(8,128)(2,1)}, u32[]{:S(2)}, u32[]{:S(2)}) collective-permute-start(bf16[8,48,768]{2,1,0:T(8,128)(2,1)} %get-tuple-element.135), channel_id=1, source_target_pairs={{0,4},{2,6},{4,0},{6,2},{8,12},{10,14},{12,8},{14,10},{16,20},{18,... | collective-permute-start | bytes 1769480 | tf_op jit(solution)/shard_map/ppermute | solution.py:190
  307.9 18.7 %collective-permute-start.38 = (bf16[8,48,512]{2,1,0:T(8,128)(2,1)}, bf16[8,48,512]{2,1,0:T(8,128)(2,1)}, u32[]{:S(2)}, u32[]{:S(2)}) collective-permute-start(bf16[8,48,512]{2,1,0:T(8,128)(2,1)} %get-tuple-element.144), channel_id=1, source_target_pairs={{0,1},{1,0},{2,3},{3,2},{4,5},{5,4},{6,7},{7,6},{8,9},{9,8},{10,11... | collective-permute-start | bytes 1179656 | tf_op jit(solution)/shard_map/ppermute | solution.py:194
  309.3 24.3 %collective-permute-start.39 = (bf16[224,768]{1,0:T(8,128)(2,1)}, bf16[224,768]{1,0:T(8,128)(2,1)}, u32[]{:S(2)}, u32[]{:S(2)}) collective-permute-start(bf16[224,768]{1,0:T(8,128)(2,1)} %get-tuple-element.147), channel_id=1, source_target_pairs={{0,1},{1,0},{2,3},{3,2},{4,5},{5,4},{6,7},{7,6},{8,9},{9,8},{10,11... | collective-permute-start | bytes 1032200 | tf_op jit(solution)/shard_map/ppermute | solution.py:194
  309.9 62.9 %all-to-all-start.1 = ((bf16[16,48,768]{2,1,0:T(8,128)(2,1)}), bf16[16,48,768]{2,1,0:T(8,128)(2,1)S(1)}, u32[]{:S(2)}, u32[]{:S(2)}) async-start(bf16[16,48,768]{2,1,0:T(8,128)(2,1)} %bitcast.67), calls=%async_computation.1 | async-start | bytes 2359296 | tf_op jit(solution)/shard_map/all_to_all | solution.py:779
  334.6 22.9 %collective-permute-start.40 = (bf16[4,48,1920]{2,1,0:T(8,128)(2,1)}, bf16[4,48,1920]{2,1,0:T(8,128)(2,1)S(1)}, u32[]{:S(2)}, u32[]{:S(2)}) collective-permute-start(bf16[4,48,1920]{2,1,0:T(8,128)(2,1)} %get-tuple-element.150), channel_id=1, source_target_pairs={{0,4},{2,6},{4,0},{6,2},{8,12},{10,14},{12,8},{14,10},{16,20},{18,... | collective-permute-start | bytes 2211848 | tf_op jit(solution)/shard_map/ppermute | solution.py:190
  336.8 30.9 %collective-permute-start.42 = (bf16[4,48,512]{1,2,0:T(8,128)(2,1)}, bf16[4,48,512]{1,2,0:T(8,128)(2,1)S(1)}, u32[]{:S(2)}, u32[]{:S(2)}) collective-permute-start(bf16[4,48,512]{1,2,0:T(8,128)(2,1)} %bitcast.139), channel_id=1, source_target_pairs={{0,4},{2,6},{4,0},{6,2},{8,12},{10,14},{12,8},{14,10},{16,20},{18,... | collective-permute-start | bytes 589832 | tf_op jit(solution)/shard_map/ppermute | solution.py:190
  361.2 18.2 %collective-permute-start.54 = (bf16[48,1920]{1,0:T(8,128)(2,1)S(1)}, bf16[48,1920]{1,0:T(8,128)(2,1)S(1)}, u32[]{:S(2)}, u32[]{:S(2)}) collective-permute-start(bf16[48,1920]{1,0:T(8,128)(2,1)S(1)} %get-tuple-element.171), channel_id=1, source_target_pairs={{0,16},{2,18},{4,20},{6,22},{8,24},{10,26},{12,28},{14,30},{16,0},... | collective-permute-start | bytes 552968 | tf_op jit(solution)/shard_map/ppermute | solution.py:190
  362.2 18.3 %collective-permute-start.55 = (bf16[48,1920]{1,0:T(8,128)(2,1)S(1)}, bf16[48,1920]{1,0:T(8,128)(2,1)S(1)}, u32[]{:S(2)}, u32[]{:S(2)}) collective-permute-start(bf16[48,1920]{1,0:T(8,128)(2,1)S(1)} %get-tuple-element.172), channel_id=1, source_target_pairs={{0,24},{2,26},{4,28},{6,30},{8,16},{10,18},{12,20},{14,22},{16,8},... | collective-permute-start | bytes 552968 | tf_op jit(solution)/shard_map/ppermute | solution.py:190
  363.6 18.0 %collective-permute-start.48 = (bf16[48,768]{1,0:T(8,128)(2,1)}, bf16[48,768]{1,0:T(8,128)(2,1)}, u32[]{:S(2)}, u32[]{:S(2)}) collective-permute-start(bf16[48,768]{1,0:T(8,128)(2,1)} %get-tuple-element.166), channel_id=1, source_target_pairs={{0,8},{2,10},{4,12},{6,14},{8,0},{10,2},{12,4},{14,6},{16,24},{18,... | collective-permute-start | bytes 221192 | tf_op jit(solution)/shard_map/ppermute | solution.py:190
  367.8 17.4 %collective-permute-start.49 = (bf16[48,768]{1,0:T(8,128)(2,1)}, bf16[48,768]{1,0:T(8,128)(2,1)}, u32[]{:S(2)}, u32[]{:S(2)}) collective-permute-start(bf16[48,768]{1,0:T(8,128)(2,1)} %get-tuple-element.167), channel_id=1, source_target_pairs={{0,16},{2,18},{4,20},{6,22},{8,24},{10,26},{12,28},{14,30},{16,0},... | collective-permute-start | bytes 221192 | tf_op jit(solution)/shard_map/ppermute | solution.py:190
  379.4 30.2 %collective-permute-start.58 = (bf16[384,768]{1,0:T(8,128)(2,1)}, bf16[384,768]{1,0:T(8,128)(2,1)S(1)}, u32[]{:S(2)}, u32[]{:S(2)}) collective-permute-start(bf16[384,768]{1,0:T(8,128)(2,1)} %bitcast.192), channel_id=1, source_target_pairs={{0,1},{1,0},{2,3},{3,2},{4,5},{5,4},{6,7},{7,6},{8,9},{9,8},{10,11... | collective-permute-start | bytes 1769480 | tf_op jit(solution)/shard_map/ppermute | solution.py:194
  380.6 24.5 %collective-permute-start.56 = (bf16[48,1920]{1,0:T(8,128)(2,1)S(1)}, bf16[48,1920]{1,0:T(8,128)(2,1)S(1)}, u32[]{:S(2)}, u32[]{:S(2)}) collective-permute-start(bf16[48,1920]{1,0:T(8,128)(2,1)S(1)} %reduce-precision_convert_fusion), channel_id=1, source_target_pairs={{0,1},{1,0},{2,3},{3,2},{4,5},{5,4},{6,7},{7,6},{8,9},{9,8},{10,11... | collective-permute-start | bytes 552968 | tf_op jit(solution)/shard_map/ppermute | solution.py:194
  (72 other events, 649.1 us)
Sparse Core Ops, SparseCore 0:
  47.3 105.8 all-gather.1
  205.9 129.7 reduce-scatter.1

commit v4 on v3

--- a/solution.py
+++ b/solution.py
@@ -1,4 +1,6 @@
 from functools import partial
+
+import math
 
 import jax
 import jax.numpy as jnp
@@ -346,6 +348,183 @@
     ]
 
 
+def back_by_norm(grad_side, normed, inv_std, gain):
+    scaled = grad_side * gain
+    mean_one = jnp.mean(scaled, axis=-1, keepdims=True)
+    mean_two = jnp.mean(scaled * normed, axis=-1, keepdims=True)
+    return inv_std * (scaled - mean_one - normed * mean_two)
+
+
+def sum_rows(values):
+    return jnp.sum(values, axis=0, keepdims=True)
+
+
+def feed_forward_kernel(
+    act_ref,
+    after_ref,
+    grad_ref,
+    live_ref,
+    gain_ref,
+    shift_ref,
+    bias_ref,
+    up_bias_ref,
+    weight_ref,
+    result_ref,
+    cross_ref,
+    sums_ref,
+    up_sums_ref,
+    wide_ref,
+    up_ref,
+    down_ref,
+    hidden_ref,
+    slope_ref,
+    side_ref,
+    term_ref,
+    in_sem,
+    out_sem,
+):
+    blocks, width, _ = up_ref.shape
+    size = wide_ref.shape[0]
+    piece = width // size
+    inner = blocks * piece
+    per = size // blocks
+    copies = []
+    for j in range(blocks):
+        for b in range(size):
+            copies.append(
+                (
+                    weight_ref.at[pl.ds(b * inner + j * piece, piece), pl.ds(0, width)],
+                    up_ref.at[j, pl.ds(b * piece, piece)],
+                    in_sem.at[j],
+                )
+            )
+        copies.append(
+            (
+                weight_ref.at[pl.ds(j * width, width), pl.ds(width, width)],
+                down_ref.at[j],
+                in_sem.at[blocks + j],
+            )
+        )
+    started = [pltpu.make_async_copy(*copy) for copy in copies]
+    for copy in started:
+        copy.start()
+
+    def wait_up(j):
+        pltpu.make_async_copy(down_ref.at[j], up_ref.at[j], in_sem.at[j]).wait()
+
+    def wait_down(j):
+        pltpu.make_async_copy(up_ref.at[j], down_ref.at[j], in_sem.at[blocks + j]).wait()
+
+    act = act_ref[...]
+    half_root, slope_scale = math.sqrt(0.5), 1.0 / math.sqrt(2.0 * math.pi)
+
+    def rise(j, total):
+        wait_up(j)
+        up = dot_of(act, up_ref[j], (((1,), (0,)), ((), ()))) + up_bias_ref[j]
+        level = 0.5 * (1.0 + lax.erf(up * half_root))
+        hidden_ref[j] = (up * level).astype(jnp.bfloat16)
+        slope_ref[j] = level + up * (slope_scale * jnp.exp(-0.5 * up * up))
+        wait_down(j)
+        return total + dot_of(hidden_ref[j], down_ref[j], (((1,), (0,)), ((), ())))
+
+    after = after_ref[...]
+    mlp = lax.fori_loop(0, blocks, rise, after + bias_ref[...])
+    normed, inv_std = layer_parts(mlp)
+    result_ref[...] = (normed * gain_ref[1:2] + shift_ref[...]).astype(jnp.bfloat16)
+    grad_out = grad_ref[...].astype(jnp.float32) * live_ref[...]
+    grad_mlp = back_by_norm(grad_out, normed, inv_std, gain_ref[1:2])
+    grad_down = grad_mlp.astype(jnp.bfloat16)
+
+    def fall(j, total):
+        grad_act = dot_of(grad_down, down_ref[j], ROWS_BY_LANES)
+        grad_up = slope_ref[j] * grad_act
+        side_ref[j] = grad_up.astype(jnp.bfloat16)
+        up_sums_ref[j] = sum_rows(grad_up)
+        return total + dot_of(side_ref[j], up_ref[j], ROWS_BY_LANES)
+
+    grad_three = lax.fori_loop(0, blocks, fall, jnp.zeros_like(mlp))
+
+    def outward(j):
+        return (
+            pltpu.make_async_copy(
+                term_ref.at[pl.ds(j * per, per), pl.ds(0, inner)],
+                wide_ref.at[pl.ds(j * per, per), pl.ds(0, inner)],
+                out_sem.at[j],
+            ),
+            pltpu.make_async_copy(
+                term_ref.at[:, pl.ds(pl.multiple_of(inner + j * piece, 16), piece)],
+                wide_ref.at[:, pl.ds(pl.multiple_of(inner + j * piece, 16), piece)],
+                out_sem.at[blocks + j],
+            ),
+        )
+
+    def weigh(j, carry):
+        down = dot_of(hidden_ref[j], grad_down, DOWN_BOTH).astype(jnp.bfloat16)
+        for t in range(per):
+            term_ref[j * per + t, :inner] = down[t * inner : (t + 1) * inner]
+        up = dot_of(act, side_ref[j], DOWN_BOTH).astype(jnp.bfloat16)
+        span = pl.ds(pl.multiple_of(inner + j * piece, 16), piece)
+        for b in range(size):
+            term_ref[b, span] = up[b * piece : (b + 1) * piece]
+        for copy in outward(j):
+            copy.start()
+        return carry
+
+    lax.fori_loop(0, blocks, weigh, 0)
+    normed_three, scale_three = layer_parts(after)
+    cross_ref[...] = grad_mlp + back_by_norm(
+        grad_three, normed_three, scale_three, gain_ref[0:1]
+    )
+    rows = [
+        grad_three * normed_three,
+        grad_three,
+        grad_out * normed,
+        grad_out,
+        grad_down.astype(jnp.float32),
+    ]
+    for i, item in enumerate(rows):
+        sums_ref[i : i + 1] = sum_rows(item)
+
+    def finish(j, carry):
+        for copy in outward(j):
+            copy.wait()
+        return carry
+
+    lax.fori_loop(0, blocks, finish, 0)
+
+
+def feed_forward(act, after, grad, live, gains, shift, bias, up_bias, weight, size):
+    rows, width = act.shape
+    blocks = up_bias.shape[0]
+    inner = blocks * width // size
+    shape = jax.ShapeDtypeStruct
+    vmem = pl.BlockSpec(memory_space=pltpu.VMEM)
+    return pl.pallas_call(
+        feed_forward_kernel,
+        out_shape=(
+            shape((rows, width), jnp.bfloat16),
+            shape((rows, width), jnp.float32),
+            shape((8, width), jnp.float32),
+            shape((blocks, 1, width), jnp.float32),
+            shape((size, 2 * inner, width), jnp.bfloat16),
+        ),
+        in_specs=[vmem] * 8 + [pl.BlockSpec(memory_space=pl.ANY)],
+        out_specs=(vmem,) * 4 + (pl.BlockSpec(memory_space=pl.ANY),),
+        scratch_shapes=[
+            pltpu.VMEM((blocks, width, width), jnp.bfloat16),
+            pltpu.VMEM((blocks, width, width), jnp.bfloat16),
+            pltpu.VMEM((blocks, rows, width), jnp.bfloat16),
+            pltpu.VMEM((blocks, rows, width), jnp.float32),
+            pltpu.VMEM((blocks, rows, width), jnp.bfloat16),
+            pltpu.VMEM((size, 2 * inner, width), jnp.bfloat16),
+            pltpu.SemaphoreType.DMA((2 * blocks,)),
+            pltpu.SemaphoreType.DMA((2 * blocks,)),
+        ],
+        cost_estimate=pl.CostEstimate(flops=0, transcendentals=0, bytes_accessed=0),
+        name="feed_forward",
+    )(act, after, grad, live, gains, shift, bias, up_bias, weight)
+
+
 def self_tail_kernel(query_ref, pair_ref, weight_ref, near_ref, far_ref, *refs):
     vectors, base_ref, (side_ref, sent_ref, column_ref) = refs[:-4], refs[-4], refs[-3:]
     rows, width = query_ref.shape
@@ -595,17 +774,16 @@
     second.state, encoder, first.state, hidden_other = lax.optimization_barrier(
         (second.state, encoder, first.state, hidden_other)
     )
+    frame_mine = lax.all_to_all(encoder, "batch", split_axis=0, concat_axis=0, tiled=True)
+    frame_mine = frame_mine.reshape(-1, model_width)
     first.step()
     second.step()
-    first.state, second.state, third, encoder = lax.optimization_barrier(
-        (first.state, second.state, third, encoder)
+    first.state, second.state, third = lax.optimization_barrier(
+        (first.state, second.state, third)
     )
     first.step()
     second.step()
-    frame_mine = lax.all_to_all(encoder, "batch", split_axis=0, concat_axis=0, tiled=True)
-    frame_mine = frame_mine.reshape(-1, model_width)
     third_all = lax.all_gather(third, "batch", axis=0, tiled=True)
-    frame_other = swap_seq(frame_mine)
     first_all = first.result()
 
     self_in_all = first_all[:, : 3 * model_width]
@@ -637,24 +815,20 @@
     query_pos = positions[None, :]
     self_mask = (key_pos <= query_pos) & ((key_pos >= offset) | (key_pos == query_pos))
     self_bias = jnp.where(self_mask, 0.0, -jnp.inf)
-    self_query, self_pairs, second.state = lax.optimization_barrier(
-        (self_query, self_pairs, second.state)
-    )
+    self_query, self_pairs, second.state, frame_mine = lax.optimization_barrier(
+        (self_query, self_pairs, second.state, frame_mine)
+    )
+    frame_other = swap_seq(frame_mine)
     second.step()
     self_mixed, self_total = attend(self_query, self_pairs, self_bias)
-    self_mixed, second.state = lax.optimization_barrier((self_mixed, second.state))
+    self_mixed, second.state, frame_other = lax.optimization_barrier(
+        (self_mixed, second.state, frame_other)
+    )
     second_all = second.result()
     self_out_all = second_all[:, :model_width]
     query_all = second_all[:, model_width : 2 * model_width]
     kv_all = second_all[:, 2 * model_width : 4 * model_width]
     cross_out_all = second_all[:, 4 * model_width :]
-    down_all = third_all[:, model_width:]
-    up_all = (
-        third_all[:, :model_width]
-        .reshape(size, blocks, shard_rows, model_width)
-        .transpose(0, 2, 1, 3)
-        .reshape(model_width, wide_cols)
-    )
     after_self = inputs + dot_right(self_mixed, self_out_all) + biases[:, 2]
     normed_two, scale_two = layer_parts(after_self)
     act_two = (normed_two * gains[:, 1] + shifts[:, 1]).astype(jnp.bfloat16)
@@ -675,39 +849,64 @@
     after_cross = after_self + dot_right(cross_mixed, cross_out_all) + biases[:, 5]
     normed_three, scale_three = layer_parts(after_cross)
     act_three = (normed_three * gains[:, 2] + shifts[:, 2]).astype(jnp.bfloat16)
-    up_value = dot_right(act_three, up_all) + up_bias_all
-    gelu_value, gelu_pull = jax.vjp(partial(jax.nn.gelu, approximate=False), up_value)
-    hidden_act = gelu_value.astype(jnp.bfloat16)
-    after_mlp = after_cross + dot_right(hidden_act, down_all) + biases[:, 6]
-    normed_last, scale_last = layer_parts(after_mlp)
-    result = (normed_last * gains[:, 3] + shifts[:, 3]).astype(jnp.bfloat16)
     corpus_match = corpus_ids[0] == jnp.arange(corpus_weights.shape[0], dtype=jnp.int32)
     seq_weight = jnp.sum(jnp.where(corpus_match, corpus_weights, 0.0))
     live_rows = (positions >= offset) & (positions < offset + length)
-    grad_out = cotangent.astype(jnp.float32) * jnp.where(live_rows, seq_weight, 0.0)[:, None]
-    grad_mlp, gain_last, shift_last = layer_back(grad_out, normed_last, scale_last, gains[:, 3])
-    grad_down = grad_mlp.astype(jnp.bfloat16)
-    down_bias = col_sum(grad_down)
-    grad_act = dot_left(grad_down, down_all)
-    grad_up = gelu_pull(grad_act)[0].astype(jnp.bfloat16)
+    live_weight = jnp.where(live_rows, seq_weight, 0.0)[:, None]
+    if splits(shard_rows):
+        result, grad_cross, norm_sums, up_sums, wide_term = feed_forward(
+            act_three,
+            after_cross,
+            cotangent,
+            live_weight,
+            gains[:, 2:].T,
+            shifts[:, 3:].T,
+            biases[:, 6:].T,
+            up_bias_all.reshape(blocks, 1, model_width),
+            third_all,
+            size,
+        )
+        gain_three, shift_three, gain_last, shift_last, down_bias = list(norm_sums[:5])
+        up_bias_sum = up_sums.reshape(-1)
+    else:
+        down_all = third_all[:, model_width:]
+        up_all = (
+            third_all[:, :model_width]
+            .reshape(size, blocks, shard_rows, model_width)
+            .transpose(0, 2, 1, 3)
+            .reshape(model_width, wide_cols)
+        )
+        up_value = dot_right(act_three, up_all) + up_bias_all
+        gelu_value, gelu_pull = jax.vjp(partial(jax.nn.gelu, approximate=False), up_value)
+        hidden_act = gelu_value.astype(jnp.bfloat16)
+        after_mlp = after_cross + dot_right(hidden_act, down_all) + biases[:, 6]
+        normed_last, scale_last = layer_parts(after_mlp)
+        result = (normed_last * gains[:, 3] + shifts[:, 3]).astype(jnp.bfloat16)
+        grad_out = cotangent.astype(jnp.float32) * live_weight
+        grad_mlp, gain_last, shift_last = layer_back(grad_out, normed_last, scale_last, gains[:, 3])
+        grad_down = grad_mlp.astype(jnp.bfloat16)
+        down_bias = col_sum(grad_down)
+        grad_act = dot_left(grad_down, down_all)
+        grad_up = gelu_pull(grad_act)[0].astype(jnp.bfloat16)
+        up_bias_sum = col_sum(grad_up)
+        wide_term = jnp.concatenate(
+            [weight_term(hidden_act, grad_down).reshape(size, -1, model_width)]
+            + [
+                weight_term(act_three, part).reshape(size, shard_rows, model_width)
+                for part in jnp.split(grad_up, blocks, axis=1)
+            ],
+            axis=1,
+        )
+        back_three, gain_three, shift_three = layer_back(
+            dot_left(grad_up, up_all), normed_three, scale_three, gains[:, 2]
+        )
+        grad_cross = grad_mlp + back_three
     up_bias_columns = jnp.pad(
-        col_sum(grad_up).astype(jnp.bfloat16).reshape(model_width, blocks),
+        up_bias_sum.astype(jnp.bfloat16).reshape(model_width, blocks),
         ((0, 0), (small_cols - blocks, LANES - small_cols)),
     )
-    wide_term = jnp.concatenate(
-        [weight_term(hidden_act, grad_down).reshape(size, -1, model_width)]
-        + [
-            weight_term(act_three, part).reshape(size, shard_rows, model_width)
-            for part in jnp.split(grad_up, blocks, axis=1)
-        ],
-        axis=1,
-    )
-    wide_term, grad_up = lax.optimization_barrier((wide_term, grad_up))
+    wide_term, grad_cross = lax.optimization_barrier((wide_term, grad_cross))
     wide_sum = lax.psum_scatter(wide_term, "batch", scatter_dimension=0, tiled=True)[0]
-    back_three, gain_three, shift_three = layer_back(
-        dot_left(grad_up, up_all), normed_three, scale_three, gains[:, 2]
-    )
-    grad_cross = grad_mlp + back_three
     grad_cross_in = grad_cross.astype(jnp.bfloat16)
     cross_out_bias = col_sum(grad_cross_in)
     grad_cross_mixed = dot_left(grad_cross_in, cross_out_all).astype(jnp.bfloat16)
@@ -784,8 +983,8 @@
         tiled=True,
     )
     advance([cross_sum, self_pair_sum], after=[self_sum])
-    norm_came = advance([self_sum], norm_came, after=[cross_sum, self_pair_sum])
-    advance([cross_sum, self_pair_sum], after=[self_sum])
+    advance([self_sum], after=[cross_sum, self_pair_sum])
+    norm_came = advance([cross_sum, self_pair_sum], norm_came, after=[self_sum])
     grad_encoder, wide_sum = advance(
         [self_sum], (grad_encoder, wide_sum), after=[cross_sum, self_pair_sum]
     )

time: 426 us -> 404 us (0.948)
  Pallas kernels: 83.7 us -> 102 us
  matrix products: 48.9 us -> 31.5 us
  waiting for transfers between devices: 103 us -> 90.5 us
  local copies, waits for them, and re-layouts: 46 us -> 34.8 us
    ppermute x14, waiting for transfers between devices: 37.7 us -> 13.1 us  [swap_seq(): return lax.ppermute(block, 'seq', FLIP)]
    pallas_call x0 -> x1, Pallas kernels: none -> 18.1 us  [feed_forward(): pl.pallas_call(feed_forward_kernel, out_shape=(shape((rows, width), jnp.b...]
    dot_general x8 -> x6, matrix products: 25.9 us -> 15.1 us  [dot_right(): return jnp.dot(left_side, weight, preferred_element_type=jnp.float32)]
    all_to_all x1, waiting for transfers between devices: 0.01 us -> 8.21 us  [body(): lax.all_to_all(encoder, 'batch', split_axis=0, concat_axis=0, tiled=True)]
    unnamed x90 -> x91, local copies, waits for them, and re-layouts: 18.3 us -> 11.3 us
    dot_general x7 -> x5, matrix products: 19.4 us -> 16.4 us  [dot_left(): jnp.einsum('cj,ij->ci', grad_side, weight, preferred_element_type=jnp.flo...]
  transfers between devices with their start and end apart: 63 -> 63, of which waited for: 20 -> 15; matrix products, arithmetic and copies ran while one was open for 24% -> 25% of each run, Pallas kernels for 20% -> 21%
where the time goes in v4:
time: 404 us; the launch traced here: 396 us
  Pallas kernels  102 us (25%)
  waiting for transfers between devices  90.5 us (22%)
  starting transfers between devices  75.9 us (19%)
  other arithmetic  43.6 us (11%)
  local copies, waits for them, and re-layouts  34.8 us (9%)
  matrix products  31.5 us (8%)
  between operations  18 us (4%)
    ppermute x45, waiting for transfers between devices, swap(): return lax.ppermute(block, 'batch', partners(stride, radix, step))  69.2 us
    ppermute x45, starting transfers between devices, swap(): return lax.ppermute(block, 'batch', partners(stride, radix, step))  44.7 us
    pallas_call x2, Pallas kernels, attend_back(): pl.pallas_call(attend_back_kernel, grid=(blocks,), out_shape=(jax.ShapeDt...  26.3 us
    pallas_call x3, Pallas kernels, begin(): pl.pallas_call(partial(grad_kernel, count=len(self.terms), first=self.fir...  21.2 us
    pallas_call x2, Pallas kernels, attend(): pl.pallas_call(attend_kernel, grid=(blocks,), out_shape=(jax.ShapeDtypeSt...  19.5 us
    pallas_call x1, Pallas kernels, feed_forward(): pl.pallas_call(feed_forward_kernel, out_shape=(shape((rows, width), jnp.b...  18.1 us
    ppermute x14, starting transfers between devices, swap_seq(): return lax.ppermute(block, 'seq', FLIP)  17 us
    dot_general x5, matrix products, dot_left(): jnp.einsum('cj,ij->ci', grad_side, weight, preferred_element_type=jnp.flo...  16.4 us
  transfers between devices with their start and end apart: 63, of which 15 were waited for; matrix products, arithmetic and copies ran while one was open for 25% of the time, Pallas kernels for 21%

profile of v4, /device:TPU:0, one launch (start us, length us, event | category | flops | bytes accessed | tf_op | source)
XLA Modules:
  0.0 395.9 jit_solution(9600823867074608267)
XLA Ops:
  11.4 3.1 collective-permute-start
  22.7 4.1 %collective-permute-done.1 = bf16[48,1280]{1,0:T(8,128)(2,1)S(1)} collective-permute-done((bf16[48,1280]{1,0:T(8,128)(2,1)S(1)}, bf16[48,1280]{1,0:T(8,128)(2,1)S(1)}, u32[]{:S(2)}, u32[]{:S(2)}) %collective-permute-start.1) | collective-permute-done | bytes 122912 | tf_op jit(solution)/shard_map/ppermute | solution.py:192
  37.3 9.7 %collective-permute-done.7 = bf16[48,1920]{1,0:T(8,128)(2,1)S(1)} collective-permute-done((bf16[48,1920]{1,0:T(8,128)(2,1)S(1)}, bf16[48,1920]{1,0:T(8,128)(2,1)S(1)}, u32[]{:S(2)}, u32[]{:S(2)}) %collective-permute-start.7) | collective-permute-done | bytes 184352 | tf_op jit(solution)/shard_map/ppermute | solution.py:192
  49.8 5.3 %all-to-all-start = ((bf16[16,48,768]{2,1,0:T(8,128)(2,1)}), bf16[16,48,768]{2,1,0:T(8,128)(2,1)S(1)}, u32[]{:S(2)}, u32[]{:S(2)}) async-start(bf16[16,48,768]{2,1,0:T(8,128)(2,1)} %param.20), calls=%async_computation | async-start | bytes 2359296 | tf_op jit(solution)/shard_map/all_to_all | solution.py:777
  62.4 4.7 %place_rows.2.weight_ref = bf16[768,2560]{1,0:T(8,128)(2,1)} custom-call(s32[4]{0:T(128)} %pad_add_fusion.1.where_ref, bf16[4,48,1280]{2,1,0:T(8,128)(2,1)} %copy-done.19, bf16[4,48,1280]{2,1,0:T(8,128)(2,1)} %copy-done.26, bf16[4,48,1280]{2,1,0:T(8,128)(2,1)} %copy-done.27, bf16[4,48,1280]{2,1,0:T(8,128)(2,1)} %collective-permute-done.9.refs_3_, ...), custom_call_target="tpu_custom_call" | custom-call | tf_op jit(solution)/shard_map/place_rows/pallas_call | solution.py:286
  77.9 12.3 %collective-permute-done.14.refs_1_ = bf16[4,48,1920]{2,1,0:T(8,128)(2,1)} collective-permute-done((bf16[4,48,1920]{2,1,0:T(8,128)(2,1)}, bf16[4,48,1920]{2,1,0:T(8,128)(2,1)}, u32[]{:S(2)}, u32[]{:S(2)}) %collective-permute-start.14) | collective-permute-done | bytes 737312 | tf_op jit(solution)/shard_map/ppermute | solution.py:192
  90.2 8.2 %all-to-all-done = bf16[16,48,768]{2,1,0:T(8,128)(2,1)S(1)} async-done(((bf16[16,48,768]{2,1,0:T(8,128)(2,1)}), bf16[16,48,768]{2,1,0:T(8,128)(2,1)S(1)}, u32[]{:S(2)}, u32[]{:S(2)}) %all-to-all-start) | async-done | bytes 1179680 | tf_op jit(solution)/shard_map/all_to_all | solution.py:777
  103.7 7.3 %attend.2 = (bf16[224,768]{1,0:T(8,128)(2,1)}, f32[6,2,224]{2,1,0:T(2,128)}) custom-call(bf16[224,768]{1,0:T(8,128)(2,1)} %slice.238.query_ref, bf16[448,1536]{1,0:T(8,128)(2,1)} %pad_maximum_fusion.key_ref.value_ref, bf16[448,1536]{1,0:T(8,128)(2,1)} %pad_maximum_fusion.key_ref.value_ref, f32[448,224]{1,0:T(8,128)} %and_select_fusion.bias_ref), custom_call_target="tpu_custom_call" | custom-call | tf_op jit(solution)/shard_map/attend/pallas_call | solution.py:136
  111.0 19.3 %collective-permute-done.16.refs_3_ = bf16[4,48,1920]{2,1,0:T(8,128)(2,1)} collective-permute-done((bf16[4,48,1920]{2,1,0:T(8,128)(2,1)}, bf16[4,48,1920]{2,1,0:T(8,128)(2,1)}, u32[]{:S(2)}, u32[]{:S(2)}) %collective-permute-start.16) | collective-permute-done | bytes 737312 | tf_op jit(solution)/shard_map/ppermute | solution.py:192
  141.1 6.0 %place_rows.3 = bf16[768,3840]{1,0:T(8,128)(2,1)} custom-call(s32[4]{0:T(128)} %pad_add_fusion.1.where_ref, bf16[4,48,1920]{2,1,0:T(8,128)(2,1)} %pad_maximum_fusion.1.refs_0_, bf16[4,48,1920]{2,1,0:T(8,128)(2,1)} %collective-permute-done.14.refs_1_, bf16[4,48,1920]{2,1,0:T(8,128)(2,1)} %collective-permute-done.15.refs_2_, ...), custom_call_target="tpu_custom_call" | custom-call | tf_op jit(solution)/shard_map/place_rows/pallas_call | solution.py:286
  152.6 7.1 %add_convert_fusion.key_ref.value_ref = bf16[1536,1536]{1,0:T(8,128)(2,1)} fusion(bf16[1536,768]{1,0:T(8,128)(2,1)S(1)} %constant_dynamic-update-slice_fusion.refs_0_, f32[1536]{0:T(1024)S(1)} %concatenate.70, bf16[768,3840]{1,0:T(8,128)(2,1)} %place_rows.3), kind=kOutput, calls=%fused_computation | convolution fusion | flops 3628597248 | bytes 9443328 | tf_op jit(solution)/shard_map/dot_general | solution.py:33
  161.2 12.3 %attend.3 = (bf16[224,768]{1,0:T(8,128)(2,1)}, f32[6,2,224]{2,1,0:T(2,128)}) custom-call(bf16[224,768]{1,0:T(8,128)(2,1)} %fusion.12.query_ref, bf16[1536,1536]{1,0:T(8,128)(2,1)} %add_convert_fusion.key_ref.value_ref, bf16[1536,1536]{1,0:T(8,128)(2,1)} %add_convert_fusion.key_ref.value_ref, f32[1536,224]{1,0:T(8,128)} %broadcast_in_dim.66.bias_ref), custom_call_target="tpu_custom_call" | custom-call | tf_op jit(solution)/shard_map/attend/pallas_call | solution.py:136
  176.5 18.1 %feed_forward.1 = (bf16[224,768]{1,0:T(8,128)(2,1)}, f32[224,768]{1,0:T(8,128)}, f32[8,768]{1,0:T(8,128)}, f32[4,1,768]{2,1,0:T(1,128)}, bf16[16,384,768]{2,1,0:T(8,128)(2,1)}) custom-call(bf16[224,768]{1,0:T(8,128)(2,1)} %add_convert_fusion.3.act_ref, f32[224,768]{1,0:T(8,128)} %copy-done.1, bf16[224,768]{1,0:T(8,128)(2,1)} %bitcast.157, ...), custom_call_target="tpu_custom_call" | custom-call | tf_op jit(solution)/shard_map/feed_forward/pallas_call | solution.py:502
  200.3 3.1 convert_reduce_fusion.3
  203.4 18.2 %attend_back.2 = (bf16[224,768]{1,0:T(8,128)(2,1)}, bf16[2,1536,768]{2,1,0:T(8,128)(2,1)}) custom-call(bf16[224,768]{1,0:T(8,128)(2,1)} %fusion.12.query_ref, bf16[1536,1536]{1,0:T(8,128)(2,1)} %add_convert_fusion.key_ref.value_ref, bf16[1536,1536]{1,0:T(8,128)(2,1)} %add_convert_fusion.key_ref.value_ref, f32[1536,224]{1,0:T(8,128)} %broadcast_in_dim.66.bias_ref, ...), custom_call_target="tpu_custom_call" | custom-call | tf_op jit(solution)/shard_map/attend_back/pallas_call | solution.py:157
  221.7 4.3 %fusion.5 = f32[1536,768]{1,0:T(8,128)S(1)} fusion(bf16[2,1536,768]{2,1,0:T(8,128)(2,1)} %get-tuple-element.129.refs_2_, bf16[768,3840]{1,0:T(8,128)(2,1)} %place_rows.3), kind=kOutput, calls=%fused_computation.10 | convolution fusion | flops 1811939328 | bytes 8257536 | tf_op jit(solution)/shard_map/cj,ij->ci/dot_general | solution.py:37
  226.8 3.4 add_convert_fusion.1
  231.9 3.0 multiply_reduce_fusion.1
  241.2 13.0 %grad_blocks.3 = (bf16[8,48,1920]{2,1,0:T(8,128)(2,1)}, bf16[8,48,1920]{2,1,0:T(8,128)(2,1)}) custom-call(s32[4]{0:T(128)} %pad_add_fusion.1.where_ref, bf16[1536,768]{1,0:T(8,128)(2,1)} %copy-done.4, bf16[1536,768]{1,0:T(8,128)(2,1)} %collective-permute-done.23.refs_1_, bf16[2,1536,768]{2,1,0:T(8,128)(2,1)} %get-tuple-element.129.refs_2_, ...), custom_call_target="tpu_custom_call" | custom-call | tf_op jit(solution)/shard_map/grad_blocks/pallas_call | solution.py:634
  254.3 8.0 %attend_back.3 = (bf16[224,768]{1,0:T(8,128)(2,1)}, bf16[2,448,768]{2,1,0:T(8,128)(2,1)}) custom-call(bf16[224,768]{1,0:T(8,128)(2,1)} %slice.238.query_ref, bf16[448,1536]{1,0:T(8,128)(2,1)} %pad_maximum_fusion.key_ref.value_ref, bf16[448,1536]{1,0:T(8,128)(2,1)} %pad_maximum_fusion.key_ref.value_ref, f32[448,224]{1,0:T(8,128)} %and_select_fusion.bias_ref, ...), custom_call_target="tpu_custom_call" | custom-call | tf_op jit(solution)/shard_map/attend_back/pallas_call | solution.py:157
  268.7 5.0 %grad_blocks.4 = (bf16[8,48,768]{2,1,0:T(8,128)(2,1)}, bf16[8,48,768]{2,1,0:T(8,128)(2,1)}) custom-call(s32[4]{0:T(128)} %pad_add_fusion.1.where_ref, bf16[448,768]{1,0:T(8,128)(2,1)} %pad_maximum_fusion.2.refs_0_, bf16[448,768]{1,0:T(8,128)(2,1)} %copy-done.24, bf16[2,448,768]{2,1,0:T(8,128)(2,1)} %get-tuple-element.140.refs_2_.pair_ref, ...), custom_call_target="tpu_custom_call" | custom-call | tf_op jit(solution)/shard_map/grad_blocks/pallas_call | solution.py:634
  277.8 5.7 %self_tail.1 = (f32[224,768]{1,0:T(8,128)}, bf16[224,768]{1,0:T(8,128)(2,1)}, bf16[768,128]{1,0:T(8,128)(2,1)}) custom-call(bf16[224,768]{1,0:T(8,128)(2,1)} %get-tuple-element.139.query_ref.refs_2_, bf16[2,448,768]{2,1,0:T(8,128)(2,1)} %get-tuple-element.140.refs_2_.pair_ref, bf16[768,2560]{1,0:T(8,128)(2,1)} %place_rows.2.weight_ref, ...), custom_call_target="tpu_custom_call" | custom-call | tf_op jit(solution)/shard_map/self_tail/pallas_call | solution.py:559
  288.2 3.2 grad_blocks.5
  293.3 8.9 %all-to-all-start.1 = ((bf16[16,48,768]{2,1,0:T(8,128)(2,1)}), bf16[16,48,768]{2,1,0:T(8,128)(2,1)S(1)}, u32[]{:S(2)}, u32[]{:S(2)}) async-start(bf16[16,48,768]{2,1,0:T(8,128)(2,1)} %bitcast.56), calls=%async_computation.1 | async-start | bytes 2359296 | tf_op jit(solution)/shard_map/all_to_all | solution.py:978
  313.1 8.6 %collective-permute-done.40 = bf16[4,48,768]{2,1,0:T(8,128)(2,1)} collective-permute-done((bf16[4,48,768]{2,1,0:T(8,128)(2,1)}, bf16[4,48,768]{2,1,0:T(8,128)(2,1)}, u32[]{:S(2)}, u32[]{:S(2)}) %collective-permute-start.40) | collective-permute-done | bytes 294944 | tf_op jit(solution)/shard_map/ppermute | solution.py:196
  323.6 10.5 %collective-permute-done.39 = bf16[4,48,1920]{2,1,0:T(8,128)(2,1)} collective-permute-done((bf16[4,48,1920]{2,1,0:T(8,128)(2,1)}, bf16[4,48,1920]{2,1,0:T(8,128)(2,1)}, u32[]{:S(2)}, u32[]{:S(2)}) %collective-permute-start.39) | collective-permute-done | bytes 737312 | tf_op jit(solution)/shard_map/ppermute | solution.py:192
  336.2 3.5 collective-permute-start.53
  339.7 3.1 collective-permute-start.54
  346.3 3.0 collective-permute-start.49
  352.5 5.0 %collective-permute-done.54 = bf16[48,1920]{1,0:T(8,128)(2,1)} collective-permute-done((bf16[48,1920]{1,0:T(8,128)(2,1)}, bf16[48,1920]{1,0:T(8,128)(2,1)}, u32[]{:S(2)}, u32[]{:S(2)}) %collective-permute-start.54) | collective-permute-done | bytes 184352 | tf_op jit(solution)/shard_map/ppermute | solution.py:192
  360.8 3.3 collective-permute-start.43
  375.7 3.4 collective-permute-done.46
  (332 shorter events, 144.0 us)
Async XLA Ops:
  7.2 169.3 %all-gather.2.cloned.1.call-start = ((), (), s32[]{:S(2)}) async-start(), calls=%async_computation.3 | async-start | bytes 10027008 | tf_op jit(solution)/shard_map/all_gather | solution.py:786
  26.9 21.1 %collective-permute-start.4 = (bf16[4,48,1280]{2,1,0:T(8,128)(2,1)S(1)}, bf16[4,48,1280]{2,1,0:T(8,128)(2,1)S(1)}, u32[]{:S(2)}, u32[]{:S(2)}) collective-permute-start(bf16[4,48,1280]{2,1,0:T(8,128)(2,1)S(1)} %pad_maximum_fusion.4.refs_0_), channel_id=1, source_target_pairs={{0,4},{2,6},{4,0},{6,2},{8,12},{10,14},{12,8},{14,10},{16,20},{18,... | collective-permute-start | bytes 1474568 | tf_op jit(solution)/shard_map/ppermute | solution.py:192
  28.5 19.6 %collective-permute-start.5 = (bf16[4,48,1280]{2,1,0:T(8,128)(2,1)S(1)}, bf16[4,48,1280]{2,1,0:T(8,128)(2,1)S(1)}, u32[]{:S(2)}, u32[]{:S(2)}) collective-permute-start(bf16[4,48,1280]{2,1,0:T(8,128)(2,1)S(1)} %pad_maximum_fusion.4.refs_0_), channel_id=1, source_target_pairs={{0,1},{1,0},{2,3},{3,2},{4,5},{5,4},{6,7},{7,6},{8,9},{9,8},{10,11... | collective-permute-start | bytes 1474568 | tf_op jit(solution)/shard_map/ppermute | solution.py:196
  31.9 15.1 %collective-permute-start.7 = (bf16[48,1920]{1,0:T(8,128)(2,1)S(1)}, bf16[48,1920]{1,0:T(8,128)(2,1)S(1)}, u32[]{:S(2)}, u32[]{:S(2)}) collective-permute-start(bf16[48,1920]{1,0:T(8,128)(2,1)S(1)} %constant_dynamic-slice_fusion.6), channel_id=1, source_target_pairs={{0,16},{2,18},{4,20},{6,22},{8,24},{10,26},{12,28},{14,30},{16,0},... | collective-permute-start | bytes 552968 | tf_op jit(solution)/shard_map/ppermute | solution.py:192
  49.8 48.6 %all-to-all-start = ((bf16[16,48,768]{2,1,0:T(8,128)(2,1)}), bf16[16,48,768]{2,1,0:T(8,128)(2,1)S(1)}, u32[]{:S(2)}, u32[]{:S(2)}) async-start(bf16[16,48,768]{2,1,0:T(8,128)(2,1)} %param.20), calls=%async_computation | async-start | bytes 2359296 | tf_op jit(solution)/shard_map/all_to_all | solution.py:777
  55.0 295.1 %reduce-scatter.2.cloned.1.call-start = ((), (), s32[]{:S(2)}) async-start(), calls=%async_computation.4 | async-start | bytes 10027008 | tf_op jit(solution)/shard_map/reduce_scatter | solution.py:909
  57.5 32.6 %collective-permute-start.14 = (bf16[4,48,1920]{2,1,0:T(8,128)(2,1)}, bf16[4,48,1920]{2,1,0:T(8,128)(2,1)}, u32[]{:S(2)}, u32[]{:S(2)}) collective-permute-start(bf16[4,48,1920]{2,1,0:T(8,128)(2,1)} %pad_maximum_fusion.1.refs_0_), channel_id=1, source_target_pairs={{0,4},{2,6},{4,0},{6,2},{8,12},{10,14},{12,8},{14,10},{16,20},{18,... | collective-permute-start | bytes 2211848 | tf_op jit(solution)/shard_map/ppermute | solution.py:192
  58.6 31.6 %collective-permute-start.15 = (bf16[4,48,1920]{2,1,0:T(8,128)(2,1)}, bf16[4,48,1920]{2,1,0:T(8,128)(2,1)}, u32[]{:S(2)}, u32[]{:S(2)}) collective-permute-start(bf16[4,48,1920]{2,1,0:T(8,128)(2,1)} %pad_maximum_fusion.1.refs_0_), channel_id=1, source_target_pairs={{0,1},{1,0},{2,3},{3,2},{4,5},{5,4},{6,7},{7,6},{8,9},{9,8},{10,11... | collective-permute-start | bytes 2211848 | tf_op jit(solution)/shard_map/ppermute | solution.py:196
  98.4 32.0 %collective-permute-start.17 = (bf16[768,768]{1,0:T(8,128)(2,1)S(1)}, bf16[768,768]{1,0:T(8,128)(2,1)}, u32[]{:S(2)}, u32[]{:S(2)}) collective-permute-start(bf16[768,768]{1,0:T(8,128)(2,1)S(1)} %bitcast.145), channel_id=1, source_target_pairs={{0,1},{1,0},{2,3},{3,2},{4,5},{5,4},{6,7},{7,6},{8,9},{9,8},{10,11... | collective-permute-start | bytes 3538952 | tf_op jit(solution)/shard_map/ppermute | solution.py:196
  100.0 30.4 %collective-permute-start.16 = (bf16[4,48,1920]{2,1,0:T(8,128)(2,1)}, bf16[4,48,1920]{2,1,0:T(8,128)(2,1)}, u32[]{:S(2)}, u32[]{:S(2)}) collective-permute-start(bf16[4,48,1920]{2,1,0:T(8,128)(2,1)} %collective-permute-done.15.refs_2_), channel_id=1, source_target_pairs={{0,4},{2,6},{4,0},{6,2},{8,12},{10,14},{12,8},{14,10},{16,20},{18,... | collective-permute-start | bytes 2211848 | tf_op jit(solution)/shard_map/ppermute | solution.py:192
  196.8 40.6 %collective-permute-start.23 = (bf16[1536,768]{1,0:T(8,128)(2,1)S(1)}, bf16[1536,768]{1,0:T(8,128)(2,1)}, u32[]{:S(2)}, u32[]{:S(2)}) collective-permute-start(bf16[1536,768]{1,0:T(8,128)(2,1)S(1)} %copy-done.5), channel_id=1, source_target_pairs={{0,2},{2,0},{4,6},{6,4},{8,10},{10,8},{12,14},{14,12},{16,18},{18,... | collective-permute-start | bytes 7077896 | tf_op jit(solution)/shard_map/ppermute | solution.py:192
  197.3 39.5 %collective-permute-start.29 = (bf16[224,768]{1,0:T(8,128)(2,1)}, bf16[224,768]{1,0:T(8,128)(2,1)}, u32[]{:S(2)}, u32[]{:S(2)}) collective-permute-start(bf16[224,768]{1,0:T(8,128)(2,1)} %get-tuple-element.115.refs_12_), channel_id=1, source_target_pairs={{0,2},{2,0},{4,6},{6,4},{8,10},{10,8},{12,14},{14,12},{16,18},{18,... | collective-permute-start | bytes 1032200 | tf_op jit(solution)/shard_map/ppermute | solution.py:192
  197.3 39.5 %collective-permute-start.25 = (bf16[224,768]{1,0:T(8,128)(2,1)}, bf16[224,768]{1,0:T(8,128)(2,1)}, u32[]{:S(2)}, u32[]{:S(2)}) collective-permute-start(bf16[224,768]{1,0:T(8,128)(2,1)} %get-tuple-element.121.refs_4_), channel_id=1, source_target_pairs={{0,2},{2,0},{4,6},{6,4},{8,10},{10,8},{12,14},{14,12},{16,18},{18,... | collective-permute-start | bytes 1032200 | tf_op jit(solution)/shard_map/ppermute | solution.py:192
  197.8 39.3 %collective-permute-start.27 = (bf16[224,768]{1,0:T(8,128)(2,1)}, bf16[224,768]{1,0:T(8,128)(2,1)}, u32[]{:S(2)}, u32[]{:S(2)}) collective-permute-start(bf16[224,768]{1,0:T(8,128)(2,1)} %copy-done.23), channel_id=1, source_target_pairs={{0,2},{2,0},{4,6},{6,4},{8,10},{10,8},{12,14},{14,12},{16,18},{18,... | collective-permute-start | bytes 1032200 | tf_op jit(solution)/shard_map/ppermute | solution.py:192
  236.8 46.8 %collective-permute-start.37 = (bf16[768,768]{1,0:T(8,128)(2,1)}, bf16[768,768]{1,0:T(8,128)(2,1)}, u32[]{:S(2)}, u32[]{:S(2)}) collective-permute-start(bf16[768,768]{1,0:T(8,128)(2,1)} %get-tuple-element.153), channel_id=1, source_target_pairs={{0,1},{1,0},{2,3},{3,2},{4,5},{5,4},{6,7},{7,6},{8,9},{9,8},{10,11... | collective-permute-start | bytes 3538952 | tf_op jit(solution)/shard_map/ppermute | solution.py:196
  240.1 27.7 %collective-permute-start.22 = (bf16[448,768]{1,0:T(8,128)(2,1)}, bf16[448,768]{1,0:T(8,128)(2,1)S(1)}, u32[]{:S(2)}, u32[]{:S(2)}) collective-permute-start(bf16[448,768]{1,0:T(8,128)(2,1)} %pad_maximum_fusion.2.refs_0_), channel_id=1, source_target_pairs={{0,2},{2,0},{4,6},{6,4},{8,10},{10,8},{12,14},{14,12},{16,18},{18,... | collective-permute-start | bytes 2064392 | tf_op jit(solution)/shard_map/ppermute | solution.py:192
  264.5 40.0 %collective-permute-start.32 = (bf16[8,48,1920]{2,1,0:T(8,128)(2,1)}, bf16[8,48,1920]{2,1,0:T(8,128)(2,1)}, u32[]{:S(2)}, u32[]{:S(2)}) collective-permute-start(bf16[8,48,1920]{2,1,0:T(8,128)(2,1)} %get-tuple-element.145), channel_id=1, source_target_pairs={{0,1},{1,0},{2,3},{3,2},{4,5},{5,4},{6,7},{7,6},{8,9},{9,8},{10,11... | collective-permute-start | bytes 4423688 | tf_op jit(solution)/shard_map/ppermute | solution.py:196
  266.5 20.2 %collective-permute-start.34 = (bf16[224,768]{1,0:T(8,128)(2,1)S(1)}, bf16[224,768]{1,0:T(8,128)(2,1)S(1)}, u32[]{:S(2)}, u32[]{:S(2)}) collective-permute-start(bf16[224,768]{1,0:T(8,128)(2,1)S(1)} %copy-done.9), channel_id=1, source_target_pairs={{0,2},{2,0},{4,6},{6,4},{8,10},{10,8},{12,14},{14,12},{16,18},{18,... | collective-permute-start | bytes 1032200 | tf_op jit(solution)/shard_map/ppermute | solution.py:192
  273.7 28.5 %collective-permute-start.33 = (bf16[8,48,768]{2,1,0:T(8,128)(2,1)}, bf16[8,48,768]{2,1,0:T(8,128)(2,1)}, u32[]{:S(2)}, u32[]{:S(2)}) collective-permute-start(bf16[8,48,768]{2,1,0:T(8,128)(2,1)} %get-tuple-element.147), channel_id=1, source_target_pairs={{0,4},{2,6},{4,0},{6,2},{8,12},{10,14},{12,8},{14,10},{16,20},{18,... | collective-permute-start | bytes 1769480 | tf_op jit(solution)/shard_map/ppermute | solution.py:192
  291.3 18.3 %collective-permute-start.38 = (bf16[8,48,512]{2,1,0:T(8,128)(2,1)}, bf16[8,48,512]{2,1,0:T(8,128)(2,1)}, u32[]{:S(2)}, u32[]{:S(2)}) collective-permute-start(bf16[8,48,512]{2,1,0:T(8,128)(2,1)} %get-tuple-element.156), channel_id=1, source_target_pairs={{0,1},{1,0},{2,3},{3,2},{4,5},{5,4},{6,7},{7,6},{8,9},{9,8},{10,11... | collective-permute-start | bytes 1179656 | tf_op jit(solution)/shard_map/ppermute | solution.py:196
  291.7 44.5 %collective-permute-start.41 = (bf16[224,768]{1,0:T(8,128)(2,1)}, bf16[224,768]{1,0:T(8,128)(2,1)S(1)}, u32[]{:S(2)}, u32[]{:S(2)}) collective-permute-start(bf16[224,768]{1,0:T(8,128)(2,1)} %get-tuple-element.164), channel_id=1, source_target_pairs={{0,1},{1,0},{2,3},{3,2},{4,5},{5,4},{6,7},{7,6},{8,9},{9,8},{10,11... | collective-permute-start | bytes 1032200 | tf_op jit(solution)/shard_map/ppermute | solution.py:196
  293.3 56.8 %all-to-all-start.1 = ((bf16[16,48,768]{2,1,0:T(8,128)(2,1)}), bf16[16,48,768]{2,1,0:T(8,128)(2,1)S(1)}, u32[]{:S(2)}, u32[]{:S(2)}) async-start(bf16[16,48,768]{2,1,0:T(8,128)(2,1)} %bitcast.56), calls=%async_computation.1 | async-start | bytes 2359296 | tf_op jit(solution)/shard_map/all_to_all | solution.py:978
  307.3 14.5 %collective-permute-start.40 = (bf16[4,48,768]{2,1,0:T(8,128)(2,1)}, bf16[4,48,768]{2,1,0:T(8,128)(2,1)}, u32[]{:S(2)}, u32[]{:S(2)}) collective-permute-start(bf16[4,48,768]{2,1,0:T(8,128)(2,1)} %get-tuple-element.162), channel_id=1, source_target_pairs={{0,1},{1,0},{2,3},{3,2},{4,5},{5,4},{6,7},{7,6},{8,9},{9,8},{10,11... | collective-permute-start | bytes 884744 | tf_op jit(solution)/shard_map/ppermute | solution.py:196
  307.7 26.4 %collective-permute-start.39 = (bf16[4,48,1920]{2,1,0:T(8,128)(2,1)}, bf16[4,48,1920]{2,1,0:T(8,128)(2,1)}, u32[]{:S(2)}, u32[]{:S(2)}) collective-permute-start(bf16[4,48,1920]{2,1,0:T(8,128)(2,1)} %get-tuple-element.160), channel_id=1, source_target_pairs={{0,4},{2,6},{4,0},{6,2},{8,12},{10,14},{12,8},{14,10},{16,20},{18,... | collective-permute-start | bytes 2211848 | tf_op jit(solution)/shard_map/ppermute | solution.py:192
  312.0 34.3 %collective-permute-start.42 = (bf16[4,48,512]{1,2,0:T(8,128)(2,1)}, bf16[4,48,512]{1,2,0:T(8,128)(2,1)S(1)}, u32[]{:S(2)}, u32[]{:S(2)}) collective-permute-start(bf16[4,48,512]{1,2,0:T(8,128)(2,1)} %bitcast.155), channel_id=1, source_target_pairs={{0,4},{2,6},{4,0},{6,2},{8,12},{10,14},{12,8},{14,10},{16,20},{18,... | collective-permute-start | bytes 589832 | tf_op jit(solution)/shard_map/ppermute | solution.py:192
  339.7 17.8 %collective-permute-start.54 = (bf16[48,1920]{1,0:T(8,128)(2,1)}, bf16[48,1920]{1,0:T(8,128)(2,1)}, u32[]{:S(2)}, u32[]{:S(2)}) collective-permute-start(bf16[48,1920]{1,0:T(8,128)(2,1)} %get-tuple-element.183), channel_id=1, source_target_pairs={{0,16},{2,18},{4,20},{6,22},{8,24},{10,26},{12,28},{14,30},{16,0},... | collective-permute-start | bytes 552968 | tf_op jit(solution)/shard_map/ppermute | solution.py:192
  342.8 16.1 %collective-permute-start.55 = (bf16[48,1920]{1,0:T(8,128)(2,1)}, bf16[48,1920]{1,0:T(8,128)(2,1)}, u32[]{:S(2)}, u32[]{:S(2)}) collective-permute-start(bf16[48,1920]{1,0:T(8,128)(2,1)} %get-tuple-element.184), channel_id=1, source_target_pairs={{0,24},{2,26},{4,28},{6,30},{8,16},{10,18},{12,20},{14,22},{16,8},... | collective-permute-start | bytes 552968 | tf_op jit(solution)/shard_map/ppermute | solution.py:192
  342.8 18.0 %collective-permute-start.48 = (bf16[48,768]{1,0:T(8,128)(2,1)}, bf16[48,768]{1,0:T(8,128)(2,1)}, u32[]{:S(2)}, u32[]{:S(2)}) collective-permute-start(bf16[48,768]{1,0:T(8,128)(2,1)} %get-tuple-element.178), channel_id=1, source_target_pairs={{0,8},{2,10},{4,12},{6,14},{8,0},{10,2},{12,4},{14,6},{16,24},{18,... | collective-permute-start | bytes 221192 | tf_op jit(solution)/shard_map/ppermute | solution.py:192
  346.3 17.9 %collective-permute-start.49 = (bf16[48,768]{1,0:T(8,128)(2,1)}, bf16[48,768]{1,0:T(8,128)(2,1)S(1)}, u32[]{:S(2)}, u32[]{:S(2)}) collective-permute-start(bf16[48,768]{1,0:T(8,128)(2,1)} %get-tuple-element.179), channel_id=1, source_target_pairs={{0,16},{2,18},{4,20},{6,22},{8,24},{10,26},{12,28},{14,30},{16,0},... | collective-permute-start | bytes 221192 | tf_op jit(solution)/shard_map/ppermute | solution.py:192
  350.2 15.0 %collective-permute-start.50 = (bf16[48,768]{1,0:T(8,128)(2,1)S(1)}, bf16[48,768]{1,0:T(8,128)(2,1)S(1)}, u32[]{:S(2)}, u32[]{:S(2)}) collective-permute-start(bf16[48,768]{1,0:T(8,128)(2,1)S(1)} %copy-done.38), channel_id=1, source_target_pairs={{0,24},{2,26},{4,28},{6,30},{8,16},{10,18},{12,20},{14,22},{16,8},... | collective-permute-start | bytes 221192 | tf_op jit(solution)/shard_map/ppermute | solution.py:192
  357.6 29.1 %collective-permute-start.58 = (bf16[384,768]{1,0:T(8,128)(2,1)}, bf16[384,768]{1,0:T(8,128)(2,1)S(1)}, u32[]{:S(2)}, u32[]{:S(2)}) collective-permute-start(bf16[384,768]{1,0:T(8,128)(2,1)} %bitcast.153), channel_id=1, source_target_pairs={{0,1},{1,0},{2,3},{3,2},{4,5},{5,4},{6,7},{7,6},{8,9},{9,8},{10,11... | collective-permute-start | bytes 1769480 | tf_op jit(solution)/shard_map/ppermute | solution.py:196
  360.1 22.1 %collective-permute-start.56 = (bf16[48,1920]{1,0:T(8,128)(2,1)S(1)}, bf16[48,1920]{1,0:T(8,128)(2,1)S(1)}, u32[]{:S(2)}, u32[]{:S(2)}) collective-permute-start(bf16[48,1920]{1,0:T(8,128)(2,1)S(1)} %reduce-precision_convert_fusion), channel_id=1, source_target_pairs={{0,1},{1,0},{2,3},{3,2},{4,5},{5,4},{6,7},{7,6},{8,9},{9,8},{10,11... | collective-permute-start | bytes 552968 | tf_op jit(solution)/shard_map/ppermute | solution.py:196
  (73 other events, 582.0 us)
Sparse Core Ops, SparseCore 0:
  48.2 117.2 all-gather.1
  194.8 130.3 reduce-scatter.1

commit v5 on v4

--- a/solution.py
+++ b/solution.py
@@ -52,6 +52,7 @@
 
 ROWS_BY_LANES = (((1,), (1,)), ((), ()))
 DOWN_BOTH = (((0,), (0,)), ((), ()))
+ROWS_BY_ROWS = (((1,), (0,)), ((), ()))
 
 
 def head_parts(block):
@@ -85,7 +86,16 @@
 
 
 def attend_back_kernel(
-    query_ref, key_ref, value_ref, bias_ref, total_ref, grad_ref, gq_ref, pair_ref
+    core_ref,
+    query_ref,
+    key_ref,
+    value_ref,
+    bias_ref,
+    total_ref,
+    grad_ref,
+    gq_ref,
+    kept_ref,
+    sent_ref,
 ):
     score_scale = HEAD_DIM ** (-0.5)
     key, value = key_ref[...], value_ref[...]
@@ -112,8 +122,19 @@
         for item, query in zip(grad_scores, queries)
     ]
     sides = [dot_of(key, item, DOWN_BOTH) for item in grad_scores]
-    pair_ref[0] = (keys[0] + keys[1]).astype(jnp.bfloat16)
-    pair_ref[1] = (values[0] + values[1]).astype(jnp.bfloat16)
+    grad_key = (keys[0] + keys[1]).astype(jnp.bfloat16)
+    grad_value = (values[0] + values[1]).astype(jnp.bfloat16)
+
+    @pl.when(core_ref[0] == 0)
+    def _():
+        kept_ref[...] = grad_key
+        sent_ref[...] = grad_value
+
+    @pl.when(core_ref[0] == 1)
+    def _():
+        kept_ref[...] = grad_value
+        sent_ref[...] = grad_key
+
     picked = [
         sides[head][head * HEAD_DIM : (head + 1) * HEAD_DIM] * score_scale for head in range(2)
     ]
@@ -150,7 +171,7 @@
     )(queries, pairs, pairs, bias)
 
 
-def attend_back(queries, pairs, bias, totals, grads):
+def attend_back(core, queries, pairs, bias, totals, grads):
     rows, width = queries.shape
     keys = pairs.shape[0]
     blocks = width // LANES
@@ -159,20 +180,23 @@
         grid=(blocks,),
         out_shape=(
             jax.ShapeDtypeStruct((rows, width), jnp.bfloat16),
-            jax.ShapeDtypeStruct((2, keys, width), jnp.bfloat16),
+            jax.ShapeDtypeStruct((keys, width), jnp.bfloat16),
+            jax.ShapeDtypeStruct((keys, width), jnp.bfloat16),
         ),
-        in_specs=head_specs(rows, keys, blocks)
+        in_specs=[pl.BlockSpec(memory_space=pltpu.SMEM)]
+        + head_specs(rows, keys, blocks)
         + [
             pl.BlockSpec((1, 2, rows), lambda i: (i, 0, 0)),
             pl.BlockSpec((rows, LANES), lambda i: (0, i)),
         ],
         out_specs=(
             pl.BlockSpec((rows, LANES), lambda i: (0, i)),
-            pl.BlockSpec((2, keys, LANES), lambda i: (0, 0, i)),
+            pl.BlockSpec((keys, LANES), lambda i: (0, i)),
+            pl.BlockSpec((keys, LANES), lambda i: (0, i)),
         ),
         cost_estimate=pl.CostEstimate(flops=0, transcendentals=0, bytes_accessed=0),
         name="attend_back",
-    )(queries, pairs, pairs, bias, totals, grads)
+    )(core.reshape(1), queries, pairs, pairs, bias, totals, grads)
 
 
 CORES = 2
@@ -290,8 +314,11 @@
     return lax.reduce_precision(values, 8, 7).astype(jnp.bfloat16)
 
 
-def grad_kernel(where_ref, *refs, count, first, rows, blend):
-    terms, refs = [refs[4 * i : 4 * i + 4] for i in range(count)], refs[4 * count :]
+def grad_kernel(where_ref, *refs, parts, split, first, rows, blend):
+    terms = []
+    for count in parts:
+        terms.append((refs[:count], refs[count : 2 * count], *refs[2 * count : 2 * count + 2]))
+        refs = refs[2 * count + 2 :]
     extras, (kept_ref, sent_ref, total_ref) = refs[:blend], refs[blend:]
     wide, core, seq = where_ref[1], where_ref[2], where_ref[3]
     height = total_ref.shape[0]
@@ -299,16 +326,22 @@
 
     def group_step(group, carry):
         start = 0
-        for left_ref, far_left_ref, right_ref, far_right_ref in terms:
+        for (lefts, far_lefts, right_ref, far_right_ref), whole in zip(terms, split):
             width = far_right_ref.shape[1]
             span = pl.ds(pl.multiple_of(group * height, LANES), height)
-            if len(right_ref.shape) == 3:
-                right = right_ref[core]
+            if whole:
+                picked = slice(None)
             else:
-                right = right_ref[:, pl.ds(pl.multiple_of(core * width, LANES), width)]
-            total_ref[:, :width] = dot_of(left_ref[:, span], right, DOWN_BOTH) + dot_of(
-                far_left_ref[:, span], far_right_ref[...], DOWN_BOTH
-            )
+                picked = pl.ds(pl.multiple_of(core * width, LANES), width)
+            total, at = 0.0, 0
+            for left_ref, far_left_ref in zip(lefts, far_lefts):
+                tokens = slice(at, at + left_ref.shape[0])
+                at += left_ref.shape[0]
+                total = total + dot_of(left_ref[:, span], right_ref[tokens, picked], DOWN_BOTH)
+                total = total + dot_of(
+                    far_left_ref[:, span], far_right_ref[tokens, :], DOWN_BOTH
+                )
+            total_ref[:, :width] = total
             cols = slice(start, start + width)
             for place, near, far in routes(group, height, first, rows, wide, seq):
                 for out_ref, base in ((kept_ref, near), (sent_ref, far)):
@@ -368,9 +401,12 @@
     shift_ref,
     bias_ref,
     up_bias_ref,
+    out_weight_ref,
     weight_ref,
     result_ref,
     cross_ref,
+    cross_in_ref,
+    mixed_ref,
     sums_ref,
     up_sums_ref,
     wide_ref,
@@ -380,10 +416,16 @@
     slope_ref,
     side_ref,
     term_ref,
+    project_ref,
     in_sem,
     out_sem,
 ):
     blocks, width, _ = up_ref.shape
+    project = pltpu.make_async_copy(
+        out_weight_ref.at[:, pl.ds(out_weight_ref.shape[1] - width, width)],
+        project_ref,
+        in_sem.at[2 * blocks],
+    )
     size = wide_ref.shape[0]
     piece = width // size
     inner = blocks * piece
@@ -408,6 +450,7 @@
     started = [pltpu.make_async_copy(*copy) for copy in copies]
     for copy in started:
         copy.start()
+    project.start()
 
     def wait_up(j):
         pltpu.make_async_copy(down_ref.at[j], up_ref.at[j], in_sem.at[j]).wait()
@@ -472,15 +515,21 @@
 
     lax.fori_loop(0, blocks, weigh, 0)
     normed_three, scale_three = layer_parts(after)
-    cross_ref[...] = grad_mlp + back_by_norm(
-        grad_three, normed_three, scale_three, gain_ref[0:1]
-    )
+    grad_cross = grad_mlp + back_by_norm(grad_three, normed_three, scale_three, gain_ref[0:1])
+    cross_ref[...] = grad_cross
+    grad_cross_in = grad_cross.astype(jnp.bfloat16)
+    cross_in_ref[...] = grad_cross_in
+    project.wait()
+    grad_mixed = dot_of(grad_cross_in, project_ref[...], ROWS_BY_LANES).astype(jnp.bfloat16)
+    mixed_ref[...] = grad_mixed
     rows = [
         grad_three * normed_three,
         grad_three,
         grad_out * normed,
         grad_out,
         grad_down.astype(jnp.float32),
+        grad_cross_in.astype(jnp.float32),
+        grad_mixed.astype(jnp.float32),
     ]
     for i, item in enumerate(rows):
         sums_ref[i : i + 1] = sum_rows(item)
@@ -493,7 +542,7 @@
     lax.fori_loop(0, blocks, finish, 0)
 
 
-def feed_forward(act, after, grad, live, gains, shift, bias, up_bias, weight, size):
+def feed_forward(act, after, grad, live, gains, shift, bias, up_bias, out_weight, weight, size):
     rows, width = act.shape
     blocks = up_bias.shape[0]
     inner = blocks * width // size
@@ -504,12 +553,14 @@
         out_shape=(
             shape((rows, width), jnp.bfloat16),
             shape((rows, width), jnp.float32),
+            shape((rows, width), jnp.bfloat16),
+            shape((rows, width), jnp.bfloat16),
             shape((8, width), jnp.float32),
             shape((blocks, 1, width), jnp.float32),
             shape((size, 2 * inner, width), jnp.bfloat16),
         ),
-        in_specs=[vmem] * 8 + [pl.BlockSpec(memory_space=pl.ANY)],
-        out_specs=(vmem,) * 4 + (pl.BlockSpec(memory_space=pl.ANY),),
+        in_specs=[vmem] * 8 + [pl.BlockSpec(memory_space=pl.ANY)] * 2,
+        out_specs=(vmem,) * 6 + (pl.BlockSpec(memory_space=pl.ANY),),
         scratch_shapes=[
             pltpu.VMEM((blocks, width, width), jnp.bfloat16),
             pltpu.VMEM((blocks, width, width), jnp.bfloat16),
@@ -517,44 +568,267 @@
             pltpu.VMEM((blocks, rows, width), jnp.float32),
             pltpu.VMEM((blocks, rows, width), jnp.bfloat16),
             pltpu.VMEM((size, 2 * inner, width), jnp.bfloat16),
-            pltpu.SemaphoreType.DMA((2 * blocks,)),
+            pltpu.VMEM((width, width), jnp.bfloat16),
+            pltpu.SemaphoreType.DMA((2 * blocks + 1,)),
             pltpu.SemaphoreType.DMA((2 * blocks,)),
         ],
         cost_estimate=pl.CostEstimate(flops=0, transcendentals=0, bytes_accessed=0),
         name="feed_forward",
-    )(act, after, grad, live, gains, shift, bias, up_bias, weight)
-
-
-def self_tail_kernel(query_ref, pair_ref, weight_ref, near_ref, far_ref, *refs):
-    vectors, base_ref, (side_ref, sent_ref, column_ref) = refs[:-4], refs[-4], refs[-3:]
+    )(act, after, grad, live, gains, shift, bias, up_bias, out_weight, weight)
+
+
+def frame_pairs_kernel(near_ref, far_ref, weight_ref, bias_ref, pair_ref):
+    half = pl.num_programs(0) // 2
+
+    @pl.when(pl.program_id(0) < half)
+    def _():
+        pair_ref[...] = (
+            dot_of(near_ref[...], weight_ref[...], ROWS_BY_ROWS) + bias_ref[...]
+        ).astype(jnp.bfloat16)
+
+    @pl.when(pl.program_id(0) >= half)
+    def _():
+        pair_ref[...] = (
+            dot_of(far_ref[...], weight_ref[...], ROWS_BY_ROWS) + bias_ref[...]
+        ).astype(jnp.bfloat16)
+
+
+def frame_pairs(near, far, weight, bias):
+    half, width = near.shape
+    steps = half // (2 * LANES)
+    return pl.pallas_call(
+        frame_pairs_kernel,
+        grid=(2 * steps,),
+        out_shape=jax.ShapeDtypeStruct((2 * half, 2 * width), jnp.bfloat16),
+        in_specs=[
+            pl.BlockSpec((2 * LANES, width), lambda i: (jnp.minimum(i, steps - 1), 0)),
+            pl.BlockSpec((2 * LANES, width), lambda i: (jnp.maximum(i - steps, 0), 0)),
+            pl.BlockSpec((width, 2 * width), lambda i: (0, 1)),
+            pl.BlockSpec((1, 2 * width), lambda i: (0, 0)),
+        ],
+        out_specs=pl.BlockSpec((2 * LANES, 2 * width), lambda i: (i, 0)),
+        cost_estimate=pl.CostEstimate(flops=0, transcendentals=0, bytes_accessed=0),
+        name="frame_pairs",
+    )(near, far, weight, bias)
+
+
+def frame_back_kernel(core_ref, kept_ref, sent_ref, weight_ref, far_weight_ref, near_ref, far_ref):
+    half = pl.num_programs(0) // 2
+    grad = dot_of(kept_ref[...], weight_ref[...], ROWS_BY_LANES) + dot_of(
+        sent_ref[...], far_weight_ref[...], ROWS_BY_LANES
+    )
+
+    @pl.when(pl.program_id(0) < half)
+    def _():
+        near_ref[...] = grad.astype(jnp.bfloat16)
+
+    @pl.when(pl.program_id(0) >= half)
+    def _():
+        far_ref[...] = grad.astype(jnp.bfloat16)
+
+
+def frame_back(core, kept, sent, weight):
+    keys, width = kept.shape
+    steps = keys // (4 * LANES)
+    shape = jax.ShapeDtypeStruct((keys // 2, width), jnp.bfloat16)
+    return pl.pallas_call(
+        frame_back_kernel,
+        grid_spec=pltpu.PrefetchScalarGridSpec(
+            num_scalar_prefetch=1,
+            grid=(2 * steps,),
+            in_specs=[
+                pl.BlockSpec((2 * LANES, width), lambda i, core: (i, 0)),
+                pl.BlockSpec((2 * LANES, width), lambda i, core: (i, 0)),
+                pl.BlockSpec((width, width), lambda i, core: (0, 2 + core[0])),
+                pl.BlockSpec((width, width), lambda i, core: (0, 3 - core[0])),
+            ],
+            out_specs=(
+                pl.BlockSpec((2 * LANES, width), lambda i, core: (jnp.minimum(i, steps - 1), 0)),
+                pl.BlockSpec((2 * LANES, width), lambda i, core: (jnp.maximum(i - steps, 0), 0)),
+            ),
+        ),
+        out_shape=(shape, shape),
+        cost_estimate=pl.CostEstimate(flops=0, transcendentals=0, bytes_accessed=0),
+        name="frame_back",
+    )(core.reshape(1), kept, sent, weight, weight)
+
+
+def self_head_kernel(
+    near_ref, far_ref, gain_ref, shift_ref, bias_ref, weight_ref, act_ref, far_act_ref, query_ref, pair_ref
+):
+    rows, width = near_ref.shape
+    tile = width // 2
+    for source_ref, out_ref in ((far_ref, far_act_ref), (near_ref, act_ref)):
+        normed, _ = layer_parts(source_ref[...].astype(jnp.float32))
+        out_ref[...] = (normed * gain_ref[...] + shift_ref[...]).astype(jnp.bfloat16)
+
+    def project(source_ref, t):
+        span = pl.ds(pl.multiple_of(t * tile, LANES), tile)
+        return (
+            dot_of(source_ref[...], weight_ref[:, span], ROWS_BY_ROWS) + bias_ref[:, span]
+        ).astype(jnp.bfloat16)
+
+    def query(t, carry):
+        query_ref[:, pl.ds(pl.multiple_of(t * tile, LANES), tile)] = project(act_ref, t)
+        return carry
+
+    def pair(t, carry):
+        span = pl.ds(pl.multiple_of(t * tile, LANES), tile)
+        pair_ref[:rows, span] = project(far_act_ref, t + 2)
+        pair_ref[rows:, span] = project(act_ref, t + 2)
+        return carry
+
+    lax.fori_loop(0, 2, query, 0)
+    lax.fori_loop(0, 4, pair, 0)
+
+
+def self_head(near, far, gain, shift, bias, weight):
+    rows, width = near.shape
+    shape = jax.ShapeDtypeStruct((rows, width), jnp.bfloat16)
+    return pl.pallas_call(
+        self_head_kernel,
+        out_shape=(
+            shape,
+            shape,
+            shape,
+            jax.ShapeDtypeStruct((2 * rows, 2 * width), jnp.bfloat16),
+        ),
+        cost_estimate=pl.CostEstimate(flops=0, transcendentals=0, bytes_accessed=0),
+        name="self_head",
+    )(near, far, gain, shift, bias, weight)
+
+
+def hidden_back_kernel(side_ref, came_ref, hidden_ref, gain_ref, self_ref, out_ref):
+    normed, inv_std = layer_parts(hidden_ref[...].astype(jnp.float32))
+    side = side_ref[...] + came_ref[...].astype(jnp.float32)
+    out_ref[...] = self_ref[...] + back_by_norm(side, normed, inv_std, gain_ref[...])
+
+
+def hidden_back(side, came, hidden, gain, grad_self):
+    return pl.pallas_call(
+        hidden_back_kernel,
+        out_shape=jax.ShapeDtypeStruct(side.shape, jnp.float32),
+        cost_estimate=pl.CostEstimate(flops=0, transcendentals=0, bytes_accessed=0),
+        name="hidden_back",
+    )(side, came, hidden, gain, grad_self)
+
+
+def query_back_kernel(
+    grad_ref,
+    cross_ref,
+    after_ref,
+    gain_ref,
+    weight_ref,
+    self_ref,
+    self_in_ref,
+    mixed_ref,
+    sums_ref,
+    held_ref,
+    sem,
+):
+    width = grad_ref.shape[1]
+    copies = [
+        pltpu.make_async_copy(
+            weight_ref.at[:, pl.ds(i * width, width)], held_ref.at[i], sem.at[i]
+        )
+        for i in (1, 0)
+    ]
+    for copy in copies:
+        copy.start()
+    copies[0].wait()
+    side = dot_of(grad_ref[...], held_ref[1], ROWS_BY_LANES)
+    normed, inv_std = layer_parts(after_ref[...])
+    grad_self = cross_ref[...] + back_by_norm(side, normed, inv_std, gain_ref[...])
+    self_ref[...] = grad_self
+    grad_self_in = grad_self.astype(jnp.bfloat16)
+    self_in_ref[...] = grad_self_in
+    copies[1].wait()
+    grad_mixed = dot_of(grad_self_in, held_ref[0], ROWS_BY_LANES).astype(jnp.bfloat16)
+    mixed_ref[...] = grad_mixed
+    rows = [
+        side * normed,
+        side,
+        grad_ref[...].astype(jnp.float32),
+        grad_self_in.astype(jnp.float32),
+        grad_mixed.astype(jnp.float32),
+    ]
+    for i, item in enumerate(rows):
+        sums_ref[i : i + 1] = sum_rows(item)
+
+
+def query_back(grad, cross, after, gain, weight):
+    shape = jax.ShapeDtypeStruct
+    rows, width = grad.shape
+    return pl.pallas_call(
+        query_back_kernel,
+        out_shape=(
+            shape((rows, width), jnp.float32),
+            shape((rows, width), jnp.bfloat16),
+            shape((rows, width), jnp.bfloat16),
+            shape((8, width), jnp.float32),
+        ),
+        in_specs=[pl.BlockSpec(memory_space=pltpu.VMEM)] * 4 + [pl.BlockSpec(memory_space=pl.ANY)],
+        out_specs=(pl.BlockSpec(memory_space=pltpu.VMEM),) * 4,
+        scratch_shapes=[
+            pltpu.VMEM((2, width, width), jnp.bfloat16),
+            pltpu.SemaphoreType.DMA((2,)),
+        ],
+        cost_estimate=pl.CostEstimate(flops=0, transcendentals=0, bytes_accessed=0),
+        name="query_back",
+    )(grad, cross, after, gain, weight)
+
+
+def self_tail_kernel(
+    core_ref,
+    query_ref,
+    kept_ref,
+    sent_ref,
+    weight_ref,
+    near_ref,
+    far_ref,
+    query_table_ref,
+    table_ref,
+    base_ref,
+    side_ref,
+    moved_ref,
+    column_ref,
+):
     rows, width = query_ref.shape
-    both = dot_of(pair_ref[0], weight_ref[:, width : 2 * width], ROWS_BY_LANES) + dot_of(
-        pair_ref[1], weight_ref[:, 2 * width : 3 * width], ROWS_BY_LANES
+    core = core_ref[0]
+    near_span = pl.ds(pl.multiple_of((1 + core) * width, LANES), width)
+    far_span = pl.ds(pl.multiple_of((2 - core) * width, LANES), width)
+    both = dot_of(kept_ref[...], weight_ref[:, near_span], ROWS_BY_LANES) + dot_of(
+        sent_ref[...], weight_ref[:, far_span], ROWS_BY_LANES
     )
     far = both[:rows]
     side = both[rows:] + dot_of(query_ref[...], weight_ref[:, :width], ROWS_BY_LANES)
     side_ref[...] = side
-    sent_ref[...] = far.astype(jnp.bfloat16)
-    sums = [
-        jnp.sum(side * near_ref[...] + far * far_ref[...], axis=0, keepdims=True),
-        jnp.sum(side + far, axis=0, keepdims=True),
-        jnp.sum(query_ref[...].astype(jnp.float32), axis=0, keepdims=True),
+    moved_ref[...] = far.astype(jnp.bfloat16)
+    normed, _ = layer_parts(near_ref[...].astype(jnp.float32))
+    normed_far, _ = layer_parts(far_ref[...].astype(jnp.float32))
+    gain_one = sum_rows(side * normed + far * normed_far)
+    shift_one = sum_rows(side + far)
+    query_bias = sum_rows(query_ref[...].astype(jnp.float32))
+    gain_two, shift_two, cross_query, self_out, value = [
+        query_table_ref[i : i + 1] for i in range(5)
     ]
-    count = len(sums) + len(vectors)
+    gain_three, shift_three, gain_last, shift_last, down, cross_out, cross_value = [
+        table_ref[i : i + 1] for i in range(7)
+    ]
+    sums = [gain_one, gain_two, gain_three, gain_last]
+    sums += [shift_one, shift_two, shift_three, shift_last]
+    sums += [query_bias, value, self_out, cross_query, cross_value, cross_out, down]
     lane = lax.broadcasted_iota(jnp.int32, (LANES, LANES), 1)
-    blank = jnp.zeros((LANES - count, LANES), jnp.float32)
+    blank = jnp.zeros((LANES - len(sums), LANES), jnp.float32)
     for i in range(width // LANES):
         here = slice(i * LANES, (i + 1) * LANES)
-        block = jnp.concatenate(
-            [item[:, here] for item in sums] + [row[i : i + 1, :] for row in vectors] + [blank],
-            axis=0,
-        )
+        block = jnp.concatenate([item[:, here] for item in sums] + [blank], axis=0)
         column_ref[here, :] = jnp.where(
-            lane < count, block.T, base_ref[here, :].astype(jnp.float32)
+            lane < len(sums), block.T, base_ref[here, :].astype(jnp.float32)
         ).astype(jnp.bfloat16)
 
 
-def self_tail(query, pairs, weight, near, far, vectors, base):
+def self_tail(core, query, kept, sent, weight, near, far, query_table, table, base):
     rows, width = query.shape
     return pl.pallas_call(
         self_tail_kernel,
@@ -563,14 +837,14 @@
             jax.ShapeDtypeStruct((rows, width), jnp.bfloat16),
             jax.ShapeDtypeStruct(base.shape, jnp.bfloat16),
         ),
+        in_specs=[pl.BlockSpec(memory_space=pltpu.SMEM)]
+        + [pl.BlockSpec(memory_space=pltpu.VMEM)] * 9,
         cost_estimate=pl.CostEstimate(flops=0, transcendentals=0, bytes_accessed=0),
         name="self_tail",
-    )(query, pairs, weight, near, far, *[vector.reshape(-1, LANES) for vector in vectors], base)
+    )(core.reshape(1), query, kept, sent, weight, near, far, query_table, table, base)
 
 
 def half_of(right, which):
-    if right.ndim == 3:
-        return lax.dynamic_index_in_dim(right, which, 0, keepdims=False)
     width = right.shape[1] // CORES
     return lax.dynamic_slice_in_dim(right, which * width, width, 1)
 
@@ -579,12 +853,13 @@
     def __init__(self, terms, first, extra=None):
         self.size = lax.axis_size("batch")
         self.depth = self.size // (CORES * PAIR)
-        self.rows = terms[0][0].shape[1] // self.size
+        self.rows = terms[0][0][0].shape[1] // self.size
         self.first = first
         self.terms, self.extra = terms, extra
         self.fast = splits(self.rows)
         self.widths = [
-            right.shape[2] if right.ndim == 3 else right.shape[1] // CORES for _, _, right in terms
+            right[0].shape[1] if isinstance(right, tuple) else right.shape[1] // CORES
+            for _, right in terms
         ]
         self.state = ()
         self.todo = (
@@ -605,10 +880,15 @@
         return self.state
 
     def plain(self):
-        whole = [
-            weight_term(left, jnp.concatenate(list(right), axis=1) if right.ndim == 3 else right)
-            for left, _, right in self.terms
-        ] + ([] if self.extra is None else [self.extra])
+        _, _, core, _ = place_of()
+        whole = [] if self.extra is None else [self.extra]
+        for left, right in reversed(self.terms):
+            if isinstance(right, tuple):
+                kept, sent = right
+                right = jnp.concatenate(
+                    [jnp.where(core == 0, kept, sent), jnp.where(core == 0, sent, kept)], axis=1
+                )
+            whole.insert(0, weight_term(jnp.concatenate(left, axis=0), right))
         mine = lax.psum_scatter(
             jnp.concatenate(whole, axis=1), "batch", scatter_dimension=0, tiled=True
         )
@@ -622,8 +902,12 @@
         self.sender = self.along_seq if self.first == "seq" else self.along_pair
         where = jnp.stack(place_of()).astype(jnp.int32)
         operands = [where]
-        for left, far_left, right in self.terms:
-            operands += [left, far_left, right, swap(half_of(right, 1 - where[2]), 1)]
+        for left, right in self.terms:
+            if isinstance(right, tuple):
+                kept, sent = right
+            else:
+                kept, sent = right, half_of(right, 1 - where[2])
+            operands += [*left, *[swap(part, 1) for part in left], kept, swap(sent, 1)]
         if self.extra is not None:
             operands += [self.extra, swap(self.extra, 1)]
         blend = 0 if self.extra is None else 2
@@ -634,7 +918,8 @@
             pl.pallas_call(
                 partial(
                     grad_kernel,
-                    count=len(self.terms),
+                    parts=[len(left) for left, _ in self.terms],
+                    split=[isinstance(right, tuple) for _, right in self.terms],
                     first=self.first,
                     rows=self.rows,
                     blend=blend,
@@ -759,7 +1044,7 @@
     size = lax.axis_size("batch")
 
     tail_width = 2 * LANES
-    far = lambda block: swap(block, 1)
+    core = place_of()[2].astype(jnp.int32)
     small = jnp.concatenate(
         [norm_gains, norm_shifts, proj_bias, up_bias.reshape(shard_rows, blocks)], axis=1
     )
@@ -786,7 +1071,6 @@
     third_all = lax.all_gather(third, "batch", axis=0, tiled=True)
     first_all = first.result()
 
-    self_in_all = first_all[:, : 3 * model_width]
     small_all = first_all[:, 3 * model_width : 3 * model_width + small_cols]
     gains = small_all[:, :4].astype(jnp.float32)
     shifts = small_all[:, 4:8].astype(jnp.float32)
@@ -800,17 +1084,10 @@
     positions_other = (1 - seq_index) * row_count + slots
     zero_row = jnp.zeros((model_width,), jnp.float32)
     inputs = hidden.astype(jnp.float32)
-    normed_one, scale_one = layer_parts(inputs)
-    act_one = (normed_one * gains[:, 0] + shifts[:, 0]).astype(jnp.bfloat16)
-    normed_far, _ = layer_parts(hidden_other.astype(jnp.float32))
-    act_far = (normed_far * gains[:, 0] + shifts[:, 0]).astype(jnp.bfloat16)
     qkv_bias = jnp.concatenate([biases[:, 0], zero_row, biases[:, 1]])
-    qkv_local = (dot_right(act_one, self_in_all) + qkv_bias).astype(jnp.bfloat16)
-    self_query = qkv_local[:, :model_width]
-    pair_far = (
-        dot_right(act_far, self_in_all[:, model_width:]) + qkv_bias[model_width:]
-    ).astype(jnp.bfloat16)
-    self_pairs = jnp.concatenate([pair_far, qkv_local[:, model_width:]], axis=0)
+    act_one, act_far, self_query, self_pairs = self_head(
+        hidden, hidden_other, gains[:, :1].T, shifts[:, :1].T, qkv_bias[None], first_all
+    )
     key_pos = jnp.concatenate([positions_other, positions])[:, None]
     query_pos = positions[None, :]
     self_mask = (key_pos <= query_pos) & ((key_pos >= offset) | (key_pos == query_pos))
@@ -833,9 +1110,8 @@
     normed_two, scale_two = layer_parts(after_self)
     act_two = (normed_two * gains[:, 1] + shifts[:, 1]).astype(jnp.bfloat16)
     cross_queries = (dot_right(act_two, query_all) + biases[:, 3]).astype(jnp.bfloat16)
-    frames = jnp.concatenate([frame_mine, frame_other], axis=0)
     kv_bias = jnp.concatenate([zero_row, biases[:, 4]])
-    cross_pairs = (dot_right(frames, kv_all) + kv_bias).astype(jnp.bfloat16)
+    cross_pairs = frame_pairs(frame_mine, frame_other, second_all, kv_bias[None])
     half_slots = frame_mine.shape[0]
     owner_frames = encoder.shape[1]
     gathered = jnp.arange(2 * half_slots, dtype=jnp.int32)
@@ -854,7 +1130,7 @@
     live_rows = (positions >= offset) & (positions < offset + length)
     live_weight = jnp.where(live_rows, seq_weight, 0.0)[:, None]
     if splits(shard_rows):
-        result, grad_cross, norm_sums, up_sums, wide_term = feed_forward(
+        result, grad_cross, grad_cross_in, grad_cross_mixed, table, up_sums, wide_term = feed_forward(
             act_three,
             after_cross,
             cotangent,
@@ -863,10 +1139,10 @@
             shifts[:, 3:].T,
             biases[:, 6:].T,
             up_bias_all.reshape(blocks, 1, model_width),
+            second_all,
             third_all,
             size,
         )
-        gain_three, shift_three, gain_last, shift_last, down_bias = list(norm_sums[:5])
         up_bias_sum = up_sums.reshape(-1)
     else:
         down_all = third_all[:, model_width:]
@@ -901,78 +1177,66 @@
             dot_left(grad_up, up_all), normed_three, scale_three, gains[:, 2]
         )
         grad_cross = grad_mlp + back_three
+        grad_cross_in = grad_cross.astype(jnp.bfloat16)
+        grad_cross_mixed = dot_left(grad_cross_in, cross_out_all).astype(jnp.bfloat16)
+        table = jnp.stack(
+            [
+                gain_three,
+                shift_three,
+                gain_last,
+                shift_last,
+                down_bias,
+                col_sum(grad_cross_in),
+                col_sum(grad_cross_mixed),
+                jnp.zeros_like(down_bias),
+            ]
+        )
     up_bias_columns = jnp.pad(
         up_bias_sum.astype(jnp.bfloat16).reshape(model_width, blocks),
         ((0, 0), (small_cols - blocks, LANES - small_cols)),
     )
-    wide_term, grad_cross = lax.optimization_barrier((wide_term, grad_cross))
+    wide_term, grad_cross_mixed = lax.optimization_barrier((wide_term, grad_cross_mixed))
     wide_sum = lax.psum_scatter(wide_term, "batch", scatter_dimension=0, tiled=True)[0]
-    grad_cross_in = grad_cross.astype(jnp.bfloat16)
-    cross_out_bias = col_sum(grad_cross_in)
-    grad_cross_mixed = dot_left(grad_cross_in, cross_out_all).astype(jnp.bfloat16)
-    grad_cq, grad_frame_pairs = attend_back(
-        cross_queries, cross_pairs, frame_bias, cross_total, grad_cross_mixed
-    )
-    frame_grads = dot_left(grad_frame_pairs[0], kv_all[:, :model_width]) + dot_left(
-        grad_frame_pairs[1], kv_all[:, model_width:]
-    )
-    frame_grads = frame_grads.astype(jnp.bfloat16)
-    grad_cq, frame_kept, frame_sent = lax.optimization_barrier(
-        (grad_cq, frame_grads[:half_slots], frame_grads[half_slots:])
-    )
-    frame_came = swap_seq(frame_sent)
-    kv_bias_term = col_sum(grad_cross_mixed)
-    query_bias = col_sum(grad_cq)
-    back_two, gain_two, shift_two = layer_back(
-        dot_left(grad_cq, query_all), normed_two, scale_two, gains[:, 1]
-    )
-    grad_self = grad_cross + back_two
-    grad_self_in = grad_self.astype(jnp.bfloat16)
-    self_out_bias = col_sum(grad_self_in)
-    grad_self_mixed = dot_left(grad_self_in, self_out_all).astype(jnp.bfloat16)
+    grad_cq, frame_kept, frame_sent = attend_back(
+        core, cross_queries, cross_pairs, frame_bias, cross_total, grad_cross_mixed
+    )
+    frame_near, frame_far = frame_back(core, frame_kept, frame_sent, second_all)
+    grad_cq, frame_near, frame_far = lax.optimization_barrier((grad_cq, frame_near, frame_far))
+    frame_came = swap_seq(frame_far)
+    grad_self, grad_self_in, grad_self_mixed, query_table = query_back(
+        grad_cq, grad_cross, after_self, gains[:, 1:2].T, second_all
+    )
     cross_sum = Reduction(
         [
-            (frames, far(frames), grad_frame_pairs),
-            (cross_mixed, far(cross_mixed), grad_cross_in),
-            (act_two, far(act_two), grad_cq),
-            (self_mixed, far(self_mixed), grad_self_in),
+            ((frame_mine, frame_other), (frame_kept, frame_sent)),
+            ((cross_mixed,), grad_cross_in),
+            ((act_two,), grad_cq),
+            ((self_mixed,), grad_self_in),
         ],
         "seq",
     )
     grad_self_mixed = advance([cross_sum], grad_self_mixed)
-    grad_self_query, grad_self_pairs = attend_back(
-        self_query, self_pairs, self_bias, self_total, grad_self_mixed
-    )
-    both_acts = jnp.concatenate([act_far, act_one], axis=0)
-    self_pair_sum = Reduction([(both_acts, far(both_acts), grad_self_pairs)], "pair")
-    grad_self_query, grad_self_pairs = advance(
-        [self_pair_sum], (grad_self_query, grad_self_pairs)
-    )
-    value_sums = col_sum(grad_self_mixed)
+    grad_self_query, self_kept, self_sent = attend_back(
+        core, self_query, self_pairs, self_bias, self_total, grad_self_mixed
+    )
+    self_pair_sum = Reduction([((act_far, act_one), (self_kept, self_sent))], "pair")
+    grad_self_query, self_kept, self_sent = advance(
+        [self_pair_sum], (grad_self_query, self_kept, self_sent)
+    )
     norm_side, norm_far, small_term = self_tail(
+        core,
         grad_self_query,
-        grad_self_pairs,
+        self_kept,
+        self_sent,
         first_all,
-        normed_one,
-        normed_far,
-        [
-            value_sums,
-            self_out_bias,
-            query_bias,
-            kv_bias_term,
-            cross_out_bias,
-            down_bias,
-            gain_two,
-            gain_three,
-            gain_last,
-            shift_two,
-            shift_three,
-            shift_last,
-        ],
+        hidden,
+        hidden_other,
+        query_table,
+        table,
         up_bias_columns,
     )
-    self_sum = Reduction([(act_one, far(act_one), grad_self_query)], "seq", small_term)
-    owner_grads = frame_kept.astype(jnp.float32) + frame_came.astype(jnp.float32)
+    self_sum = Reduction([((act_one,), grad_self_query)], "seq", small_term)
+    owner_grads = frame_near.astype(jnp.float32) + frame_came.astype(jnp.float32)
     norm_far, owner_grads = advance([self_sum], (norm_far, owner_grads.astype(jnp.bfloat16)))
     norm_came = swap_seq(norm_far)
     grad_encoder = lax.all_to_all(
@@ -989,10 +1253,7 @@
         [self_sum], (grad_encoder, wide_sum), after=[cross_sum, self_pair_sum]
     )
     grad_encoder = grad_encoder.astype(jnp.float32)
-    back_one, _, _ = layer_back(
-        norm_side + norm_came.astype(jnp.float32), normed_one, scale_one, gains[:, 0]
-    )
-    grad_hidden = grad_self + back_one
+    grad_hidden = hidden_back(norm_side, norm_came, hidden, gains[:, :1].T, grad_self)
     wide_sum = wide_sum.astype(jnp.float32) + swap_seq(wide_sum).astype(jnp.float32)
     inner_rows = down_weight.shape[0]
     grad_up_weight = (
@@ -1008,14 +1269,14 @@
         result[None],
         grad_hidden[None],
         grad_encoder,
-        jnp.concatenate([small_sum[:, :1], small_sum[:, 9:12]], axis=1),
-        jnp.concatenate([small_sum[:, 1:2], small_sum[:, 12:15]], axis=1),
+        small_sum[:, :4],
+        small_sum[:, 4:8],
         jnp.concatenate([grad_self_queries, grad_self_keys], axis=1),
         grad_self_out,
         grad_cross_query,
         grad_cross_kv,
         grad_cross_out,
-        small_sum[:, 2:9],
+        small_sum[:, 8:15],
         grad_up_weight,
         small_sum[:, 15:small_cols].reshape(-1),
         wide_sum[:inner_rows],

time: 404 us -> 395 us (0.978); the launches traced: 396 us -> 394 us
  Pallas kernels: 102 us -> 136 us
  matrix products: 31.5 us -> 6.42 us
  other arithmetic: 43.6 us -> 26.1 us
  waiting for transfers between devices: 90.5 us -> 103 us
  local copies, waits for them, and re-layouts: 34.8 us -> 28.7 us
    pallas_call x3 -> x8, Pallas kernels: 21.2 us -> 53.9 us  [the longest x3 21 us: begin(): pl.pallas_call(partial(grad_kernel, parts=[len(left) for left, _ in self....]
    dot_general x5 -> x0, matrix products: 16.4 us -> none  [dot_left(): jnp.einsum('cj,ij->ci', grad_side, weight, preferred_element_type=jnp.flo...]
    ppermute x14, waiting for transfers between devices: 13.1 us -> 27.1 us  [swap_seq(): return lax.ppermute(block, 'seq', FLIP)]
    dot_general x6 -> x3, matrix products: 15.1 us -> 6.42 us  [dot_right(): return jnp.dot(left_side, weight, preferred_element_type=jnp.float32)]
    ppermute x45 -> x46, starting transfers between devices: 44.7 us -> 50.8 us  [swap(): return lax.ppermute(block, 'batch', partners(stride, radix, step))]
    reduce_sum x7 -> x0, other arithmetic: 5.38 us -> none  [the longest x4 4.83 us: col_sum(): return jnp.sum(grad_side, axis=0, dtype=jnp.float32)]
    ppermute x14, starting transfers between devices: 17 us -> 12.5 us  [swap_seq(): return lax.ppermute(block, 'seq', FLIP)]
    concatenate x4 -> x0, other arithmetic: 4.47 us -> none  [the longest x1 2.14 us: body(): both_acts = jnp.concatenate([act_far, act_one], axis=0)]
  transfers between devices with their start and end apart: 63 -> 64, of which waited for: 15 -> 22; matrix products, arithmetic and copies ran while one was open for 25% -> 13% of each run, Pallas kernels for 21% -> 30%
where the time goes in v5:
time: 395 us; the launch traced here: 394 us
  Pallas kernels  136 us (34%)
  waiting for transfers between devices  103 us (26%)
  starting transfers between devices  76.7 us (19%)
  local copies, waits for them, and re-layouts  28.7 us (7%)
  other arithmetic  26.1 us (7%)
  between operations  17.4 us (4%)
  matrix products  6.42 us (2%)
    ppermute x46, waiting for transfers between devices, swap(): return lax.ppermute(block, 'batch', partners(stride, radix, step))  69.6 us
    ppermute x46, starting transfers between devices, swap(): return lax.ppermute(block, 'batch', partners(stride, radix, step))  50.8 us
    pallas_call x2, Pallas kernels, attend_back(): pl.pallas_call(attend_back_kernel, grid=(blocks,), out_shape=(jax.ShapeDt...  27.5 us
    ppermute x14, waiting for transfers between devices, swap_seq(): return lax.ppermute(block, 'seq', FLIP)  27.1 us
    pallas_call x3, Pallas kernels, begin(): pl.pallas_call(partial(grad_kernel, parts=[len(left) for left, _ in self....  21 us
    pallas_call x2, Pallas kernels, attend(): pl.pallas_call(attend_kernel, grid=(blocks,), out_shape=(jax.ShapeDtypeSt...  19.4 us
    pallas_call x1, Pallas kernels, feed_forward(): pl.pallas_call(feed_forward_kernel, out_shape=(shape((rows, width), jnp.b...  18.3 us
    ppermute x14, starting transfers between devices, swap_seq(): return lax.ppermute(block, 'seq', FLIP)  12.5 us
  transfers between devices with their start and end apart: 64, of which 22 were waited for; matrix products, arithmetic and copies ran while one was open for 13% of the time, Pallas kernels for 30%

profile of v5, /device:TPU:0, one launch (start us, length us, event | category | flops | bytes accessed | tf_op | source)
XLA Modules:
  0.0 393.9 jit_solution(11951802260740390852)
XLA Ops:
  11.4 3.1 collective-permute-start
  21.8 5.1 %collective-permute-done.1 = bf16[48,1280]{1,0:T(8,128)(2,1)S(1)} collective-permute-done((bf16[48,1280]{1,0:T(8,128)(2,1)S(1)}, bf16[48,1280]{1,0:T(8,128)(2,1)S(1)}, u32[]{:S(2)}, u32[]{:S(2)}) %collective-permute-start.1) | collective-permute-done | bytes 122912 | tf_op jit(solution)/shard_map/ppermute | solution.py:216
  34.5 2.9 collective-permute-done.6
  37.4 9.7 %collective-permute-done.7 = bf16[48,1920]{1,0:T(8,128)(2,1)S(1)} collective-permute-done((bf16[48,1920]{1,0:T(8,128)(2,1)S(1)}, bf16[48,1920]{1,0:T(8,128)(2,1)S(1)}, u32[]{:S(2)}, u32[]{:S(2)}) %collective-permute-start.7) | collective-permute-done | bytes 184352 | tf_op jit(solution)/shard_map/ppermute | solution.py:216
  48.1 5.3 %all-to-all-start = ((bf16[16,48,768]{2,1,0:T(8,128)(2,1)}), bf16[16,48,768]{2,1,0:T(8,128)(2,1)S(1)}, u32[]{:S(2)}, u32[]{:S(2)}) async-start(bf16[16,48,768]{2,1,0:T(8,128)(2,1)} %param.20), calls=%async_computation | async-start | bytes 2359296 | tf_op jit(solution)/shard_map/all_to_all | solution.py:1062
  54.7 12.5 %collective-permute-done.9.refs_3_ = bf16[4,48,1280]{2,1,0:T(8,128)(2,1)} collective-permute-done((bf16[4,48,1280]{2,1,0:T(8,128)(2,1)S(1)}, bf16[4,48,1280]{2,1,0:T(8,128)(2,1)}, u32[]{:S(2)}, u32[]{:S(2)}) %collective-permute-start.9) | collective-permute-done | bytes 491552 | tf_op jit(solution)/shard_map/ppermute | solution.py:220
  69.9 4.7 %place_rows.2.weight_ref = bf16[768,2560]{1,0:T(8,128)(2,1)} custom-call(s32[4]{0:T(128)} %pad_add_fusion.1.where_ref, bf16[4,48,1280]{2,1,0:T(8,128)(2,1)} %copy-done.10, bf16[4,48,1280]{2,1,0:T(8,128)(2,1)} %copy-done.22, bf16[4,48,1280]{2,1,0:T(8,128)(2,1)} %copy-done.23, bf16[4,48,1280]{2,1,0:T(8,128)(2,1)} %collective-permute-done.9.refs_3_, ...), custom_call_target="tpu_custom_call" | custom-call | tf_op jit(solution)/shard_map/place_rows/pallas_call | solution.py:310
  81.2 6.9 %self_head.1 = (bf16[224,768]{1,0:T(8,128)(2,1)}, bf16[224,768]{1,0:T(8,128)(2,1)}, bf16[224,768]{1,0:T(8,128)(2,1)}, bf16[448,1536]{1,0:T(8,128)(2,1)}) custom-call(bf16[224,768]{1,0:T(8,128)(2,1)} %bitcast.115, bf16[224,768]{1,0:T(8,128)(2,1)} %copy-done.16, f32[1,768]{1,0:T(1,128)} %get-tuple-element.270.gain_ref, f32[1,768]{1,0:T(1,128)} %transpose.44.shift_ref, ...), custom_call_target="tpu_custom_call" | custom-call | tf_op jit(solution)/shard_map/self_head/pallas_call | solution.py:688
  89.8 6.1 %all-to-all-done = bf16[16,48,768]{2,1,0:T(8,128)(2,1)S(1)} async-done(((bf16[16,48,768]{2,1,0:T(8,128)(2,1)}), bf16[16,48,768]{2,1,0:T(8,128)(2,1)S(1)}, u32[]{:S(2)}, u32[]{:S(2)}) %all-to-all-start) | async-done | bytes 1179680 | tf_op jit(solution)/shard_map/all_to_all | solution.py:1062
  100.4 7.1 %attend.2 = (bf16[224,768]{1,0:T(8,128)(2,1)}, f32[6,2,224]{2,1,0:T(2,128)}) custom-call(bf16[224,768]{1,0:T(8,128)(2,1)} %get-tuple-element.125.query_ref, bf16[448,1536]{1,0:T(8,128)(2,1)} %get-tuple-element.126.key_ref.value_ref, bf16[448,1536]{1,0:T(8,128)(2,1)} %get-tuple-element.126.key_ref.value_ref, f32[448,224]{1,0:T(8,128)} %and_select_fusion.bias_ref), custom_call_target="tpu_custom_call" | custom-call | tf_op jit(solution)/shard_map/attend/pallas_call | solution.py:157
  107.5 17.9 %collective-permute-done.16.refs_3_ = bf16[4,48,1920]{2,1,0:T(8,128)(2,1)} collective-permute-done((bf16[4,48,1920]{2,1,0:T(8,128)(2,1)}, bf16[4,48,1920]{2,1,0:T(8,128)(2,1)}, u32[]{:S(2)}, u32[]{:S(2)}) %collective-permute-start.16) | collective-permute-done | bytes 737312 | tf_op jit(solution)/shard_map/ppermute | solution.py:216
  136.7 6.0 %place_rows.3.weight_ref.out_weight_ref.far_weight_ref = bf16[768,3840]{1,0:T(8,128)(2,1)} custom-call(s32[4]{0:T(128)} %pad_add_fusion.1.where_ref, bf16[4,48,1920]{2,1,0:T(8,128)(2,1)} %copy-done.7, bf16[4,48,1920]{2,1,0:T(8,128)(2,1)} %collective-permute-done.14.refs_1_, bf16[4,48,1920]{2,1,0:T(8,128)(2,1)} %collective-permute-done.15.refs_2_, ...), custom_call_target="tpu_custom_call" | custom-call | tf_op jit(solution)/shard_map/place_rows/pallas_call | solution.py:310
  142.7 8.7 %frame_pairs.1.key_ref.value_ref = bf16[1536,1536]{1,0:T(8,128)(2,1)} custom-call(bf16[768,768]{1,0:T(8,128)(2,1)} %bitcast.110, bf16[768,768]{1,0:T(8,128)(2,1)} %copy-done.4, bf16[768,3840]{1,0:T(8,128)(2,1)} %place_rows.3.weight_ref.out_weight_ref.far_weight_ref, f32[1,1536]{1,0:T(1,128)} %broadcast_in_dim.60.bias_ref), custom_call_target="tpu_custom_call" | custom-call | tf_op jit(solution)/shard_map/frame_pairs/pallas_call | solution.py:599
  157.8 12.3 %attend.3 = (bf16[224,768]{1,0:T(8,128)(2,1)}, f32[6,2,224]{2,1,0:T(2,128)}) custom-call(bf16[224,768]{1,0:T(8,128)(2,1)} %fusion.2.query_ref, bf16[1536,1536]{1,0:T(8,128)(2,1)} %frame_pairs.1.key_ref.value_ref, bf16[1536,1536]{1,0:T(8,128)(2,1)} %frame_pairs.1.key_ref.value_ref, f32[1536,224]{1,0:T(8,128)} %broadcast_in_dim.63.bias_ref), custom_call_target="tpu_custom_call" | custom-call | tf_op jit(solution)/shard_map/attend/pallas_call | solution.py:157
  173.2 18.3 %feed_forward.1 = (bf16[224,768]{1,0:T(8,128)(2,1)}, f32[224,768]{1,0:T(8,128)}, bf16[224,768]{1,0:T(8,128)(2,1)}, bf16[224,768]{1,0:T(8,128)(2,1)}, f32[8,768]{...) custom-call(bf16[224,768]{1,0:T(8,128)(2,1)} %add_convert_fusion.1.act_ref, f32[224,768]{1,0:T(8,128)} %copy-done.1, ...), custom_call_target="tpu_custom_call" | custom-call | tf_op jit(solution)/shard_map/feed_forward/pallas_call | solution.py:551
  191.6 19.0 %attend_back.2 = (bf16[224,768]{1,0:T(8,128)(2,1)}, bf16[1536,768]{1,0:T(8,128)(2,1)}, bf16[1536,768]{1,0:T(8,128)(2,1)}) custom-call(s32[1]{0:T(128)} %bitcast.7.core_ref, bf16[224,768]{1,0:T(8,128)(2,1)} %fusion.2.query_ref, bf16[1536,1536]{1,0:T(8,128)(2,1)} %frame_pairs.1.key_ref.value_ref, bf16[1536,1536]{1,0:T(8,128)(2,1)} %frame_pairs.1.key_ref.value_ref, ...), custom_call_target="tpu_custom_call" | custom-call | tf_op jit(solution)/shard_map/attend_back/pallas_call | solution.py:178
  212.1 9.3 %frame_back.1 = (bf16[768,768]{1,0:T(8,128)(2,1)}, bf16[768,768]{1,0:T(8,128)(2,1)}) custom-call(s32[1]{0:T(128)} %bitcast.7.core_ref, bf16[1536,768]{1,0:T(8,128)(2,1)} %get-tuple-element.148.kept_ref.refs_4_, bf16[1536,768]{1,0:T(8,128)(2,1)} %get-tuple-element.149.sent_ref, bf16[768,3840]{1,0:T(8,128)(2,1)} %place_rows.3.weight_ref.out_weight_ref.far_weight_ref, ...), custom_call_target="tpu_custom_call" | custom-call | tf_op jit(solution)/shard_map/frame_back/pallas_call | solution.py:634
  221.4 5.1 %query_back.1 = (f32[224,768]{1,0:T(8,128)}, bf16[224,768]{1,0:T(8,128)(2,1)}, bf16[224,768]{1,0:T(8,128)(2,1)}, f32[8,768]{1,0:T(8,128)}) custom-call(bf16[224,768]{1,0:T(8,128)(2,1)} %get-tuple-element.154.grad_ref.refs_12_, f32[224,768]{1,0:T(8,128)} %get-tuple-element.155.cross_ref, f32[224,768]{1,0:T(8,128)} %copy-done, ...), custom_call_target="tpu_custom_call" | custom-call | tf_op jit(solution)/shard_map/query_back/pallas_call | solution.py:762
  232.6 13.0 %grad_blocks.3 = (bf16[8,48,1920]{2,1,0:T(8,128)(2,1)}, bf16[8,48,1920]{2,1,0:T(8,128)(2,1)}) custom-call(s32[4]{0:T(128)} %pad_add_fusion.1.where_ref, bf16[768,768]{1,0:T(8,128)(2,1)} %bitcast.111, bf16[768,768]{1,0:T(8,128)(2,1)} %copy-done.4, bf16[768,768]{1,0:T(8,128)(2,1)} %collective-permute-done.24.refs_2_, ...), custom_call_target="tpu_custom_call" | custom-call | tf_op jit(solution)/shard_map/grad_blocks/pallas_call | solution.py:918
  245.6 8.5 %attend_back.3 = (bf16[224,768]{1,0:T(8,128)(2,1)}, bf16[448,768]{1,0:T(8,128)(2,1)}, bf16[448,768]{1,0:T(8,128)(2,1)}) custom-call(s32[1]{0:T(128)} %bitcast.7.core_ref, bf16[224,768]{1,0:T(8,128)(2,1)} %get-tuple-element.125.query_ref, bf16[448,1536]{1,0:T(8,128)(2,1)} %get-tuple-element.126.key_ref.value_ref, ...), custom_call_target="tpu_custom_call" | custom-call | tf_op jit(solution)/shard_map/attend_back/pallas_call | solution.py:178
  258.5 4.8 %grad_blocks.4 = (bf16[8,48,768]{2,1,0:T(8,128)(2,1)}, bf16[8,48,768]{2,1,0:T(8,128)(2,1)}) custom-call(s32[4]{0:T(128)} %pad_add_fusion.1.where_ref, bf16[224,768]{1,0:T(8,128)(2,1)} %get-tuple-element.141.refs_0_, bf16[224,768]{1,0:T(8,128)(2,1)} %get-tuple-element.142.refs_1_.refs_0_, bf16[224,768]{1,0:T(8,128)(2,1)} %copy-done.27, ...), custom_call_target="tpu_custom_call" | custom-call | tf_op jit(solution)/shard_map/grad_blocks/pallas_call | solution.py:918
  266.9 5.8 %self_tail.1 = (f32[224,768]{1,0:T(8,128)}, bf16[224,768]{1,0:T(8,128)(2,1)}, bf16[768,128]{1,0:T(8,128)(2,1)}) custom-call(s32[1]{0:T(128)} %bitcast.7.core_ref, bf16[224,768]{1,0:T(8,128)(2,1)} %get-tuple-element.166.query_ref.refs_2_, bf16[448,768]{1,0:T(8,128)(2,1)} %get-tuple-element.167.refs_4_.kept_ref, bf16[448,768]{1,0:T(8,128)(2,1)} %get-tuple-element.168.sent_ref, ...), custom_call_target="tpu_custom_call" | custom-call | tf_op jit(solution)/shard_map/self_tail/pallas_call | solution.py:833
  277.3 3.2 grad_blocks.5
  282.5 8.0 %all-to-all-start.1 = ((bf16[16,48,768]{2,1,0:T(8,128)(2,1)}), bf16[16,48,768]{2,1,0:T(8,128)(2,1)S(1)}, u32[]{:S(2)}, u32[]{:S(2)}) async-start(bf16[16,48,768]{2,1,0:T(8,128)(2,1)} %bitcast.47), calls=%async_computation.1 | async-start | bytes 2359296 | tf_op jit(solution)/shard_map/all_to_all | solution.py:1242
  302.5 8.8 %collective-permute-done.41 = bf16[4,48,768]{2,1,0:T(8,128)(2,1)} collective-permute-done((bf16[4,48,768]{2,1,0:T(8,128)(2,1)}, bf16[4,48,768]{2,1,0:T(8,128)(2,1)}, u32[]{:S(2)}, u32[]{:S(2)}) %collective-permute-start.41) | collective-permute-done | bytes 294944 | tf_op jit(solution)/shard_map/ppermute | solution.py:220
  313.1 15.9 %collective-permute-done.40 = bf16[4,48,1920]{2,1,0:T(8,128)(2,1)} collective-permute-done((bf16[4,48,1920]{2,1,0:T(8,128)(2,1)}, bf16[4,48,1920]{2,1,0:T(8,128)(2,1)}, u32[]{:S(2)}, u32[]{:S(2)}) %collective-permute-start.40) | collective-permute-done | bytes 737312 | tf_op jit(solution)/shard_map/ppermute | solution.py:216
  331.1 3.3 collective-permute-start.54
  339.6 3.7 collective-permute-start.50
  343.5 2.9 hidden_back.1
  349.0 5.4 %collective-permute-done.55 = bf16[48,1920]{1,0:T(8,128)(2,1)} collective-permute-done((bf16[48,1920]{1,0:T(8,128)(2,1)}, bf16[48,1920]{1,0:T(8,128)(2,1)}, u32[]{:S(2)}, u32[]{:S(2)}) %collective-permute-start.55) | collective-permute-done | bytes 184352 | tf_op jit(solution)/shard_map/ppermute | solution.py:216
  357.7 4.0 %collective-permute-start.44 = (bf16[48,512]{0,1:T(8,128)(2,1)S(1)}, bf16[48,512]{0,1:T(8,128)(2,1)S(1)}, u32[]{:S(2)}, u32[]{:S(2)}) collective-permute-start(bf16[48,512]{0,1:T(8,128)(2,1)S(1)} %get-tuple-element.204), channel_id=1, source_target_pairs={{0,8},{2,10},{4,12},{6,14},{8,0},{10,2},{12,4},{14,6},{16,24},{18,... | collective-permute-start | bytes 147464 | tf_op jit(solution)/shard_map/ppermute | solution.py:216
  367.2 6.0 %collective-permute-done.45 = bf16[48,512]{0,1:T(8,128)(2,1)S(1)} collective-permute-done((bf16[48,512]{0,1:T(8,128)(2,1)S(1)}, bf16[48,512]{0,1:T(8,128)(2,1)S(1)}, u32[]{:S(2)}, u32[]{:S(2)}) %collective-permute-start.45) | collective-permute-done | bytes 49184 | tf_op jit(solution)/shard_map/ppermute | solution.py:216
  (287 shorter events, 123.1 us)
Async XLA Ops:
  7.2 166.0 %all-gather.2.cloned.1.call-start = ((), (), s32[]{:S(2)}) async-start(), calls=%async_computation.3 | async-start | bytes 10027008 | tf_op jit(solution)/shard_map/all_gather | solution.py:1071
  27.0 20.2 %collective-permute-start.4 = (bf16[4,48,1280]{2,1,0:T(8,128)(2,1)S(1)}, bf16[4,48,1280]{2,1,0:T(8,128)(2,1)S(1)}, u32[]{:S(2)}, u32[]{:S(2)}) collective-permute-start(bf16[4,48,1280]{2,1,0:T(8,128)(2,1)S(1)} %pad_maximum_fusion.2.refs_0_), channel_id=1, source_target_pairs={{0,4},{2,6},{4,0},{6,2},{8,12},{10,14},{12,8},{14,10},{16,20},{18,... | collective-permute-start | bytes 1474568 | tf_op jit(solution)/shard_map/ppermute | solution.py:216
  28.5 18.7 %collective-permute-start.5 = (bf16[4,48,1280]{2,1,0:T(8,128)(2,1)S(1)}, bf16[4,48,1280]{2,1,0:T(8,128)(2,1)S(1)}, u32[]{:S(2)}, u32[]{:S(2)}) collective-permute-start(bf16[4,48,1280]{2,1,0:T(8,128)(2,1)S(1)} %pad_maximum_fusion.2.refs_0_), channel_id=1, source_target_pairs={{0,1},{1,0},{2,3},{3,2},{4,5},{5,4},{6,7},{7,6},{8,9},{9,8},{10,11... | collective-permute-start | bytes 1474568 | tf_op jit(solution)/shard_map/ppermute | solution.py:220
  48.1 47.9 %all-to-all-start = ((bf16[16,48,768]{2,1,0:T(8,128)(2,1)}), bf16[16,48,768]{2,1,0:T(8,128)(2,1)S(1)}, u32[]{:S(2)}, u32[]{:S(2)}) async-start(bf16[16,48,768]{2,1,0:T(8,128)(2,1)} %param.20), calls=%async_computation | async-start | bytes 2359296 | tf_op jit(solution)/shard_map/all_to_all | solution.py:1062
  53.4 293.1 %reduce-scatter.2.cloned.1.call-start = ((), (), s32[]{:S(2)}) async-start(), calls=%async_computation.4 | async-start | bytes 10027008 | tf_op jit(solution)/shard_map/reduce_scatter | solution.py:1199
  54.0 15.9 %collective-permute-start.11 = (bf16[4,48,1280]{2,1,0:T(8,128)(2,1)S(1)}, bf16[4,48,1280]{2,1,0:T(8,128)(2,1)}, u32[]{:S(2)}, u32[]{:S(2)}) collective-permute-start(bf16[4,48,1280]{2,1,0:T(8,128)(2,1)S(1)} %collective-permute-done.4.refs_1_), channel_id=1, source_target_pairs={{0,2},{2,0},{4,6},{6,4},{8,10},{10,8},{12,14},{14,12},{16,18},{18,... | collective-permute-start | bytes 1474568 | tf_op jit(solution)/shard_map/ppermute | solution.py:216
  54.5 15.4 %collective-permute-start.12 = (bf16[4,48,1280]{2,1,0:T(8,128)(2,1)}, bf16[4,48,1280]{2,1,0:T(8,128)(2,1)}, u32[]{:S(2)}, u32[]{:S(2)}) collective-permute-start(bf16[4,48,1280]{2,1,0:T(8,128)(2,1)} %copy-done.23), channel_id=1, source_target_pairs={{0,2},{2,0},{4,6},{6,4},{8,10},{10,8},{12,14},{14,12},{16,18},{18,... | collective-permute-start | bytes 1474568 | tf_op jit(solution)/shard_map/ppermute | solution.py:216
  67.7 22.1 %collective-permute-start.14 = (bf16[4,48,1920]{2,1,0:T(8,128)(2,1)S(1)}, bf16[4,48,1920]{2,1,0:T(8,128)(2,1)}, u32[]{:S(2)}, u32[]{:S(2)}) collective-permute-start(bf16[4,48,1920]{2,1,0:T(8,128)(2,1)S(1)} %pad_maximum_fusion.refs_0_), channel_id=1, source_target_pairs={{0,4},{2,6},{4,0},{6,2},{8,12},{10,14},{12,8},{14,10},{16,20},{18,... | collective-permute-start | bytes 2211848 | tf_op jit(solution)/shard_map/ppermute | solution.py:216
  69.4 20.4 %collective-permute-start.15 = (bf16[4,48,1920]{2,1,0:T(8,128)(2,1)S(1)}, bf16[4,48,1920]{2,1,0:T(8,128)(2,1)}, u32[]{:S(2)}, u32[]{:S(2)}) collective-permute-start(bf16[4,48,1920]{2,1,0:T(8,128)(2,1)S(1)} %pad_maximum_fusion.refs_0_), channel_id=1, source_target_pairs={{0,1},{1,0},{2,3},{3,2},{4,5},{5,4},{6,7},{7,6},{8,9},{9,8},{10,11... | collective-permute-start | bytes 2211848 | tf_op jit(solution)/shard_map/ppermute | solution.py:220
  96.0 29.4 %collective-permute-start.17 = (bf16[768,768]{1,0:T(8,128)(2,1)S(1)}, bf16[768,768]{1,0:T(8,128)(2,1)S(1)}, u32[]{:S(2)}, u32[]{:S(2)}) collective-permute-start(bf16[768,768]{1,0:T(8,128)(2,1)S(1)} %bitcast.109), channel_id=1, source_target_pairs={{0,1},{1,0},{2,3},{3,2},{4,5},{5,4},{6,7},{7,6},{8,9},{9,8},{10,11... | collective-permute-start | bytes 3538952 | tf_op jit(solution)/shard_map/ppermute | solution.py:220
  96.0 29.4 %collective-permute-start.16 = (bf16[4,48,1920]{2,1,0:T(8,128)(2,1)}, bf16[4,48,1920]{2,1,0:T(8,128)(2,1)}, u32[]{:S(2)}, u32[]{:S(2)}) collective-permute-start(bf16[4,48,1920]{2,1,0:T(8,128)(2,1)} %collective-permute-done.15.refs_2_), channel_id=1, source_target_pairs={{0,4},{2,6},{4,0},{6,2},{8,12},{10,14},{12,8},{14,10},{16,20},{18,... | collective-permute-start | bytes 2211848 | tf_op jit(solution)/shard_map/ppermute | solution.py:216
  210.6 21.3 %collective-permute-start.26 = (bf16[1536,768]{1,0:T(8,128)(2,1)}, bf16[1536,768]{1,0:T(8,128)(2,1)}, u32[]{:S(2)}, u32[]{:S(2)}) collective-permute-start(bf16[1536,768]{1,0:T(8,128)(2,1)} %get-tuple-element.149.sent_ref), channel_id=1, source_target_pairs={{0,2},{2,0},{4,6},{6,4},{8,10},{10,8},{12,14},{14,12},{16,18},{18,... | collective-permute-start | bytes 7077896 | tf_op jit(solution)/shard_map/ppermute | solution.py:216
  211.1 15.4 %collective-permute-start.24 = (bf16[768,768]{1,0:T(8,128)(2,1)S(1)}, bf16[768,768]{1,0:T(8,128)(2,1)}, u32[]{:S(2)}, u32[]{:S(2)}) collective-permute-start(bf16[768,768]{1,0:T(8,128)(2,1)S(1)} %bitcast.112), channel_id=1, source_target_pairs={{0,2},{2,0},{4,6},{6,4},{8,10},{10,8},{12,14},{14,12},{16,18},{18,... | collective-permute-start | bytes 3538952 | tf_op jit(solution)/shard_map/ppermute | solution.py:216
  211.2 19.3 %collective-permute-start.25 = (bf16[768,768]{1,0:T(8,128)(2,1)S(1)}, bf16[768,768]{1,0:T(8,128)(2,1)}, u32[]{:S(2)}, u32[]{:S(2)}) collective-permute-start(bf16[768,768]{1,0:T(8,128)(2,1)S(1)} %copy-done.5), channel_id=1, source_target_pairs={{0,2},{2,0},{4,6},{6,4},{8,10},{10,8},{12,14},{14,12},{16,18},{18,... | collective-permute-start | bytes 3538952 | tf_op jit(solution)/shard_map/ppermute | solution.py:216
  211.6 16.1 %collective-permute-start.31 = (bf16[224,768]{1,0:T(8,128)(2,1)}, bf16[224,768]{1,0:T(8,128)(2,1)}, u32[]{:S(2)}, u32[]{:S(2)}) collective-permute-start(bf16[224,768]{1,0:T(8,128)(2,1)} %get-tuple-element.132.refs_14_), channel_id=1, source_target_pairs={{0,2},{2,0},{4,6},{6,4},{8,10},{10,8},{12,14},{14,12},{16,18},{18,... | collective-permute-start | bytes 1032200 | tf_op jit(solution)/shard_map/ppermute | solution.py:216
  211.7 18.2 %collective-permute-start.27 = (bf16[224,768]{1,0:T(8,128)(2,1)S(1)}, bf16[224,768]{1,0:T(8,128)(2,1)}, u32[]{:S(2)}, u32[]{:S(2)}) collective-permute-start(bf16[224,768]{1,0:T(8,128)(2,1)S(1)} %copy-done.13), channel_id=1, source_target_pairs={{0,2},{2,0},{4,6},{6,4},{8,10},{10,8},{12,14},{14,12},{16,18},{18,... | collective-permute-start | bytes 1032200 | tf_op jit(solution)/shard_map/ppermute | solution.py:216
  227.8 45.6 %collective-permute-start.38 = (bf16[768,768]{1,0:T(8,128)(2,1)}, bf16[768,768]{1,0:T(8,128)(2,1)}, u32[]{:S(2)}, u32[]{:S(2)}) collective-permute-start(bf16[768,768]{1,0:T(8,128)(2,1)} %get-tuple-element.182), channel_id=1, source_target_pairs={{0,1},{1,0},{2,3},{3,2},{4,5},{5,4},{6,7},{7,6},{8,9},{9,8},{10,11... | collective-permute-start | bytes 3538952 | tf_op jit(solution)/shard_map/ppermute | solution.py:220
  254.5 38.2 %collective-permute-start.34 = (bf16[8,48,1920]{2,1,0:T(8,128)(2,1)}, bf16[8,48,1920]{2,1,0:T(8,128)(2,1)S(1)}, u32[]{:S(2)}, u32[]{:S(2)}) collective-permute-start(bf16[8,48,1920]{2,1,0:T(8,128)(2,1)} %get-tuple-element.174), channel_id=1, source_target_pairs={{0,1},{1,0},{2,3},{3,2},{4,5},{5,4},{6,7},{7,6},{8,9},{9,8},{10,11... | collective-permute-start | bytes 4423688 | tf_op jit(solution)/shard_map/ppermute | solution.py:220
  263.3 27.4 %collective-permute-start.35 = (bf16[8,48,768]{2,1,0:T(8,128)(2,1)}, bf16[8,48,768]{2,1,0:T(8,128)(2,1)}, u32[]{:S(2)}, u32[]{:S(2)}) collective-permute-start(bf16[8,48,768]{2,1,0:T(8,128)(2,1)} %get-tuple-element.176), channel_id=1, source_target_pairs={{0,4},{2,6},{4,0},{6,2},{8,12},{10,14},{12,8},{14,10},{16,20},{18,... | collective-permute-start | bytes 1769480 | tf_op jit(solution)/shard_map/ppermute | solution.py:216
  280.5 17.9 %collective-permute-start.39 = (bf16[8,48,512]{2,1,0:T(8,128)(2,1)}, bf16[8,48,512]{2,1,0:T(8,128)(2,1)}, u32[]{:S(2)}, u32[]{:S(2)}) collective-permute-start(bf16[8,48,512]{2,1,0:T(8,128)(2,1)} %get-tuple-element.185), channel_id=1, source_target_pairs={{0,1},{1,0},{2,3},{3,2},{4,5},{5,4},{6,7},{7,6},{8,9},{9,8},{10,11... | collective-permute-start | bytes 1179656 | tf_op jit(solution)/shard_map/ppermute | solution.py:220
  281.6 49.5 %collective-permute-start.42 = (bf16[224,768]{1,0:T(8,128)(2,1)}, bf16[224,768]{1,0:T(8,128)(2,1)}, u32[]{:S(2)}, u32[]{:S(2)}) collective-permute-start(bf16[224,768]{1,0:T(8,128)(2,1)} %get-tuple-element.193), channel_id=1, source_target_pairs={{0,1},{1,0},{2,3},{3,2},{4,5},{5,4},{6,7},{7,6},{8,9},{9,8},{10,11... | collective-permute-start | bytes 1032200 | tf_op jit(solution)/shard_map/ppermute | solution.py:220
  282.5 63.9 %all-to-all-start.1 = ((bf16[16,48,768]{2,1,0:T(8,128)(2,1)}), bf16[16,48,768]{2,1,0:T(8,128)(2,1)S(1)}, u32[]{:S(2)}, u32[]{:S(2)}) async-start(bf16[16,48,768]{2,1,0:T(8,128)(2,1)} %bitcast.47), calls=%async_computation.1 | async-start | bytes 2359296 | tf_op jit(solution)/shard_map/all_to_all | solution.py:1242
  294.1 17.2 %collective-permute-start.41 = (bf16[4,48,768]{2,1,0:T(8,128)(2,1)}, bf16[4,48,768]{2,1,0:T(8,128)(2,1)}, u32[]{:S(2)}, u32[]{:S(2)}) collective-permute-start(bf16[4,48,768]{2,1,0:T(8,128)(2,1)} %get-tuple-element.191), channel_id=1, source_target_pairs={{0,1},{1,0},{2,3},{3,2},{4,5},{5,4},{6,7},{7,6},{8,9},{9,8},{10,11... | collective-permute-start | bytes 884744 | tf_op jit(solution)/shard_map/ppermute | solution.py:220
  295.4 33.5 %collective-permute-start.40 = (bf16[4,48,1920]{2,1,0:T(8,128)(2,1)}, bf16[4,48,1920]{2,1,0:T(8,128)(2,1)}, u32[]{:S(2)}, u32[]{:S(2)}) collective-permute-start(bf16[4,48,1920]{2,1,0:T(8,128)(2,1)} %get-tuple-element.189), channel_id=1, source_target_pairs={{0,4},{2,6},{4,0},{6,2},{8,12},{10,14},{12,8},{14,10},{16,20},{18,... | collective-permute-start | bytes 2211848 | tf_op jit(solution)/shard_map/ppermute | solution.py:216
  300.1 39.6 %collective-permute-start.43 = (bf16[4,48,512]{1,2,0:T(8,128)(2,1)S(1)}, bf16[4,48,512]{1,2,0:T(8,128)(2,1)S(1)}, u32[]{:S(2)}, u32[]{:S(2)}) collective-permute-start(bf16[4,48,512]{1,2,0:T(8,128)(2,1)S(1)} %bitcast.127), channel_id=1, source_target_pairs={{0,4},{2,6},{4,0},{6,2},{8,12},{10,14},{12,8},{14,10},{16,20},{18,... | collective-permute-start | bytes 589832 | tf_op jit(solution)/shard_map/ppermute | solution.py:216
  331.1 15.3 %collective-permute-start.54 = (bf16[48,1920]{1,0:T(8,128)(2,1)}, bf16[48,1920]{1,0:T(8,128)(2,1)S(1)}, u32[]{:S(2)}, u32[]{:S(2)}) collective-permute-start(bf16[48,1920]{1,0:T(8,128)(2,1)} %get-tuple-element.212), channel_id=1, source_target_pairs={{0,8},{2,10},{4,12},{6,14},{8,0},{10,2},{12,4},{14,6},{16,24},{18,... | collective-permute-start | bytes 552968 | tf_op jit(solution)/shard_map/ppermute | solution.py:216
  334.4 20.1 %collective-permute-start.55 = (bf16[48,1920]{1,0:T(8,128)(2,1)}, bf16[48,1920]{1,0:T(8,128)(2,1)}, u32[]{:S(2)}, u32[]{:S(2)}) collective-permute-start(bf16[48,1920]{1,0:T(8,128)(2,1)} %get-tuple-element.213), channel_id=1, source_target_pairs={{0,16},{2,18},{4,20},{6,22},{8,24},{10,26},{12,28},{14,30},{16,0},... | collective-permute-start | bytes 552968 | tf_op jit(solution)/shard_map/ppermute | solution.py:216
  335.8 20.2 %collective-permute-start.56 = (bf16[48,1920]{1,0:T(8,128)(2,1)}, bf16[48,1920]{1,0:T(8,128)(2,1)}, u32[]{:S(2)}, u32[]{:S(2)}) collective-permute-start(bf16[48,1920]{1,0:T(8,128)(2,1)} %get-tuple-element.214), channel_id=1, source_target_pairs={{0,24},{2,26},{4,28},{6,30},{8,16},{10,18},{12,20},{14,22},{16,8},... | collective-permute-start | bytes 552968 | tf_op jit(solution)/shard_map/ppermute | solution.py:216
  336.8 20.9 %collective-permute-start.49 = (bf16[48,768]{1,0:T(8,128)(2,1)}, bf16[48,768]{1,0:T(8,128)(2,1)}, u32[]{:S(2)}, u32[]{:S(2)}) collective-permute-start(bf16[48,768]{1,0:T(8,128)(2,1)} %get-tuple-element.208), channel_id=1, source_target_pairs={{0,8},{2,10},{4,12},{6,14},{8,0},{10,2},{12,4},{14,6},{16,24},{18,... | collective-permute-start | bytes 221192 | tf_op jit(solution)/shard_map/ppermute | solution.py:216
  339.6 22.1 %collective-permute-start.50 = (bf16[48,768]{1,0:T(8,128)(2,1)}, bf16[48,768]{1,0:T(8,128)(2,1)S(1)}, u32[]{:S(2)}, u32[]{:S(2)}) collective-permute-start(bf16[48,768]{1,0:T(8,128)(2,1)} %get-tuple-element.209), channel_id=1, source_target_pairs={{0,16},{2,18},{4,20},{6,22},{8,24},{10,26},{12,28},{14,30},{16,0},... | collective-permute-start | bytes 221192 | tf_op jit(solution)/shard_map/ppermute | solution.py:216
  354.5 30.7 %collective-permute-start.59 = (bf16[384,768]{1,0:T(8,128)(2,1)}, bf16[384,768]{1,0:T(8,128)(2,1)S(1)}, u32[]{:S(2)}, u32[]{:S(2)}) collective-permute-start(bf16[384,768]{1,0:T(8,128)(2,1)} %bitcast.125), channel_id=1, source_target_pairs={{0,1},{1,0},{2,3},{3,2},{4,5},{5,4},{6,7},{7,6},{8,9},{9,8},{10,11... | collective-permute-start | bytes 1769480 | tf_op jit(solution)/shard_map/ppermute | solution.py:220
  357.1 23.5 %collective-permute-start.57 = (bf16[48,1920]{1,0:T(8,128)(2,1)S(1)}, bf16[48,1920]{1,0:T(8,128)(2,1)S(1)}, u32[]{:S(2)}, u32[]{:S(2)}) collective-permute-start(bf16[48,1920]{1,0:T(8,128)(2,1)S(1)} %reduce-precision_convert_fusion), channel_id=1, source_target_pairs={{0,1},{1,0},{2,3},{3,2},{4,5},{5,4},{6,7},{7,6},{8,9},{9,8},{10,11... | collective-permute-start | bytes 552968 | tf_op jit(solution)/shard_map/ppermute | solution.py:220
  (68 other events, 677.2 us)
Sparse Core Ops, SparseCore 0:
  47.4 115.3 all-gather.1
  191.7 151.0 reduce-scatter.1

commit v6 on v5

--- a/solution.py
+++ b/solution.py
@@ -292,10 +292,10 @@
 
     def by_last(self, column, across, side):
         far = swap_seq(across) if self.last == "seq" else swap(side, CORES)
-        return column, across, side, far
-
-    def place(self, *mine):
-        other = tuple(swap(piece, 1) for piece in mine)
+        return column, across, side, far, swap(column, 1), swap(across, 1), swap(side, 1)
+
+    def place(self, *pieces):
+        mine, other = pieces[:4], (*pieces[4:], swap(pieces[3], 1))
         total = lax.axis_size("batch") * self.rows
         call = pl.pallas_call(
             partial(place_kernel, depth=self.depth, rows=self.rows, half=self.half),
@@ -1092,26 +1092,10 @@
     query_pos = positions[None, :]
     self_mask = (key_pos <= query_pos) & ((key_pos >= offset) | (key_pos == query_pos))
     self_bias = jnp.where(self_mask, 0.0, -jnp.inf)
-    self_query, self_pairs, second.state, frame_mine = lax.optimization_barrier(
-        (self_query, self_pairs, second.state, frame_mine)
-    )
-    frame_other = swap_seq(frame_mine)
+    self_query, self_pairs, second.state = lax.optimization_barrier(
+        (self_query, self_pairs, second.state)
+    )
     second.step()
-    self_mixed, self_total = attend(self_query, self_pairs, self_bias)
-    self_mixed, second.state, frame_other = lax.optimization_barrier(
-        (self_mixed, second.state, frame_other)
-    )
-    second_all = second.result()
-    self_out_all = second_all[:, :model_width]
-    query_all = second_all[:, model_width : 2 * model_width]
-    kv_all = second_all[:, 2 * model_width : 4 * model_width]
-    cross_out_all = second_all[:, 4 * model_width :]
-    after_self = inputs + dot_right(self_mixed, self_out_all) + biases[:, 2]
-    normed_two, scale_two = layer_parts(after_self)
-    act_two = (normed_two * gains[:, 1] + shifts[:, 1]).astype(jnp.bfloat16)
-    cross_queries = (dot_right(act_two, query_all) + biases[:, 3]).astype(jnp.bfloat16)
-    kv_bias = jnp.concatenate([zero_row, biases[:, 4]])
-    cross_pairs = frame_pairs(frame_mine, frame_other, second_all, kv_bias[None])
     half_slots = frame_mine.shape[0]
     owner_frames = encoder.shape[1]
     gathered = jnp.arange(2 * half_slots, dtype=jnp.int32)
@@ -1121,24 +1105,81 @@
     frame_bias = jnp.broadcast_to(
         jnp.where(frame_ids < frame_count, 0.0, -jnp.inf)[:, None], (2 * half_slots, row_count)
     )
-    cross_mixed, cross_total = attend(cross_queries, cross_pairs, frame_bias)
-    after_cross = after_self + dot_right(cross_mixed, cross_out_all) + biases[:, 5]
-    normed_three, scale_three = layer_parts(after_cross)
-    act_three = (normed_three * gains[:, 2] + shifts[:, 2]).astype(jnp.bfloat16)
     corpus_match = corpus_ids[0] == jnp.arange(corpus_weights.shape[0], dtype=jnp.int32)
     seq_weight = jnp.sum(jnp.where(corpus_match, corpus_weights, 0.0))
     live_rows = (positions >= offset) & (positions < offset + length)
     live_weight = jnp.where(live_rows, seq_weight, 0.0)[:, None]
+    up_bias_blocks = up_bias_all.reshape(blocks, 1, model_width)
+    kv_bias = jnp.concatenate([zero_row, biases[:, 4]])[None]
+    side_rows = (
+        gains[:, :1].T,
+        gains[:, 1:2].T,
+        gains[:, 2:].T,
+        shifts[:, 3:].T,
+        biases[:, 6:].T,
+        biases[:, 2][None],
+        biases[:, 3][None],
+        biases[:, 5][None],
+        shifts[:, 1][None],
+        gains[:, 2][None],
+        shifts[:, 2][None],
+    )
+    self_query, self_pairs, frame_mine, side_rows, frame_bias, live_weight, up_bias_blocks, kv_bias = (
+        lax.optimization_barrier(
+            (
+                self_query,
+                self_pairs,
+                frame_mine,
+                side_rows,
+                frame_bias,
+                live_weight,
+                up_bias_blocks,
+                kv_bias,
+            )
+        )
+    )
+    (
+        gain_self,
+        gain_query,
+        gain_end,
+        shift_end,
+        bias_down,
+        bias_self_out,
+        bias_query,
+        bias_cross_out,
+        shift_query,
+        gain_up,
+        shift_up,
+    ) = side_rows
+    frame_other = swap_seq(frame_mine)
+    self_mixed, self_total = attend(self_query, self_pairs, self_bias)
+    self_mixed, second.state, frame_other = lax.optimization_barrier(
+        (self_mixed, second.state, frame_other)
+    )
+    second_all = second.result()
+    self_out_all = second_all[:, :model_width]
+    query_all = second_all[:, model_width : 2 * model_width]
+    kv_all = second_all[:, 2 * model_width : 4 * model_width]
+    cross_out_all = second_all[:, 4 * model_width :]
+    after_self = inputs + dot_right(self_mixed, self_out_all) + bias_self_out
+    normed_two, scale_two = layer_parts(after_self)
+    act_two = (normed_two * gain_query + shift_query).astype(jnp.bfloat16)
+    cross_queries = (dot_right(act_two, query_all) + bias_query).astype(jnp.bfloat16)
+    cross_pairs = frame_pairs(frame_mine, frame_other, second_all, kv_bias)
+    cross_mixed, cross_total = attend(cross_queries, cross_pairs, frame_bias)
+    after_cross = after_self + dot_right(cross_mixed, cross_out_all) + bias_cross_out
+    normed_three, scale_three = layer_parts(after_cross)
+    act_three = (normed_three * gain_up + shift_up).astype(jnp.bfloat16)
     if splits(shard_rows):
         result, grad_cross, grad_cross_in, grad_cross_mixed, table, up_sums, wide_term = feed_forward(
             act_three,
             after_cross,
             cotangent,
             live_weight,
-            gains[:, 2:].T,
-            shifts[:, 3:].T,
-            biases[:, 6:].T,
-            up_bias_all.reshape(blocks, 1, model_width),
+            gain_end,
+            shift_end,
+            bias_down,
+            up_bias_blocks,
             second_all,
             third_all,
             size,
@@ -1204,7 +1245,7 @@
     grad_cq, frame_near, frame_far = lax.optimization_barrier((grad_cq, frame_near, frame_far))
     frame_came = swap_seq(frame_far)
     grad_self, grad_self_in, grad_self_mixed, query_table = query_back(
-        grad_cq, grad_cross, after_self, gains[:, 1:2].T, second_all
+        grad_cq, grad_cross, after_self, gain_query, second_all
     )
     cross_sum = Reduction(
         [
@@ -1253,7 +1294,7 @@
         [self_sum], (grad_encoder, wide_sum), after=[cross_sum, self_pair_sum]
     )
     grad_encoder = grad_encoder.astype(jnp.float32)
-    grad_hidden = hidden_back(norm_side, norm_came, hidden, gains[:, :1].T, grad_self)
+    grad_hidden = hidden_back(norm_side, norm_came, hidden, gain_self, grad_self)
     wide_sum = wide_sum.astype(jnp.float32) + swap_seq(wide_sum).astype(jnp.float32)
     inner_rows = down_weight.shape[0]
     grad_up_weight = (

time: 395 us -> 391 us (0.990)
  waiting for transfers between devices: 103 us -> 94.5 us
  starting transfers between devices: 76.7 us -> 81.1 us
    ppermute x14, waiting for transfers between devices: 27.1 us -> 14.8 us  [swap_seq(): return lax.ppermute(block, 'seq', FLIP)]
    ppermute x46, waiting for transfers between devices: 69.6 us -> 74.9 us  [swap(): return lax.ppermute(block, 'batch', partners(stride, radix, step))]
where the time goes in v6:
time: 391 us; the launch traced here: 390 us
  Pallas kernels  136 us (35%)
  waiting for transfers between devices  94.5 us (24%)
  starting transfers between devices  81.1 us (21%)
  local copies, waits for them, and re-layouts  28.2 us (7%)
  other arithmetic  26.2 us (7%)
  between operations  17.5 us (4%)
  matrix products  6.42 us (2%)
    ppermute x46, waiting for transfers between devices, swap(): return lax.ppermute(block, 'batch', partners(stride, radix, step))  74.9 us
    ppermute x46, starting transfers between devices, swap(): return lax.ppermute(block, 'batch', partners(stride, radix, step))  54.6 us
    pallas_call x2, Pallas kernels, attend_back(): pl.pallas_call(attend_back_kernel, grid=(blocks,), out_shape=(jax.ShapeDt...  27.5 us
    pallas_call x3, Pallas kernels, begin(): pl.pallas_call(partial(grad_kernel, parts=[len(left) for left, _ in self....  20.9 us
    pallas_call x2, Pallas kernels, attend(): pl.pallas_call(attend_kernel, grid=(blocks,), out_shape=(jax.ShapeDtypeSt...  19.6 us
    pallas_call x1, Pallas kernels, feed_forward(): pl.pallas_call(feed_forward_kernel, out_shape=(shape((rows, width), jnp.b...  18.3 us
    ppermute x14, waiting for transfers between devices, swap_seq(): return lax.ppermute(block, 'seq', FLIP)  14.8 us
    ppermute x14, starting transfers between devices, swap_seq(): return lax.ppermute(block, 'seq', FLIP)  13.8 us
  transfers between devices with their start and end apart: 64, of which 22 were waited for; matrix products, arithmetic and copies ran while one was open for 13% of the time, Pallas kernels for 30%

profile of v6, /device:TPU:0, one launch (start us, length us, event | category | flops | bytes accessed | tf_op | source)
XLA Modules:
  0.0 389.6 jit_solution(15258397002970498215)
XLA Ops:
  11.4 3.1 collective-permute-start
  21.8 5.1 %collective-permute-done.1 = bf16[48,1280]{1,0:T(8,128)(2,1)S(1)} collective-permute-done((bf16[48,1280]{1,0:T(8,128)(2,1)S(1)}, bf16[48,1280]{1,0:T(8,128)(2,1)S(1)}, u32[]{:S(2)}, u32[]{:S(2)}) %collective-permute-start.1) | collective-permute-done | bytes 122912 | tf_op jit(solution)/shard_map/ppermute | solution.py:216
  37.4 9.7 %collective-permute-done.7 = bf16[48,1920]{1,0:T(8,128)(2,1)S(1)} collective-permute-done((bf16[48,1920]{1,0:T(8,128)(2,1)S(1)}, bf16[48,1920]{1,0:T(8,128)(2,1)S(1)}, u32[]{:S(2)}, u32[]{:S(2)}) %collective-permute-start.7) | collective-permute-done | bytes 184352 | tf_op jit(solution)/shard_map/ppermute | solution.py:216
  48.1 5.3 %all-to-all-start = ((bf16[16,48,768]{2,1,0:T(8,128)(2,1)}), bf16[16,48,768]{2,1,0:T(8,128)(2,1)S(1)}, u32[]{:S(2)}, u32[]{:S(2)}) async-start(bf16[16,48,768]{2,1,0:T(8,128)(2,1)} %param.20), calls=%async_computation | async-start | bytes 2359296 | tf_op jit(solution)/shard_map/all_to_all | solution.py:1062
  62.9 4.8 %place_rows.2.weight_ref = bf16[768,2560]{1,0:T(8,128)(2,1)} custom-call(s32[4]{0:T(128)} %pad_add_fusion.1.where_ref, bf16[4,48,1280]{2,1,0:T(8,128)(2,1)} %copy-done.10, bf16[4,48,1280]{2,1,0:T(8,128)(2,1)} %copy-done.22, bf16[4,48,1280]{2,1,0:T(8,128)(2,1)} %copy-done.23, bf16[4,48,1280]{2,1,0:T(8,128)(2,1)} %collective-permute-done.9.refs_3_, ...), custom_call_target="tpu_custom_call" | custom-call | tf_op jit(solution)/shard_map/place_rows/pallas_call | solution.py:310
  74.2 6.9 %self_head.1 = (bf16[224,768]{1,0:T(8,128)(2,1)}, bf16[224,768]{1,0:T(8,128)(2,1)}, bf16[224,768]{1,0:T(8,128)(2,1)}, bf16[448,1536]{1,0:T(8,128)(2,1)}) custom-call(bf16[224,768]{1,0:T(8,128)(2,1)} %bitcast.117, bf16[224,768]{1,0:T(8,128)(2,1)} %copy-done.16, f32[1,768]{1,0:T(1,128)} %get-tuple-element.234.gain_ref, f32[1,768]{1,0:T(1,128)} %transpose.46.shift_ref, ...), custom_call_target="tpu_custom_call" | custom-call | tf_op jit(solution)/shard_map/self_head/pallas_call | solution.py:688
  81.1 7.3 %collective-permute-done.14.refs_1_ = bf16[4,48,1920]{2,1,0:T(8,128)(2,1)} collective-permute-done((bf16[4,48,1920]{2,1,0:T(8,128)(2,1)S(1)}, bf16[4,48,1920]{2,1,0:T(8,128)(2,1)}, u32[]{:S(2)}, u32[]{:S(2)}) %collective-permute-start.14) | collective-permute-done | bytes 737312 | tf_op jit(solution)/shard_map/ppermute | solution.py:216
  91.1 4.8 %all-to-all-done = bf16[16,48,768]{2,1,0:T(8,128)(2,1)S(1)} async-done(((bf16[16,48,768]{2,1,0:T(8,128)(2,1)}), bf16[16,48,768]{2,1,0:T(8,128)(2,1)S(1)}, u32[]{:S(2)}, u32[]{:S(2)}) %all-to-all-start) | async-done | bytes 1179680 | tf_op jit(solution)/shard_map/all_to_all | solution.py:1062
  104.1 7.3 %attend.2 = (bf16[224,768]{1,0:T(8,128)(2,1)}, f32[6,2,224]{2,1,0:T(2,128)}) custom-call(bf16[224,768]{1,0:T(8,128)(2,1)} %get-tuple-element.147.query_ref, bf16[448,1536]{1,0:T(8,128)(2,1)} %get-tuple-element.148.key_ref.value_ref, bf16[448,1536]{1,0:T(8,128)(2,1)} %get-tuple-element.148.key_ref.value_ref, f32[448,224]{1,0:T(8,128)} %and_select_fusion.bias_ref), custom_call_target="tpu_custom_call" | custom-call | tf_op jit(solution)/shard_map/attend/pallas_call | solution.py:157
  111.4 18.0 %collective-permute-done.16.refs_3_ = bf16[4,48,1920]{2,1,0:T(8,128)(2,1)} collective-permute-done((bf16[4,48,1920]{2,1,0:T(8,128)(2,1)}, bf16[4,48,1920]{2,1,0:T(8,128)(2,1)}, u32[]{:S(2)}, u32[]{:S(2)}) %collective-permute-start.16) | collective-permute-done | bytes 737312 | tf_op jit(solution)/shard_map/ppermute | solution.py:216
  135.2 6.0 %place_rows.3.weight_ref.out_weight_ref.far_weight_ref = bf16[768,3840]{1,0:T(8,128)(2,1)} custom-call(s32[4]{0:T(128)} %pad_add_fusion.1.where_ref, bf16[4,48,1920]{2,1,0:T(8,128)(2,1)} %copy-done.7, bf16[4,48,1920]{2,1,0:T(8,128)(2,1)} %collective-permute-done.14.refs_1_, bf16[4,48,1920]{2,1,0:T(8,128)(2,1)} %collective-permute-done.15.refs_2_, ...), custom_call_target="tpu_custom_call" | custom-call | tf_op jit(solution)/shard_map/place_rows/pallas_call | solution.py:310
  141.2 8.7 %frame_pairs.1.key_ref.value_ref = bf16[1536,1536]{1,0:T(8,128)(2,1)} custom-call(bf16[768,768]{1,0:T(8,128)(2,1)} %bitcast.112, bf16[768,768]{1,0:T(8,128)(2,1)} %copy-done.4, bf16[768,3840]{1,0:T(8,128)(2,1)} %place_rows.3.weight_ref.out_weight_ref.far_weight_ref, f32[1,1536]{1,0:T(1,128)} %broadcast_in_dim.64.bias_ref), custom_call_target="tpu_custom_call" | custom-call | tf_op jit(solution)/shard_map/frame_pairs/pallas_call | solution.py:599
  154.9 12.2 %attend.3 = (bf16[224,768]{1,0:T(8,128)(2,1)}, f32[6,2,224]{2,1,0:T(2,128)}) custom-call(bf16[224,768]{1,0:T(8,128)(2,1)} %fusion.2.query_ref, bf16[1536,1536]{1,0:T(8,128)(2,1)} %frame_pairs.1.key_ref.value_ref, bf16[1536,1536]{1,0:T(8,128)(2,1)} %frame_pairs.1.key_ref.value_ref, f32[1536,224]{1,0:T(8,128)} %broadcast_in_dim.60.bias_ref), custom_call_target="tpu_custom_call" | custom-call | tf_op jit(solution)/shard_map/attend/pallas_call | solution.py:157
  170.2 18.3 %feed_forward.1 = (bf16[224,768]{1,0:T(8,128)(2,1)}, f32[224,768]{1,0:T(8,128)}, bf16[224,768]{1,0:T(8,128)(2,1)}, bf16[224,768]{1,0:T(8,128)(2,1)}, f32[8,768]{...) custom-call(bf16[224,768]{1,0:T(8,128)(2,1)} %add_convert_fusion.1.act_ref, f32[224,768]{1,0:T(8,128)} %copy-done.1, ...), custom_call_target="tpu_custom_call" | custom-call | tf_op jit(solution)/shard_map/feed_forward/pallas_call | solution.py:551
  188.6 19.0 %attend_back.2 = (bf16[224,768]{1,0:T(8,128)(2,1)}, bf16[1536,768]{1,0:T(8,128)(2,1)}, bf16[1536,768]{1,0:T(8,128)(2,1)}) custom-call(s32[1]{0:T(128)} %bitcast.7.core_ref, bf16[224,768]{1,0:T(8,128)(2,1)} %fusion.2.query_ref, bf16[1536,1536]{1,0:T(8,128)(2,1)} %frame_pairs.1.key_ref.value_ref, bf16[1536,1536]{1,0:T(8,128)(2,1)} %frame_pairs.1.key_ref.value_ref, ...), custom_call_target="tpu_custom_call" | custom-call | tf_op jit(solution)/shard_map/attend_back/pallas_call | solution.py:178
  209.0 9.3 %frame_back.1 = (bf16[768,768]{1,0:T(8,128)(2,1)}, bf16[768,768]{1,0:T(8,128)(2,1)}) custom-call(s32[1]{0:T(128)} %bitcast.7.core_ref, bf16[1536,768]{1,0:T(8,128)(2,1)} %get-tuple-element.187.kept_ref.refs_4_, bf16[1536,768]{1,0:T(8,128)(2,1)} %get-tuple-element.188.sent_ref, bf16[768,3840]{1,0:T(8,128)(2,1)} %place_rows.3.weight_ref.out_weight_ref.far_weight_ref, ...), custom_call_target="tpu_custom_call" | custom-call | tf_op jit(solution)/shard_map/frame_back/pallas_call | solution.py:634
  218.3 5.1 %query_back.1 = (f32[224,768]{1,0:T(8,128)}, bf16[224,768]{1,0:T(8,128)(2,1)}, bf16[224,768]{1,0:T(8,128)(2,1)}, f32[8,768]{1,0:T(8,128)}) custom-call(bf16[224,768]{1,0:T(8,128)(2,1)} %get-tuple-element.193.grad_ref.refs_12_, f32[224,768]{1,0:T(8,128)} %get-tuple-element.194.cross_ref, f32[224,768]{1,0:T(8,128)} %copy-done, f32[1,768]{1,0:T(1,128)} %copy-done.34, ...), custom_call_target="tpu_custom_call" | custom-call | tf_op jit(solution)/shard_map/query_back/pallas_call | solution.py:762
  228.4 13.0 %grad_blocks.3 = (bf16[8,48,1920]{2,1,0:T(8,128)(2,1)}, bf16[8,48,1920]{2,1,0:T(8,128)(2,1)}) custom-call(s32[4]{0:T(128)} %pad_add_fusion.1.where_ref, bf16[768,768]{1,0:T(8,128)(2,1)} %bitcast.113, bf16[768,768]{1,0:T(8,128)(2,1)} %copy-done.4, bf16[768,768]{1,0:T(8,128)(2,1)} %collective-permute-done.24.refs_2_, ...), custom_call_target="tpu_custom_call" | custom-call | tf_op jit(solution)/shard_map/grad_blocks/pallas_call | solution.py:918
  241.4 8.5 %attend_back.3 = (bf16[224,768]{1,0:T(8,128)(2,1)}, bf16[448,768]{1,0:T(8,128)(2,1)}, bf16[448,768]{1,0:T(8,128)(2,1)}) custom-call(s32[1]{0:T(128)} %bitcast.7.core_ref, bf16[224,768]{1,0:T(8,128)(2,1)} %get-tuple-element.147.query_ref, bf16[448,1536]{1,0:T(8,128)(2,1)} %get-tuple-element.148.key_ref.value_ref, ...), custom_call_target="tpu_custom_call" | custom-call | tf_op jit(solution)/shard_map/attend_back/pallas_call | solution.py:178
  255.4 4.8 %grad_blocks.4 = (bf16[8,48,768]{2,1,0:T(8,128)(2,1)}, bf16[8,48,768]{2,1,0:T(8,128)(2,1)}) custom-call(s32[4]{0:T(128)} %pad_add_fusion.1.where_ref, bf16[224,768]{1,0:T(8,128)(2,1)} %get-tuple-element.180.refs_0_, bf16[224,768]{1,0:T(8,128)(2,1)} %get-tuple-element.181.refs_1_.refs_0_, bf16[224,768]{1,0:T(8,128)(2,1)} %copy-done.27, ...), custom_call_target="tpu_custom_call" | custom-call | tf_op jit(solution)/shard_map/grad_blocks/pallas_call | solution.py:918
  264.2 5.8 %self_tail.1 = (f32[224,768]{1,0:T(8,128)}, bf16[224,768]{1,0:T(8,128)(2,1)}, bf16[768,128]{1,0:T(8,128)(2,1)}) custom-call(s32[1]{0:T(128)} %bitcast.7.core_ref, bf16[224,768]{1,0:T(8,128)(2,1)} %get-tuple-element.205.query_ref.refs_2_, bf16[448,768]{1,0:T(8,128)(2,1)} %get-tuple-element.206.refs_4_.kept_ref, bf16[448,768]{1,0:T(8,128)(2,1)} %get-tuple-element.207.sent_ref, ...), custom_call_target="tpu_custom_call" | custom-call | tf_op jit(solution)/shard_map/self_tail/pallas_call | solution.py:833
  274.6 3.2 grad_blocks.5
  279.8 7.3 %all-to-all-start.1 = ((bf16[16,48,768]{2,1,0:T(8,128)(2,1)}), bf16[16,48,768]{2,1,0:T(8,128)(2,1)S(1)}, u32[]{:S(2)}, u32[]{:S(2)}) async-start(bf16[16,48,768]{2,1,0:T(8,128)(2,1)} %bitcast.48), calls=%async_computation.1 | async-start | bytes 2359296 | tf_op jit(solution)/shard_map/all_to_all | solution.py:1283
  295.9 2.9 collective-permute-start.43
  298.8 8.6 %collective-permute-done.41 = bf16[4,48,768]{2,1,0:T(8,128)(2,1)} collective-permute-done((bf16[4,48,768]{2,1,0:T(8,128)(2,1)}, bf16[4,48,768]{2,1,0:T(8,128)(2,1)}, u32[]{:S(2)}, u32[]{:S(2)}) %collective-permute-start.41) | collective-permute-done | bytes 294944 | tf_op jit(solution)/shard_map/ppermute | solution.py:220
  309.1 16.4 %collective-permute-done.40 = bf16[4,48,1920]{2,1,0:T(8,128)(2,1)} collective-permute-done((bf16[4,48,1920]{2,1,0:T(8,128)(2,1)}, bf16[4,48,1920]{2,1,0:T(8,128)(2,1)}, u32[]{:S(2)}, u32[]{:S(2)}) %collective-permute-start.40) | collective-permute-done | bytes 737312 | tf_op jit(solution)/shard_map/ppermute | solution.py:216
  327.7 3.6 collective-permute-start.54
  336.2 4.2 %collective-permute-start.50 = (bf16[48,768]{1,0:T(8,128)(2,1)}, bf16[48,768]{1,0:T(8,128)(2,1)S(1)}, u32[]{:S(2)}, u32[]{:S(2)}) collective-permute-start(bf16[48,768]{1,0:T(8,128)(2,1)} %get-tuple-element.249), channel_id=1, source_target_pairs={{0,16},{2,18},{4,20},{6,22},{8,24},{10,26},{12,28},{14,30},{16,0},... | collective-permute-start | bytes 221192 | tf_op jit(solution)/shard_map/ppermute | solution.py:216
  345.9 3.7 collective-permute-done.55
  352.8 5.2 %collective-permute-start.44 = (bf16[48,512]{0,1:T(8,128)(2,1)S(1)}, bf16[48,512]{0,1:T(8,128)(2,1)S(1)}, u32[]{:S(2)}, u32[]{:S(2)}) collective-permute-start(bf16[48,512]{0,1:T(8,128)(2,1)S(1)} %get-tuple-element.244), channel_id=1, source_target_pairs={{0,8},{2,10},{4,12},{6,14},{8,0},{10,2},{12,4},{14,6},{16,24},{18,... | collective-permute-start | bytes 147464 | tf_op jit(solution)/shard_map/ppermute | solution.py:216
  363.9 4.9 %collective-permute-done.45 = bf16[48,512]{0,1:T(8,128)(2,1)S(1)} collective-permute-done((bf16[48,512]{0,1:T(8,128)(2,1)S(1)}, bf16[48,512]{0,1:T(8,128)(2,1)S(1)}, u32[]{:S(2)}, u32[]{:S(2)}) %collective-permute-start.45) | collective-permute-done | bytes 49184 | tf_op jit(solution)/shard_map/ppermute | solution.py:216
  369.9 4.1 %collective-permute-done.47 = bf16[48,512]{0,1:T(8,128)(2,1)S(1)} collective-permute-done((bf16[48,512]{0,1:T(8,128)(2,1)S(1)}, bf16[48,512]{0,1:T(8,128)(2,1)S(1)}, u32[]{:S(2)}, u32[]{:S(2)}) %collective-permute-start.47) | collective-permute-done | bytes 49184 | tf_op jit(solution)/shard_map/ppermute | solution.py:220
  (302 shorter events, 125.0 us)
Async XLA Ops:
  7.2 163.0 %all-gather.2.cloned.1.call-start = ((), (), s32[]{:S(2)}) async-start(), calls=%async_computation.3 | async-start | bytes 10027008 | tf_op jit(solution)/shard_map/all_gather | solution.py:1071
  27.0 20.2 %collective-permute-start.4 = (bf16[4,48,1280]{2,1,0:T(8,128)(2,1)S(1)}, bf16[4,48,1280]{2,1,0:T(8,128)(2,1)S(1)}, u32[]{:S(2)}, u32[]{:S(2)}) collective-permute-start(bf16[4,48,1280]{2,1,0:T(8,128)(2,1)S(1)} %pad_maximum_fusion.2.refs_0_), channel_id=1, source_target_pairs={{0,4},{2,6},{4,0},{6,2},{8,12},{10,14},{12,8},{14,10},{16,20},{18,... | collective-permute-start | bytes 1474568 | tf_op jit(solution)/shard_map/ppermute | solution.py:216
  28.5 18.7 %collective-permute-start.5 = (bf16[4,48,1280]{2,1,0:T(8,128)(2,1)S(1)}, bf16[4,48,1280]{2,1,0:T(8,128)(2,1)S(1)}, u32[]{:S(2)}, u32[]{:S(2)}) collective-permute-start(bf16[4,48,1280]{2,1,0:T(8,128)(2,1)S(1)} %pad_maximum_fusion.2.refs_0_), channel_id=1, source_target_pairs={{0,1},{1,0},{2,3},{3,2},{4,5},{5,4},{6,7},{7,6},{8,9},{9,8},{10,11... | collective-permute-start | bytes 1474568 | tf_op jit(solution)/shard_map/ppermute | solution.py:220
  48.1 47.8 %all-to-all-start = ((bf16[16,48,768]{2,1,0:T(8,128)(2,1)}), bf16[16,48,768]{2,1,0:T(8,128)(2,1)S(1)}, u32[]{:S(2)}, u32[]{:S(2)}) async-start(bf16[16,48,768]{2,1,0:T(8,128)(2,1)} %param.20), calls=%async_computation | async-start | bytes 2359296 | tf_op jit(solution)/shard_map/all_to_all | solution.py:1062
  53.3 290.2 %reduce-scatter.2.cloned.1.call-start = ((), (), s32[]{:S(2)}) async-start(), calls=%async_computation.4 | async-start | bytes 10027008 | tf_op jit(solution)/shard_map/reduce_scatter | solution.py:1240
  61.4 27.0 %collective-permute-start.14 = (bf16[4,48,1920]{2,1,0:T(8,128)(2,1)S(1)}, bf16[4,48,1920]{2,1,0:T(8,128)(2,1)}, u32[]{:S(2)}, u32[]{:S(2)}) collective-permute-start(bf16[4,48,1920]{2,1,0:T(8,128)(2,1)S(1)} %pad_maximum_fusion.refs_0_), channel_id=1, source_target_pairs={{0,4},{2,6},{4,0},{6,2},{8,12},{10,14},{12,8},{14,10},{16,20},{18,... | collective-permute-start | bytes 2211848 | tf_op jit(solution)/shard_map/ppermute | solution.py:216
  61.9 26.5 %collective-permute-start.15 = (bf16[4,48,1920]{2,1,0:T(8,128)(2,1)S(1)}, bf16[4,48,1920]{2,1,0:T(8,128)(2,1)}, u32[]{:S(2)}, u32[]{:S(2)}) collective-permute-start(bf16[4,48,1920]{2,1,0:T(8,128)(2,1)S(1)} %pad_maximum_fusion.refs_0_), channel_id=1, source_target_pairs={{0,1},{1,0},{2,3},{3,2},{4,5},{5,4},{6,7},{7,6},{8,9},{9,8},{10,11... | collective-permute-start | bytes 2211848 | tf_op jit(solution)/shard_map/ppermute | solution.py:220
  97.4 32.1 %collective-permute-start.20 = (bf16[768,768]{1,0:T(8,128)(2,1)S(1)}, bf16[768,768]{1,0:T(8,128)(2,1)S(1)}, u32[]{:S(2)}, u32[]{:S(2)}) collective-permute-start(bf16[768,768]{1,0:T(8,128)(2,1)S(1)} %bitcast.111), channel_id=1, source_target_pairs={{0,1},{1,0},{2,3},{3,2},{4,5},{5,4},{6,7},{7,6},{8,9},{9,8},{10,11... | collective-permute-start | bytes 3538952 | tf_op jit(solution)/shard_map/ppermute | solution.py:220
  98.4 31.1 %collective-permute-start.16 = (bf16[4,48,1920]{2,1,0:T(8,128)(2,1)}, bf16[4,48,1920]{2,1,0:T(8,128)(2,1)}, u32[]{:S(2)}, u32[]{:S(2)}) collective-permute-start(bf16[4,48,1920]{2,1,0:T(8,128)(2,1)} %collective-permute-done.15.refs_2_), channel_id=1, source_target_pairs={{0,4},{2,6},{4,0},{6,2},{8,12},{10,14},{12,8},{14,10},{16,20},{18,... | collective-permute-start | bytes 2211848 | tf_op jit(solution)/shard_map/ppermute | solution.py:216
  100.9 28.6 %collective-permute-start.17 = (bf16[4,48,1920]{2,1,0:T(8,128)(2,1)S(1)}, bf16[4,48,1920]{2,1,0:T(8,128)(2,1)}, u32[]{:S(2)}, u32[]{:S(2)}) collective-permute-start(bf16[4,48,1920]{2,1,0:T(8,128)(2,1)S(1)} %pad_maximum_fusion.refs_0_), channel_id=1, source_target_pairs={{0,2},{2,0},{4,6},{6,4},{8,10},{10,8},{12,14},{14,12},{16,18},{18,... | collective-permute-start | bytes 2211848 | tf_op jit(solution)/shard_map/ppermute | solution.py:216
  102.4 27.0 %collective-permute-start.18 = (bf16[4,48,1920]{2,1,0:T(8,128)(2,1)}, bf16[4,48,1920]{2,1,0:T(8,128)(2,1)}, u32[]{:S(2)}, u32[]{:S(2)}) collective-permute-start(bf16[4,48,1920]{2,1,0:T(8,128)(2,1)} %collective-permute-done.14.refs_1_), channel_id=1, source_target_pairs={{0,2},{2,0},{4,6},{6,4},{8,10},{10,8},{12,14},{14,12},{16,18},{18,... | collective-permute-start | bytes 2211848 | tf_op jit(solution)/shard_map/ppermute | solution.py:216
  102.4 27.0 %collective-permute-start.19 = (bf16[4,48,1920]{2,1,0:T(8,128)(2,1)}, bf16[4,48,1920]{2,1,0:T(8,128)(2,1)}, u32[]{:S(2)}, u32[]{:S(2)}) collective-permute-start(bf16[4,48,1920]{2,1,0:T(8,128)(2,1)} %collective-permute-done.15.refs_2_), channel_id=1, source_target_pairs={{0,2},{2,0},{4,6},{6,4},{8,10},{10,8},{12,14},{14,12},{16,18},{18,... | collective-permute-start | bytes 2211848 | tf_op jit(solution)/shard_map/ppermute | solution.py:216
  207.6 20.2 %collective-permute-start.26 = (bf16[1536,768]{1,0:T(8,128)(2,1)}, bf16[1536,768]{1,0:T(8,128)(2,1)}, u32[]{:S(2)}, u32[]{:S(2)}) collective-permute-start(bf16[1536,768]{1,0:T(8,128)(2,1)} %get-tuple-element.188.sent_ref), channel_id=1, source_target_pairs={{0,2},{2,0},{4,6},{6,4},{8,10},{10,8},{12,14},{14,12},{16,18},{18,... | collective-permute-start | bytes 7077896 | tf_op jit(solution)/shard_map/ppermute | solution.py:216
  208.1 18.3 %collective-permute-start.25 = (bf16[768,768]{1,0:T(8,128)(2,1)S(1)}, bf16[768,768]{1,0:T(8,128)(2,1)}, u32[]{:S(2)}, u32[]{:S(2)}) collective-permute-start(bf16[768,768]{1,0:T(8,128)(2,1)S(1)} %copy-done.5), channel_id=1, source_target_pairs={{0,2},{2,0},{4,6},{6,4},{8,10},{10,8},{12,14},{14,12},{16,18},{18,... | collective-permute-start | bytes 3538952 | tf_op jit(solution)/shard_map/ppermute | solution.py:216
  208.5 16.2 %collective-permute-start.31 = (bf16[224,768]{1,0:T(8,128)(2,1)}, bf16[224,768]{1,0:T(8,128)(2,1)}, u32[]{:S(2)}, u32[]{:S(2)}) collective-permute-start(bf16[224,768]{1,0:T(8,128)(2,1)} %get-tuple-element.154.refs_14_), channel_id=1, source_target_pairs={{0,2},{2,0},{4,6},{6,4},{8,10},{10,8},{12,14},{14,12},{16,18},{18,... | collective-permute-start | bytes 1032200 | tf_op jit(solution)/shard_map/ppermute | solution.py:216
  208.6 17.1 %collective-permute-start.27 = (bf16[224,768]{1,0:T(8,128)(2,1)S(1)}, bf16[224,768]{1,0:T(8,128)(2,1)}, u32[]{:S(2)}, u32[]{:S(2)}) collective-permute-start(bf16[224,768]{1,0:T(8,128)(2,1)S(1)} %copy-done.13), channel_id=1, source_target_pairs={{0,2},{2,0},{4,6},{6,4},{8,10},{10,8},{12,14},{14,12},{16,18},{18,... | collective-permute-start | bytes 1032200 | tf_op jit(solution)/shard_map/ppermute | solution.py:216
  224.7 45.9 %collective-permute-start.38 = (bf16[768,768]{1,0:T(8,128)(2,1)}, bf16[768,768]{1,0:T(8,128)(2,1)}, u32[]{:S(2)}, u32[]{:S(2)}) collective-permute-start(bf16[768,768]{1,0:T(8,128)(2,1)} %get-tuple-element.221), channel_id=1, source_target_pairs={{0,1},{1,0},{2,3},{3,2},{4,5},{5,4},{6,7},{7,6},{8,9},{9,8},{10,11... | collective-permute-start | bytes 3538952 | tf_op jit(solution)/shard_map/ppermute | solution.py:220
  250.3 39.8 %collective-permute-start.34 = (bf16[8,48,1920]{2,1,0:T(8,128)(2,1)}, bf16[8,48,1920]{2,1,0:T(8,128)(2,1)S(1)}, u32[]{:S(2)}, u32[]{:S(2)}) collective-permute-start(bf16[8,48,1920]{2,1,0:T(8,128)(2,1)} %get-tuple-element.213), channel_id=1, source_target_pairs={{0,1},{1,0},{2,3},{3,2},{4,5},{5,4},{6,7},{7,6},{8,9},{9,8},{10,11... | collective-permute-start | bytes 4423688 | tf_op jit(solution)/shard_map/ppermute | solution.py:220
  260.2 28.0 %collective-permute-start.35 = (bf16[8,48,768]{2,1,0:T(8,128)(2,1)}, bf16[8,48,768]{2,1,0:T(8,128)(2,1)}, u32[]{:S(2)}, u32[]{:S(2)}) collective-permute-start(bf16[8,48,768]{2,1,0:T(8,128)(2,1)} %get-tuple-element.215), channel_id=1, source_target_pairs={{0,4},{2,6},{4,0},{6,2},{8,12},{10,14},{12,8},{14,10},{16,20},{18,... | collective-permute-start | bytes 1769480 | tf_op jit(solution)/shard_map/ppermute | solution.py:216
  277.7 16.4 %collective-permute-start.39 = (bf16[8,48,512]{2,1,0:T(8,128)(2,1)}, bf16[8,48,512]{2,1,0:T(8,128)(2,1)}, u32[]{:S(2)}, u32[]{:S(2)}) collective-permute-start(bf16[8,48,512]{2,1,0:T(8,128)(2,1)} %get-tuple-element.224), channel_id=1, source_target_pairs={{0,1},{1,0},{2,3},{3,2},{4,5},{5,4},{6,7},{7,6},{8,9},{9,8},{10,11... | collective-permute-start | bytes 1179656 | tf_op jit(solution)/shard_map/ppermute | solution.py:220
  278.4 49.2 %collective-permute-start.42 = (bf16[224,768]{1,0:T(8,128)(2,1)}, bf16[224,768]{1,0:T(8,128)(2,1)}, u32[]{:S(2)}, u32[]{:S(2)}) collective-permute-start(bf16[224,768]{1,0:T(8,128)(2,1)} %get-tuple-element.232), channel_id=1, source_target_pairs={{0,1},{1,0},{2,3},{3,2},{4,5},{5,4},{6,7},{7,6},{8,9},{9,8},{10,11... | collective-permute-start | bytes 1032200 | tf_op jit(solution)/shard_map/ppermute | solution.py:220
  279.8 63.7 %all-to-all-start.1 = ((bf16[16,48,768]{2,1,0:T(8,128)(2,1)}), bf16[16,48,768]{2,1,0:T(8,128)(2,1)S(1)}, u32[]{:S(2)}, u32[]{:S(2)}) async-start(bf16[16,48,768]{2,1,0:T(8,128)(2,1)} %bitcast.48), calls=%async_computation.1 | async-start | bytes 2359296 | tf_op jit(solution)/shard_map/all_to_all | solution.py:1283
  291.5 15.9 %collective-permute-start.41 = (bf16[4,48,768]{2,1,0:T(8,128)(2,1)}, bf16[4,48,768]{2,1,0:T(8,128)(2,1)}, u32[]{:S(2)}, u32[]{:S(2)}) collective-permute-start(bf16[4,48,768]{2,1,0:T(8,128)(2,1)} %get-tuple-element.230), channel_id=1, source_target_pairs={{0,1},{1,0},{2,3},{3,2},{4,5},{5,4},{6,7},{7,6},{8,9},{9,8},{10,11... | collective-permute-start | bytes 884744 | tf_op jit(solution)/shard_map/ppermute | solution.py:220
  291.6 33.9 %collective-permute-start.40 = (bf16[4,48,1920]{2,1,0:T(8,128)(2,1)}, bf16[4,48,1920]{2,1,0:T(8,128)(2,1)}, u32[]{:S(2)}, u32[]{:S(2)}) collective-permute-start(bf16[4,48,1920]{2,1,0:T(8,128)(2,1)} %get-tuple-element.228), channel_id=1, source_target_pairs={{0,4},{2,6},{4,0},{6,2},{8,12},{10,14},{12,8},{14,10},{16,20},{18,... | collective-permute-start | bytes 2211848 | tf_op jit(solution)/shard_map/ppermute | solution.py:216
  295.9 40.4 %collective-permute-start.43 = (bf16[4,48,512]{1,2,0:T(8,128)(2,1)S(1)}, bf16[4,48,512]{1,2,0:T(8,128)(2,1)S(1)}, u32[]{:S(2)}, u32[]{:S(2)}) collective-permute-start(bf16[4,48,512]{1,2,0:T(8,128)(2,1)S(1)} %bitcast.129), channel_id=1, source_target_pairs={{0,4},{2,6},{4,0},{6,2},{8,12},{10,14},{12,8},{14,10},{16,20},{18,... | collective-permute-start | bytes 589832 | tf_op jit(solution)/shard_map/ppermute | solution.py:216
  327.7 15.8 %collective-permute-start.54 = (bf16[48,1920]{1,0:T(8,128)(2,1)}, bf16[48,1920]{1,0:T(8,128)(2,1)S(1)}, u32[]{:S(2)}, u32[]{:S(2)}) collective-permute-start(bf16[48,1920]{1,0:T(8,128)(2,1)} %get-tuple-element.252), channel_id=1, source_target_pairs={{0,8},{2,10},{4,12},{6,14},{8,0},{10,2},{12,4},{14,6},{16,24},{18,... | collective-permute-start | bytes 552968 | tf_op jit(solution)/shard_map/ppermute | solution.py:216
  331.3 18.3 %collective-permute-start.55 = (bf16[48,1920]{1,0:T(8,128)(2,1)}, bf16[48,1920]{1,0:T(8,128)(2,1)}, u32[]{:S(2)}, u32[]{:S(2)}) collective-permute-start(bf16[48,1920]{1,0:T(8,128)(2,1)} %get-tuple-element.253), channel_id=1, source_target_pairs={{0,16},{2,18},{4,20},{6,22},{8,24},{10,26},{12,28},{14,30},{16,0},... | collective-permute-start | bytes 552968 | tf_op jit(solution)/shard_map/ppermute | solution.py:216
  332.8 17.6 %collective-permute-start.56 = (bf16[48,1920]{1,0:T(8,128)(2,1)}, bf16[48,1920]{1,0:T(8,128)(2,1)}, u32[]{:S(2)}, u32[]{:S(2)}) collective-permute-start(bf16[48,1920]{1,0:T(8,128)(2,1)} %get-tuple-element.254), channel_id=1, source_target_pairs={{0,24},{2,26},{4,28},{6,30},{8,16},{10,18},{12,20},{14,22},{16,8},... | collective-permute-start | bytes 552968 | tf_op jit(solution)/shard_map/ppermute | solution.py:216
  334.3 18.6 %collective-permute-start.49 = (bf16[48,768]{1,0:T(8,128)(2,1)}, bf16[48,768]{1,0:T(8,128)(2,1)}, u32[]{:S(2)}, u32[]{:S(2)}) collective-permute-start(bf16[48,768]{1,0:T(8,128)(2,1)} %get-tuple-element.248), channel_id=1, source_target_pairs={{0,8},{2,10},{4,12},{6,14},{8,0},{10,2},{12,4},{14,6},{16,24},{18,... | collective-permute-start | bytes 221192 | tf_op jit(solution)/shard_map/ppermute | solution.py:216
  336.2 21.8 %collective-permute-start.50 = (bf16[48,768]{1,0:T(8,128)(2,1)}, bf16[48,768]{1,0:T(8,128)(2,1)S(1)}, u32[]{:S(2)}, u32[]{:S(2)}) collective-permute-start(bf16[48,768]{1,0:T(8,128)(2,1)} %get-tuple-element.249), channel_id=1, source_target_pairs={{0,16},{2,18},{4,20},{6,22},{8,24},{10,26},{12,28},{14,30},{16,0},... | collective-permute-start | bytes 221192 | tf_op jit(solution)/shard_map/ppermute | solution.py:216
  349.6 31.2 %collective-permute-start.59 = (bf16[384,768]{1,0:T(8,128)(2,1)}, bf16[384,768]{1,0:T(8,128)(2,1)S(1)}, u32[]{:S(2)}, u32[]{:S(2)}) collective-permute-start(bf16[384,768]{1,0:T(8,128)(2,1)} %bitcast.127), channel_id=1, source_target_pairs={{0,1},{1,0},{2,3},{3,2},{4,5},{5,4},{6,7},{7,6},{8,9},{9,8},{10,11... | collective-permute-start | bytes 1769480 | tf_op jit(solution)/shard_map/ppermute | solution.py:220
  351.5 24.8 %collective-permute-start.57 = (bf16[48,1920]{1,0:T(8,128)(2,1)S(1)}, bf16[48,1920]{1,0:T(8,128)(2,1)S(1)}, u32[]{:S(2)}, u32[]{:S(2)}) collective-permute-start(bf16[48,1920]{1,0:T(8,128)(2,1)S(1)} %reduce-precision_convert_fusion), channel_id=1, source_target_pairs={{0,1},{1,0},{2,3},{3,2},{4,5},{5,4},{6,7},{7,6},{8,9},{9,8},{10,11... | collective-permute-start | bytes 552968 | tf_op jit(solution)/shard_map/ppermute | solution.py:220
  (69 other events, 686.2 us)
Sparse Core Ops, SparseCore 0:
  47.4 117.6 all-gather.1
  188.7 148.4 reduce-scatter.1
